TPU v7x, 256 devices: a whole 4x4x8 slice. The times are simulated.
256 devices in a mesh: db: 64 (over x, z, core), pb: 4 (over y).
Axes of the slice: x: 4, y: 4, z: 8, core: 2. Of those that a mesh axis runs over, the one named last changes fastest.
Arguments:
- affinity_tiles: bfloat16 [1024, 16, 128, 128], P('db', None, 'pb'), as said below
- block_ids: int32 [1024, 16], P('db'), may hold values from 0 to 1023, as said below
- valid_counts: int32 [1024], P('db'), may hold values from 4 to 16
- queries: bfloat16 [131072, 512], P('db', 'pb'), may hold values from -6 to 6
Outputs:
- ranked: bfloat16 [131072, 512], P('db', 'pb')
Inputs may be any that keep to these rules, and one draw needn't show every extreme that they name: `block_ids`: slot 0 of row block b names b itself. Slots 1 and 2 name blocks held by other indices of db; over the 16 row blocks of one index of db, these slots name blocks of any single other index at most 2 times, and exactly 2 times for some index. Slots 3 and above name blocks no more than 2 blocks outside the range of the row block's own index of db. `affinity_tiles`: tiles in slots at or beyond their row block's count are zero.
All inputs are finite; a program needn't handle non-finite values.
Results may differ from a plain program's by a relative error of at most 0.0034.
Values may be sent and summed in bfloat16 or wider, within the bound.
No kernel may reach another device: no remote copies, remote signals or barrier semaphores. Data moves between devices by JAX's collectives and lax.ppermute only.
A program may use at most 192 MiB of HBM per device.

v0:
```python
import jax
import jax.numpy as jnp
from jax import lax
from jax.sharding import PartitionSpec as P

EDGE = 2
ITERS = 2


def padded(block, sides, width):
    for axis, dim in sides:
        count = lax.axis_size(axis)
        forward = [(i, i + 1) for i in range(count - 1)]
        backward = [(target, source) for source, target in forward]
        low = lax.ppermute(
            lax.slice_in_dim(block, block.shape[dim] - width, None, axis=dim), axis, forward
        )
        high = lax.ppermute(lax.slice_in_dim(block, 0, width, axis=dim), axis, backward)
        block = jnp.concatenate([low, block, high], axis=dim)
    return block


def contract(tile_set, panel_set):
    return jnp.einsum("rtij,rtjq->riq", tile_set, panel_set, preferred_element_type=jnp.float32)


def on_device(affinity_tiles, block_ids, valid_counts, queries):
    row_blocks, slot_count = block_ids.shape
    block_size = affinity_tiles.shape[3]
    query_cols = queries.shape[1]
    device_count = lax.axis_size("db")
    first_block = lax.axis_index("db") * row_blocks
    capacity = max(2, (4 * row_blocks + device_count - 1) // device_count)
    full_tiles = lax.all_gather(affinity_tiles, "pb", axis=2, tiled=True)
    slot_mask = (jnp.arange(slot_count, dtype=jnp.int32)[None, :] < valid_counts[:, None]).astype(
        jnp.bfloat16
    )
    full_tiles = full_tiles * slot_mask[:, :, None, None]
    near_index = jnp.concatenate([block_ids[:, :1], block_ids[:, 3:]], axis=1) - first_block + EDGE
    far_global = block_ids[:, 1:3].reshape(-1)
    ranking = queries.reshape(row_blocks, block_size, query_cols)
    prior_field = ranking.astype(jnp.float32)
    owner_index = far_global // row_blocks
    owner_hits = (
        owner_index[:, None] == jnp.arange(device_count, dtype=jnp.int32)[None, :]
    ).astype(jnp.int32)
    order_rank = jnp.sum(jnp.cumsum(owner_hits, axis=0) * owner_hits, axis=1) - 1
    slot_index = owner_index * capacity + order_rank
    slot_hits = (
        slot_index[:, None] == jnp.arange(device_count * capacity, dtype=jnp.int32)[None, :]
    ).astype(jnp.int32)
    wanted = jnp.sum(slot_hits * (far_global % row_blocks)[:, None], axis=0).reshape(
        device_count, capacity
    )
    asked_blocks = lax.all_to_all(wanted, "db", split_axis=0, concat_axis=0, tiled=True).reshape(-1)
    far_slot = slot_index.reshape(row_blocks, 2)
    for step_index in range(ITERS):
        outgoing = jnp.take(ranking, asked_blocks, axis=0).reshape(
            device_count, capacity, block_size, query_cols
        )
        arrived = lax.all_to_all(outgoing, "db", split_axis=0, concat_axis=0, tiled=True)
        arrived = arrived.reshape(device_count * capacity, block_size, query_cols)
        far_panels = jnp.take(arrived, far_slot, axis=0)
        extended = padded(ranking, (("db", 0),), EDGE)
        near_panels = jnp.take(extended, near_index, axis=0)
        panels = jnp.concatenate([near_panels[:, :1], far_panels, near_panels[:, 1:]], axis=1)
        summed = contract(full_tiles, panels)
        ranking = (0.99 * summed + prior_field).astype(jnp.bfloat16)
    return ranking.reshape(row_blocks * block_size, query_cols)


def solution(mesh):
    return jax.shard_map(
        on_device,
        mesh=mesh,
        in_specs=(P("db", None, "pb", None), P("db", None), P("db"), P("db", "pb")),
        out_specs=P("db", "pb"),
        check_vma=False,
    )
```

profile of v0, /device:TPU:1, one launch (start us, length us, event | category | flops | bytes accessed | tf_op | source)
XLA Modules:
  0.0 311.5 jit_solution(15627738038291390927)
XLA Ops:
  8.7 22.1 %all_to_all.19 = s32[64,1,2]{2,1,0:T(1,128)S(1)} all-to-all(s32[64,1,2]{2,1,0:T(1,128)S(1)} %bitcast.42), channel_id=1, replica_groups=mesh['db'=64,'pb'=4] {'db'}, dimensions={0} | all-to-all | bytes 1024 | tf_op jit(solution)/shard_map/all_to_all | solution.py:55
  32.2 4.1 %gather_fusion.1 = bf16[128,128,128]{2,1,0:T(8,128)(2,1)} fusion(bf16[16,128,128]{2,1,0:T(8,128)(2,1)} %bitcast.32, s32[1024]{0:T(1024)S(1)} %pad_clamp_fusion.1), kind=kCustom, calls=%fused_computation.1.clone | custom fusion | bytes 8389120 | tf_op jit(solution)/shard_map/jit(_take)/gather | solution.py:58
  36.3 4.7 %broadcast_select_fusion.3 = bf16[128,128,128]{2,1,0:T(8,128)(2,1)} fusion(bf16[128,128,128]{2,1,0:T(8,128)(2,1)} %gather_fusion.1, pred[128]{0:T(512)(128)(4,1)S(1)} %compare_and_fusion.2), kind=kLoop, calls=%fused_computation.25 | loop fusion | flops 2097152 | bytes 8388736 | tf_op jit(solution)/shard_map/jit(_take)/select_n | solution.py:58
  41.0 5.7 %all-to-all-start.1 = ((bf16[64,2,128,128]{3,2,1,0:T(8,128)(2,1)}), bf16[64,2,128,128]{3,2,1,0:T(8,128)(2,1)}, u32[]{:S(2)}, u32[]{:S(2)}) async-start(bf16[64,2,128,128]{3,2,1,0:T(8,128)(2,1)} %bitcast.38), calls=%async_computation.1 | async-start | bytes 8388608 | tf_op jit(solution)/shard_map/all_to_all | solution.py:61
  46.8 3.5 %collective-permute-start = (bf16[2,128,128]{2,1,0:T(8,128)(2,1)S(1)}, bf16[2,128,128]{2,1,0:T(8,128)(2,1)S(1)}, u32[]{:S(2)}, u32[]{:S(2)}) collective-permute-start(bf16[2,128,128]{2,1,0:T(8,128)(2,1)S(1)} %bitcast.45), channel_id=1, source_target_pairs={{0,4},{4,8},{8,12},{12,16},{16,20},{20,24},{24,28},{28,32},{32,36}... | collective-permute-start | bytes 196616 | tf_op jit(solution)/shard_map/ppermute | solution.py:15
  53.3 83.4 %collective-permute-done = bf16[2,128,128]{2,1,0:T(8,128)(2,1)S(1)} collective-permute-done((bf16[2,128,128]{2,1,0:T(8,128)(2,1)S(1)}, bf16[2,128,128]{2,1,0:T(8,128)(2,1)S(1)}, u32[]{:S(2)}, u32[]{:S(2)}) %collective-permute-start) | collective-permute-done | bytes 65568 | tf_op jit(solution)/shard_map/ppermute | solution.py:15
  136.7 3.0 collective-permute-done.1
  139.8 8.4 %gather_fusion = bf16[224,128,128]{2,1,0:T(8,128)(2,1)} fusion(bf16[20,128,128]{2,1,0:T(8,128)(2,1)S(1)} %pad_maximum_fusion, s32[1024]{0:T(1024)S(1)} %pad_clamp_fusion.2), kind=kCustom, calls=%fused_computation.clone | custom fusion | bytes 14680960 | tf_op jit(solution)/shard_map/jit(_take)/gather | solution.py:65
  148.2 3.8 %broadcast_select_fusion = bf16[16,14,128,128]{3,2,1,0:T(8,128)(2,1)S(1)} fusion(bf16[16,14,128,128]{3,2,1,0:T(8,128)(2,1)} %bitcast.37, pred[16,14]{1,0:T(8,128)(4,1)S(1)} %get-tuple-element.10), kind=kLoop, calls=%fused_computation.20 | loop fusion | flops 3670016 | bytes 14680288 | tf_op jit(solution)/shard_map/jit(_take)/select_n | solution.py:65
  152.0 4.4 %slice.65 = bf16[16,13,128,128]{3,2,1,0:T(8,128)(2,1)} slice(bf16[16,14,128,128]{3,2,1,0:T(8,128)(2,1)S(1)} %broadcast_select_fusion), slice={[0:16], [1:14], [0:128], [0:128]} | slice | bytes 13631488 | tf_op jit(solution)/shard_map/slice | solution.py:66
  156.4 2.9 gather_fusion.2
  159.6 7.2 %fusion.51 = bf16[16,128,128]{2,1,0:T(8,128)(2,1)S(1)} fusion(bf16[16,128,128]{2,1,0:T(8,128)(2,1)S(1)} %bitcast.34, bf16[16,13,128,128]{3,2,1,0:T(8,128)(2,1)} %slice.65, bf16[16,2,128,128]{3,2,1,0:T(8,128)(2,1)S(1)} %broadcast_select_fusion.5, bf16[16,1,128,128]{3,2,1,0:T(8,128)(2,1)S(1)} %slice.64, ...), kind=kOutput, calls=%fused_computation.33 | convolution fusion | flops 1087373312 | bytes 17826304 | tf_op jit(solution)/shard_map/rtij,rtjq->riq/dot_general | solution.py:24
  166.8 3.1 gather_fusion.4
  169.8 4.6 %broadcast_select_fusion.2 = bf16[128,128,128]{2,1,0:T(8,128)(2,1)} fusion(bf16[128,128,128]{2,1,0:T(8,128)(2,1)} %gather_fusion.4, pred[128]{0:T(512)(128)(4,1)S(1)} %compare_and_fusion.2), kind=kLoop, calls=%fused_computation.24 | loop fusion | flops 2097152 | bytes 8388736 | tf_op jit(solution)/shard_map/jit(_take)/select_n | solution.py:58
  174.5 9.4 %all-to-all-start.2 = ((bf16[64,2,128,128]{3,2,1,0:T(8,128)(2,1)}), bf16[64,2,128,128]{3,2,1,0:T(8,128)(2,1)}, u32[]{:S(2)}, u32[]{:S(2)}) async-start(bf16[64,2,128,128]{3,2,1,0:T(8,128)(2,1)} %bitcast.39), calls=%async_computation.2 | async-start | bytes 8388608 | tf_op jit(solution)/shard_map/all_to_all | solution.py:61
  183.9 3.5 %collective-permute-start.2 = (bf16[2,128,128]{2,1,0:T(8,128)(2,1)S(1)}, bf16[2,128,128]{2,1,0:T(8,128)(2,1)S(1)}, u32[]{:S(2)}, u32[]{:S(2)}) collective-permute-start(bf16[2,128,128]{2,1,0:T(8,128)(2,1)S(1)} %get-tuple-element.12), channel_id=1, source_target_pairs={{0,4},{4,8},{8,12},{12,16},{16,20},{20,24},{24,28},{28,32},{32,36}... | collective-permute-start | bytes 196616 | tf_op jit(solution)/shard_map/ppermute | solution.py:15
  187.5 2.1 collective-permute-start.3
  189.6 84.3 %collective-permute-done.2 = bf16[2,128,128]{2,1,0:T(8,128)(2,1)S(1)} collective-permute-done((bf16[2,128,128]{2,1,0:T(8,128)(2,1)S(1)}, bf16[2,128,128]{2,1,0:T(8,128)(2,1)S(1)}, u32[]{:S(2)}, u32[]{:S(2)}) %collective-permute-start.2) | collective-permute-done | bytes 65568 | tf_op jit(solution)/shard_map/ppermute | solution.py:15
  273.9 3.0 collective-permute-done.3
  277.0 8.4 %gather_fusion.3 = bf16[224,128,128]{2,1,0:T(8,128)(2,1)} fusion(bf16[20,128,128]{2,1,0:T(8,128)(2,1)S(1)} %pad_maximum_fusion.1, s32[1024]{0:T(1024)S(1)} %pad_clamp_fusion.2), kind=kCustom, calls=%fused_computation.3.clone | custom fusion | bytes 14680960 | tf_op jit(solution)/shard_map/jit(_take)/gather | solution.py:65
  285.3 3.8 %broadcast_select_fusion.1 = bf16[16,14,128,128]{3,2,1,0:T(8,128)(2,1)S(1)} fusion(bf16[16,14,128,128]{3,2,1,0:T(8,128)(2,1)} %bitcast.36, pred[16,14]{1,0:T(8,128)(4,1)S(1)} %get-tuple-element.10), kind=kLoop, calls=%fused_computation.21 | loop fusion | flops 3670016 | bytes 14680288 | tf_op jit(solution)/shard_map/jit(_take)/select_n | solution.py:65
  289.2 4.4 %slice.69 = bf16[16,13,128,128]{3,2,1,0:T(8,128)(2,1)} slice(bf16[16,14,128,128]{3,2,1,0:T(8,128)(2,1)S(1)} %broadcast_select_fusion.1), slice={[0:16], [1:14], [0:128], [0:128]} | slice | bytes 13631488 | tf_op jit(solution)/shard_map/slice | solution.py:66
  293.6 2.9 gather_fusion.5
  296.7 8.0 %fusion.46 = bf16[16,128,128]{2,1,0:T(8,128)(2,1)} fusion(bf16[16,128,128]{2,1,0:T(8,128)(2,1)S(1)} %bitcast.35, bf16[16,13,128,128]{3,2,1,0:T(8,128)(2,1)} %slice.69, bf16[16,2,128,128]{3,2,1,0:T(8,128)(2,1)S(1)} %broadcast_select_fusion.4, bf16[16,1,128,128]{3,2,1,0:T(8,128)(2,1)S(1)} %slice.68, ...), kind=kOutput, calls=%fused_computation.32 | convolution fusion | flops 1087373312 | bytes 17826304 | tf_op jit(solution)/shard_map/rtij,rtjq->riq/dot_general | solution.py:24
  (48 shorter events, 7.1 us)
Async XLA Ops:
  6.5 153.0 %all-gather.2.cloned.1.call-start = ((), (), s32[]{:S(2)}) async-start(), calls=%async_computation.3 | async-start | bytes 10485760 | tf_op jit(solution)/shard_map/all_gather | solution.py:34
  36.3 10.4 %copy-start = (bf16[2048,128]{1,0:T(8,128)(2,1)S(1)}, bf16[2048,128]{1,0:T(8,128)(2,1)}, u32[]{:S(2)}) copy-start(bf16[2048,128]{1,0:T(8,128)(2,1)} %param.13) | copy-start | bytes 1572868
  36.3 16.2 %copy-start.1 = (s32[16,16]{1,0:T(8,128)S(1)}, s32[16,16]{1,0:T(8,128)}, u32[]{:S(2)}) copy-start(s32[16,16]{1,0:T(8,128)} %param.11) | copy-start | bytes 3076
  36.3 16.9 %copy-start.2 = (s32[16]{0:T(128)S(1)}, s32[16]{0:T(128)}, u32[]{:S(2)}) copy-start(s32[16]{0:T(128)} %param.12) | copy-start | bytes 196
  41.0 115.4 %all-to-all-start.1 = ((bf16[64,2,128,128]{3,2,1,0:T(8,128)(2,1)}), bf16[64,2,128,128]{3,2,1,0:T(8,128)(2,1)}, u32[]{:S(2)}, u32[]{:S(2)}) async-start(bf16[64,2,128,128]{3,2,1,0:T(8,128)(2,1)} %bitcast.38), calls=%async_computation.1 | async-start | bytes 8388608 | tf_op jit(solution)/shard_map/all_to_all | solution.py:61
  46.8 90.0 %collective-permute-start = (bf16[2,128,128]{2,1,0:T(8,128)(2,1)S(1)}, bf16[2,128,128]{2,1,0:T(8,128)(2,1)S(1)}, u32[]{:S(2)}, u32[]{:S(2)}) collective-permute-start(bf16[2,128,128]{2,1,0:T(8,128)(2,1)S(1)} %bitcast.45), channel_id=1, source_target_pairs={{0,4},{4,8},{8,12},{12,16},{16,20},{20,24},{24,28},{28,32},{32,36}... | collective-permute-start | bytes 196616 | tf_op jit(solution)/shard_map/ppermute | solution.py:15
  50.3 89.4 %collective-permute-start.1 = (bf16[2,128,128]{2,1,0:T(8,128)(2,1)S(1)}, bf16[2,128,128]{2,1,0:T(8,128)(2,1)S(1)}, u32[]{:S(2)}, u32[]{:S(2)}) collective-permute-start(bf16[2,128,128]{2,1,0:T(8,128)(2,1)S(1)} %bitcast.44), channel_id=1, source_target_pairs={{4,0},{8,4},{12,8},{16,12},{20,16},{24,20},{28,24},{32,28},{36,32}... | collective-permute-start | bytes 196616 | tf_op jit(solution)/shard_map/ppermute | solution.py:18
  174.5 119.1 %all-to-all-start.2 = ((bf16[64,2,128,128]{3,2,1,0:T(8,128)(2,1)}), bf16[64,2,128,128]{3,2,1,0:T(8,128)(2,1)}, u32[]{:S(2)}, u32[]{:S(2)}) async-start(bf16[64,2,128,128]{3,2,1,0:T(8,128)(2,1)} %bitcast.39), calls=%async_computation.2 | async-start | bytes 8388608 | tf_op jit(solution)/shard_map/all_to_all | solution.py:61
  183.9 90.0 %collective-permute-start.2 = (bf16[2,128,128]{2,1,0:T(8,128)(2,1)S(1)}, bf16[2,128,128]{2,1,0:T(8,128)(2,1)S(1)}, u32[]{:S(2)}, u32[]{:S(2)}) collective-permute-start(bf16[2,128,128]{2,1,0:T(8,128)(2,1)S(1)} %get-tuple-element.12), channel_id=1, source_target_pairs={{0,4},{4,8},{8,12},{12,16},{16,20},{20,24},{24,28},{28,32},{32,36}... | collective-permute-start | bytes 196616 | tf_op jit(solution)/shard_map/ppermute | solution.py:15
  187.5 89.4 %collective-permute-start.3 = (bf16[2,128,128]{2,1,0:T(8,128)(2,1)S(1)}, bf16[2,128,128]{2,1,0:T(8,128)(2,1)S(1)}, u32[]{:S(2)}, u32[]{:S(2)}) collective-permute-start(bf16[2,128,128]{2,1,0:T(8,128)(2,1)S(1)} %get-tuple-element.13), channel_id=1, source_target_pairs={{4,0},{8,4},{12,8},{16,12},{20,16},{24,20},{28,24},{32,28},{36,32}... | collective-permute-start | bytes 196616 | tf_op jit(solution)/shard_map/ppermute | solution.py:18
Sparse Core Ops, SparseCore 0:
  9.2 89.4 all-gather.1
where the time goes:
time: 312 us
  waiting for transfers between devices  174 us (56%)
  local copies, waits for them, and re-layouts  41 us (13%)
  starting transfers between devices  26.4 us (8%)
  blocking collectives  22.1 us (7%)
  other arithmetic  18.8 us (6%)
  matrix products  15.2 us (5%)
  between operations  13.7 us (4%)
    ppermute x2, waiting for transfers between devices, padded(): lax.ppermute(lax.slice_in_dim(block, block.shape[dim] - width, None, axis...  168 us
    all_to_all x1, blocking collectives, on_device(): lax.all_to_all(wanted, 'db', split_axis=0, concat_axis=0, tiled=True)  22.1 us
    gather x2, local copies, waits for them, and re-layouts, on_device(): near_panels = jnp.take(extended, near_index, axis=0)  16.8 us
    dot_general x2, matrix products, contract(): jnp.einsum('rtij,rtjq->riq', tile_set, panel_set, preferred_element_type=...  15.2 us
    all_to_all x2, starting transfers between devices, on_device(): lax.all_to_all(outgoing, 'db', split_axis=0, concat_axis=0, tiled=True)  15.1 us
    select_n x3, other arithmetic, on_device(): jnp.take(ranking, asked_blocks, axis=0)  9.33 us
    slice x2, local copies, waits for them, and re-layouts, on_device(): near_panels[:, 1:]  8.73 us
    select_n x2, other arithmetic, on_device(): near_panels = jnp.take(extended, near_index, axis=0)  7.63 us
  transfers between devices with their start and end apart: 7, of which 4 were waited for; matrix products, arithmetic and copies ran while one was open for 16% of the time, Pallas kernels for 0%

commit v1 on v0

v1 whole, which is shorter than its diff:
```python
import jax
import jax.numpy as jnp
from jax import lax
from jax.experimental import pallas as pl
from jax.experimental.pallas import tpu as pltpu
from jax.sharding import PartitionSpec as P

EDGE = 2
ITERS = 2
NEAR = (0,) + tuple(range(3, 16))


def rows_to_pieces(wide, pieces_ref, blocks, size, owners):
    cols = wide.shape[1]
    for k in range(owners):
        for part in range(size // owners):
            rows = wide[pl.ds(part * owners + k, blocks, stride=size), :]
            pieces_ref[k * blocks : (k + 1) * blocks, part * cols : (part + 1) * cols] = rows.astype(
                pieces_ref.dtype
            )


def split_blocks(queries, blocks, size, owners):
    cols = queries.shape[1]

    def kernel(q_ref, pieces_ref, wide):
        wide[...] = q_ref[...].astype(jnp.float32)
        rows_to_pieces(wide, pieces_ref, blocks, size, owners)

    return pl.pallas_call(
        kernel,
        out_shape=jax.ShapeDtypeStruct((owners * blocks, size // owners * cols), queries.dtype),
        in_specs=[pl.BlockSpec(memory_space=pltpu.VMEM)],
        out_specs=pl.BlockSpec(memory_space=pltpu.VMEM),
        scratch_shapes=[pltpu.VMEM(queries.shape, jnp.float32)],
        name="split_blocks",
    )(queries)


def select_pieces(wanted, pieces):
    slots, devices = wanted.shape
    block_total, width = pieces.shape

    def kernel(wanted_ref, pieces_ref, out_ref, hits):
        for d in range(devices):
            ids = jnp.broadcast_to(wanted_ref[:, d : d + 1], (slots, block_total))
            column = lax.broadcasted_iota(jnp.int32, (slots, block_total), 1)
            hits[d * slots : (d + 1) * slots, :] = jnp.where(ids == column, 1.0, 0.0).astype(hits.dtype)
        step = 256

        @pl.loop(0, devices * slots // step)
        def _(i):
            rows = pl.ds(pl.multiple_of(i * step, step), step)
            out_ref[rows, :] = jnp.dot(
                hits[rows, :], pieces_ref[...], preferred_element_type=jnp.float32
            ).astype(out_ref.dtype)

    return pl.pallas_call(
        kernel,
        out_shape=jax.ShapeDtypeStruct((devices * slots, width), pieces.dtype),
        in_specs=[pl.BlockSpec(memory_space=pltpu.VMEM)] * 2,
        out_specs=pl.BlockSpec(memory_space=pltpu.VMEM),
        scratch_shapes=[pltpu.VMEM((devices * slots, block_total), jnp.bfloat16)],
        compiler_params=pltpu.CompilerParams(vmem_limit_bytes=32 << 20),
        cost_estimate=pl.CostEstimate(
            flops=2 * devices * slots * block_total * width, bytes_accessed=2 << 20, transcendentals=0
        ),
        name="select_pieces",
    )(wanted, pieces)


def near_product(near_index, counts, tiles, low, own, high):
    blocks, slots, rows, size = tiles.shape
    cols = own.shape[2]
    group = 4

    def kernel(index_ref, count_ref, tiles_ref, low_ref, own_ref, high_ref, out_ref, panels):
        step = pl.program_id(0)

        @pl.when(step == 0)
        def _():
            panels[:EDGE] = low_ref[...]
            panels[EDGE : EDGE + blocks] = own_ref[...]
            panels[EDGE + blocks :] = high_ref[...]

        for r in range(group):
            b = step * group + r
            total = jnp.zeros((rows, cols), jnp.float32)
            for first in range(0, len(NEAR), 2):
                pair = NEAR[first : first + 2]
                left = [
                    jnp.where(t < count_ref[b], tiles_ref[r, t], jnp.zeros((rows, size), tiles.dtype))
                    for t in pair
                ]
                right = [panels[index_ref[b, t]] for t in pair]
                total += jnp.dot(
                    jnp.concatenate(left, axis=1),
                    jnp.concatenate(right, axis=0),
                    preferred_element_type=jnp.float32,
                )
            out_ref[r] = total

    whole = pl.BlockSpec(memory_space=pltpu.VMEM)
    return pl.pallas_call(
        kernel,
        out_shape=jax.ShapeDtypeStruct((blocks, rows, cols), jnp.float32),
        grid_spec=pltpu.PrefetchScalarGridSpec(
            num_scalar_prefetch=2,
            grid=(blocks // group,),
            in_specs=[
                pl.BlockSpec((group, slots, rows, size), lambda i, *_: (i, 0, 0, 0)),
                whole,
                whole,
                whole,
            ],
            out_specs=pl.BlockSpec((group, rows, cols), lambda i, *_: (i, 0, 0)),
            scratch_shapes=[pltpu.VMEM((blocks + 2 * EDGE, size, cols), own.dtype)],
        ),
        compiler_params=pltpu.CompilerParams(vmem_limit_bytes=32 << 20),
        cost_estimate=pl.CostEstimate(
            flops=2 * blocks * len(NEAR) * rows * size * cols, bytes_accessed=9 << 20, transcendentals=0
        ),
        name="near_product",
    )(near_index, counts, tiles, low, own, high)


def add_far(counts, far_tiles, arrived, partial, queries, owners, split):
    blocks, _, size, _ = far_tiles.shape
    cols = queries.shape[1]
    far = arrived.shape[0] // owners

    def kernel(count_ref, tiles_ref, arrived_ref, partial_ref, q_ref, *rest):
        if split:
            out_ref, pieces_ref, upper, lower, wide = rest
        else:
            out_ref, upper, lower = rest
        upper[...] = arrived_ref[:, :cols].astype(jnp.float32)
        lower[...] = arrived_ref[:, cols:].astype(jnp.float32)
        for b in range(blocks):
            left, right = [], []
            for s in range(2):
                j = 2 * b + s
                left.append(
                    jnp.where(s + 1 < count_ref[b], tiles_ref[b, s], jnp.zeros((size, size), far_tiles.dtype))
                )
                for half in (upper, lower):
                    right.append(half[pl.ds(j, owners, stride=far), :].astype(far_tiles.dtype))
            total = partial_ref[b] + jnp.dot(
                jnp.concatenate(left, axis=1),
                jnp.concatenate(right, axis=0),
                preferred_element_type=jnp.float32,
            )
            rows = slice(b * size, (b + 1) * size)
            result = (0.99 * total + q_ref[rows, :].astype(jnp.float32)).astype(out_ref.dtype)
            out_ref[rows, :] = result
            if split:
                wide[rows, :] = result.astype(jnp.float32)
        if split:
            rows_to_pieces(wide, pieces_ref, blocks, size, owners)

    out_shape = [jax.ShapeDtypeStruct(queries.shape, queries.dtype)]
    scratch = [pltpu.VMEM((owners * far, cols), jnp.float32)] * 2
    if split:
        out_shape.append(jax.ShapeDtypeStruct((owners * blocks, size // owners * cols), queries.dtype))
        scratch.append(pltpu.VMEM(queries.shape, jnp.float32))
    return pl.pallas_call(
        kernel,
        out_shape=out_shape,
        in_specs=[pl.BlockSpec(memory_space=pltpu.SMEM)] + [pl.BlockSpec(memory_space=pltpu.VMEM)] * 4,
        out_specs=[pl.BlockSpec(memory_space=pltpu.VMEM)] * len(out_shape),
        scratch_shapes=scratch,
        compiler_params=pltpu.CompilerParams(vmem_limit_bytes=32 << 20),
        cost_estimate=pl.CostEstimate(
            flops=4 * blocks * size * size * cols, bytes_accessed=4 << 20, transcendentals=0
        ),
        name="add_far",
    )(counts, far_tiles, arrived, partial, queries)


def exchange(array, axis, parts):
    shape = array.shape
    array = array.reshape((parts, shape[0] // parts) + shape[1:])
    return lax.all_to_all(array, axis, split_axis=0, concat_axis=0, tiled=True).reshape(shape)


def on_device(affinity_tiles, block_ids, valid_counts, queries):
    blocks, slots = block_ids.shape
    size = affinity_tiles.shape[3]
    cols = queries.shape[1]
    owners = lax.axis_size("db")
    first_block = lax.axis_index("db") * blocks
    full_tiles = lax.all_gather(affinity_tiles, "pb", axis=2, tiled=True)
    far_tiles = full_tiles[:, 1:3]
    near_index = jnp.clip(block_ids - first_block + EDGE, 0, blocks + 2 * EDGE - 1)
    named = jnp.broadcast_to(block_ids[:, 1:3].reshape(1, 1, -1), (owners, 1, 2 * blocks))
    wanted = lax.all_to_all(named, "db", split_axis=0, concat_axis=0, tiled=True)
    wanted = wanted.reshape(owners, 2 * blocks).T
    up = [(i, i + 1) for i in range(owners - 1)]
    down = [(i + 1, i) for i in range(owners - 1)]
    ranking = queries
    pieces = split_blocks(queries, blocks, size, owners)
    for step in range(ITERS):
        own = ranking.reshape(blocks, size, cols)
        held = exchange(pieces, "db", owners)
        low = lax.ppermute(own[blocks - EDGE :], "db", up)
        high = lax.ppermute(own[:EDGE], "db", down)
        arrived = exchange(select_pieces(wanted, held), "db", owners)
        partial = near_product(near_index, valid_counts, full_tiles, low, own, high)
        done = add_far(valid_counts, far_tiles, arrived, partial, queries, owners, step < ITERS - 1)
        ranking = done[0]
        pieces = done[-1]
    return ranking


def solution(mesh):
    return jax.shard_map(
        on_device,
        mesh=mesh,
        in_specs=(P("db", None, "pb", None), P("db", None), P("db"), P("db", "pb")),
        out_specs=P("db", "pb"),
        check_vma=False,
    )
```

time: 312 us -> 193 us (0.62)
  waiting for transfers between devices: 174 us -> 73.9 us
  local copies, waits for them, and re-layouts: 41 us -> 9.67 us
  Pallas kernels: 0 us -> 25.2 us
  other arithmetic: 18.8 us -> 0.01 us
  starting transfers between devices: 26.4 us -> 41.8 us
  matrix products: 15.2 us -> 0 us
  blocking collectives: 22.1 us -> 27.8 us
    ppermute x4, waiting for transfers between devices: 174 us -> 19.9 us  [the longest x2 16.6 us: on_device(): low = lax.ppermute(own[blocks - EDGE:], 'db', up)]
    gather x6 -> x0, local copies, waits for them, and re-layouts: 29.8 us -> none  [the longest x2 16.8 us: on_device(): near_panels = jnp.take(extended, near_index, axis=0)]
    all_gather x1, waiting for transfers between devices: 0.02 us -> 29.3 us  [on_device(): full_tiles = lax.all_gather(affinity_tiles, 'pb', axis=2, tiled=True)]
    pallas_call x0 -> x7, Pallas kernels: none -> 25.2 us  [the longest x2 8.37 us: select_pieces(): pl.pallas_call(kernel, out_shape=jax.ShapeDtypeStruct((devices * slots, w...]
    all_to_all x2 -> x4, waiting for transfers between devices: 0.01 us -> 24.1 us  [the longest x3 17.3 us: exchange(): lax.all_to_all(array, axis, split_axis=0, concat_axis=0, tiled=True)]
    select_n x8 -> x0, other arithmetic: 17.3 us -> none  [the longest x3 9.33 us: on_device(): jnp.take(ranking, asked_blocks, axis=0)]
    all_to_all x2 -> x4, starting transfers between devices: 15.1 us -> 30.7 us  [the longest x3 17.7 us: exchange(): lax.all_to_all(array, axis, split_axis=0, concat_axis=0, tiled=True)]
    dot_general x2 -> x0, matrix products: 15.2 us -> none  [contract(): jnp.einsum('rtij,rtjq->riq', tile_set, panel_set, preferred_element_type=...]
  transfers between devices with their start and end apart: 7 -> 9, of which waited for: 4 -> 5; matrix products, arithmetic and copies ran while one was open for 16% -> 2% of each run, Pallas kernels for 0% -> 7%
where the time goes in v1:
time: 193 us; the launch traced here: 192 us
  waiting for transfers between devices  73.9 us (38%)
  starting transfers between devices  41.8 us (22%)
  blocking collectives  27.8 us (14%)
  Pallas kernels  25.2 us (13%)
  between operations  13.6 us (7%)
  local copies, waits for them, and re-layouts  9.67 us (5%)
    all_gather x1, waiting for transfers between devices, on_device(): full_tiles = lax.all_gather(affinity_tiles, 'pb', axis=2, tiled=True)  29.3 us
    all_to_all x1, blocking collectives, exchange(): lax.all_to_all(array, axis, split_axis=0, concat_axis=0, tiled=True)  27.8 us
    all_to_all x3, starting transfers between devices, exchange(): lax.all_to_all(array, axis, split_axis=0, concat_axis=0, tiled=True)  17.7 us
    all_to_all x3, waiting for transfers between devices, exchange(): lax.all_to_all(array, axis, split_axis=0, concat_axis=0, tiled=True)  17.3 us
    ppermute x2, waiting for transfers between devices, on_device(): low = lax.ppermute(own[blocks - EDGE:], 'db', up)  16.6 us
    all_to_all x1, starting transfers between devices, on_device(): lax.all_to_all(named, 'db', split_axis=0, concat_axis=0, tiled=True)  13 us
    pallas_call x2, Pallas kernels, select_pieces(): pl.pallas_call(kernel, out_shape=jax.ShapeDtypeStruct((devices * slots, w...  8.37 us
    pallas_call x2, Pallas kernels, add_far(): pl.pallas_call(kernel, out_shape=out_shape, in_specs=[pl.BlockSpec(memory...  7.6 us
  transfers between devices with their start and end apart: 9, of which 5 were waited for; matrix products, arithmetic and copies ran while one was open for 2% of the time, Pallas kernels for 7%

profile of v1, /device:TPU:1, one launch (start us, length us, event | category | flops | bytes accessed | tf_op | source)
XLA Modules:
  0.0 192.0 jit_solution(17450631173474571568)
XLA Ops:
  8.8 13.0 %all-to-all-start = ((s32[64,1,32]{2,1,0:T(1,128)}), s32[64,1,32]{2,1,0:T(1,128)S(1)}, u32[]{:S(2)}, u32[]{:S(2)}) async-start(s32[64,1,32]{2,1,0:T(1,128)} %broadcast_in_dim.8), calls=%async_computation | async-start | bytes 65536 | tf_op jit(solution)/shard_map/all_to_all | solution.py:196
  21.8 2.5 %split_blocks.1 = bf16[1024,256]{1,0:T(8,128)(2,1)} custom-call(bf16[2048,128]{1,0:T(8,128)(2,1)} %q_ref.5), custom_call_target="tpu_custom_call" | custom-call | tf_op jit(solution)/shard_map/split_blocks/pallas_call | solution.py:30
  24.3 6.8 %all-to-all-done = s32[64,1,32]{2,1,0:T(1,128)S(1)} async-done(((s32[64,1,32]{2,1,0:T(1,128)}), s32[64,1,32]{2,1,0:T(1,128)S(1)}, u32[]{:S(2)}, u32[]{:S(2)}) %all-to-all-start) | async-done | bytes 8224 | tf_op jit(solution)/shard_map/all_to_all | solution.py:196
  31.0 4.7 %all-to-all-start.1 = ((bf16[64,16,256]{2,1,0:T(8,128)(2,1)}), bf16[64,16,256]{2,1,0:T(8,128)(2,1)S(1)}, u32[]{:S(2)}, u32[]{:S(2)}) async-start(bf16[64,16,256]{2,1,0:T(8,128)(2,1)} %bitcast.24), calls=%async_computation.1 | async-start | bytes 1048576 | tf_op jit(solution)/shard_map/all_to_all | solution.py:183
  35.8 17.3 %all-to-all-done.1 = bf16[64,16,256]{2,1,0:T(8,128)(2,1)S(1)} async-done(((bf16[64,16,256]{2,1,0:T(8,128)(2,1)}), bf16[64,16,256]{2,1,0:T(8,128)(2,1)S(1)}, u32[]{:S(2)}, u32[]{:S(2)}) %all-to-all-start.1) | async-done | bytes 524320 | tf_op jit(solution)/shard_map/all_to_all | solution.py:183
  53.1 4.2 %select_pieces.2 = bf16[2048,256]{1,0:T(8,128)(2,1)} custom-call(s32[32,64]{1,0:T(8,128)S(1)} %bitcast.22, bf16[1024,256]{1,0:T(8,128)(2,1)S(1)} %bitcast.19), custom_call_target="tpu_custom_call" | custom-call | flops 1073741824 | bytes 2097152 | tf_op jit(solution)/shard_map/select_pieces/pallas_call | solution.py:58
  57.3 6.5 %all-to-all-start.2 = ((bf16[64,32,256]{2,1,0:T(8,128)(2,1)}), bf16[64,32,256]{2,1,0:T(8,128)(2,1)}, u32[]{:S(2)}, u32[]{:S(2)}) async-start(bf16[64,32,256]{2,1,0:T(8,128)(2,1)} %bitcast.5), calls=%async_computation.2 | async-start | bytes 2097152 | tf_op jit(solution)/shard_map/all_to_all | solution.py:183
  63.9 3.5 %collective-permute-start = (bf16[2,128,128]{2,1,0:T(8,128)(2,1)S(1)}, bf16[2,128,128]{2,1,0:T(8,128)(2,1)S(1)}, u32[]{:S(2)}, u32[]{:S(2)}) collective-permute-start(bf16[2,128,128]{2,1,0:T(8,128)(2,1)S(1)} %bitcast.26), channel_id=1, source_target_pairs={{0,4},{4,8},{8,12},{12,16},{16,20},{20,24},{24,28},{28,32},{32,36}... | collective-permute-start | bytes 196616 | tf_op jit(solution)/shard_map/ppermute | solution.py:205
  67.4 1.9 %collective-permute-start.1 = (bf16[2,128,128]{2,1,0:T(8,128)(2,1)S(1)}, bf16[2,128,128]{2,1,0:T(8,128)(2,1)S(1)}, u32[]{:S(2)}, u32[]{:S(2)}) collective-permute-start(bf16[2,128,128]{2,1,0:T(8,128)(2,1)S(1)} %bitcast.25), channel_id=1, source_target_pairs={{4,0},{8,4},{12,8},{16,12},{20,16},{24,20},{28,24},{32,28},{36,32}... | collective-permute-start | bytes 196616 | tf_op jit(solution)/shard_map/ppermute | solution.py:206
  69.4 29.3 %all-gather.2.cloned.1.call-done.tiles_ref = bf16[16,16,128,128]{3,2,1,0:T(8,128)(2,1)} async-done(((bf16[16,16,32,128]{3,2,1,0:T(8,128)(2,1)}), bf16[16,16,128,128]{3,2,1,0:T(8,128)(2,1)}) %all-gather.2.cloned.1.call-update) | async-done | bytes 8388624 | tf_op jit(solution)/shard_map/all_gather | solution.py:192
  98.7 1.3 slice.40.tiles_ref
  100.1 3.4 %copy-done = bf16[16,16,128,128]{3,2,1,0:T(8,128)(2,1)S(1)} copy-done((bf16[16,16,128,128]{3,2,1,0:T(8,128)(2,1)S(1)}, bf16[16,16,128,128]{3,2,1,0:T(8,128)(2,1)}, u32[]{:S(2)}) %copy-start) | copy-done | bytes 8388632
  103.4 3.4 %near_product.2.partial_ref = f32[16,128,128]{2,1,0:T(8,128)S(1)} custom-call(s32[16,16]{1,0:T(8,128)S(1)} %add_clamp_fusion.index_ref, s32[16]{0:T(128)S(1)} %copy-done.3, bf16[16,16,128,128]{3,2,1,0:T(8,128)(2,1)S(1)} %copy-done, bf16[2,128,128]{2,1,0:T(8,128)(2,1)S(1)} %collective-permute-done.low_ref, bf16[16,128,128]{2,1,0:T(8,128)(2,1)S(1)} %bitcast.17, ...), custom_call_target="tpu_custom_call" | custom-call | flops 939524096 | bytes 9437184 | tf_op jit(solution)/shard_map/near_product/pallas_call | solution.py:104
  106.8 3.8 %add_far.2 = (bf16[2048,128]{1,0:T(8,128)(2,1)S(1)}, bf16[1024,256]{1,0:T(8,128)(2,1)S(1)}) custom-call(s32[16]{0:T(128)S(1)} %copy-done.3, bf16[16,2,128,128]{3,2,1,0:T(8,128)(2,1)S(1)} %slice.40.tiles_ref, bf16[2048,256]{1,0:T(8,128)(2,1)} %bitcast.6.arrived_ref, f32[16,128,128]{2,1,0:T(8,128)S(1)} %near_product.2.partial_ref, bf16[2048,128]{1,0:T(8,128)(2,1)S(1)} %copy-done.2), custom_call_target="tpu_custom_call" | custom-call | flops 134217728 | bytes 4194304 | tf_op jit(solution)/shard_map/add_far/pallas_call | solution.py:166
  110.6 27.8 %all_to_all.25 = bf16[64,16,256]{2,1,0:T(8,128)(2,1)S(1)} all-to-all(bf16[64,16,256]{2,1,0:T(8,128)(2,1)S(1)} %bitcast.20), channel_id=1, replica_groups=mesh['db'=64,'pb'=4] {'db'}, dimensions={0} | all-to-all | bytes 1048576 | tf_op jit(solution)/shard_map/all_to_all | solution.py:183
  138.4 4.2 %select_pieces.3 = bf16[2048,256]{1,0:T(8,128)(2,1)} custom-call(s32[32,64]{1,0:T(8,128)S(1)} %bitcast.23, bf16[1024,256]{1,0:T(8,128)(2,1)S(1)} %bitcast.21), custom_call_target="tpu_custom_call" | custom-call | flops 1073741824 | bytes 2097152 | tf_op jit(solution)/shard_map/select_pieces/pallas_call | solution.py:58
  142.6 6.5 %all-to-all-start.4 = ((bf16[64,32,256]{2,1,0:T(8,128)(2,1)}), bf16[64,32,256]{2,1,0:T(8,128)(2,1)}, u32[]{:S(2)}, u32[]{:S(2)}) async-start(bf16[64,32,256]{2,1,0:T(8,128)(2,1)} %bitcast.12), calls=%async_computation.4 | async-start | bytes 2097152 | tf_op jit(solution)/shard_map/all_to_all | solution.py:183
  149.1 3.5 %collective-permute-start.2 = (bf16[2,128,128]{2,1,0:T(8,128)(2,1)S(1)}, bf16[2,128,128]{2,1,0:T(8,128)(2,1)S(1)}, u32[]{:S(2)}, u32[]{:S(2)}) collective-permute-start(bf16[2,128,128]{2,1,0:T(8,128)(2,1)S(1)} %bitcast.28), channel_id=1, source_target_pairs={{0,4},{4,8},{8,12},{12,16},{16,20},{20,24},{24,28},{28,32},{32,36}... | collective-permute-start | bytes 196616 | tf_op jit(solution)/shard_map/ppermute | solution.py:205
  152.6 2.1 %collective-permute-start.3 = (bf16[2,128,128]{2,1,0:T(8,128)(2,1)S(1)}, bf16[2,128,128]{2,1,0:T(8,128)(2,1)S(1)}, u32[]{:S(2)}, u32[]{:S(2)}) collective-permute-start(bf16[2,128,128]{2,1,0:T(8,128)(2,1)S(1)} %bitcast.27), channel_id=1, source_target_pairs={{4,0},{8,4},{12,8},{16,12},{20,16},{24,20},{28,24},{32,28},{36,32}... | collective-permute-start | bytes 196616 | tf_op jit(solution)/shard_map/ppermute | solution.py:206
  154.7 16.6 %collective-permute-done.2.low_ref = bf16[2,128,128]{2,1,0:T(8,128)(2,1)S(1)} collective-permute-done((bf16[2,128,128]{2,1,0:T(8,128)(2,1)S(1)}, bf16[2,128,128]{2,1,0:T(8,128)(2,1)S(1)}, u32[]{:S(2)}, u32[]{:S(2)}) %collective-permute-start.2) | collective-permute-done | bytes 65568 | tf_op jit(solution)/shard_map/ppermute | solution.py:205
  171.3 3.3 %collective-permute-done.3.high_ref = bf16[2,128,128]{2,1,0:T(8,128)(2,1)S(1)} collective-permute-done((bf16[2,128,128]{2,1,0:T(8,128)(2,1)S(1)}, bf16[2,128,128]{2,1,0:T(8,128)(2,1)S(1)}, u32[]{:S(2)}, u32[]{:S(2)}) %collective-permute-start.3) | collective-permute-done | bytes 65568 | tf_op jit(solution)/shard_map/ppermute | solution.py:206
  174.6 3.4 %copy-done.1 = bf16[16,16,128,128]{3,2,1,0:T(8,128)(2,1)S(1)} copy-done((bf16[16,16,128,128]{3,2,1,0:T(8,128)(2,1)S(1)}, bf16[16,16,128,128]{3,2,1,0:T(8,128)(2,1)}, u32[]{:S(2)}) %copy-start.1) | copy-done | bytes 8388632
  178.0 3.4 %near_product.3.partial_ref = f32[16,128,128]{2,1,0:T(8,128)S(1)} custom-call(s32[16,16]{1,0:T(8,128)S(1)} %add_clamp_fusion.index_ref, s32[16]{0:T(128)S(1)} %copy-done.3, bf16[16,16,128,128]{3,2,1,0:T(8,128)(2,1)S(1)} %copy-done.1, bf16[2,128,128]{2,1,0:T(8,128)(2,1)S(1)} %collective-permute-done.2.low_ref, bf16[16,128,128]{2,1,0:T(8,128)(2,1)S(1)} %bitcast.18, ...), custom_call_target="tpu_custom_call" | custom-call | flops 939524096 | bytes 9437184 | tf_op jit(solution)/shard_map/near_product/pallas_call | solution.py:104
  181.4 3.8 %add_far.3 = bf16[2048,128]{1,0:T(8,128)(2,1)} custom-call(s32[16]{0:T(128)S(1)} %copy-done.3, bf16[16,2,128,128]{3,2,1,0:T(8,128)(2,1)S(1)} %slice.40.tiles_ref, bf16[2048,256]{1,0:T(8,128)(2,1)} %bitcast.13.arrived_ref, f32[16,128,128]{2,1,0:T(8,128)S(1)} %near_product.3.partial_ref, bf16[2048,128]{1,0:T(8,128)(2,1)S(1)} %copy-done.2), custom_call_target="tpu_custom_call" | custom-call | flops 134217728 | bytes 4194304 | tf_op jit(solution)/shard_map/add_far/pallas_call | solution.py:166
  (21 shorter events, 2.3 us)
Async XLA Ops:
  6.5 62.8 %copy-start.4 = (s32[16,16]{1,0:T(8,128)S(1)}, s32[16,16]{1,0:T(8,128)}, u32[]{:S(2)}) copy-start(s32[16,16]{1,0:T(8,128)} %param.5) | copy-start | bytes 3076
  6.5 57.3 %copy-start.2 = (bf16[2048,128]{1,0:T(8,128)(2,1)S(1)}, bf16[2048,128]{1,0:T(8,128)(2,1)}, u32[]{:S(2)}) copy-start(bf16[2048,128]{1,0:T(8,128)(2,1)} %q_ref.5) | copy-start | bytes 1572868
  6.5 93.5 %copy-start.3 = (s32[16]{0:T(128)S(1)}, s32[16]{0:T(128)}, u32[]{:S(2)}) copy-start(s32[16]{0:T(128)} %count_ref.7) | copy-start | bytes 196
  6.5 92.1 %all-gather.2.cloned.1.call-start = ((), (), s32[]{:S(2)}) async-start(), calls=%async_computation.5 | async-start | bytes 10485760 | tf_op jit(solution)/shard_map/all_gather | solution.py:192
  8.8 22.3 %all-to-all-start = ((s32[64,1,32]{2,1,0:T(1,128)}), s32[64,1,32]{2,1,0:T(1,128)S(1)}, u32[]{:S(2)}, u32[]{:S(2)}) async-start(s32[64,1,32]{2,1,0:T(1,128)} %broadcast_in_dim.8), calls=%async_computation | async-start | bytes 65536 | tf_op jit(solution)/shard_map/all_to_all | solution.py:196
  31.0 22.1 %all-to-all-start.1 = ((bf16[64,16,256]{2,1,0:T(8,128)(2,1)}), bf16[64,16,256]{2,1,0:T(8,128)(2,1)S(1)}, u32[]{:S(2)}, u32[]{:S(2)}) async-start(bf16[64,16,256]{2,1,0:T(8,128)(2,1)} %bitcast.24), calls=%async_computation.1 | async-start | bytes 1048576 | tf_op jit(solution)/shard_map/all_to_all | solution.py:183
  57.3 49.5 %all-to-all-start.2 = ((bf16[64,32,256]{2,1,0:T(8,128)(2,1)}), bf16[64,32,256]{2,1,0:T(8,128)(2,1)}, u32[]{:S(2)}, u32[]{:S(2)}) async-start(bf16[64,32,256]{2,1,0:T(8,128)(2,1)} %bitcast.5), calls=%async_computation.2 | async-start | bytes 2097152 | tf_op jit(solution)/shard_map/all_to_all | solution.py:183
  63.9 36.1 %collective-permute-start = (bf16[2,128,128]{2,1,0:T(8,128)(2,1)S(1)}, bf16[2,128,128]{2,1,0:T(8,128)(2,1)S(1)}, u32[]{:S(2)}, u32[]{:S(2)}) collective-permute-start(bf16[2,128,128]{2,1,0:T(8,128)(2,1)S(1)} %bitcast.26), channel_id=1, source_target_pairs={{0,4},{4,8},{8,12},{12,16},{16,20},{20,24},{24,28},{28,32},{32,36}... | collective-permute-start | bytes 196616 | tf_op jit(solution)/shard_map/ppermute | solution.py:205
  67.4 32.6 %collective-permute-start.1 = (bf16[2,128,128]{2,1,0:T(8,128)(2,1)S(1)}, bf16[2,128,128]{2,1,0:T(8,128)(2,1)S(1)}, u32[]{:S(2)}, u32[]{:S(2)}) collective-permute-start(bf16[2,128,128]{2,1,0:T(8,128)(2,1)S(1)} %bitcast.25), channel_id=1, source_target_pairs={{4,0},{8,4},{12,8},{16,12},{20,16},{24,20},{28,24},{32,28},{36,32}... | collective-permute-start | bytes 196616 | tf_op jit(solution)/shard_map/ppermute | solution.py:206
  100.0 3.4 %copy-start = (bf16[16,16,128,128]{3,2,1,0:T(8,128)(2,1)S(1)}, bf16[16,16,128,128]{3,2,1,0:T(8,128)(2,1)}, u32[]{:S(2)}) copy-start(bf16[16,16,128,128]{3,2,1,0:T(8,128)(2,1)} %all-gather.2.cloned.1.call-done.tiles_ref) | copy-start | bytes 25165828
  142.6 38.8 %all-to-all-start.4 = ((bf16[64,32,256]{2,1,0:T(8,128)(2,1)}), bf16[64,32,256]{2,1,0:T(8,128)(2,1)}, u32[]{:S(2)}, u32[]{:S(2)}) async-start(bf16[64,32,256]{2,1,0:T(8,128)(2,1)} %bitcast.12), calls=%async_computation.4 | async-start | bytes 2097152 | tf_op jit(solution)/shard_map/all_to_all | solution.py:183
  149.1 22.3 %collective-permute-start.2 = (bf16[2,128,128]{2,1,0:T(8,128)(2,1)S(1)}, bf16[2,128,128]{2,1,0:T(8,128)(2,1)S(1)}, u32[]{:S(2)}, u32[]{:S(2)}) collective-permute-start(bf16[2,128,128]{2,1,0:T(8,128)(2,1)S(1)} %bitcast.28), channel_id=1, source_target_pairs={{0,4},{4,8},{8,12},{12,16},{16,20},{20,24},{24,28},{28,32},{32,36}... | collective-permute-start | bytes 196616 | tf_op jit(solution)/shard_map/ppermute | solution.py:205
  152.6 22.0 %collective-permute-start.3 = (bf16[2,128,128]{2,1,0:T(8,128)(2,1)S(1)}, bf16[2,128,128]{2,1,0:T(8,128)(2,1)S(1)}, u32[]{:S(2)}, u32[]{:S(2)}) collective-permute-start(bf16[2,128,128]{2,1,0:T(8,128)(2,1)S(1)} %bitcast.27), channel_id=1, source_target_pairs={{4,0},{8,4},{12,8},{16,12},{20,16},{24,20},{28,24},{32,28},{36,32}... | collective-permute-start | bytes 196616 | tf_op jit(solution)/shard_map/ppermute | solution.py:206
  174.6 3.4 %copy-start.1 = (bf16[16,16,128,128]{3,2,1,0:T(8,128)(2,1)S(1)}, bf16[16,16,128,128]{3,2,1,0:T(8,128)(2,1)}, u32[]{:S(2)}) copy-start(bf16[16,16,128,128]{3,2,1,0:T(8,128)(2,1)} %all-gather.2.cloned.1.call-done.tiles_ref) | copy-start | bytes 25165828
Sparse Core Ops, SparseCore 0:
  9.2 89.4 all-gather.1

commit v2 on v1

v2 whole, which is shorter than its diff:
```python
import jax
import jax.numpy as jnp
from jax import lax
from jax.experimental import pallas as pl
from jax.experimental.pallas import tpu as pltpu
from jax.sharding import PartitionSpec as P

EDGE = 2
ITERS = 2
BASE = 256
FAR = (1, 2)
LOW = tuple(range(1, 9))
HIGH = tuple(range(9, 16)) + (0,)
VMEM = pl.BlockSpec(memory_space=pltpu.VMEM)
SMEM = pl.BlockSpec(memory_space=pltpu.SMEM)


def rows_to_pieces(wide, pieces_ref, blocks, size, owners):
    for k in range(owners):
        for part in range(size // owners):
            rows = wide[pl.ds(part * owners + k, blocks, stride=size), :]
            pieces_ref[k, part * blocks : (part + 1) * blocks, :] = rows.astype(pieces_ref.dtype)


def split_blocks(queries, digits, blocks, size, owners):
    cols = queries.shape[1]
    rows = size // owners * blocks

    def kernel(q_ref, digits_ref, pieces_ref, wide):
        wide[...] = q_ref[...].astype(jnp.float32)
        rows_to_pieces(wide, pieces_ref, blocks, size, owners)
        for k in range(owners):
            pieces_ref[k, rows:, :] = jnp.broadcast_to(digits_ref[...], (8, cols)).astype(pieces_ref.dtype)

    return pl.pallas_call(
        kernel,
        out_shape=jax.ShapeDtypeStruct((owners, rows + 8, cols), queries.dtype),
        in_specs=[VMEM, VMEM],
        out_specs=VMEM,
        scratch_shapes=[pltpu.VMEM(queries.shape, jnp.float32)],
        name="split_blocks",
    )(queries, digits)


def select_pieces(held, slots, wanted=None):
    devices, height, cols = held.shape
    blocks = height // 16 * 8
    parts = 2
    block_total = devices * blocks
    group = 8

    def kernel(held_ref, *rest):
        if wanted is None:
            out_ref, wanted_out, flat = rest
            digits = held_ref[:, parts * blocks :, :].astype(jnp.float32)[:, 0, :].T
            ids = (digits[:slots] * BASE + digits[slots : 2 * slots]).astype(jnp.int32)
            wanted_out[...] = ids
        else:
            wanted_ref, out_ref, flat = rest
            ids = wanted_ref[...]
        for s in range(devices):
            for part in range(parts):
                flat[s * blocks : (s + 1) * blocks, part * cols : (part + 1) * cols] = held_ref[
                    s, part * blocks : (part + 1) * blocks, :
                ]
        column = lax.broadcasted_iota(jnp.int32, (slots, block_total), 1)
        for first in range(0, devices, group):
            hits = [
                jnp.where(
                    jnp.broadcast_to(ids[:, d : d + 1], (slots, block_total)) == column, 1.0, 0.0
                ).astype(held.dtype)
                for d in range(first, first + group)
            ]
            out_ref[first * slots : (first + group) * slots, :] = jnp.dot(
                jnp.concatenate(hits, axis=0), flat[...], preferred_element_type=jnp.float32
            ).astype(out_ref.dtype)

    out_shape = [jax.ShapeDtypeStruct((devices * slots, parts * cols), held.dtype)]
    if wanted is None:
        out_shape.append(jax.ShapeDtypeStruct((slots, devices), jnp.int32))
    operands = (held,) if wanted is None else (held, wanted)
    return pl.pallas_call(
        kernel,
        out_shape=out_shape,
        in_specs=[VMEM] * len(operands),
        out_specs=[VMEM] * len(out_shape),
        scratch_shapes=[pltpu.VMEM((block_total, parts * cols), held.dtype)],
        compiler_params=pltpu.CompilerParams(vmem_limit_bytes=32 << 20),
        cost_estimate=pl.CostEstimate(
            flops=2 * devices * slots * block_total * parts * cols, bytes_accessed=2 << 20, transcendentals=0
        ),
        name="select_pieces",
    )(*operands)


def near_product(near_index, counts, quarters, low, own, high):
    blocks, _, rows, size = quarters[0][0].shape
    cols = own.shape[2]
    group = 4
    number = len(quarters)
    near = [(half, place, t) for half, names in enumerate((LOW, HIGH)) for place, t in enumerate(names)]
    near = [entry for entry in near if entry[2] not in FAR]

    def kernel(index_ref, count_ref, *refs):
        tiles = [refs[2 * n : 2 * n + 2] for n in range(number)]
        low_ref, own_ref, high_ref, out_ref, panels = refs[2 * number :]
        step = pl.program_id(0)

        @pl.when(step == 0)
        def _():
            panels[:EDGE] = low_ref[...]
            panels[EDGE : EDGE + blocks] = own_ref[...]
            panels[EDGE + blocks :] = high_ref[...]

        for r in range(group):
            b = step * group + r
            total = jnp.zeros((number * rows, cols), jnp.float32)
            for first in range(0, len(near), 2):
                left, right = [], []
                for half, place, t in near[first : first + 2]:
                    tile = jnp.concatenate([pair[half][r, place] for pair in tiles], axis=0)
                    left.append(jnp.where(t < count_ref[b], tile, jnp.zeros_like(tile)))
                    right.append(panels[index_ref[b, t]])
                total += jnp.dot(
                    jnp.concatenate(left, axis=1),
                    jnp.concatenate(right, axis=0),
                    preferred_element_type=jnp.float32,
                )
            out_ref[r] = total

    return pl.pallas_call(
        kernel,
        out_shape=jax.ShapeDtypeStruct((blocks, number * rows, cols), jnp.float32),
        grid_spec=pltpu.PrefetchScalarGridSpec(
            num_scalar_prefetch=2,
            grid=(blocks // group,),
            in_specs=[
                pl.BlockSpec((group, half.shape[1], rows, size), lambda i, *_: (i, 0, 0, 0))
                for pair in quarters
                for half in pair
            ]
            + [VMEM] * 3,
            out_specs=pl.BlockSpec((group, number * rows, cols), lambda i, *_: (i, 0, 0)),
            scratch_shapes=[pltpu.VMEM((blocks + 2 * EDGE, size, cols), own.dtype)],
        ),
        compiler_params=pltpu.CompilerParams(vmem_limit_bytes=32 << 20),
        cost_estimate=pl.CostEstimate(
            flops=2 * blocks * len(near) * number * rows * size * cols,
            bytes_accessed=number << 21,
            transcendentals=0,
        ),
        name="near_product",
    )(near_index, counts, *[half for pair in quarters for half in pair], low, own, high)


def add_far(offsets, counts, far_tiles, arrived, partials, queries, owners, split):
    blocks, _, rows, size = far_tiles[0].shape
    cols = queries.shape[1]
    far = arrived.shape[0] // owners
    number = len(far_tiles)

    def kernel(offset_ref, count_ref, *refs):
        tiles = refs[:number]
        arrived_ref = refs[number]
        partial_refs = refs[number + 1 : number + 1 + len(partials)]
        q_ref, out_ref, *rest = refs[number + 1 + len(partials) :]
        if split:
            pieces_ref, upper, lower, wide = rest
        else:
            upper, lower = rest
        upper[...] = arrived_ref[:, :cols].astype(jnp.float32)
        lower[...] = arrived_ref[:, cols:].astype(jnp.float32)
        for b in range(blocks):
            left, right = [], []
            for s, t in enumerate(FAR):
                tile = jnp.concatenate([ref[b, s] for ref in tiles], axis=0)
                left.append(jnp.where(t < count_ref[b], tile, jnp.zeros_like(tile)))
                for half in (upper, lower):
                    right.append(half[pl.ds(2 * b + s, owners, stride=far), :].astype(queries.dtype))
            total = jnp.concatenate([ref[b] for ref in partial_refs], axis=0) + jnp.dot(
                jnp.concatenate(left, axis=1),
                jnp.concatenate(right, axis=0),
                preferred_element_type=jnp.float32,
            )
            for n in range(number):
                place = pl.ds(pl.multiple_of(b * size + offset_ref[n], rows), rows)
                result = 0.99 * total[n * rows : (n + 1) * rows] + q_ref[place, :].astype(jnp.float32)
                result = result.astype(out_ref.dtype)
                out_ref[place, :] = result
                if split:
                    wide[place, :] = result.astype(jnp.float32)
        if split:
            rows_to_pieces(wide, pieces_ref, blocks, size, owners)

    out_shape = [jax.ShapeDtypeStruct(queries.shape, queries.dtype)]
    out_specs = [pl.BlockSpec(queries.shape, lambda i, *_: (0, 0))]
    scratch = [pltpu.VMEM((owners * far, cols), jnp.float32)] * 2
    if split:
        shape = (owners, size // owners * blocks, cols)
        out_shape.append(jax.ShapeDtypeStruct(shape, queries.dtype))
        out_specs.append(pl.BlockSpec(shape, lambda i, *_: (0, 0, 0)))
        scratch.append(pltpu.VMEM(queries.shape, jnp.float32))
    return pl.pallas_call(
        kernel,
        out_shape=out_shape,
        grid_spec=pltpu.PrefetchScalarGridSpec(
            num_scalar_prefetch=2,
            grid=(1,),
            in_specs=[pl.BlockSpec((blocks, len(FAR), rows, size), lambda i, *_: (0, 0, 0, 0))] * number
            + [VMEM] * (2 + len(partials)),
            out_specs=out_specs,
            scratch_shapes=scratch,
        ),
        compiler_params=pltpu.CompilerParams(vmem_limit_bytes=32 << 20),
        cost_estimate=pl.CostEstimate(
            flops=4 * blocks * size * size * cols, bytes_accessed=4 << 20, transcendentals=0
        ),
        name="add_far",
    )(offsets, counts, *far_tiles, arrived, *partials, queries)


def gather_rows(tiles):
    count = lax.axis_size("pb")
    up = [(i, (i + 1) % count) for i in range(count)]
    down = [((i + 1) % count, i) for i in range(count)]
    low = tiles[:, LOW[0] : LOW[-1] + 1]
    high = jnp.concatenate([tiles[:, HIGH[0] :], tiles[:, :1]], axis=1)
    before_low = lax.ppermute(low, "pb", up)
    after_high = lax.ppermute(high, "pb", down)
    before_high = lax.ppermute(high, "pb", up)
    after_low = lax.ppermute(low, "pb", down)
    far_low = lax.ppermute(before_low, "pb", up)
    far_high = lax.ppermute(after_high, "pb", down)
    return [(low, high), (before_low, before_high), (after_low, after_high), (far_low, far_high)]


def on_device(affinity_tiles, block_ids, valid_counts, queries):
    blocks, slots = block_ids.shape
    rows, size = affinity_tiles.shape[2:]
    cols = queries.shape[1]
    owners = lax.axis_size("db")
    first_block = lax.axis_index("db") * blocks
    quarters = gather_rows(affinity_tiles)
    far_tiles = [pair[0] for pair in quarters]
    place = lax.axis_index("pb")
    offsets = jnp.stack([(place + shift) % lax.axis_size("pb") * rows for shift in (0, -1, 1, 2)])
    near_index = jnp.clip(block_ids - first_block + EDGE, 0, blocks + 2 * EDGE - 1)
    far = block_ids[:, FAR[0] : FAR[-1] + 1].reshape(1, -1)
    slots = far.shape[1]
    digits = jnp.concatenate([far // BASE, far % BASE], axis=1).astype(jnp.float32)
    digits = jnp.pad(digits, ((0, 0), (0, cols - 2 * slots)))
    up = [(i, i + 1) for i in range(owners - 1)]
    down = [(i + 1, i) for i in range(owners - 1)]
    ranking, wanted = queries, None
    pieces = split_blocks(queries, digits, blocks, size, owners)
    for step in range(ITERS):
        own = ranking.reshape(blocks, size, cols)
        held = lax.all_to_all(pieces, "db", split_axis=0, concat_axis=0, tiled=True)
        low = lax.ppermute(own[blocks - EDGE :], "db", up)
        high = lax.ppermute(own[:EDGE], "db", down)
        if wanted is None:
            chosen, wanted = select_pieces(held, slots)
        else:
            (chosen,) = select_pieces(held, slots, wanted)
        arrived = lax.all_to_all(
            chosen.reshape(owners, slots, -1), "db", split_axis=0, concat_axis=0, tiled=True
        ).reshape(chosen.shape)
        partials = [
            near_product(near_index, valid_counts, part, low, own, high)
            for part in ([quarters[:3], quarters[3:]] if step == 0 else [quarters])
        ]
        done = add_far(offsets, valid_counts, far_tiles, arrived, partials, queries, owners, step < ITERS - 1)
        ranking = done[0]
        pieces = done[-1]
    return ranking


def solution(mesh):
    return jax.shard_map(
        on_device,
        mesh=mesh,
        in_specs=(P("db", None, "pb", None), P("db", None), P("db"), P("db", "pb")),
        out_specs=P("db", "pb"),
        check_vma=False,
    )
```

time: 193 us -> 188 us (0.974)
  between operations: 13.6 us -> 0.29 us
  waiting for transfers between devices: 73.9 us -> 64.7 us
  local copies, waits for them, and re-layouts: 9.67 us -> 15.9 us
  starting transfers between devices: 41.8 us -> 46.4 us
  Pallas kernels: 25.2 us -> 29.2 us
    all_gather x1 -> x0, waiting for transfers between devices: 29.3 us -> none  [on_device(): full_tiles = lax.all_gather(affinity_tiles, 'pb', axis=2, tiled=True)]
    ppermute x0 -> x6, waiting for transfers between devices: none -> 14.8 us  [the longest x1 14.8 us: gather_rows(): far_low = lax.ppermute(before_low, 'pb', up)]
    ppermute x2, waiting for transfers between devices: 16.6 us -> 27.3 us  [on_device(): low = lax.ppermute(own[blocks - EDGE:], 'db', up)]
    all_to_all x4 -> x3, waiting for transfers between devices: 24.1 us -> 14.8 us  [the longest x1 14.8 us: on_device(): held = lax.all_to_all(pieces, 'db', split_axis=0, concat_axis=0, tiled=True)]
    ppermute x0 -> x6, starting transfers between devices: none -> 8.46 us  [the longest x1 2.82 us: gather_rows(): after_low = lax.ppermute(low, 'pb', down)]
    all_to_all x4 -> x3, starting transfers between devices: 30.7 us -> 26 us  [the longest x2 13 us: on_device(): lax.all_to_all(chosen.reshape(owners, slots, -1), 'db', split_axis=0, con...]
    ppermute x2, waiting for transfers between devices: 3.27 us -> 7.88 us  [on_device(): high = lax.ppermute(own[:EDGE], 'db', down)]
    unnamed x10 -> x28, local copies, waits for them, and re-layouts: 6.77 us -> 11.3 us
  transfers between devices with their start and end apart: 9 -> 13, of which waited for: 5 -> 6; matrix products, arithmetic and copies ran while one was open for 2% -> 2% of each run, Pallas kernels for 7% -> 9%
where the time goes in v2:
time: 188 us; the launch traced here: 186 us
  waiting for transfers between devices  64.7 us (34%)
  starting transfers between devices  46.4 us (25%)
  Pallas kernels  29.2 us (16%)
  blocking collectives  28.8 us (15%)
  local copies, waits for them, and re-layouts  15.9 us (8%)
    all_to_all x1, blocking collectives, on_device(): held = lax.all_to_all(pieces, 'db', split_axis=0, concat_axis=0, tiled=True)  28.8 us
    ppermute x2, waiting for transfers between devices, on_device(): low = lax.ppermute(own[blocks - EDGE:], 'db', up)  27.3 us
    ppermute x1, waiting for transfers between devices, gather_rows(): far_low = lax.ppermute(before_low, 'pb', up)  14.8 us
    all_to_all x1, waiting for transfers between devices, on_device(): held = lax.all_to_all(pieces, 'db', split_axis=0, concat_axis=0, tiled=True)  14.8 us
    pallas_call x3, Pallas kernels, near_product(): pl.pallas_call(kernel, out_shape=jax.ShapeDtypeStruct((blocks, number * r...  14.3 us
    all_to_all x2, starting transfers between devices, on_device(): lax.all_to_all(chosen.reshape(owners, slots, -1), 'db', split_axis=0, con...  13 us
    all_to_all x1, starting transfers between devices, on_device(): held = lax.all_to_all(pieces, 'db', split_axis=0, concat_axis=0, tiled=True)  13 us
    unnamed x28, local copies, waits for them, and re-layouts  11.3 us
  transfers between devices with their start and end apart: 13, of which 6 were waited for; matrix products, arithmetic and copies ran while one was open for 2% of the time, Pallas kernels for 9%

profile of v2, /device:TPU:1, one launch (start us, length us, event | category | flops | bytes accessed | tf_op | source)
XLA Modules:
  0.0 186.5 jit_solution(7567816351947477952)
XLA Ops:
  1.5 2.6 %split_blocks.1 = bf16[64,40,128]{2,1,0:T(8,128)(2,1)} custom-call(bf16[2048,128]{1,0:T(8,128)(2,1)} %refs_6_.1, f32[1,128]{1,0:T(1,128)} %pad.4.digits_ref), custom_call_target="tpu_custom_call" | custom-call | tf_op jit(solution)/shard_map/split_blocks/pallas_call | solution.py:35
  4.0 13.0 %all-to-all-start = ((bf16[64,40,128]{2,1,0:T(8,128)(2,1)}), bf16[64,40,128]{2,1,0:T(8,128)(2,1)S(1)}, u32[]{:S(2)}, u32[]{:S(2)}) async-start(bf16[64,40,128]{2,1,0:T(8,128)(2,1)} %split_blocks.1), calls=%async_computation | async-start | bytes 1310720 | tf_op jit(solution)/shard_map/all_to_all | solution.py:258
  20.9 1.5 collective-permute-start.4
  22.4 14.8 %all-to-all-done.held_ref = bf16[64,40,128]{2,1,0:T(8,128)(2,1)S(1)} async-done(((bf16[64,40,128]{2,1,0:T(8,128)(2,1)}), bf16[64,40,128]{2,1,0:T(8,128)(2,1)S(1)}, u32[]{:S(2)}, u32[]{:S(2)}) %all-to-all-start) | async-done | bytes 655392 | tf_op jit(solution)/shard_map/all_to_all | solution.py:258
  39.1 2.4 %select_pieces.2 = (bf16[2048,256]{1,0:T(8,128)(2,1)}, s32[32,64]{1,0:T(8,128)S(1)}) custom-call(bf16[64,40,128]{2,1,0:T(8,128)(2,1)S(1)} %copy-done.11), custom_call_target="tpu_custom_call" | custom-call | flops 1073741824 | bytes 2097152 | tf_op jit(solution)/shard_map/select_pieces/pallas_call | solution.py:82
  41.5 6.6 %all-to-all-start.1 = ((bf16[64,32,256]{2,1,0:T(8,128)(2,1)}), bf16[64,32,256]{2,1,0:T(8,128)(2,1)}, u32[]{:S(2)}, u32[]{:S(2)}) async-start(bf16[64,32,256]{2,1,0:T(8,128)(2,1)} %bitcast.6), calls=%async_computation.1 | async-start | bytes 2097152 | tf_op jit(solution)/shard_map/all_to_all | solution.py:265
  48.1 2.8 %collective-permute-start.1 = (bf16[16,8,32,128]{3,2,1,0:T(8,128)(2,1)S(1)}, bf16[16,8,32,128]{3,2,1,0:T(8,128)(2,1)S(1)}, u32[]{:S(2)}, u32[]{:S(2)}) collective-permute-start(bf16[16,8,32,128]{3,2,1,0:T(8,128)(2,1)S(1)} %slice.36.refs_0_), channel_id=1, source_target_pairs={{1,0},{2,1},{3,2},{0,3},{5,4},{6,5},{7,6},{4,7},{9,8},{10,9},{11,1... | collective-permute-start | bytes 3145736 | tf_op jit(solution)/shard_map/ppermute | solution.py:231
  50.9 2.7 %collective-permute-start.7 = (bf16[16,8,32,128]{3,2,1,0:T(8,128)(2,1)}, bf16[16,8,32,128]{3,2,1,0:T(8,128)(2,1)}, u32[]{:S(2)}, u32[]{:S(2)}) collective-permute-start(bf16[16,8,32,128]{3,2,1,0:T(8,128)(2,1)} %collective-permute-done.4.refs_5_), channel_id=1, source_target_pairs={{1,0},{2,1},{3,2},{0,3},{5,4},{6,5},{7,6},{4,7},{9,8},{10,9},{11,1... | collective-permute-start | bytes 3145736 | tf_op jit(solution)/shard_map/ppermute | solution.py:233
  54.6 4.4 %collective-permute-start.5 = (bf16[2,128,128]{2,1,0:T(8,128)(2,1)S(1)}, bf16[2,128,128]{2,1,0:T(8,128)(2,1)S(1)}, u32[]{:S(2)}, u32[]{:S(2)}) collective-permute-start(bf16[2,128,128]{2,1,0:T(8,128)(2,1)S(1)} %bitcast.23), channel_id=1, source_target_pairs={{0,4},{4,8},{8,12},{12,16},{16,20},{20,24},{24,28},{28,32},{32,36}... | collective-permute-start | bytes 196616 | tf_op jit(solution)/shard_map/ppermute | solution.py:259
  59.0 11.4 %collective-permute-done.5.refs_6_.refs_2_ = bf16[2,128,128]{2,1,0:T(8,128)(2,1)S(1)} collective-permute-done((bf16[2,128,128]{2,1,0:T(8,128)(2,1)S(1)}, bf16[2,128,128]{2,1,0:T(8,128)(2,1)S(1)}, u32[]{:S(2)}, u32[]{:S(2)}) %collective-permute-start.5) | collective-permute-done | bytes 65568 | tf_op jit(solution)/shard_map/ppermute | solution.py:259
  70.4 2.1 %collective-permute-start.6 = (bf16[2,128,128]{2,1,0:T(8,128)(2,1)S(1)}, bf16[2,128,128]{2,1,0:T(8,128)(2,1)S(1)}, u32[]{:S(2)}, u32[]{:S(2)}) collective-permute-start(bf16[2,128,128]{2,1,0:T(8,128)(2,1)S(1)} %bitcast.22), channel_id=1, source_target_pairs={{4,0},{8,4},{12,8},{16,12},{20,16},{24,20},{28,24},{32,28},{36,32}... | collective-permute-start | bytes 196616 | tf_op jit(solution)/shard_map/ppermute | solution.py:260
  72.5 4.6 %collective-permute-done.6.refs_8_.refs_4_ = bf16[2,128,128]{2,1,0:T(8,128)(2,1)S(1)} collective-permute-done((bf16[2,128,128]{2,1,0:T(8,128)(2,1)S(1)}, bf16[2,128,128]{2,1,0:T(8,128)(2,1)S(1)}, u32[]{:S(2)}, u32[]{:S(2)}) %collective-permute-start.6) | collective-permute-done | bytes 65568 | tf_op jit(solution)/shard_map/ppermute | solution.py:260
  78.2 4.8 %near_product.3.refs_5_ = f32[16,96,128]{2,1,0:T(8,128)S(1)} custom-call(s32[16,16]{1,0:T(8,128)S(1)} %add_clamp_fusion.index_ref, s32[16]{0:T(128)S(1)} %copy-done.12, bf16[16,8,32,128]{3,2,1,0:T(8,128)(2,1)S(1)} %slice.36.refs_0_, bf16[16,8,32,128]{3,2,1,0:T(8,128)(2,1)} %pad_maximum_fusion.refs_1_, ...), custom_call_target="tpu_custom_call" | custom-call | flops 704643072 | bytes 6291456 | tf_op jit(solution)/shard_map/near_product/pallas_call | solution.py:131
  84.0 14.8 %collective-permute-done.2.refs_0_.refs_3_.refs_6_ = bf16[16,8,32,128]{3,2,1,0:T(8,128)(2,1)} collective-permute-done((bf16[16,8,32,128]{3,2,1,0:T(8,128)(2,1)S(1)}, bf16[16,8,32,128]{3,2,1,0:T(8,128)(2,1)}, u32[]{:S(2)}, u32[]{:S(2)}) %collective-permute-start.2) | collective-permute-done | bytes 1048608 | tf_op jit(solution)/shard_map/ppermute | solution.py:232
  98.8 4.1 %near_product.4.refs_6_ = f32[16,32,128]{2,1,0:T(8,128)S(1)} custom-call(s32[16,16]{1,0:T(8,128)S(1)} %add_clamp_fusion.index_ref, s32[16]{0:T(128)S(1)} %copy-done.12, bf16[16,8,32,128]{3,2,1,0:T(8,128)(2,1)} %collective-permute-done.2.refs_0_.refs_3_.refs_6_, bf16[16,8,32,128]{3,2,1,0:T(8,128)(2,1)} %collective-permute-done.7.refs_1_.refs_7_, ...), custom_call_target="tpu_custom_call" | custom-call | flops 234881024 | bytes 2097152 | tf_op jit(solution)/shard_map/near_product/pallas_call | solution.py:131
  105.1 4.2 %add_far.2 = (bf16[2048,128]{1,0:T(8,128)(2,1)S(1)}, bf16[64,32,128]{2,1,0:T(8,128)(2,1)S(1)}) custom-call(s32[4]{0:T(128)S(1)} %pad_add_fusion.offset_ref, s32[16]{0:T(128)S(1)} %copy-done.12, bf16[16,8,32,128]{3,2,1,0:T(8,128)(2,1)S(1)} %slice.36.refs_0_, bf16[16,8,32,128]{3,2,1,0:T(8,128)(2,1)S(1)} %collective-permute-done.refs_2_.refs_1_, ...), custom_call_target="tpu_custom_call" | custom-call | flops 134217728 | bytes 4194304 | tf_op jit(solution)/shard_map/add_far/pallas_call | solution.py:203
  109.3 28.8 %all_to_all.20.held_ref = bf16[64,32,128]{2,1,0:T(8,128)(2,1)S(1)} all-to-all(bf16[64,32,128]{2,1,0:T(8,128)(2,1)S(1)} %get-tuple-element.10), channel_id=1, replica_groups=mesh['db'=64,'pb'=4] {'db'}, dimensions={0} | all-to-all | bytes 1048576 | tf_op jit(solution)/shard_map/all_to_all | solution.py:258
  140.4 6.5 %all-to-all-start.3 = ((bf16[64,32,256]{2,1,0:T(8,128)(2,1)}), bf16[64,32,256]{2,1,0:T(8,128)(2,1)}, u32[]{:S(2)}, u32[]{:S(2)}) async-start(bf16[64,32,256]{2,1,0:T(8,128)(2,1)} %bitcast.20), calls=%async_computation.3 | async-start | bytes 2097152 | tf_op jit(solution)/shard_map/all_to_all | solution.py:265
  147.8 3.5 %collective-permute-start.8 = (bf16[2,128,128]{2,1,0:T(8,128)(2,1)S(1)}, bf16[2,128,128]{2,1,0:T(8,128)(2,1)S(1)}, u32[]{:S(2)}, u32[]{:S(2)}) collective-permute-start(bf16[2,128,128]{2,1,0:T(8,128)(2,1)S(1)} %bitcast.25), channel_id=1, source_target_pairs={{0,4},{4,8},{8,12},{12,16},{16,20},{20,24},{24,28},{28,32},{32,36}... | collective-permute-start | bytes 196616 | tf_op jit(solution)/shard_map/ppermute | solution.py:259
  151.3 1.9 %collective-permute-start.9 = (bf16[2,128,128]{2,1,0:T(8,128)(2,1)S(1)}, bf16[2,128,128]{2,1,0:T(8,128)(2,1)S(1)}, u32[]{:S(2)}, u32[]{:S(2)}) collective-permute-start(bf16[2,128,128]{2,1,0:T(8,128)(2,1)S(1)} %bitcast.24), channel_id=1, source_target_pairs={{4,0},{8,4},{12,8},{16,12},{20,16},{24,20},{28,24},{32,28},{36,32}... | collective-permute-start | bytes 196616 | tf_op jit(solution)/shard_map/ppermute | solution.py:260
  153.2 15.9 %collective-permute-done.8.refs_8_ = bf16[2,128,128]{2,1,0:T(8,128)(2,1)S(1)} collective-permute-done((bf16[2,128,128]{2,1,0:T(8,128)(2,1)S(1)}, bf16[2,128,128]{2,1,0:T(8,128)(2,1)S(1)}, u32[]{:S(2)}, u32[]{:S(2)}) %collective-permute-start.8) | collective-permute-done | bytes 65568 | tf_op jit(solution)/shard_map/ppermute | solution.py:259
  169.2 3.3 %collective-permute-done.9.refs_10_ = bf16[2,128,128]{2,1,0:T(8,128)(2,1)S(1)} collective-permute-done((bf16[2,128,128]{2,1,0:T(8,128)(2,1)S(1)}, bf16[2,128,128]{2,1,0:T(8,128)(2,1)S(1)}, u32[]{:S(2)}, u32[]{:S(2)}) %collective-permute-start.9) | collective-permute-done | bytes 65568 | tf_op jit(solution)/shard_map/ppermute | solution.py:260
  173.5 5.4 %near_product.5.refs_5_ = f32[16,128,128]{2,1,0:T(8,128)S(1)} custom-call(s32[16,16]{1,0:T(8,128)S(1)} %add_clamp_fusion.index_ref, s32[16]{0:T(128)S(1)} %copy-done.12, bf16[16,8,32,128]{3,2,1,0:T(8,128)(2,1)S(1)} %slice.36.refs_0_, bf16[16,8,32,128]{3,2,1,0:T(8,128)(2,1)} %pad_maximum_fusion.refs_1_, ...), custom_call_target="tpu_custom_call" | custom-call | flops 939524096 | bytes 8388608 | tf_op jit(solution)/shard_map/near_product/pallas_call | solution.py:131
  182.1 4.4 %add_far.3 = bf16[2048,128]{1,0:T(8,128)(2,1)} custom-call(s32[4]{0:T(128)S(1)} %pad_add_fusion.offset_ref, s32[16]{0:T(128)S(1)} %copy-done.12, bf16[16,8,32,128]{3,2,1,0:T(8,128)(2,1)S(1)} %slice.36.refs_0_, bf16[16,8,32,128]{3,2,1,0:T(8,128)(2,1)S(1)} %collective-permute-done.refs_2_.refs_1_, ...), custom_call_target="tpu_custom_call" | custom-call | flops 134217728 | bytes 4194304 | tf_op jit(solution)/shard_map/add_far/pallas_call | solution.py:203
  (54 shorter events, 19.8 us)
Async XLA Ops:
  4.0 33.1 %all-to-all-start = ((bf16[64,40,128]{2,1,0:T(8,128)(2,1)}), bf16[64,40,128]{2,1,0:T(8,128)(2,1)S(1)}, u32[]{:S(2)}, u32[]{:S(2)}) async-start(bf16[64,40,128]{2,1,0:T(8,128)(2,1)} %split_blocks.1), calls=%async_computation | async-start | bytes 1310720 | tf_op jit(solution)/shard_map/all_to_all | solution.py:258
  17.0 2.8 %slice-start = ((bf16[16,16,32,128]{3,2,1,0:T(8,128)(2,1)}), bf16[16,1,32,128]{3,2,1,0:T(8,128)(2,1)S(1)}, s32[]{:S(2)}) async-start(bf16[16,16,32,128]{3,2,1,0:T(8,128)(2,1)} %param.4), calls=%async_computation.4 | async-start | bytes 262144 | tf_op jit(solution)/shard_map/slice | solution.py:227
  17.0 2.8 %slice-start.1 = ((bf16[16,16,32,128]{3,2,1,0:T(8,128)(2,1)}), bf16[16,7,32,128]{3,2,1,0:T(8,128)(2,1)S(1)}, s32[]{:S(2)}) async-start(bf16[16,16,32,128]{3,2,1,0:T(8,128)(2,1)} %param.4), calls=%async_computation.5 | async-start | bytes 1835008 | tf_op jit(solution)/shard_map/slice | solution.py:227
  18.4 32.5 %collective-permute-start = (bf16[16,8,32,128]{3,2,1,0:T(8,128)(2,1)S(1)}, bf16[16,8,32,128]{3,2,1,0:T(8,128)(2,1)S(1)}, u32[]{:S(2)}, u32[]{:S(2)}) collective-permute-start(bf16[16,8,32,128]{3,2,1,0:T(8,128)(2,1)S(1)} %slice.36.refs_0_), channel_id=1, source_target_pairs={{0,1},{1,2},{2,3},{3,0},{4,5},{5,6},{6,7},{7,4},{8,9},{9,10},{10,1... | collective-permute-start | bytes 3145736 | tf_op jit(solution)/shard_map/ppermute | solution.py:228
  20.9 30.1 %collective-permute-start.4 = (bf16[16,8,32,128]{3,2,1,0:T(8,128)(2,1)}, bf16[16,8,32,128]{3,2,1,0:T(8,128)(2,1)}, u32[]{:S(2)}, u32[]{:S(2)}) collective-permute-start(bf16[16,8,32,128]{3,2,1,0:T(8,128)(2,1)} %pad_maximum_fusion.refs_1_), channel_id=1, source_target_pairs={{1,0},{2,1},{3,2},{0,3},{5,4},{6,5},{7,6},{4,7},{9,8},{10,9},{11,1... | collective-permute-start | bytes 3145736 | tf_op jit(solution)/shard_map/ppermute | solution.py:229
  38.0 1.1 copy-start.11
  41.5 17.4 %copy-start.13 = (s32[16,16]{1,0:T(8,128)S(1)}, s32[16,16]{1,0:T(8,128)}, u32[]{:S(2)}) copy-start(s32[16,16]{1,0:T(8,128)} %param.5) | copy-start | bytes 3076
  41.5 35.7 %copy-start.12 = (s32[16]{0:T(128)S(1)}, s32[16]{0:T(128)}, u32[]{:S(2)}) copy-start(s32[16]{0:T(128)} %count_ref.9) | copy-start | bytes 196
  41.5 61.4 %all-to-all-start.1 = ((bf16[64,32,256]{2,1,0:T(8,128)(2,1)}), bf16[64,32,256]{2,1,0:T(8,128)(2,1)}, u32[]{:S(2)}, u32[]{:S(2)}) async-start(bf16[64,32,256]{2,1,0:T(8,128)(2,1)} %bitcast.6), calls=%async_computation.1 | async-start | bytes 2097152 | tf_op jit(solution)/shard_map/all_to_all | solution.py:265
  48.1 29.1 %collective-permute-start.1 = (bf16[16,8,32,128]{3,2,1,0:T(8,128)(2,1)S(1)}, bf16[16,8,32,128]{3,2,1,0:T(8,128)(2,1)S(1)}, u32[]{:S(2)}, u32[]{:S(2)}) collective-permute-start(bf16[16,8,32,128]{3,2,1,0:T(8,128)(2,1)S(1)} %slice.36.refs_0_), channel_id=1, source_target_pairs={{1,0},{2,1},{3,2},{0,3},{5,4},{6,5},{7,6},{4,7},{9,8},{10,9},{11,1... | collective-permute-start | bytes 3145736 | tf_op jit(solution)/shard_map/ppermute | solution.py:231
  50.9 26.3 %collective-permute-start.3 = (bf16[16,8,32,128]{3,2,1,0:T(8,128)(2,1)}, bf16[16,8,32,128]{3,2,1,0:T(8,128)(2,1)}, u32[]{:S(2)}, u32[]{:S(2)}) collective-permute-start(bf16[16,8,32,128]{3,2,1,0:T(8,128)(2,1)} %pad_maximum_fusion.refs_1_), channel_id=1, source_target_pairs={{0,1},{1,2},{2,3},{3,0},{4,5},{5,6},{6,7},{7,4},{8,9},{9,10},{10,1... | collective-permute-start | bytes 3145736 | tf_op jit(solution)/shard_map/ppermute | solution.py:230
  50.9 47.9 %collective-permute-start.2 = (bf16[16,8,32,128]{3,2,1,0:T(8,128)(2,1)S(1)}, bf16[16,8,32,128]{3,2,1,0:T(8,128)(2,1)}, u32[]{:S(2)}, u32[]{:S(2)}) collective-permute-start(bf16[16,8,32,128]{3,2,1,0:T(8,128)(2,1)S(1)} %collective-permute-done.refs_2_.refs_1_), channel_id=1, source_target_pairs={{0,1},{1,2},{2,3},{3,0},{4,5},{5,6},{6,7},{7,4},{8,9},{9,10},{10,1... | collective-permute-start | bytes 3145736 | tf_op jit(solution)/shard_map/ppermute | solution.py:232
  50.9 47.8 %collective-permute-start.7 = (bf16[16,8,32,128]{3,2,1,0:T(8,128)(2,1)}, bf16[16,8,32,128]{3,2,1,0:T(8,128)(2,1)}, u32[]{:S(2)}, u32[]{:S(2)}) collective-permute-start(bf16[16,8,32,128]{3,2,1,0:T(8,128)(2,1)} %collective-permute-done.4.refs_5_), channel_id=1, source_target_pairs={{1,0},{2,1},{3,2},{0,3},{5,4},{6,5},{7,6},{4,7},{9,8},{10,9},{11,1... | collective-permute-start | bytes 3145736 | tf_op jit(solution)/shard_map/ppermute | solution.py:233
  54.6 15.8 %collective-permute-start.5 = (bf16[2,128,128]{2,1,0:T(8,128)(2,1)S(1)}, bf16[2,128,128]{2,1,0:T(8,128)(2,1)S(1)}, u32[]{:S(2)}, u32[]{:S(2)}) collective-permute-start(bf16[2,128,128]{2,1,0:T(8,128)(2,1)S(1)} %bitcast.23), channel_id=1, source_target_pairs={{0,4},{4,8},{8,12},{12,16},{16,20},{20,24},{24,28},{28,32},{32,36}... | collective-permute-start | bytes 196616 | tf_op jit(solution)/shard_map/ppermute | solution.py:259
  70.4 6.8 %collective-permute-start.6 = (bf16[2,128,128]{2,1,0:T(8,128)(2,1)S(1)}, bf16[2,128,128]{2,1,0:T(8,128)(2,1)S(1)}, u32[]{:S(2)}, u32[]{:S(2)}) collective-permute-start(bf16[2,128,128]{2,1,0:T(8,128)(2,1)S(1)} %bitcast.22), channel_id=1, source_target_pairs={{4,0},{8,4},{12,8},{16,12},{20,16},{24,20},{28,24},{32,28},{36,32}... | collective-permute-start | bytes 196616 | tf_op jit(solution)/shard_map/ppermute | solution.py:260
  77.2 1.0 copy-start
  102.9 1.0 copy-start.1
  104.0 1.1 copy-start.6
  109.3 30.1 %copy-start.8 = (bf16[2048,128]{1,0:T(8,128)(2,1)}, bf16[2048,128]{1,0:T(8,128)(2,1)S(1)}, u32[]{:S(2)}) copy-start(bf16[2048,128]{1,0:T(8,128)(2,1)S(1)} %get-tuple-element.12) | copy-start | bytes 1572868
  140.4 39.4 %all-to-all-start.3 = ((bf16[64,32,256]{2,1,0:T(8,128)(2,1)}), bf16[64,32,256]{2,1,0:T(8,128)(2,1)}, u32[]{:S(2)}, u32[]{:S(2)}) async-start(bf16[64,32,256]{2,1,0:T(8,128)(2,1)} %bitcast.20), calls=%async_computation.3 | async-start | bytes 2097152 | tf_op jit(solution)/shard_map/all_to_all | solution.py:265
  147.8 21.4 %collective-permute-start.8 = (bf16[2,128,128]{2,1,0:T(8,128)(2,1)S(1)}, bf16[2,128,128]{2,1,0:T(8,128)(2,1)S(1)}, u32[]{:S(2)}, u32[]{:S(2)}) collective-permute-start(bf16[2,128,128]{2,1,0:T(8,128)(2,1)S(1)} %bitcast.25), channel_id=1, source_target_pairs={{0,4},{4,8},{8,12},{12,16},{16,20},{20,24},{24,28},{28,32},{32,36}... | collective-permute-start | bytes 196616 | tf_op jit(solution)/shard_map/ppermute | solution.py:259
  151.3 21.1 %collective-permute-start.9 = (bf16[2,128,128]{2,1,0:T(8,128)(2,1)S(1)}, bf16[2,128,128]{2,1,0:T(8,128)(2,1)S(1)}, u32[]{:S(2)}, u32[]{:S(2)}) collective-permute-start(bf16[2,128,128]{2,1,0:T(8,128)(2,1)S(1)} %bitcast.24), channel_id=1, source_target_pairs={{4,0},{8,4},{12,8},{16,12},{20,16},{24,20},{28,24},{32,28},{36,32}... | collective-permute-start | bytes 196616 | tf_op jit(solution)/shard_map/ppermute | solution.py:260
  179.8 1.0 copy-start.2
  180.9 1.2 copy-start.4
  (5 other events, 4.8 us)

commit v3 on v2

--- a/solution.py
+++ b/solution.py
@@ -9,8 +9,7 @@
 ITERS = 2
 BASE = 256
 FAR = (1, 2)
-LOW = tuple(range(1, 9))
-HIGH = tuple(range(9, 16)) + (0,)
+LIMIT = 12 << 20
 VMEM = pl.BlockSpec(memory_space=pltpu.VMEM)
 SMEM = pl.BlockSpec(memory_space=pltpu.SMEM)
 
@@ -42,7 +41,7 @@
     )(queries, digits)
 
 
-def select_pieces(held, slots, wanted=None):
+def select_pieces(held, slots, wanted, after):
     devices, height, cols = held.shape
     blocks = height // 16 * 8
     parts = 2
@@ -50,6 +49,7 @@
     group = 8
 
     def kernel(held_ref, *rest):
+        rest = rest[len(after) :]
         if wanted is None:
             out_ref, wanted_out, flat = rest
             digits = held_ref[:, parts * blocks :, :].astype(jnp.float32)[:, 0, :].T
@@ -78,79 +78,66 @@
     out_shape = [jax.ShapeDtypeStruct((devices * slots, parts * cols), held.dtype)]
     if wanted is None:
         out_shape.append(jax.ShapeDtypeStruct((slots, devices), jnp.int32))
-    operands = (held,) if wanted is None else (held, wanted)
+    operands = () if wanted is None else (wanted,)
     return pl.pallas_call(
         kernel,
         out_shape=out_shape,
-        in_specs=[VMEM] * len(operands),
+        in_specs=[VMEM] + [pl.BlockSpec(memory_space=pl.ANY)] * len(after) + [VMEM] * len(operands),
         out_specs=[VMEM] * len(out_shape),
         scratch_shapes=[pltpu.VMEM((block_total, parts * cols), held.dtype)],
-        compiler_params=pltpu.CompilerParams(vmem_limit_bytes=32 << 20),
+        compiler_params=pltpu.CompilerParams(vmem_limit_bytes=LIMIT),
         cost_estimate=pl.CostEstimate(
             flops=2 * devices * slots * block_total * parts * cols, bytes_accessed=2 << 20, transcendentals=0
         ),
         name="select_pieces",
-    )(*operands)
-
-
-def near_product(near_index, counts, quarters, low, own, high):
-    blocks, _, rows, size = quarters[0][0].shape
-    cols = own.shape[2]
+    )(held, *after, *operands)
+
+
+def near_product(near_index, counts, tiles, panels):
+    blocks, slots, rows, size = tiles.shape
+    reach, _, cols = panels[0].shape
+    number = len(panels)
     group = 4
-    number = len(quarters)
-    near = [(half, place, t) for half, names in enumerate((LOW, HIGH)) for place, t in enumerate(names)]
-    near = [entry for entry in near if entry[2] not in FAR]
-
-    def kernel(index_ref, count_ref, *refs):
-        tiles = [refs[2 * n : 2 * n + 2] for n in range(number)]
-        low_ref, own_ref, high_ref, out_ref, panels = refs[2 * number :]
+    near = [t for t in range(slots) if t not in FAR]
+
+    def kernel(index_ref, count_ref, tiles_ref, *refs):
+        panel_refs, out_refs = refs[:number], refs[number:]
         step = pl.program_id(0)
-
-        @pl.when(step == 0)
-        def _():
-            panels[:EDGE] = low_ref[...]
-            panels[EDGE : EDGE + blocks] = own_ref[...]
-            panels[EDGE + blocks :] = high_ref[...]
-
         for r in range(group):
             b = step * group + r
-            total = jnp.zeros((number * rows, cols), jnp.float32)
+            total = jnp.zeros((rows, number * cols), jnp.float32)
             for first in range(0, len(near), 2):
                 left, right = [], []
-                for half, place, t in near[first : first + 2]:
-                    tile = jnp.concatenate([pair[half][r, place] for pair in tiles], axis=0)
+                for t in near[first : first + 2]:
+                    tile = tiles_ref[r, t]
                     left.append(jnp.where(t < count_ref[b], tile, jnp.zeros_like(tile)))
-                    right.append(panels[index_ref[b, t]])
+                    right.append(jnp.concatenate([ref[index_ref[b, t]] for ref in panel_refs], axis=1))
                 total += jnp.dot(
                     jnp.concatenate(left, axis=1),
                     jnp.concatenate(right, axis=0),
                     preferred_element_type=jnp.float32,
                 )
-            out_ref[r] = total
-
-    return pl.pallas_call(
-        kernel,
-        out_shape=jax.ShapeDtypeStruct((blocks, number * rows, cols), jnp.float32),
+            for n in range(number):
+                out_refs[n][r] = total[:, n * cols : (n + 1) * cols]
+
+    out_shape = jax.ShapeDtypeStruct((blocks, rows, cols), jnp.float32)
+    return pl.pallas_call(
+        kernel,
+        out_shape=[out_shape] * number,
         grid_spec=pltpu.PrefetchScalarGridSpec(
             num_scalar_prefetch=2,
             grid=(blocks // group,),
-            in_specs=[
-                pl.BlockSpec((group, half.shape[1], rows, size), lambda i, *_: (i, 0, 0, 0))
-                for pair in quarters
-                for half in pair
-            ]
-            + [VMEM] * 3,
-            out_specs=pl.BlockSpec((group, number * rows, cols), lambda i, *_: (i, 0, 0)),
-            scratch_shapes=[pltpu.VMEM((blocks + 2 * EDGE, size, cols), own.dtype)],
-        ),
-        compiler_params=pltpu.CompilerParams(vmem_limit_bytes=32 << 20),
+            in_specs=[pl.BlockSpec((group, slots, rows, size), lambda i, *_: (i, 0, 0, 0))] + [VMEM] * number,
+            out_specs=[pl.BlockSpec((group, rows, cols), lambda i, *_: (i, 0, 0))] * number,
+        ),
+        compiler_params=pltpu.CompilerParams(vmem_limit_bytes=LIMIT),
         cost_estimate=pl.CostEstimate(
             flops=2 * blocks * len(near) * number * rows * size * cols,
-            bytes_accessed=number << 21,
+            bytes_accessed=6 << 20,
             transcendentals=0,
         ),
         name="near_product",
-    )(near_index, counts, *[half for pair in quarters for half in pair], low, own, high)
+    )(near_index, counts, tiles, *panels)
 
 
 def add_far(offsets, counts, far_tiles, arrived, partials, queries, owners, split):
@@ -206,12 +193,11 @@
         grid_spec=pltpu.PrefetchScalarGridSpec(
             num_scalar_prefetch=2,
             grid=(1,),
-            in_specs=[pl.BlockSpec((blocks, len(FAR), rows, size), lambda i, *_: (0, 0, 0, 0))] * number
-            + [VMEM] * (2 + len(partials)),
+            in_specs=[VMEM] * (number + 2 + len(partials)),
             out_specs=out_specs,
             scratch_shapes=scratch,
         ),
-        compiler_params=pltpu.CompilerParams(vmem_limit_bytes=32 << 20),
+        compiler_params=pltpu.CompilerParams(vmem_limit_bytes=LIMIT),
         cost_estimate=pl.CostEstimate(
             flops=4 * blocks * size * size * cols, bytes_accessed=4 << 20, transcendentals=0
         ),
@@ -219,19 +205,17 @@
     )(offsets, counts, *far_tiles, arrived, *partials, queries)
 
 
-def gather_rows(tiles):
+def from_all(mine):
     count = lax.axis_size("pb")
     up = [(i, (i + 1) % count) for i in range(count)]
     down = [((i + 1) % count, i) for i in range(count)]
-    low = tiles[:, LOW[0] : LOW[-1] + 1]
-    high = jnp.concatenate([tiles[:, HIGH[0] :], tiles[:, :1]], axis=1)
-    before_low = lax.ppermute(low, "pb", up)
-    after_high = lax.ppermute(high, "pb", down)
-    before_high = lax.ppermute(high, "pb", up)
-    after_low = lax.ppermute(low, "pb", down)
-    far_low = lax.ppermute(before_low, "pb", up)
-    far_high = lax.ppermute(after_high, "pb", down)
-    return [(low, high), (before_low, before_high), (after_low, after_high), (far_low, far_high)]
+    across = [(i, (i + 2) % count) for i in range(count)]
+    return [
+        mine[0],
+        lax.ppermute(mine[2], "pb", up),
+        lax.ppermute(mine[1], "pb", down),
+        lax.ppermute(mine[3], "pb", across),
+    ]
 
 
 def on_device(affinity_tiles, block_ids, valid_counts, queries):
@@ -240,8 +224,7 @@
     cols = queries.shape[1]
     owners = lax.axis_size("db")
     first_block = lax.axis_index("db") * blocks
-    quarters = gather_rows(affinity_tiles)
-    far_tiles = [pair[0] for pair in quarters]
+    far_tiles = from_all([affinity_tiles[:, FAR[0] : FAR[-1] + 1]] * 4)
     place = lax.axis_index("pb")
     offsets = jnp.stack([(place + shift) % lax.axis_size("pb") * rows for shift in (0, -1, 1, 2)])
     near_index = jnp.clip(block_ids - first_block + EDGE, 0, blocks + 2 * EDGE - 1)
@@ -255,20 +238,18 @@
     pieces = split_blocks(queries, digits, blocks, size, owners)
     for step in range(ITERS):
         own = ranking.reshape(blocks, size, cols)
-        held = lax.all_to_all(pieces, "db", split_axis=0, concat_axis=0, tiled=True)
         low = lax.ppermute(own[blocks - EDGE :], "db", up)
         high = lax.ppermute(own[:EDGE], "db", down)
+        panels = from_all([jnp.concatenate([low, own, high], axis=0)] * 4)
+        held = lax.all_to_all(pieces, "db", split_axis=0, concat_axis=0, tiled=True)
         if wanted is None:
-            chosen, wanted = select_pieces(held, slots)
+            chosen, wanted = select_pieces(held, slots, None, panels)
         else:
-            (chosen,) = select_pieces(held, slots, wanted)
+            (chosen,) = select_pieces(held, slots, wanted, panels)
         arrived = lax.all_to_all(
             chosen.reshape(owners, slots, -1), "db", split_axis=0, concat_axis=0, tiled=True
         ).reshape(chosen.shape)
-        partials = [
-            near_product(near_index, valid_counts, part, low, own, high)
-            for part in ([quarters[:3], quarters[3:]] if step == 0 else [quarters])
-        ]
+        partials = from_all(near_product(near_index, valid_counts, affinity_tiles, panels))
         done = add_far(offsets, valid_counts, far_tiles, arrived, partials, queries, owners, step < ITERS - 1)
         ranking = done[0]
         pieces = done[-1]

time: 188 us -> 238 us (1.27)
  starting transfers between devices: 46.4 us -> 93.5 us
  blocking collectives: 28.8 us -> 0 us
  local copies, waits for them, and re-layouts: 15.9 us -> 32 us
  waiting for transfers between devices: 64.7 us -> 79.8 us
    ppermute x6 -> x15, waiting for transfers between devices: 14.8 us -> 56.7 us  [the longest x5 35.2 us: from_all(): lax.ppermute(mine[3], 'pb', across)]
    all_to_all x1 -> x0, blocking collectives: 28.8 us -> none  [on_device(): held = lax.all_to_all(pieces, 'db', split_axis=0, concat_axis=0, tiled=True)]
    ppermute x2, waiting for transfers between devices: 27.3 us -> 0.01 us  [on_device(): low = lax.ppermute(own[blocks - EDGE:], 'db', up)]
    all_to_all x2, starting transfers between devices: 13 us -> 38.2 us  [on_device(): lax.all_to_all(chosen.reshape(owners, slots, -1), 'db', split_axis=0, con...]
    unnamed x28 -> x74, local copies, waits for them, and re-layouts: 11.3 us -> 30.5 us
    all_to_all x1 -> x2, waiting for transfers between devices: 14.8 us -> 0.01 us  [on_device(): held = lax.all_to_all(pieces, 'db', split_axis=0, concat_axis=0, tiled=True)]
    all_to_all x1 -> x2, starting transfers between devices: 13 us -> 25.6 us  [on_device(): held = lax.all_to_all(pieces, 'db', split_axis=0, concat_axis=0, tiled=True)]
    ppermute x2, waiting for transfers between devices: 7.88 us -> 20.3 us  [on_device(): high = lax.ppermute(own[:EDGE], 'db', down)]
  transfers between devices with their start and end apart: 13 -> 23, of which waited for: 6 -> 11; matrix products, arithmetic and copies ran while one was open for 2% -> 1% of each run, Pallas kernels for 9% -> 5%
where the time goes in v3:
time: 238 us; the launch traced here: 236 us
  starting transfers between devices  93.5 us (39%)
  waiting for transfers between devices  79.8 us (34%)
  local copies, waits for them, and re-layouts  32 us (13%)
  Pallas kernels  28.8 us (12%)
    all_to_all x2, starting transfers between devices, on_device(): lax.all_to_all(chosen.reshape(owners, slots, -1), 'db', split_axis=0, con...  38.2 us
    ppermute x5, waiting for transfers between devices, from_all(): lax.ppermute(mine[3], 'pb', across)  35.2 us
    unnamed x74, local copies, waits for them, and re-layouts  30.5 us
    all_to_all x2, starting transfers between devices, on_device(): held = lax.all_to_all(pieces, 'db', split_axis=0, concat_axis=0, tiled=True)  25.6 us
    ppermute x2, waiting for transfers between devices, on_device(): high = lax.ppermute(own[:EDGE], 'db', down)  20.3 us
    pallas_call x2, Pallas kernels, near_product(): pl.pallas_call(kernel, out_shape=[out_shape] * number, grid_spec=pltpu.Pr...  12.6 us
    ppermute x5, waiting for transfers between devices, from_all(): lax.ppermute(mine[1], 'pb', down)  12.3 us
    ppermute x5, waiting for transfers between devices, from_all(): lax.ppermute(mine[2], 'pb', up)  9.29 us
  transfers between devices with their start and end apart: 23, of which 11 were waited for; matrix products, arithmetic and copies ran while one was open for 1% of the time, Pallas kernels for 5%

profile of v3, /device:TPU:1, one launch (start us, length us, event | category | flops | bytes accessed | tf_op | source)
XLA Modules:
  0.0 236.4 jit_solution(11175030749015819031)
XLA Ops:
  1.5 2.6 %split_blocks.1 = bf16[64,40,128]{2,1,0:T(8,128)(2,1)} custom-call(bf16[2048,128]{1,0:T(8,128)(2,1)} %refs_9_.3, f32[1,128]{1,0:T(1,128)} %pad.4.digits_ref), custom_call_target="tpu_custom_call" | custom-call | tf_op jit(solution)/shard_map/split_blocks/pallas_call | solution.py:34
  4.1 13.2 %all-to-all-start = ((bf16[64,40,128]{2,1,0:T(8,128)(2,1)}), bf16[64,40,128]{2,1,0:T(8,128)(2,1)}, u32[]{:S(2)}, u32[]{:S(2)}) async-start(bf16[64,40,128]{2,1,0:T(8,128)(2,1)} %split_blocks.1), calls=%async_computation | async-start | bytes 1310720 | tf_op jit(solution)/shard_map/all_to_all | solution.py:244
  19.7 3.1 %collective-permute-start.3 = (bf16[2,128,128]{2,1,0:T(8,128)(2,1)S(1)}, bf16[2,128,128]{2,1,0:T(8,128)(2,1)S(1)}, u32[]{:S(2)}, u32[]{:S(2)}) collective-permute-start(bf16[2,128,128]{2,1,0:T(8,128)(2,1)S(1)} %bitcast.22), channel_id=1, source_target_pairs={{0,4},{4,8},{8,12},{12,16},{16,20},{20,24},{24,28},{28,32},{32,36}... | collective-permute-start | bytes 196616 | tf_op jit(solution)/shard_map/ppermute | solution.py:241
  22.9 11.5 %collective-permute-done.4 = bf16[2,128,128]{2,1,0:T(8,128)(2,1)S(1)} collective-permute-done((bf16[2,128,128]{2,1,0:T(8,128)(2,1)S(1)}, bf16[2,128,128]{2,1,0:T(8,128)(2,1)S(1)}, u32[]{:S(2)}, u32[]{:S(2)}) %collective-permute-start.4) | collective-permute-done | bytes 65568 | tf_op jit(solution)/shard_map/ppermute | solution.py:242
  34.5 3.0 %collective-permute-start.7 = (bf16[20,128,128]{2,1,0:T(8,128)(2,1)S(1)}, bf16[20,128,128]{2,1,0:T(8,128)(2,1)S(1)}, u32[]{:S(2)}, u32[]{:S(2)}) collective-permute-start(bf16[20,128,128]{2,1,0:T(8,128)(2,1)S(1)} %pad_maximum_fusion.rest_0_.refs_0_), channel_id=1, source_target_pairs={{0,2},{1,3},{2,0},{3,1},{4,6},{5,7},{6,4},{7,5},{8,10},{9,11},{10,... | collective-permute-start | bytes 1966088 | tf_op jit(solution)/shard_map/ppermute | solution.py:217
  39.0 9.8 %collective-permute-done.7.rest_3_.refs_3_ = bf16[20,128,128]{2,1,0:T(8,128)(2,1)S(1)} collective-permute-done((bf16[20,128,128]{2,1,0:T(8,128)(2,1)S(1)}, bf16[20,128,128]{2,1,0:T(8,128)(2,1)S(1)}, u32[]{:S(2)}, u32[]{:S(2)}) %collective-permute-start.7) | collective-permute-done | bytes 655392 | tf_op jit(solution)/shard_map/ppermute | solution.py:217
  49.7 6.4 %collective-permute-done.6.rest_2_.refs_2_ = bf16[20,128,128]{2,1,0:T(8,128)(2,1)S(1)} collective-permute-done((bf16[20,128,128]{2,1,0:T(8,128)(2,1)S(1)}, bf16[20,128,128]{2,1,0:T(8,128)(2,1)S(1)}, u32[]{:S(2)}, u32[]{:S(2)}) %collective-permute-start.6) | collective-permute-done | bytes 655392 | tf_op jit(solution)/shard_map/ppermute | solution.py:216
  65.2 20.5 %all-to-all-start.1 = ((bf16[64,32,256]{2,1,0:T(8,128)(2,1)}), bf16[64,32,256]{2,1,0:T(8,128)(2,1)}, u32[]{:S(2)}, u32[]{:S(2)}) async-start(bf16[64,32,256]{2,1,0:T(8,128)(2,1)} %bitcast.20), calls=%async_computation.1 | async-start | bytes 2097152 | tf_op jit(solution)/shard_map/all_to_all | solution.py:249
  93.1 6.7 %near_product.2 = (f32[16,32,128]{2,1,0:T(8,128)S(1)}, f32[16,32,128]{2,1,0:T(8,128)}, f32[16,32,128]{2,1,0:T(8,128)}, f32[16,32,128]{2,1,0:T(8,128)}) custom-call(s32[16,16]{1,0:T(8,128)S(1)} %add_clamp_fusion.index_ref, s32[16]{0:T(128)S(1)} %copy-done.36, bf16[16,16,32,128]{3,2,1,0:T(8,128)(2,1)S(1)} %copy-done, ...), custom_call_target="tpu_custom_call" | custom-call | flops 939524096 | bytes 6291456 | tf_op jit(solution)/shard_map/near_product/pallas_call | solution.py:124
  104.4 4.2 %collective-permute-done.8.refs_6_ = f32[16,32,128]{2,1,0:T(8,128)S(1)} collective-permute-done((f32[16,32,128]{2,1,0:T(8,128)}, f32[16,32,128]{2,1,0:T(8,128)S(1)}, u32[]{:S(2)}, u32[]{:S(2)}) %collective-permute-start.8) | collective-permute-done | bytes 262176 | tf_op jit(solution)/shard_map/ppermute | solution.py:215
  109.9 5.2 %collective-permute-done.10.refs_8_ = f32[16,32,128]{2,1,0:T(8,128)} collective-permute-done((f32[16,32,128]{2,1,0:T(8,128)}, f32[16,32,128]{2,1,0:T(8,128)}, u32[]{:S(2)}, u32[]{:S(2)}) %collective-permute-start.10) | collective-permute-done | bytes 262176 | tf_op jit(solution)/shard_map/ppermute | solution.py:217
  118.0 4.3 %add_far.2 = (bf16[2048,128]{1,0:T(8,128)(2,1)S(1)}, bf16[64,32,128]{2,1,0:T(8,128)(2,1)S(1)}) custom-call(s32[4]{0:T(128)S(1)} %pad_add_fusion.offset_ref, s32[16]{0:T(128)S(1)} %copy-done.36, bf16[16,2,32,128]{3,2,1,0:T(8,128)(2,1)S(1)} %slice.30.refs_0_, bf16[16,2,32,128]{3,2,1,0:T(8,128)(2,1)} %collective-permute-done.refs_1_, ...), custom_call_target="tpu_custom_call" | custom-call | flops 134217728 | bytes 4194304 | tf_op jit(solution)/shard_map/add_far/pallas_call | solution.py:190
  123.1 12.4 %all-to-all-start.2 = ((bf16[64,32,128]{2,1,0:T(8,128)(2,1)}), bf16[64,32,128]{2,1,0:T(8,128)(2,1)}, u32[]{:S(2)}, u32[]{:S(2)}) async-start(bf16[64,32,128]{2,1,0:T(8,128)(2,1)} %copy-done.23), calls=%async_computation.2 | async-start | bytes 1048576 | tf_op jit(solution)/shard_map/all_to_all | solution.py:244
  138.1 3.1 %collective-permute-start.11 = (bf16[2,128,128]{2,1,0:T(8,128)(2,1)S(1)}, bf16[2,128,128]{2,1,0:T(8,128)(2,1)S(1)}, u32[]{:S(2)}, u32[]{:S(2)}) collective-permute-start(bf16[2,128,128]{2,1,0:T(8,128)(2,1)S(1)} %bitcast.23), channel_id=1, source_target_pairs={{0,4},{4,8},{8,12},{12,16},{16,20},{20,24},{24,28},{28,32},{32,36}... | collective-permute-start | bytes 196616 | tf_op jit(solution)/shard_map/ppermute | solution.py:241
  141.2 8.7 %collective-permute-done.12 = bf16[2,128,128]{2,1,0:T(8,128)(2,1)S(1)} collective-permute-done((bf16[2,128,128]{2,1,0:T(8,128)(2,1)S(1)}, bf16[2,128,128]{2,1,0:T(8,128)(2,1)S(1)}, u32[]{:S(2)}, u32[]{:S(2)}) %collective-permute-start.12) | collective-permute-done | bytes 65568 | tf_op jit(solution)/shard_map/ppermute | solution.py:242
  151.3 3.0 %collective-permute-start.14 = (bf16[20,128,128]{2,1,0:T(8,128)(2,1)S(1)}, bf16[20,128,128]{2,1,0:T(8,128)(2,1)S(1)}, u32[]{:S(2)}, u32[]{:S(2)}) collective-permute-start(bf16[20,128,128]{2,1,0:T(8,128)(2,1)S(1)} %pad_maximum_fusion.1.rest_0_.refs_0_), channel_id=1, source_target_pairs={{1,0},{2,1},{3,2},{0,3},{5,4},{6,5},{7,6},{4,7},{9,8},{10,9},{11,1... | collective-permute-start | bytes 1966088 | tf_op jit(solution)/shard_map/ppermute | solution.py:216
  154.4 13.7 %collective-permute-done.15.rest_3_.refs_3_ = bf16[20,128,128]{2,1,0:T(8,128)(2,1)S(1)} collective-permute-done((bf16[20,128,128]{2,1,0:T(8,128)(2,1)S(1)}, bf16[20,128,128]{2,1,0:T(8,128)(2,1)S(1)}, u32[]{:S(2)}, u32[]{:S(2)}) %collective-permute-start.15) | collective-permute-done | bytes 655392 | tf_op jit(solution)/shard_map/ppermute | solution.py:217
  169.0 5.8 %collective-permute-done.14.rest_2_.refs_2_ = bf16[20,128,128]{2,1,0:T(8,128)(2,1)S(1)} collective-permute-done((bf16[20,128,128]{2,1,0:T(8,128)(2,1)S(1)}, bf16[20,128,128]{2,1,0:T(8,128)(2,1)S(1)}, u32[]{:S(2)}, u32[]{:S(2)}) %collective-permute-start.14) | collective-permute-done | bytes 655392 | tf_op jit(solution)/shard_map/ppermute | solution.py:216
  183.8 17.7 %all-to-all-start.3 = ((bf16[64,32,256]{2,1,0:T(8,128)(2,1)}), bf16[64,32,256]{2,1,0:T(8,128)(2,1)}, u32[]{:S(2)}, u32[]{:S(2)}) async-start(bf16[64,32,256]{2,1,0:T(8,128)(2,1)} %bitcast.19), calls=%async_computation.3 | async-start | bytes 2097152 | tf_op jit(solution)/shard_map/all_to_all | solution.py:249
  204.8 5.9 %near_product.3 = (f32[16,32,128]{2,1,0:T(8,128)S(1)}, f32[16,32,128]{2,1,0:T(8,128)S(1)}, f32[16,32,128]{2,1,0:T(8,128)S(1)}, f32[16,32,128]{2,1,0:T(8,128)S(1)}) custom-call(s32[16,16]{1,0:T(8,128)S(1)} %add_clamp_fusion.index_ref, s32[16]{0:T(128)S(1)} %copy-done.36, bf16[16,16,32,128]{3,2,1,0:T(8,128)(2,1)S(1)} %copy-done, ...), custom_call_target="tpu_custom_call" | custom-call | flops 939524096 | bytes 6291456 | tf_op jit(solution)/shard_map/near_product/pallas_call | solution.py:124
  215.0 5.1 %collective-permute-done.16.refs_6_ = f32[16,32,128]{2,1,0:T(8,128)S(1)} collective-permute-done((f32[16,32,128]{2,1,0:T(8,128)S(1)}, f32[16,32,128]{2,1,0:T(8,128)S(1)}, u32[]{:S(2)}, u32[]{:S(2)}) %collective-permute-start.16) | collective-permute-done | bytes 262176 | tf_op jit(solution)/shard_map/ppermute | solution.py:215
  220.1 6.4 %collective-permute-done.18.refs_8_ = f32[16,32,128]{2,1,0:T(8,128)S(1)} collective-permute-done((f32[16,32,128]{2,1,0:T(8,128)S(1)}, f32[16,32,128]{2,1,0:T(8,128)S(1)}, u32[]{:S(2)}, u32[]{:S(2)}) %collective-permute-start.18) | collective-permute-done | bytes 262176 | tf_op jit(solution)/shard_map/ppermute | solution.py:217
  227.2 2.8 %all-to-all-done.3 = bf16[64,32,256]{2,1,0:T(8,128)(2,1)} async-done(((bf16[64,32,256]{2,1,0:T(8,128)(2,1)}), bf16[64,32,256]{2,1,0:T(8,128)(2,1)}, u32[]{:S(2)}, u32[]{:S(2)}) %all-to-all-start.3) | async-done | bytes 1048608 | tf_op jit(solution)/shard_map/all_to_all | solution.py:249
  231.9 4.5 %add_far.3 = bf16[2048,128]{1,0:T(8,128)(2,1)} custom-call(s32[4]{0:T(128)S(1)} %pad_add_fusion.offset_ref, s32[16]{0:T(128)S(1)} %copy-done.36, bf16[16,2,32,128]{3,2,1,0:T(8,128)(2,1)S(1)} %slice.30.refs_0_, bf16[16,2,32,128]{3,2,1,0:T(8,128)(2,1)} %collective-permute-done.refs_1_, bf16[16,2,32,128]{3,2,1,0:T(8,128)(2,1)} %collective-permute-done.1.refs_2_, ...), custom_call_target="tpu_custom_call" | custom-call | flops 134217728 | bytes 4194304 | tf_op jit(solution)/shard_map/add_far/pallas_call | solution.py:190
  (115 shorter events, 56.3 us)
Async XLA Ops:
  4.1 53.7 %all-to-all-start = ((bf16[64,40,128]{2,1,0:T(8,128)(2,1)}), bf16[64,40,128]{2,1,0:T(8,128)(2,1)}, u32[]{:S(2)}, u32[]{:S(2)}) async-start(bf16[64,40,128]{2,1,0:T(8,128)(2,1)} %split_blocks.1), calls=%async_computation | async-start | bytes 1310720 | tf_op jit(solution)/shard_map/all_to_all | solution.py:244
  17.3 17.1 %collective-permute-start.4 = (bf16[2,128,128]{2,1,0:T(8,128)(2,1)S(1)}, bf16[2,128,128]{2,1,0:T(8,128)(2,1)S(1)}, u32[]{:S(2)}, u32[]{:S(2)}) collective-permute-start(bf16[2,128,128]{2,1,0:T(8,128)(2,1)S(1)} %bitcast.24), channel_id=1, source_target_pairs={{4,0},{8,4},{12,8},{16,12},{20,16},{24,20},{28,24},{32,28},{36,32}... | collective-permute-start | bytes 196616 | tf_op jit(solution)/shard_map/ppermute | solution.py:242
  19.7 14.7 %collective-permute-start.3 = (bf16[2,128,128]{2,1,0:T(8,128)(2,1)S(1)}, bf16[2,128,128]{2,1,0:T(8,128)(2,1)S(1)}, u32[]{:S(2)}, u32[]{:S(2)}) collective-permute-start(bf16[2,128,128]{2,1,0:T(8,128)(2,1)S(1)} %bitcast.22), channel_id=1, source_target_pairs={{0,4},{4,8},{8,12},{12,16},{16,20},{20,24},{24,28},{28,32},{32,36}... | collective-permute-start | bytes 196616 | tf_op jit(solution)/shard_map/ppermute | solution.py:241
  34.5 51.2 %copy-start = (bf16[16,16,32,128]{3,2,1,0:T(8,128)(2,1)S(1)}, bf16[16,16,32,128]{3,2,1,0:T(8,128)(2,1)}, u32[]{:S(2)}) copy-start(bf16[16,16,32,128]{3,2,1,0:T(8,128)(2,1)} %tiles_ref.3) | copy-start | bytes 6291460
  34.5 14.3 %collective-permute-start.7 = (bf16[20,128,128]{2,1,0:T(8,128)(2,1)S(1)}, bf16[20,128,128]{2,1,0:T(8,128)(2,1)S(1)}, u32[]{:S(2)}, u32[]{:S(2)}) collective-permute-start(bf16[20,128,128]{2,1,0:T(8,128)(2,1)S(1)} %pad_maximum_fusion.rest_0_.refs_0_), channel_id=1, source_target_pairs={{0,2},{1,3},{2,0},{3,1},{4,6},{5,7},{6,4},{7,5},{8,10},{9,11},{10,... | collective-permute-start | bytes 1966088 | tf_op jit(solution)/shard_map/ppermute | solution.py:217
  37.5 18.6 %collective-permute-start.6 = (bf16[20,128,128]{2,1,0:T(8,128)(2,1)S(1)}, bf16[20,128,128]{2,1,0:T(8,128)(2,1)S(1)}, u32[]{:S(2)}, u32[]{:S(2)}) collective-permute-start(bf16[20,128,128]{2,1,0:T(8,128)(2,1)S(1)} %pad_maximum_fusion.rest_0_.refs_0_), channel_id=1, source_target_pairs={{1,0},{2,1},{3,2},{0,3},{5,4},{6,5},{7,6},{4,7},{9,8},{10,9},{11,1... | collective-permute-start | bytes 1966088 | tf_op jit(solution)/shard_map/ppermute | solution.py:216
  38.3 18.7 %collective-permute-start.5 = (bf16[20,128,128]{2,1,0:T(8,128)(2,1)S(1)}, bf16[20,128,128]{2,1,0:T(8,128)(2,1)S(1)}, u32[]{:S(2)}, u32[]{:S(2)}) collective-permute-start(bf16[20,128,128]{2,1,0:T(8,128)(2,1)S(1)} %pad_maximum_fusion.rest_0_.refs_0_), channel_id=1, source_target_pairs={{0,1},{1,2},{2,3},{3,0},{4,5},{5,6},{6,7},{7,4},{8,9},{9,10},{10,1... | collective-permute-start | bytes 1966088 | tf_op jit(solution)/shard_map/ppermute | solution.py:215
  65.2 50.0 %all-to-all-start.1 = ((bf16[64,32,256]{2,1,0:T(8,128)(2,1)}), bf16[64,32,256]{2,1,0:T(8,128)(2,1)}, u32[]{:S(2)}, u32[]{:S(2)}) async-start(bf16[64,32,256]{2,1,0:T(8,128)(2,1)} %bitcast.20), calls=%async_computation.1 | async-start | bytes 2097152 | tf_op jit(solution)/shard_map/all_to_all | solution.py:249
  85.7 17.4 %collective-permute-start.2 = (bf16[16,2,32,128]{3,2,1,0:T(8,128)(2,1)S(1)}, bf16[16,2,32,128]{3,2,1,0:T(8,128)(2,1)}, u32[]{:S(2)}, u32[]{:S(2)}) collective-permute-start(bf16[16,2,32,128]{3,2,1,0:T(8,128)(2,1)S(1)} %slice.30.refs_0_), channel_id=1, source_target_pairs={{0,2},{1,3},{2,0},{3,1},{4,6},{5,7},{6,4},{7,5},{8,10},{9,11},{10,... | collective-permute-start | bytes 786440 | tf_op jit(solution)/shard_map/ppermute | solution.py:217
  87.5 16.9 %collective-permute-start.1 = (bf16[16,2,32,128]{3,2,1,0:T(8,128)(2,1)S(1)}, bf16[16,2,32,128]{3,2,1,0:T(8,128)(2,1)}, u32[]{:S(2)}, u32[]{:S(2)}) collective-permute-start(bf16[16,2,32,128]{3,2,1,0:T(8,128)(2,1)S(1)} %slice.30.refs_0_), channel_id=1, source_target_pairs={{1,0},{2,1},{3,2},{0,3},{5,4},{6,5},{7,6},{4,7},{9,8},{10,9},{11,1... | collective-permute-start | bytes 786440 | tf_op jit(solution)/shard_map/ppermute | solution.py:216
  89.1 15.3 %collective-permute-start = (bf16[16,2,32,128]{3,2,1,0:T(8,128)(2,1)S(1)}, bf16[16,2,32,128]{3,2,1,0:T(8,128)(2,1)}, u32[]{:S(2)}, u32[]{:S(2)}) collective-permute-start(bf16[16,2,32,128]{3,2,1,0:T(8,128)(2,1)S(1)} %slice.30.refs_0_), channel_id=1, source_target_pairs={{0,1},{1,2},{2,3},{3,0},{4,5},{5,6},{6,7},{7,4},{8,9},{9,10},{10,1... | collective-permute-start | bytes 786440 | tf_op jit(solution)/shard_map/ppermute | solution.py:215
  100.4 8.1 %collective-permute-start.8 = (f32[16,32,128]{2,1,0:T(8,128)}, f32[16,32,128]{2,1,0:T(8,128)S(1)}, u32[]{:S(2)}, u32[]{:S(2)}) collective-permute-start(f32[16,32,128]{2,1,0:T(8,128)} %get-tuple-element.19), channel_id=1, source_target_pairs={{0,1},{1,2},{2,3},{3,0},{4,5},{5,6},{6,7},{7,4},{8,9},{9,10},{10,1... | collective-permute-start | bytes 786440 | tf_op jit(solution)/shard_map/ppermute | solution.py:215
  101.5 7.7 %collective-permute-start.9 = (f32[16,32,128]{2,1,0:T(8,128)}, f32[16,32,128]{2,1,0:T(8,128)S(1)}, u32[]{:S(2)}, u32[]{:S(2)}) collective-permute-start(f32[16,32,128]{2,1,0:T(8,128)} %get-tuple-element.20), channel_id=1, source_target_pairs={{1,0},{2,1},{3,2},{0,3},{5,4},{6,5},{7,6},{4,7},{9,8},{10,9},{11,1... | collective-permute-start | bytes 786440 | tf_op jit(solution)/shard_map/ppermute | solution.py:216
  103.1 12.1 %collective-permute-start.10 = (f32[16,32,128]{2,1,0:T(8,128)}, f32[16,32,128]{2,1,0:T(8,128)}, u32[]{:S(2)}, u32[]{:S(2)}) collective-permute-start(f32[16,32,128]{2,1,0:T(8,128)} %get-tuple-element.21), channel_id=1, source_target_pairs={{0,2},{1,3},{2,0},{3,1},{4,6},{5,7},{6,4},{7,5},{8,10},{9,11},{10,... | collective-permute-start | bytes 786440 | tf_op jit(solution)/shard_map/ppermute | solution.py:217
  123.1 53.3 %all-to-all-start.2 = ((bf16[64,32,128]{2,1,0:T(8,128)(2,1)}), bf16[64,32,128]{2,1,0:T(8,128)(2,1)}, u32[]{:S(2)}, u32[]{:S(2)}) async-start(bf16[64,32,128]{2,1,0:T(8,128)(2,1)} %copy-done.23), calls=%async_computation.2 | async-start | bytes 1048576 | tf_op jit(solution)/shard_map/all_to_all | solution.py:244
  135.6 14.3 %collective-permute-start.12 = (bf16[2,128,128]{2,1,0:T(8,128)(2,1)S(1)}, bf16[2,128,128]{2,1,0:T(8,128)(2,1)S(1)}, u32[]{:S(2)}, u32[]{:S(2)}) collective-permute-start(bf16[2,128,128]{2,1,0:T(8,128)(2,1)S(1)} %bitcast.25), channel_id=1, source_target_pairs={{4,0},{8,4},{12,8},{16,12},{20,16},{24,20},{28,24},{32,28},{36,32}... | collective-permute-start | bytes 196616 | tf_op jit(solution)/shard_map/ppermute | solution.py:242
  138.1 11.9 %collective-permute-start.11 = (bf16[2,128,128]{2,1,0:T(8,128)(2,1)S(1)}, bf16[2,128,128]{2,1,0:T(8,128)(2,1)S(1)}, u32[]{:S(2)}, u32[]{:S(2)}) collective-permute-start(bf16[2,128,128]{2,1,0:T(8,128)(2,1)S(1)} %bitcast.23), channel_id=1, source_target_pairs={{0,4},{4,8},{8,12},{12,16},{16,20},{20,24},{24,28},{28,32},{32,36}... | collective-permute-start | bytes 196616 | tf_op jit(solution)/shard_map/ppermute | solution.py:241
  151.1 17.1 %collective-permute-start.15 = (bf16[20,128,128]{2,1,0:T(8,128)(2,1)S(1)}, bf16[20,128,128]{2,1,0:T(8,128)(2,1)S(1)}, u32[]{:S(2)}, u32[]{:S(2)}) collective-permute-start(bf16[20,128,128]{2,1,0:T(8,128)(2,1)S(1)} %pad_maximum_fusion.1.rest_0_.refs_0_), channel_id=1, source_target_pairs={{0,2},{1,3},{2,0},{3,1},{4,6},{5,7},{6,4},{7,5},{8,10},{9,11},{10,... | collective-permute-start | bytes 1966088 | tf_op jit(solution)/shard_map/ppermute | solution.py:217
  151.3 23.5 %collective-permute-start.14 = (bf16[20,128,128]{2,1,0:T(8,128)(2,1)S(1)}, bf16[20,128,128]{2,1,0:T(8,128)(2,1)S(1)}, u32[]{:S(2)}, u32[]{:S(2)}) collective-permute-start(bf16[20,128,128]{2,1,0:T(8,128)(2,1)S(1)} %pad_maximum_fusion.1.rest_0_.refs_0_), channel_id=1, source_target_pairs={{1,0},{2,1},{3,2},{0,3},{5,4},{6,5},{7,6},{4,7},{9,8},{10,9},{11,1... | collective-permute-start | bytes 1966088 | tf_op jit(solution)/shard_map/ppermute | solution.py:216
  154.4 21.2 %collective-permute-start.13 = (bf16[20,128,128]{2,1,0:T(8,128)(2,1)S(1)}, bf16[20,128,128]{2,1,0:T(8,128)(2,1)S(1)}, u32[]{:S(2)}, u32[]{:S(2)}) collective-permute-start(bf16[20,128,128]{2,1,0:T(8,128)(2,1)S(1)} %pad_maximum_fusion.1.rest_0_.refs_0_), channel_id=1, source_target_pairs={{0,1},{1,2},{2,3},{3,0},{4,5},{5,6},{6,7},{7,4},{8,9},{9,10},{10,1... | collective-permute-start | bytes 1966088 | tf_op jit(solution)/shard_map/ppermute | solution.py:215
  183.8 46.2 %all-to-all-start.3 = ((bf16[64,32,256]{2,1,0:T(8,128)(2,1)}), bf16[64,32,256]{2,1,0:T(8,128)(2,1)}, u32[]{:S(2)}, u32[]{:S(2)}) async-start(bf16[64,32,256]{2,1,0:T(8,128)(2,1)} %bitcast.19), calls=%async_computation.3 | async-start | bytes 2097152 | tf_op jit(solution)/shard_map/all_to_all | solution.py:249
  211.5 8.7 %collective-permute-start.16 = (f32[16,32,128]{2,1,0:T(8,128)S(1)}, f32[16,32,128]{2,1,0:T(8,128)S(1)}, u32[]{:S(2)}, u32[]{:S(2)}) collective-permute-start(f32[16,32,128]{2,1,0:T(8,128)S(1)} %get-tuple-element.26), channel_id=1, source_target_pairs={{0,1},{1,2},{2,3},{3,0},{4,5},{5,6},{6,7},{7,4},{8,9},{9,10},{10,1... | collective-permute-start | bytes 786440 | tf_op jit(solution)/shard_map/ppermute | solution.py:215
  212.6 7.6 %collective-permute-start.17 = (f32[16,32,128]{2,1,0:T(8,128)S(1)}, f32[16,32,128]{2,1,0:T(8,128)S(1)}, u32[]{:S(2)}, u32[]{:S(2)}) collective-permute-start(f32[16,32,128]{2,1,0:T(8,128)S(1)} %get-tuple-element.27), channel_id=1, source_target_pairs={{1,0},{2,1},{3,2},{0,3},{5,4},{6,5},{7,6},{4,7},{9,8},{10,9},{11,1... | collective-permute-start | bytes 786440 | tf_op jit(solution)/shard_map/ppermute | solution.py:216
  214.1 12.4 %collective-permute-start.18 = (f32[16,32,128]{2,1,0:T(8,128)S(1)}, f32[16,32,128]{2,1,0:T(8,128)S(1)}, u32[]{:S(2)}, u32[]{:S(2)}) collective-permute-start(f32[16,32,128]{2,1,0:T(8,128)S(1)} %get-tuple-element.28), channel_id=1, source_target_pairs={{0,2},{1,3},{2,0},{3,1},{4,6},{5,7},{6,4},{7,5},{8,10},{9,11},{10,... | collective-permute-start | bytes 786440 | tf_op jit(solution)/shard_map/ppermute | solution.py:217
  (36 other events, 99.8 us)

commit v4 on v3

--- a/solution.py
+++ b/solution.py
@@ -41,7 +41,7 @@
     )(queries, digits)
 
 
-def select_pieces(held, slots, wanted, after):
+def select_pieces(held, slots, wanted=None):
     devices, height, cols = held.shape
     blocks = height // 16 * 8
     parts = 2
@@ -49,7 +49,6 @@
     group = 8
 
     def kernel(held_ref, *rest):
-        rest = rest[len(after) :]
         if wanted is None:
             out_ref, wanted_out, flat = rest
             digits = held_ref[:, parts * blocks :, :].astype(jnp.float32)[:, 0, :].T
@@ -82,7 +81,7 @@
     return pl.pallas_call(
         kernel,
         out_shape=out_shape,
-        in_specs=[VMEM] + [pl.BlockSpec(memory_space=pl.ANY)] * len(after) + [VMEM] * len(operands),
+        in_specs=[VMEM] * (1 + len(operands)),
         out_specs=[VMEM] * len(out_shape),
         scratch_shapes=[pltpu.VMEM((block_total, parts * cols), held.dtype)],
         compiler_params=pltpu.CompilerParams(vmem_limit_bytes=LIMIT),
@@ -90,19 +89,27 @@
             flops=2 * devices * slots * block_total * parts * cols, bytes_accessed=2 << 20, transcendentals=0
         ),
         name="select_pieces",
-    )(held, *after, *operands)
-
-
-def near_product(near_index, counts, tiles, panels):
+    )(held, *operands)
+
+
+def near_product(near_index, counts, places, tiles, own, edges):
     blocks, slots, rows, size = tiles.shape
-    reach, _, cols = panels[0].shape
-    number = len(panels)
+    cols = own.shape[3]
+    number = len(edges)
     group = 4
     near = [t for t in range(slots) if t not in FAR]
 
-    def kernel(index_ref, count_ref, tiles_ref, *refs):
-        panel_refs, out_refs = refs[:number], refs[number:]
+    def kernel(index_ref, count_ref, place_ref, tiles_ref, own_ref, *refs):
+        edge_refs, out_refs, panels = refs[:number], refs[number : 2 * number], refs[2 * number]
         step = pl.program_id(0)
+
+        @pl.when(step == 0)
+        def _():
+            for n in range(number):
+                panels[n, :EDGE] = edge_refs[n][:EDGE]
+                panels[n, EDGE : EDGE + blocks] = own_ref[place_ref[n]]
+                panels[n, EDGE + blocks :] = edge_refs[n][EDGE:]
+
         for r in range(group):
             b = step * group + r
             total = jnp.zeros((rows, number * cols), jnp.float32)
@@ -111,7 +118,7 @@
                 for t in near[first : first + 2]:
                     tile = tiles_ref[r, t]
                     left.append(jnp.where(t < count_ref[b], tile, jnp.zeros_like(tile)))
-                    right.append(jnp.concatenate([ref[index_ref[b, t]] for ref in panel_refs], axis=1))
+                    right.append(jnp.concatenate([panels[n, index_ref[b, t]] for n in range(number)], axis=1))
                 total += jnp.dot(
                     jnp.concatenate(left, axis=1),
                     jnp.concatenate(right, axis=0),
@@ -125,10 +132,12 @@
         kernel,
         out_shape=[out_shape] * number,
         grid_spec=pltpu.PrefetchScalarGridSpec(
-            num_scalar_prefetch=2,
+            num_scalar_prefetch=3,
             grid=(blocks // group,),
-            in_specs=[pl.BlockSpec((group, slots, rows, size), lambda i, *_: (i, 0, 0, 0))] + [VMEM] * number,
+            in_specs=[pl.BlockSpec((group, slots, rows, size), lambda i, *_: (i, 0, 0, 0))]
+            + [VMEM] * (1 + number),
             out_specs=[pl.BlockSpec((group, rows, cols), lambda i, *_: (i, 0, 0))] * number,
+            scratch_shapes=[pltpu.VMEM((number, blocks + 2 * EDGE, size, cols), own.dtype)],
         ),
         compiler_params=pltpu.CompilerParams(vmem_limit_bytes=LIMIT),
         cost_estimate=pl.CostEstimate(
@@ -137,7 +146,7 @@
             transcendentals=0,
         ),
         name="near_product",
-    )(near_index, counts, tiles, *panels)
+    )(near_index, counts, places, tiles, own, *edges)
 
 
 def add_far(offsets, counts, far_tiles, arrived, partials, queries, owners, split):
@@ -226,7 +235,8 @@
     first_block = lax.axis_index("db") * blocks
     far_tiles = from_all([affinity_tiles[:, FAR[0] : FAR[-1] + 1]] * 4)
     place = lax.axis_index("pb")
-    offsets = jnp.stack([(place + shift) % lax.axis_size("pb") * rows for shift in (0, -1, 1, 2)])
+    places = jnp.stack([(place + shift) % lax.axis_size("pb") for shift in (0, -1, 1, 2)])
+    offsets = places * rows
     near_index = jnp.clip(block_ids - first_block + EDGE, 0, blocks + 2 * EDGE - 1)
     far = block_ids[:, FAR[0] : FAR[-1] + 1].reshape(1, -1)
     slots = far.shape[1]
@@ -240,16 +250,17 @@
         own = ranking.reshape(blocks, size, cols)
         low = lax.ppermute(own[blocks - EDGE :], "db", up)
         high = lax.ppermute(own[:EDGE], "db", down)
-        panels = from_all([jnp.concatenate([low, own, high], axis=0)] * 4)
+        whole = lax.all_gather(own, "pb", axis=0)
+        edges = from_all([jnp.concatenate([low, high], axis=0)] * 4)
         held = lax.all_to_all(pieces, "db", split_axis=0, concat_axis=0, tiled=True)
         if wanted is None:
-            chosen, wanted = select_pieces(held, slots, None, panels)
+            chosen, wanted = select_pieces(held, slots)
         else:
-            (chosen,) = select_pieces(held, slots, wanted, panels)
+            (chosen,) = select_pieces(held, slots, wanted)
         arrived = lax.all_to_all(
             chosen.reshape(owners, slots, -1), "db", split_axis=0, concat_axis=0, tiled=True
         ).reshape(chosen.shape)
-        partials = from_all(near_product(near_index, valid_counts, affinity_tiles, panels))
+        partials = from_all(near_product(near_index, valid_counts, places, affinity_tiles, whole, edges))
         done = add_far(offsets, valid_counts, far_tiles, arrived, partials, queries, owners, step < ITERS - 1)
         ranking = done[0]
         pieces = done[-1]

time: 238 us -> 240 us (level)
  the two profiles are of different devices: /device:TPU:1 before, /device:TPU:4 now
where the time goes in v4:
time: 240 us; the launch traced here: 239 us
  waiting for transfers between devices  61 us (25%)
  blocking collectives  57.7 us (24%)
  starting transfers between devices  50.6 us (21%)
  Pallas kernels  28.7 us (12%)
  local copies, waits for them, and re-layouts  26.1 us (11%)
  between operations  13.6 us (6%)
    all_to_all x2, blocking collectives, on_device(): held = lax.all_to_all(pieces, 'db', split_axis=0, concat_axis=0, tiled=True)  57.7 us
    ppermute x2, waiting for transfers between devices, on_device(): low = lax.ppermute(own[blocks - EDGE:], 'db', up)  30.9 us
    unnamed x60, local copies, waits for them, and re-layouts  22.3 us
    ppermute x5, waiting for transfers between devices, from_all(): lax.ppermute(mine[2], 'pb', up)  17.9 us
    pallas_call x2, Pallas kernels, near_product(): pl.pallas_call(kernel, out_shape=[out_shape] * number, grid_spec=pltpu.Pr...  14.8 us
    all_to_all x2, starting transfers between devices, on_device(): lax.all_to_all(chosen.reshape(owners, slots, -1), 'db', split_axis=0, con...  14.5 us
    ppermute x2, starting transfers between devices, on_device(): high = lax.ppermute(own[:EDGE], 'db', down)  10.7 us
    ppermute x5, starting transfers between devices, from_all(): lax.ppermute(mine[1], 'pb', down)  10.6 us
  transfers between devices with their start and end apart: 23, of which 12 were waited for; matrix products, arithmetic and copies ran while one was open for 3% of the time, Pallas kernels for 8%

profile of v4, /device:TPU:4, one launch (start us, length us, event | category | flops | bytes accessed | tf_op | source)
XLA Modules:
  0.0 239.1 jit_solution(1285102266276105004)
XLA Ops:
  8.7 2.6 %split_blocks.1 = bf16[64,40,128]{2,1,0:T(8,128)(2,1)} custom-call(bf16[2048,128]{1,0:T(8,128)(2,1)} %refs_9_.3, f32[1,128]{1,0:T(1,128)} %pad.4.digits_ref), custom_call_target="tpu_custom_call" | custom-call | tf_op jit(solution)/shard_map/split_blocks/pallas_call | solution.py:34
  11.3 31.4 %all_to_all.20.held_ref = bf16[64,40,128]{2,1,0:T(8,128)(2,1)S(1)} all-to-all(bf16[64,40,128]{2,1,0:T(8,128)(2,1)} %split_blocks.1), channel_id=1, replica_groups=mesh['db'=64,'pb'=4] {'db'}, dimensions={0} | all-to-all | bytes 1310720 | tf_op jit(solution)/shard_map/all_to_all | solution.py:255
  45.7 7.4 %all-to-all-start.1 = ((bf16[64,32,256]{2,1,0:T(8,128)(2,1)}), bf16[64,32,256]{2,1,0:T(8,128)(2,1)}, u32[]{:S(2)}, u32[]{:S(2)}) async-start(bf16[64,32,256]{2,1,0:T(8,128)(2,1)} %bitcast.19), calls=%async_computation.1 | async-start | bytes 2097152 | tf_op jit(solution)/shard_map/all_to_all | solution.py:260
  55.9 3.3 %collective-permute-start.2 = (bf16[16,2,32,128]{3,2,1,0:T(8,128)(2,1)S(1)}, bf16[16,2,32,128]{3,2,1,0:T(8,128)(2,1)S(1)}, u32[]{:S(2)}, u32[]{:S(2)}) collective-permute-start(bf16[16,2,32,128]{3,2,1,0:T(8,128)(2,1)S(1)} %slice.30.refs_0_), channel_id=1, source_target_pairs={{0,2},{1,3},{2,0},{3,1},{4,6},{5,7},{6,4},{7,5},{8,10},{9,11},{10,... | collective-permute-start | bytes 786440 | tf_op jit(solution)/shard_map/ppermute | solution.py:226
  60.3 5.0 %collective-permute-start.4 = (bf16[2,128,128]{2,1,0:T(8,128)(2,1)}, bf16[2,128,128]{2,1,0:T(8,128)(2,1)}, u32[]{:S(2)}, u32[]{:S(2)}) collective-permute-start(bf16[2,128,128]{2,1,0:T(8,128)(2,1)} %bitcast.10), channel_id=1, source_target_pairs={{4,0},{8,4},{12,8},{16,12},{20,16},{24,20},{28,24},{32,28},{36,32}... | collective-permute-start | bytes 196616 | tf_op jit(solution)/shard_map/ppermute | solution.py:252
  65.3 13.7 %collective-permute-done.3 = bf16[2,128,128]{2,1,0:T(8,128)(2,1)} collective-permute-done((bf16[2,128,128]{2,1,0:T(8,128)(2,1)S(1)}, bf16[2,128,128]{2,1,0:T(8,128)(2,1)}, u32[]{:S(2)}, u32[]{:S(2)}) %collective-permute-start.3) | collective-permute-done | bytes 65568 | tf_op jit(solution)/shard_map/ppermute | solution.py:251
  80.7 3.3 %collective-permute-start.7 = (bf16[4,128,128]{2,1,0:T(8,128)(2,1)S(1)}, bf16[4,128,128]{2,1,0:T(8,128)(2,1)}, u32[]{:S(2)}, u32[]{:S(2)}) collective-permute-start(bf16[4,128,128]{2,1,0:T(8,128)(2,1)S(1)} %constant_dynamic-update-slice_fusion.refs_0_), channel_id=1, source_target_pairs={{0,2},{1,3},{2,0},{3,1},{4,6},{5,7},{6,4},{7,5},{8,10},{9,11},{10,... | collective-permute-start | bytes 393224 | tf_op jit(solution)/shard_map/ppermute | solution.py:226
  89.8 3.1 %collective-permute-done.5.refs_1_ = bf16[4,128,128]{2,1,0:T(8,128)(2,1)} collective-permute-done((bf16[4,128,128]{2,1,0:T(8,128)(2,1)S(1)}, bf16[4,128,128]{2,1,0:T(8,128)(2,1)}, u32[]{:S(2)}, u32[]{:S(2)}) %collective-permute-start.5) | collective-permute-done | bytes 131104 | tf_op jit(solution)/shard_map/ppermute | solution.py:224
  95.0 7.9 %near_product.2 = (f32[16,32,128]{2,1,0:T(8,128)S(1)}, f32[16,32,128]{2,1,0:T(8,128)}, f32[16,32,128]{2,1,0:T(8,128)}, f32[16,32,128]{2,1,0:T(8,128)}) custom-call(s32[16,16]{1,0:T(8,128)S(1)} %add_clamp_fusion.index_ref, s32[16]{0:T(128)S(1)} %copy-done.24, s32[4]{0:T(128)S(1)} %copy-done.25, bf16[16,16,32,128]{3,2,1,0:T(8,128)(2,1)S(1)} %copy-done.1, ...), custom_call_target="tpu_custom_call" | custom-call | flops 939524096 | bytes 6291456 | tf_op jit(solution)/shard_map/near_product/pallas_call | solution.py:131
  103.7 3.2 %collective-permute-start.9 = (f32[16,32,128]{2,1,0:T(8,128)}, f32[16,32,128]{2,1,0:T(8,128)}, u32[]{:S(2)}, u32[]{:S(2)}) collective-permute-start(f32[16,32,128]{2,1,0:T(8,128)} %get-tuple-element.20), channel_id=1, source_target_pairs={{1,0},{2,1},{3,2},{0,3},{5,4},{6,5},{7,6},{4,7},{9,8},{10,9},{11,1... | collective-permute-start | bytes 786440 | tf_op jit(solution)/shard_map/ppermute | solution.py:225
  106.9 9.4 %collective-permute-done.8.refs_6_ = f32[16,32,128]{2,1,0:T(8,128)} collective-permute-done((f32[16,32,128]{2,1,0:T(8,128)}, f32[16,32,128]{2,1,0:T(8,128)}, u32[]{:S(2)}, u32[]{:S(2)}) %collective-permute-start.8) | collective-permute-done | bytes 262176 | tf_op jit(solution)/shard_map/ppermute | solution.py:224
  117.3 4.3 %add_far.2 = (bf16[2048,128]{1,0:T(8,128)(2,1)S(1)}, bf16[64,32,128]{2,1,0:T(8,128)(2,1)S(1)}) custom-call(s32[4]{0:T(128)S(1)} %get-tuple-element.29.offset_ref, s32[16]{0:T(128)S(1)} %copy-done.24, bf16[16,2,32,128]{3,2,1,0:T(8,128)(2,1)S(1)} %slice.30.refs_0_, bf16[16,2,32,128]{3,2,1,0:T(8,128)(2,1)} %collective-permute-done.refs_1_, ...), custom_call_target="tpu_custom_call" | custom-call | flops 134217728 | bytes 4194304 | tf_op jit(solution)/shard_map/add_far/pallas_call | solution.py:199
  123.2 26.3 %all_to_all.21.held_ref = bf16[64,32,128]{2,1,0:T(8,128)(2,1)S(1)} all-to-all(bf16[64,32,128]{2,1,0:T(8,128)(2,1)} %copy-done.7), channel_id=1, replica_groups=mesh['db'=64,'pb'=4] {'db'}, dimensions={0} | all-to-all | bytes 1048576 | tf_op jit(solution)/shard_map/all_to_all | solution.py:255
  151.9 7.1 %all-to-all-start.3 = ((bf16[64,32,256]{2,1,0:T(8,128)(2,1)}), bf16[64,32,256]{2,1,0:T(8,128)(2,1)}, u32[]{:S(2)}, u32[]{:S(2)}) async-start(bf16[64,32,256]{2,1,0:T(8,128)(2,1)} %bitcast.20), calls=%async_computation.3 | async-start | bytes 2097152 | tf_op jit(solution)/shard_map/all_to_all | solution.py:260
  159.9 2.1 collective-permute-start.11
  161.9 5.6 %collective-permute-start.12 = (bf16[2,128,128]{2,1,0:T(8,128)(2,1)S(1)}, bf16[2,128,128]{2,1,0:T(8,128)(2,1)S(1)}, u32[]{:S(2)}, u32[]{:S(2)}) collective-permute-start(bf16[2,128,128]{2,1,0:T(8,128)(2,1)S(1)} %bitcast.23), channel_id=1, source_target_pairs={{4,0},{8,4},{12,8},{16,12},{20,16},{24,20},{28,24},{32,28},{36,32}... | collective-permute-start | bytes 196616 | tf_op jit(solution)/shard_map/ppermute | solution.py:252
  167.5 17.2 %collective-permute-done.11 = bf16[2,128,128]{2,1,0:T(8,128)(2,1)S(1)} collective-permute-done((bf16[2,128,128]{2,1,0:T(8,128)(2,1)S(1)}, bf16[2,128,128]{2,1,0:T(8,128)(2,1)S(1)}, u32[]{:S(2)}, u32[]{:S(2)}) %collective-permute-start.11) | collective-permute-done | bytes 65568 | tf_op jit(solution)/shard_map/ppermute | solution.py:251
  185.5 3.1 %collective-permute-start.14 = (bf16[4,128,128]{2,1,0:T(8,128)(2,1)S(1)}, bf16[4,128,128]{2,1,0:T(8,128)(2,1)S(1)}, u32[]{:S(2)}, u32[]{:S(2)}) collective-permute-start(bf16[4,128,128]{2,1,0:T(8,128)(2,1)S(1)} %constant_dynamic-update-slice_fusion.2.refs_0_), channel_id=1, source_target_pairs={{1,0},{2,1},{3,2},{0,3},{5,4},{6,5},{7,6},{4,7},{9,8},{10,9},{11,1... | collective-permute-start | bytes 393224 | tf_op jit(solution)/shard_map/ppermute | solution.py:225
  188.6 4.2 %collective-permute-done.15.refs_3_ = bf16[4,128,128]{2,1,0:T(8,128)(2,1)S(1)} collective-permute-done((bf16[4,128,128]{2,1,0:T(8,128)(2,1)S(1)}, bf16[4,128,128]{2,1,0:T(8,128)(2,1)S(1)}, u32[]{:S(2)}, u32[]{:S(2)}) %collective-permute-start.15) | collective-permute-done | bytes 131104 | tf_op jit(solution)/shard_map/ppermute | solution.py:226
  200.6 6.9 %near_product.3 = (f32[16,32,128]{2,1,0:T(8,128)S(1)}, f32[16,32,128]{2,1,0:T(8,128)}, f32[16,32,128]{2,1,0:T(8,128)}, f32[16,32,128]{2,1,0:T(8,128)}) custom-call(s32[16,16]{1,0:T(8,128)S(1)} %add_clamp_fusion.index_ref, s32[16]{0:T(128)S(1)} %copy-done.24, s32[4]{0:T(128)S(1)} %copy-done.26, bf16[16,16,32,128]{3,2,1,0:T(8,128)(2,1)S(1)} %copy-done.1, ...), custom_call_target="tpu_custom_call" | custom-call | flops 939524096 | bytes 6291456 | tf_op jit(solution)/shard_map/near_product/pallas_call | solution.py:131
  209.2 2.2 collective-permute-start.17
  211.9 5.0 %collective-permute-done.16.refs_6_ = f32[16,32,128]{2,1,0:T(8,128)S(1)} collective-permute-done((f32[16,32,128]{2,1,0:T(8,128)}, f32[16,32,128]{2,1,0:T(8,128)S(1)}, u32[]{:S(2)}, u32[]{:S(2)}) %collective-permute-start.16) | collective-permute-done | bytes 262176 | tf_op jit(solution)/shard_map/ppermute | solution.py:224
  219.3 4.2 %collective-permute-done.18.refs_8_ = f32[16,32,128]{2,1,0:T(8,128)S(1)} collective-permute-done((f32[16,32,128]{2,1,0:T(8,128)}, f32[16,32,128]{2,1,0:T(8,128)S(1)}, u32[]{:S(2)}, u32[]{:S(2)}) %collective-permute-start.18) | collective-permute-done | bytes 262176 | tf_op jit(solution)/shard_map/ppermute | solution.py:226
  228.0 4.3 %add_far.3 = bf16[2048,128]{1,0:T(8,128)(2,1)} custom-call(s32[4]{0:T(128)S(1)} %get-tuple-element.29.offset_ref, s32[16]{0:T(128)S(1)} %copy-done.24, bf16[16,2,32,128]{3,2,1,0:T(8,128)(2,1)S(1)} %slice.30.refs_0_, bf16[16,2,32,128]{3,2,1,0:T(8,128)(2,1)} %collective-permute-done.refs_1_, bf16[16,2,32,128]{3,2,1,0:T(8,128)(2,1)S(1)} %collective-permute-done.1.refs_2_, ...), custom_call_target="tpu_custom_call" | custom-call | flops 134217728 | bytes 4194304 | tf_op jit(solution)/shard_map/add_far/pallas_call | solution.py:199
  (105 shorter events, 42.8 us)
Async XLA Ops:
  6.5 86.3 %all-gather.3.cloned.1.call-start = ((), (), s32[]{:S(2)}) async-start(), calls=%async_computation.4 | async-start | bytes 2621440 | tf_op jit(solution)/shard_map/all_gather | solution.py:253
  45.7 47.1 %copy-start.24 = (s32[16]{0:T(128)S(1)}, s32[16]{0:T(128)}, u32[]{:S(2)}) copy-start(s32[16]{0:T(128)} %count_ref.7) | copy-start | bytes 196
  45.7 61.2 %all-to-all-start.1 = ((bf16[64,32,256]{2,1,0:T(8,128)(2,1)}), bf16[64,32,256]{2,1,0:T(8,128)(2,1)}, u32[]{:S(2)}, u32[]{:S(2)}) async-start(bf16[64,32,256]{2,1,0:T(8,128)(2,1)} %bitcast.19), calls=%async_computation.1 | async-start | bytes 2097152 | tf_op jit(solution)/shard_map/all_to_all | solution.py:260
  53.1 142.5 %all-gather.5.cloned.1.call-start = ((), (), s32[]{:S(2)}) async-start(), calls=%async_computation.5 | async-start | bytes 2621440 | tf_op jit(solution)/shard_map/all_gather | solution.py:253
  53.8 25.2 %collective-permute-start.3 = (bf16[2,128,128]{2,1,0:T(8,128)(2,1)S(1)}, bf16[2,128,128]{2,1,0:T(8,128)(2,1)}, u32[]{:S(2)}, u32[]{:S(2)}) collective-permute-start(bf16[2,128,128]{2,1,0:T(8,128)(2,1)S(1)} %bitcast.22), channel_id=1, source_target_pairs={{0,4},{4,8},{8,12},{12,16},{16,20},{20,24},{24,28},{28,32},{32,36}... | collective-permute-start | bytes 196616 | tf_op jit(solution)/shard_map/ppermute | solution.py:251
  55.9 50.9 %collective-permute-start.2 = (bf16[16,2,32,128]{3,2,1,0:T(8,128)(2,1)S(1)}, bf16[16,2,32,128]{3,2,1,0:T(8,128)(2,1)S(1)}, u32[]{:S(2)}, u32[]{:S(2)}) collective-permute-start(bf16[16,2,32,128]{3,2,1,0:T(8,128)(2,1)S(1)} %slice.30.refs_0_), channel_id=1, source_target_pairs={{0,2},{1,3},{2,0},{3,1},{4,6},{5,7},{6,4},{7,5},{8,10},{9,11},{10,... | collective-permute-start | bytes 786440 | tf_op jit(solution)/shard_map/ppermute | solution.py:226
  59.2 47.7 %collective-permute-start.1 = (bf16[16,2,32,128]{3,2,1,0:T(8,128)(2,1)S(1)}, bf16[16,2,32,128]{3,2,1,0:T(8,128)(2,1)S(1)}, u32[]{:S(2)}, u32[]{:S(2)}) collective-permute-start(bf16[16,2,32,128]{3,2,1,0:T(8,128)(2,1)S(1)} %slice.30.refs_0_), channel_id=1, source_target_pairs={{1,0},{2,1},{3,2},{0,3},{5,4},{6,5},{7,6},{4,7},{9,8},{10,9},{11,1... | collective-permute-start | bytes 786440 | tf_op jit(solution)/shard_map/ppermute | solution.py:225
  60.3 19.6 %collective-permute-start.4 = (bf16[2,128,128]{2,1,0:T(8,128)(2,1)}, bf16[2,128,128]{2,1,0:T(8,128)(2,1)}, u32[]{:S(2)}, u32[]{:S(2)}) collective-permute-start(bf16[2,128,128]{2,1,0:T(8,128)(2,1)} %bitcast.10), channel_id=1, source_target_pairs={{4,0},{8,4},{12,8},{16,12},{20,16},{24,20},{28,24},{32,28},{36,32}... | collective-permute-start | bytes 196616 | tf_op jit(solution)/shard_map/ppermute | solution.py:252
  80.7 8.1 %collective-permute-start.7 = (bf16[4,128,128]{2,1,0:T(8,128)(2,1)S(1)}, bf16[4,128,128]{2,1,0:T(8,128)(2,1)}, u32[]{:S(2)}, u32[]{:S(2)}) collective-permute-start(bf16[4,128,128]{2,1,0:T(8,128)(2,1)S(1)} %constant_dynamic-update-slice_fusion.refs_0_), channel_id=1, source_target_pairs={{0,2},{1,3},{2,0},{3,1},{4,6},{5,7},{6,4},{7,5},{8,10},{9,11},{10,... | collective-permute-start | bytes 393224 | tf_op jit(solution)/shard_map/ppermute | solution.py:226
  84.0 5.7 %collective-permute-start.6 = (bf16[4,128,128]{2,1,0:T(8,128)(2,1)S(1)}, bf16[4,128,128]{2,1,0:T(8,128)(2,1)}, u32[]{:S(2)}, u32[]{:S(2)}) collective-permute-start(bf16[4,128,128]{2,1,0:T(8,128)(2,1)S(1)} %constant_dynamic-update-slice_fusion.refs_0_), channel_id=1, source_target_pairs={{1,0},{2,1},{3,2},{0,3},{5,4},{6,5},{7,6},{4,7},{9,8},{10,9},{11,1... | collective-permute-start | bytes 393224 | tf_op jit(solution)/shard_map/ppermute | solution.py:225
  85.1 7.7 %collective-permute-start.5 = (bf16[4,128,128]{2,1,0:T(8,128)(2,1)S(1)}, bf16[4,128,128]{2,1,0:T(8,128)(2,1)}, u32[]{:S(2)}, u32[]{:S(2)}) collective-permute-start(bf16[4,128,128]{2,1,0:T(8,128)(2,1)S(1)} %constant_dynamic-update-slice_fusion.refs_0_), channel_id=1, source_target_pairs={{0,1},{1,2},{2,3},{3,0},{4,5},{5,6},{6,7},{7,4},{8,9},{9,10},{10,1... | collective-permute-start | bytes 393224 | tf_op jit(solution)/shard_map/ppermute | solution.py:224
  88.8 18.0 %collective-permute-start = (bf16[16,2,32,128]{3,2,1,0:T(8,128)(2,1)S(1)}, bf16[16,2,32,128]{3,2,1,0:T(8,128)(2,1)}, u32[]{:S(2)}, u32[]{:S(2)}) collective-permute-start(bf16[16,2,32,128]{3,2,1,0:T(8,128)(2,1)S(1)} %slice.30.refs_0_), channel_id=1, source_target_pairs={{0,1},{1,2},{2,3},{3,0},{4,5},{5,6},{6,7},{7,4},{8,9},{9,10},{10,1... | collective-permute-start | bytes 786440 | tf_op jit(solution)/shard_map/ppermute | solution.py:224
  103.6 12.7 %collective-permute-start.8 = (f32[16,32,128]{2,1,0:T(8,128)}, f32[16,32,128]{2,1,0:T(8,128)}, u32[]{:S(2)}, u32[]{:S(2)}) collective-permute-start(f32[16,32,128]{2,1,0:T(8,128)} %get-tuple-element.19), channel_id=1, source_target_pairs={{0,1},{1,2},{2,3},{3,0},{4,5},{5,6},{6,7},{7,4},{8,9},{9,10},{10,1... | collective-permute-start | bytes 786440 | tf_op jit(solution)/shard_map/ppermute | solution.py:224
  103.7 12.6 %collective-permute-start.9 = (f32[16,32,128]{2,1,0:T(8,128)}, f32[16,32,128]{2,1,0:T(8,128)}, u32[]{:S(2)}, u32[]{:S(2)}) collective-permute-start(f32[16,32,128]{2,1,0:T(8,128)} %get-tuple-element.20), channel_id=1, source_target_pairs={{1,0},{2,1},{3,2},{0,3},{5,4},{6,5},{7,6},{4,7},{9,8},{10,9},{11,1... | collective-permute-start | bytes 786440 | tf_op jit(solution)/shard_map/ppermute | solution.py:225
  106.9 9.5 %collective-permute-start.10 = (f32[16,32,128]{2,1,0:T(8,128)}, f32[16,32,128]{2,1,0:T(8,128)}, u32[]{:S(2)}, u32[]{:S(2)}) collective-permute-start(f32[16,32,128]{2,1,0:T(8,128)} %get-tuple-element.21), channel_id=1, source_target_pairs={{0,2},{1,3},{2,0},{3,1},{4,6},{5,7},{6,4},{7,5},{8,10},{9,11},{10,... | collective-permute-start | bytes 786440 | tf_op jit(solution)/shard_map/ppermute | solution.py:226
  151.9 60.0 %all-to-all-start.3 = ((bf16[64,32,256]{2,1,0:T(8,128)(2,1)}), bf16[64,32,256]{2,1,0:T(8,128)(2,1)}, u32[]{:S(2)}, u32[]{:S(2)}) async-start(bf16[64,32,256]{2,1,0:T(8,128)(2,1)} %bitcast.20), calls=%async_computation.3 | async-start | bytes 2097152 | tf_op jit(solution)/shard_map/all_to_all | solution.py:260
  159.9 24.9 %collective-permute-start.11 = (bf16[2,128,128]{2,1,0:T(8,128)(2,1)S(1)}, bf16[2,128,128]{2,1,0:T(8,128)(2,1)S(1)}, u32[]{:S(2)}, u32[]{:S(2)}) collective-permute-start(bf16[2,128,128]{2,1,0:T(8,128)(2,1)S(1)} %bitcast.24), channel_id=1, source_target_pairs={{0,4},{4,8},{8,12},{12,16},{16,20},{20,24},{24,28},{28,32},{32,36}... | collective-permute-start | bytes 196616 | tf_op jit(solution)/shard_map/ppermute | solution.py:251
  161.9 22.9 %collective-permute-start.12 = (bf16[2,128,128]{2,1,0:T(8,128)(2,1)S(1)}, bf16[2,128,128]{2,1,0:T(8,128)(2,1)S(1)}, u32[]{:S(2)}, u32[]{:S(2)}) collective-permute-start(bf16[2,128,128]{2,1,0:T(8,128)(2,1)S(1)} %bitcast.23), channel_id=1, source_target_pairs={{4,0},{8,4},{12,8},{16,12},{20,16},{24,20},{28,24},{32,28},{36,32}... | collective-permute-start | bytes 196616 | tf_op jit(solution)/shard_map/ppermute | solution.py:252
  184.8 8.0 %collective-permute-start.15 = (bf16[4,128,128]{2,1,0:T(8,128)(2,1)S(1)}, bf16[4,128,128]{2,1,0:T(8,128)(2,1)S(1)}, u32[]{:S(2)}, u32[]{:S(2)}) collective-permute-start(bf16[4,128,128]{2,1,0:T(8,128)(2,1)S(1)} %constant_dynamic-update-slice_fusion.2.refs_0_), channel_id=1, source_target_pairs={{0,2},{1,3},{2,0},{3,1},{4,6},{5,7},{6,4},{7,5},{8,10},{9,11},{10,... | collective-permute-start | bytes 393224 | tf_op jit(solution)/shard_map/ppermute | solution.py:226
  185.5 8.4 %collective-permute-start.14 = (bf16[4,128,128]{2,1,0:T(8,128)(2,1)S(1)}, bf16[4,128,128]{2,1,0:T(8,128)(2,1)S(1)}, u32[]{:S(2)}, u32[]{:S(2)}) collective-permute-start(bf16[4,128,128]{2,1,0:T(8,128)(2,1)S(1)} %constant_dynamic-update-slice_fusion.2.refs_0_), channel_id=1, source_target_pairs={{1,0},{2,1},{3,2},{0,3},{5,4},{6,5},{7,6},{4,7},{9,8},{10,9},{11,1... | collective-permute-start | bytes 393224 | tf_op jit(solution)/shard_map/ppermute | solution.py:225
  188.6 6.4 %collective-permute-start.13 = (bf16[4,128,128]{2,1,0:T(8,128)(2,1)S(1)}, bf16[4,128,128]{2,1,0:T(8,128)(2,1)S(1)}, u32[]{:S(2)}, u32[]{:S(2)}) collective-permute-start(bf16[4,128,128]{2,1,0:T(8,128)(2,1)S(1)} %constant_dynamic-update-slice_fusion.2.refs_0_), channel_id=1, source_target_pairs={{0,1},{1,2},{2,3},{3,0},{4,5},{5,6},{6,7},{7,4},{8,9},{9,10},{10,1... | collective-permute-start | bytes 393224 | tf_op jit(solution)/shard_map/ppermute | solution.py:224
  208.1 8.8 %collective-permute-start.16 = (f32[16,32,128]{2,1,0:T(8,128)}, f32[16,32,128]{2,1,0:T(8,128)S(1)}, u32[]{:S(2)}, u32[]{:S(2)}) collective-permute-start(f32[16,32,128]{2,1,0:T(8,128)} %get-tuple-element.26), channel_id=1, source_target_pairs={{0,1},{1,2},{2,3},{3,0},{4,5},{5,6},{6,7},{7,4},{8,9},{9,10},{10,1... | collective-permute-start | bytes 786440 | tf_op jit(solution)/shard_map/ppermute | solution.py:224
  209.2 9.4 %collective-permute-start.17 = (f32[16,32,128]{2,1,0:T(8,128)}, f32[16,32,128]{2,1,0:T(8,128)S(1)}, u32[]{:S(2)}, u32[]{:S(2)}) collective-permute-start(f32[16,32,128]{2,1,0:T(8,128)} %get-tuple-element.27), channel_id=1, source_target_pairs={{1,0},{2,1},{3,2},{0,3},{5,4},{6,5},{7,6},{4,7},{9,8},{10,9},{11,1... | collective-permute-start | bytes 786440 | tf_op jit(solution)/shard_map/ppermute | solution.py:225
  211.4 12.1 %collective-permute-start.18 = (f32[16,32,128]{2,1,0:T(8,128)}, f32[16,32,128]{2,1,0:T(8,128)S(1)}, u32[]{:S(2)}, u32[]{:S(2)}) collective-permute-start(f32[16,32,128]{2,1,0:T(8,128)} %get-tuple-element.28), channel_id=1, source_target_pairs={{0,2},{1,3},{2,0},{3,1},{4,6},{5,7},{6,4},{7,5},{8,10},{9,11},{10,... | collective-permute-start | bytes 786440 | tf_op jit(solution)/shard_map/ppermute | solution.py:226
  (28 other events, 74.5 us)
Sparse Core Ops, SparseCore 0:
  9.2 36.3 all-gather.2
  123.4 32.9 all-gather.4

commit v5 on v4

--- a/solution.py
+++ b/solution.py
@@ -11,7 +11,11 @@
 FAR = (1, 2)
 LIMIT = 12 << 20
 VMEM = pl.BlockSpec(memory_space=pltpu.VMEM)
-SMEM = pl.BlockSpec(memory_space=pltpu.SMEM)
+HBM = pl.BlockSpec(memory_space=pltpu.HBM)
+
+
+def in_hbm(arrays):
+    return [pltpu.with_memory_space_constraint(array, pltpu.HBM) for array in arrays]
 
 
 def rows_to_pieces(wide, pieces_ref, blocks, size, owners):
@@ -41,7 +45,7 @@
     )(queries, digits)
 
 
-def select_pieces(held, slots, wanted=None):
+def select_pieces(held, slots, after, wanted=None):
     devices, height, cols = held.shape
     blocks = height // 16 * 8
     parts = 2
@@ -49,6 +53,7 @@
     group = 8
 
     def kernel(held_ref, *rest):
+        rest = rest[len(after) :]
         if wanted is None:
             out_ref, wanted_out, flat = rest
             digits = held_ref[:, parts * blocks :, :].astype(jnp.float32)[:, 0, :].T
@@ -81,7 +86,7 @@
     return pl.pallas_call(
         kernel,
         out_shape=out_shape,
-        in_specs=[VMEM] * (1 + len(operands)),
+        in_specs=[VMEM] + [HBM] * len(after) + [VMEM] * len(operands),
         out_specs=[VMEM] * len(out_shape),
         scratch_shapes=[pltpu.VMEM((block_total, parts * cols), held.dtype)],
         compiler_params=pltpu.CompilerParams(vmem_limit_bytes=LIMIT),
@@ -89,7 +94,7 @@
             flops=2 * devices * slots * block_total * parts * cols, bytes_accessed=2 << 20, transcendentals=0
         ),
         name="select_pieces",
-    )(held, *operands)
+    )(held, *in_hbm(after), *operands)
 
 
 def near_product(near_index, counts, places, tiles, own, edges):
@@ -100,15 +105,25 @@
     near = [t for t in range(slots) if t not in FAR]
 
     def kernel(index_ref, count_ref, place_ref, tiles_ref, own_ref, *refs):
-        edge_refs, out_refs, panels = refs[:number], refs[number : 2 * number], refs[2 * number]
+        edge_refs, out_refs = refs[:number], refs[number : 2 * number]
+        panels, sems = refs[2 * number :]
         step = pl.program_id(0)
 
         @pl.when(step == 0)
         def _():
+            copies = []
             for n in range(number):
-                panels[n, :EDGE] = edge_refs[n][:EDGE]
-                panels[n, EDGE : EDGE + blocks] = own_ref[place_ref[n]]
-                panels[n, EDGE + blocks :] = edge_refs[n][EDGE:]
+                moves = (
+                    (edge_refs[n].at[:EDGE], panels.at[n, :EDGE]),
+                    (own_ref.at[place_ref[n]], panels.at[n, EDGE : EDGE + blocks]),
+                    (edge_refs[n].at[EDGE:], panels.at[n, EDGE + blocks :]),
+                )
+                for m, (source, target) in enumerate(moves):
+                    copies.append(pltpu.make_async_copy(source, target, sems.at[n, m]))
+            for copy in copies:
+                copy.start()
+            for copy in copies:
+                copy.wait()
 
         for r in range(group):
             b = step * group + r
@@ -135,9 +150,12 @@
             num_scalar_prefetch=3,
             grid=(blocks // group,),
             in_specs=[pl.BlockSpec((group, slots, rows, size), lambda i, *_: (i, 0, 0, 0))]
-            + [VMEM] * (1 + number),
+            + [HBM] * (1 + number),
             out_specs=[pl.BlockSpec((group, rows, cols), lambda i, *_: (i, 0, 0))] * number,
-            scratch_shapes=[pltpu.VMEM((number, blocks + 2 * EDGE, size, cols), own.dtype)],
+            scratch_shapes=[
+                pltpu.VMEM((number, blocks + 2 * EDGE, size, cols), own.dtype),
+                pltpu.SemaphoreType.DMA((number, 3)),
+            ],
         ),
         compiler_params=pltpu.CompilerParams(vmem_limit_bytes=LIMIT),
         cost_estimate=pl.CostEstimate(
@@ -146,7 +164,7 @@
             transcendentals=0,
         ),
         name="near_product",
-    )(near_index, counts, places, tiles, own, *edges)
+    )(near_index, counts, places, tiles, *in_hbm([own, *edges]))
 
 
 def add_far(offsets, counts, far_tiles, arrived, partials, queries, owners, split):
@@ -156,24 +174,31 @@
     number = len(far_tiles)
 
     def kernel(offset_ref, count_ref, *refs):
-        tiles = refs[:number]
-        arrived_ref = refs[number]
-        partial_refs = refs[number + 1 : number + 1 + len(partials)]
-        q_ref, out_ref, *rest = refs[number + 1 + len(partials) :]
+        arrived_ref, q_ref, out_ref = refs[2 * number : 2 * number + 3]
+        rest = refs[2 * number + 3 :]
         if split:
-            pieces_ref, upper, lower, wide = rest
+            pieces_ref, upper, lower, tiles, sums, sems, wide = rest
         else:
-            upper, lower = rest
+            upper, lower, tiles, sums, sems = rest
+        copies = [
+            pltpu.make_async_copy(refs[number * kind + n], target.at[n], sems.at[kind, n])
+            for kind, target in enumerate((tiles, sums))
+            for n in range(number)
+        ]
+        for copy in copies:
+            copy.start()
         upper[...] = arrived_ref[:, :cols].astype(jnp.float32)
         lower[...] = arrived_ref[:, cols:].astype(jnp.float32)
+        for copy in copies:
+            copy.wait()
         for b in range(blocks):
             left, right = [], []
             for s, t in enumerate(FAR):
-                tile = jnp.concatenate([ref[b, s] for ref in tiles], axis=0)
+                tile = tiles[:, b, s].reshape(size, size)
                 left.append(jnp.where(t < count_ref[b], tile, jnp.zeros_like(tile)))
                 for half in (upper, lower):
                     right.append(half[pl.ds(2 * b + s, owners, stride=far), :].astype(queries.dtype))
-            total = jnp.concatenate([ref[b] for ref in partial_refs], axis=0) + jnp.dot(
+            total = sums[:, b].reshape(size, cols) + jnp.dot(
                 jnp.concatenate(left, axis=1),
                 jnp.concatenate(right, axis=0),
                 preferred_element_type=jnp.float32,
@@ -190,7 +215,13 @@
 
     out_shape = [jax.ShapeDtypeStruct(queries.shape, queries.dtype)]
     out_specs = [pl.BlockSpec(queries.shape, lambda i, *_: (0, 0))]
-    scratch = [pltpu.VMEM((owners * far, cols), jnp.float32)] * 2
+    scratch = [
+        pltpu.VMEM((owners * far, cols), jnp.float32),
+        pltpu.VMEM((owners * far, cols), jnp.float32),
+        pltpu.VMEM((number,) + far_tiles[0].shape, far_tiles[0].dtype),
+        pltpu.VMEM((number,) + partials[0].shape, partials[0].dtype),
+        pltpu.SemaphoreType.DMA((2, number)),
+    ]
     if split:
         shape = (owners, size // owners * blocks, cols)
         out_shape.append(jax.ShapeDtypeStruct(shape, queries.dtype))
@@ -202,7 +233,7 @@
         grid_spec=pltpu.PrefetchScalarGridSpec(
             num_scalar_prefetch=2,
             grid=(1,),
-            in_specs=[VMEM] * (number + 2 + len(partials)),
+            in_specs=[HBM] * (2 * number) + [VMEM] * 2,
             out_specs=out_specs,
             scratch_shapes=scratch,
         ),
@@ -211,7 +242,7 @@
             flops=4 * blocks * size * size * cols, bytes_accessed=4 << 20, transcendentals=0
         ),
         name="add_far",
-    )(offsets, counts, *far_tiles, arrived, *partials, queries)
+    )(offsets, counts, *in_hbm(far_tiles), *in_hbm(partials), arrived, queries)
 
 
 def from_all(mine):
@@ -254,9 +285,9 @@
         edges = from_all([jnp.concatenate([low, high], axis=0)] * 4)
         held = lax.all_to_all(pieces, "db", split_axis=0, concat_axis=0, tiled=True)
         if wanted is None:
-            chosen, wanted = select_pieces(held, slots)
+            chosen, wanted = select_pieces(held, slots, edges)
         else:
-            (chosen,) = select_pieces(held, slots, wanted)
+            (chosen,) = select_pieces(held, slots, edges, wanted)
         arrived = lax.all_to_all(
             chosen.reshape(owners, slots, -1), "db", split_axis=0, concat_axis=0, tiled=True
         ).reshape(chosen.shape)

time: 240 us -> 195 us (0.81)
  the two profiles are of different devices: /device:TPU:4 before, /device:TPU:1 now
where the time goes in v5:
time: 195 us; the launch traced here: 194 us
  starting transfers between devices  75.3 us (39%)
  waiting for transfers between devices  63.6 us (33%)
  Pallas kernels  32.6 us (17%)
  between operations  13.7 us (7%)
  local copies, waits for them, and re-layouts  8.51 us (4%)
    all_to_all x2, waiting for transfers between devices, on_device(): lax.all_to_all(chosen.reshape(owners, slots, -1), 'db', split_axis=0, con...  28.1 us
    all_to_all x2, starting transfers between devices, on_device(): held = lax.all_to_all(pieces, 'db', split_axis=0, concat_axis=0, tiled=True)  23.6 us
    all_to_all x2, starting transfers between devices, on_device(): lax.all_to_all(chosen.reshape(owners, slots, -1), 'db', split_axis=0, con...  22.2 us
    pallas_call x2, Pallas kernels, near_product(): pl.pallas_call(kernel, out_shape=[out_shape] * number, grid_spec=pltpu.Pr...  15.5 us
    ppermute x2, waiting for transfers between devices, on_device(): low = lax.ppermute(own[blocks - EDGE:], 'db', up)  12.8 us
    pallas_call x2, Pallas kernels, add_far(): pl.pallas_call(kernel, out_shape=out_shape, grid_spec=pltpu.PrefetchScala...  11.8 us
    ppermute x5, waiting for transfers between devices, from_all(): lax.ppermute(mine[3], 'pb', across)  9.31 us
    ppermute x5, starting transfers between devices, from_all(): lax.ppermute(mine[1], 'pb', down)  9.15 us
  transfers between devices with their start and end apart: 25, of which 11 were waited for; matrix products, arithmetic and copies ran while one was open for 2% of the time, Pallas kernels for 11%

profile of v5, /device:TPU:1, one launch (start us, length us, event | category | flops | bytes accessed | tf_op | source)
XLA Modules:
  0.0 193.9 jit_solution(3099768977490807012)
XLA Ops:
  8.7 2.6 %split_blocks.1 = bf16[64,40,128]{2,1,0:T(8,128)(2,1)} custom-call(bf16[2048,128]{1,0:T(8,128)(2,1)} %refs_9_.3, f32[1,128]{1,0:T(1,128)} %pad.4.digits_ref), custom_call_target="tpu_custom_call" | custom-call | tf_op jit(solution)/shard_map/split_blocks/pallas_call | solution.py:38
  11.3 13.0 %all-to-all-start = ((bf16[64,40,128]{2,1,0:T(8,128)(2,1)}), bf16[64,40,128]{2,1,0:T(8,128)(2,1)S(1)}, u32[]{:S(2)}, u32[]{:S(2)}) async-start(bf16[64,40,128]{2,1,0:T(8,128)(2,1)} %split_blocks.1), calls=%async_computation | async-start | bytes 1310720 | tf_op jit(solution)/shard_map/all_to_all | solution.py:286
  24.3 3.5 %collective-permute-start.3 = (bf16[2,128,128]{2,1,0:T(8,128)(2,1)S(1)}, bf16[2,128,128]{2,1,0:T(8,128)(2,1)S(1)}, u32[]{:S(2)}, u32[]{:S(2)}) collective-permute-start(bf16[2,128,128]{2,1,0:T(8,128)(2,1)S(1)} %bitcast.23), channel_id=1, source_target_pairs={{0,4},{4,8},{8,12},{12,16},{16,20},{20,24},{24,28},{28,32},{32,36}... | collective-permute-start | bytes 196616 | tf_op jit(solution)/shard_map/ppermute | solution.py:282
  29.8 8.4 %collective-permute-done.3 = bf16[2,128,128]{2,1,0:T(8,128)(2,1)S(1)} collective-permute-done((bf16[2,128,128]{2,1,0:T(8,128)(2,1)S(1)}, bf16[2,128,128]{2,1,0:T(8,128)(2,1)S(1)}, u32[]{:S(2)}, u32[]{:S(2)}) %collective-permute-start.3) | collective-permute-done | bytes 65568 | tf_op jit(solution)/shard_map/ppermute | solution.py:282
  38.2 3.4 %collective-permute-done.4 = bf16[2,128,128]{2,1,0:T(8,128)(2,1)S(1)} collective-permute-done((bf16[2,128,128]{2,1,0:T(8,128)(2,1)S(1)}, bf16[2,128,128]{2,1,0:T(8,128)(2,1)S(1)}, u32[]{:S(2)}, u32[]{:S(2)}) %collective-permute-start.4) | collective-permute-done | bytes 65568 | tf_op jit(solution)/shard_map/ppermute | solution.py:283
  41.6 3.0 %collective-permute-start.7 = (bf16[4,128,128]{2,1,0:T(8,128)(2,1)S(1)}, bf16[4,128,128]{2,1,0:T(8,128)(2,1)S(1)}, u32[]{:S(2)}, u32[]{:S(2)}) collective-permute-start(bf16[4,128,128]{2,1,0:T(8,128)(2,1)S(1)} %constant_dynamic-update-slice_fusion.refs_0_.rest_0_), channel_id=1, source_target_pairs={{0,2},{1,3},{2,0},{3,1},{4,6},{5,7},{6,4},{7,5},{8,10},{9,11},{10,... | collective-permute-start | bytes 393224 | tf_op jit(solution)/shard_map/ppermute | solution.py:257
  46.1 3.8 %collective-permute-done.7.refs_3_.rest_3_ = bf16[4,128,128]{2,1,0:T(8,128)(2,1)S(1)} collective-permute-done((bf16[4,128,128]{2,1,0:T(8,128)(2,1)S(1)}, bf16[4,128,128]{2,1,0:T(8,128)(2,1)S(1)}, u32[]{:S(2)}, u32[]{:S(2)}) %collective-permute-start.7) | collective-permute-done | bytes 131104 | tf_op jit(solution)/shard_map/ppermute | solution.py:257
  54.2 11.2 %all-to-all-start.1 = ((bf16[64,32,256]{2,1,0:T(8,128)(2,1)}), bf16[64,32,256]{2,1,0:T(8,128)(2,1)}, u32[]{:S(2)}, u32[]{:S(2)}) async-start(bf16[64,32,256]{2,1,0:T(8,128)(2,1)} %bitcast.19), calls=%async_computation.1 | async-start | bytes 2097152 | tf_op jit(solution)/shard_map/all_to_all | solution.py:291
  69.6 7.8 %near_product.2 = (f32[16,32,128]{2,1,0:T(8,128)S(1)}, f32[16,32,128]{2,1,0:T(8,128)S(1)}, f32[16,32,128]{2,1,0:T(8,128)S(1)}, f32[16,32,128]{2,1,0:T(8,128)S(1)}) custom-call(s32[16,16]{1,0:T(8,128)S(1)} %add_clamp_fusion.index_ref, s32[16]{0:T(128)S(1)} %copy-done.6, s32[4]{0:T(128)S(1)} %get-tuple-element.30.place_ref, ...), custom_call_target="tpu_custom_call" | custom-call | flops 939524096 | bytes 6291456 | tf_op jit(solution)/shard_map/near_product/pallas_call | solution.py:146
  78.6 2.1 %collective-permute-start.9 = (f32[16,32,128]{2,1,0:T(8,128)S(1)}, f32[16,32,128]{2,1,0:T(8,128)}, u32[]{:S(2)}, u32[]{:S(2)}) collective-permute-start(f32[16,32,128]{2,1,0:T(8,128)S(1)} %get-tuple-element.19), channel_id=1, source_target_pairs={{1,0},{2,1},{3,2},{0,3},{5,4},{6,5},{7,6},{4,7},{9,8},{10,9},{11,1... | collective-permute-start | bytes 786440 | tf_op jit(solution)/shard_map/ppermute | solution.py:256
  81.8 12.0 %all-to-all-done.1 = bf16[64,32,256]{2,1,0:T(8,128)(2,1)} async-done(((bf16[64,32,256]{2,1,0:T(8,128)(2,1)}), bf16[64,32,256]{2,1,0:T(8,128)(2,1)}, u32[]{:S(2)}, u32[]{:S(2)}) %all-to-all-start.1) | async-done | bytes 1048608 | tf_op jit(solution)/shard_map/all_to_all | solution.py:291
  93.9 6.2 %add_far.2 = (bf16[2048,128]{1,0:T(8,128)(2,1)}, bf16[64,32,128]{2,1,0:T(8,128)(2,1)}) custom-call(s32[4]{0:T(128)S(1)} %get-tuple-element.29.offset_ref, s32[16]{0:T(128)S(1)} %copy-done.6, bf16[16,2,32,128]{3,2,1,0:T(8,128)(2,1)} %slice.30.refs_0_, bf16[16,2,32,128]{3,2,1,0:T(8,128)(2,1)} %collective-permute-done.refs_1_, ...), custom_call_target="tpu_custom_call" | custom-call | flops 134217728 | bytes 4194304 | tf_op jit(solution)/shard_map/add_far/pallas_call | solution.py:230
  100.1 10.6 %all-to-all-start.2 = ((bf16[64,32,128]{2,1,0:T(8,128)(2,1)}), bf16[64,32,128]{2,1,0:T(8,128)(2,1)S(1)}, u32[]{:S(2)}, u32[]{:S(2)}) async-start(bf16[64,32,128]{2,1,0:T(8,128)(2,1)} %get-tuple-element.27), calls=%async_computation.2 | async-start | bytes 1048576 | tf_op jit(solution)/shard_map/all_to_all | solution.py:286
  111.6 3.5 %collective-permute-start.11 = (bf16[2,128,128]{2,1,0:T(8,128)(2,1)S(1)}, bf16[2,128,128]{2,1,0:T(8,128)(2,1)S(1)}, u32[]{:S(2)}, u32[]{:S(2)}) collective-permute-start(bf16[2,128,128]{2,1,0:T(8,128)(2,1)S(1)} %bitcast.24), channel_id=1, source_target_pairs={{0,4},{4,8},{8,12},{12,16},{16,20},{20,24},{24,28},{28,32},{32,36}... | collective-permute-start | bytes 196616 | tf_op jit(solution)/shard_map/ppermute | solution.py:282
  117.1 4.4 %collective-permute-done.11 = bf16[2,128,128]{2,1,0:T(8,128)(2,1)S(1)} collective-permute-done((bf16[2,128,128]{2,1,0:T(8,128)(2,1)S(1)}, bf16[2,128,128]{2,1,0:T(8,128)(2,1)S(1)}, u32[]{:S(2)}, u32[]{:S(2)}) %collective-permute-start.11) | collective-permute-done | bytes 65568 | tf_op jit(solution)/shard_map/ppermute | solution.py:282
  121.5 3.7 %collective-permute-done.12 = bf16[2,128,128]{2,1,0:T(8,128)(2,1)S(1)} collective-permute-done((bf16[2,128,128]{2,1,0:T(8,128)(2,1)S(1)}, bf16[2,128,128]{2,1,0:T(8,128)(2,1)S(1)}, u32[]{:S(2)}, u32[]{:S(2)}) %collective-permute-start.12) | collective-permute-done | bytes 65568 | tf_op jit(solution)/shard_map/ppermute | solution.py:283
  126.2 2.4 %collective-permute-start.14 = (bf16[4,128,128]{2,1,0:T(8,128)(2,1)S(1)}, bf16[4,128,128]{2,1,0:T(8,128)(2,1)S(1)}, u32[]{:S(2)}, u32[]{:S(2)}) collective-permute-start(bf16[4,128,128]{2,1,0:T(8,128)(2,1)S(1)} %constant_dynamic-update-slice_fusion.2.refs_0_.rest_0_), channel_id=1, source_target_pairs={{1,0},{2,1},{3,2},{0,3},{5,4},{6,5},{7,6},{4,7},{9,8},{10,9},{11,1... | collective-permute-start | bytes 393224 | tf_op jit(solution)/shard_map/ppermute | solution.py:256
  128.6 5.5 %collective-permute-done.15.refs_3_.rest_3_ = bf16[4,128,128]{2,1,0:T(8,128)(2,1)S(1)} collective-permute-done((bf16[4,128,128]{2,1,0:T(8,128)(2,1)S(1)}, bf16[4,128,128]{2,1,0:T(8,128)(2,1)S(1)}, u32[]{:S(2)}, u32[]{:S(2)}) %collective-permute-start.15) | collective-permute-done | bytes 131104 | tf_op jit(solution)/shard_map/ppermute | solution.py:257
  134.2 4.0 %collective-permute-done.14.refs_2_.rest_2_ = bf16[4,128,128]{2,1,0:T(8,128)(2,1)S(1)} collective-permute-done((bf16[4,128,128]{2,1,0:T(8,128)(2,1)S(1)}, bf16[4,128,128]{2,1,0:T(8,128)(2,1)S(1)}, u32[]{:S(2)}, u32[]{:S(2)}) %collective-permute-start.14) | collective-permute-done | bytes 131104 | tf_op jit(solution)/shard_map/ppermute | solution.py:256
  141.1 11.0 %all-to-all-start.3 = ((bf16[64,32,256]{2,1,0:T(8,128)(2,1)}), bf16[64,32,256]{2,1,0:T(8,128)(2,1)}, u32[]{:S(2)}, u32[]{:S(2)}) async-start(bf16[64,32,256]{2,1,0:T(8,128)(2,1)} %bitcast.20), calls=%async_computation.3 | async-start | bytes 2097152 | tf_op jit(solution)/shard_map/all_to_all | solution.py:291
  152.2 7.8 %near_product.3 = (f32[16,32,128]{2,1,0:T(8,128)S(1)}, f32[16,32,128]{2,1,0:T(8,128)S(1)}, f32[16,32,128]{2,1,0:T(8,128)S(1)}, f32[16,32,128]{2,1,0:T(8,128)S(1)}) custom-call(s32[16,16]{1,0:T(8,128)S(1)} %add_clamp_fusion.index_ref, s32[16]{0:T(128)S(1)} %copy-done.6, s32[4]{0:T(128)S(1)} %get-tuple-element.30.place_ref, ...), custom_call_target="tpu_custom_call" | custom-call | flops 939524096 | bytes 6291456 | tf_op jit(solution)/shard_map/near_product/pallas_call | solution.py:146
  160.6 2.7 %collective-permute-start.17 = (f32[16,32,128]{2,1,0:T(8,128)S(1)}, f32[16,32,128]{2,1,0:T(8,128)S(1)}, u32[]{:S(2)}, u32[]{:S(2)}) collective-permute-start(f32[16,32,128]{2,1,0:T(8,128)S(1)} %get-tuple-element.25), channel_id=1, source_target_pairs={{1,0},{2,1},{3,2},{0,3},{5,4},{6,5},{7,6},{4,7},{9,8},{10,9},{11,1... | collective-permute-start | bytes 786440 | tf_op jit(solution)/shard_map/ppermute | solution.py:256
  164.5 16.1 %all-to-all-done.3 = bf16[64,32,256]{2,1,0:T(8,128)(2,1)} async-done(((bf16[64,32,256]{2,1,0:T(8,128)(2,1)}), bf16[64,32,256]{2,1,0:T(8,128)(2,1)}, u32[]{:S(2)}, u32[]{:S(2)}) %all-to-all-start.3) | async-done | bytes 1048608 | tf_op jit(solution)/shard_map/all_to_all | solution.py:291
  181.5 5.6 %add_far.3 = bf16[2048,128]{1,0:T(8,128)(2,1)} custom-call(s32[4]{0:T(128)S(1)} %get-tuple-element.29.offset_ref, s32[16]{0:T(128)S(1)} %copy-done.6, bf16[16,2,32,128]{3,2,1,0:T(8,128)(2,1)} %slice.30.refs_0_, bf16[16,2,32,128]{3,2,1,0:T(8,128)(2,1)} %collective-permute-done.refs_1_, bf16[16,2,32,128]{3,2,1,0:T(8,128)(2,1)} %collective-permute-done.1.refs_2_, ...), custom_call_target="tpu_custom_call" | custom-call | flops 134217728 | bytes 4194304 | tf_op jit(solution)/shard_map/add_far/pallas_call | solution.py:230
  (83 shorter events, 25.9 us)
Async XLA Ops:
  6.5 63.0 %all-gather.3.cloned.1.call-start = ((), (), s32[]{:S(2)}) async-start(), calls=%async_computation.4 | async-start | bytes 2621440 | tf_op jit(solution)/shard_map/all_gather | solution.py:284
  11.3 40.4 %all-to-all-start = ((bf16[64,40,128]{2,1,0:T(8,128)(2,1)}), bf16[64,40,128]{2,1,0:T(8,128)(2,1)S(1)}, u32[]{:S(2)}, u32[]{:S(2)}) async-start(bf16[64,40,128]{2,1,0:T(8,128)(2,1)} %split_blocks.1), calls=%async_computation | async-start | bytes 1310720 | tf_op jit(solution)/shard_map/all_to_all | solution.py:286
  24.3 13.8 %collective-permute-start.3 = (bf16[2,128,128]{2,1,0:T(8,128)(2,1)S(1)}, bf16[2,128,128]{2,1,0:T(8,128)(2,1)S(1)}, u32[]{:S(2)}, u32[]{:S(2)}) collective-permute-start(bf16[2,128,128]{2,1,0:T(8,128)(2,1)S(1)} %bitcast.23), channel_id=1, source_target_pairs={{0,4},{4,8},{8,12},{12,16},{16,20},{20,24},{24,28},{28,32},{32,36}... | collective-permute-start | bytes 196616 | tf_op jit(solution)/shard_map/ppermute | solution.py:282
  27.9 13.7 %collective-permute-start.4 = (bf16[2,128,128]{2,1,0:T(8,128)(2,1)S(1)}, bf16[2,128,128]{2,1,0:T(8,128)(2,1)S(1)}, u32[]{:S(2)}, u32[]{:S(2)}) collective-permute-start(bf16[2,128,128]{2,1,0:T(8,128)(2,1)S(1)} %bitcast.21), channel_id=1, source_target_pairs={{4,0},{8,4},{12,8},{16,12},{20,16},{24,20},{28,24},{32,28},{36,32}... | collective-permute-start | bytes 196616 | tf_op jit(solution)/shard_map/ppermute | solution.py:283
  41.6 8.2 %collective-permute-start.7 = (bf16[4,128,128]{2,1,0:T(8,128)(2,1)S(1)}, bf16[4,128,128]{2,1,0:T(8,128)(2,1)S(1)}, u32[]{:S(2)}, u32[]{:S(2)}) collective-permute-start(bf16[4,128,128]{2,1,0:T(8,128)(2,1)S(1)} %constant_dynamic-update-slice_fusion.refs_0_.rest_0_), channel_id=1, source_target_pairs={{0,2},{1,3},{2,0},{3,1},{4,6},{5,7},{6,4},{7,5},{8,10},{9,11},{10,... | collective-permute-start | bytes 393224 | tf_op jit(solution)/shard_map/ppermute | solution.py:257
  44.6 6.4 %collective-permute-start.6 = (bf16[4,128,128]{2,1,0:T(8,128)(2,1)S(1)}, bf16[4,128,128]{2,1,0:T(8,128)(2,1)S(1)}, u32[]{:S(2)}, u32[]{:S(2)}) collective-permute-start(bf16[4,128,128]{2,1,0:T(8,128)(2,1)S(1)} %constant_dynamic-update-slice_fusion.refs_0_.rest_0_), channel_id=1, source_target_pairs={{1,0},{2,1},{3,2},{0,3},{5,4},{6,5},{7,6},{4,7},{9,8},{10,9},{11,1... | collective-permute-start | bytes 393224 | tf_op jit(solution)/shard_map/ppermute | solution.py:256
  54.2 39.7 %all-to-all-start.1 = ((bf16[64,32,256]{2,1,0:T(8,128)(2,1)}), bf16[64,32,256]{2,1,0:T(8,128)(2,1)}, u32[]{:S(2)}, u32[]{:S(2)}) async-start(bf16[64,32,256]{2,1,0:T(8,128)(2,1)} %bitcast.19), calls=%async_computation.1 | async-start | bytes 2097152 | tf_op jit(solution)/shard_map/all_to_all | solution.py:291
  65.4 86.7 %all-gather.5.cloned.1.call-start = ((), (), s32[]{:S(2)}) async-start(), calls=%async_computation.5 | async-start | bytes 2621440 | tf_op jit(solution)/shard_map/all_gather | solution.py:284
  66.2 14.5 %collective-permute-start.2 = (bf16[16,2,32,128]{3,2,1,0:T(8,128)(2,1)}, bf16[16,2,32,128]{3,2,1,0:T(8,128)(2,1)}, u32[]{:S(2)}, u32[]{:S(2)}) collective-permute-start(bf16[16,2,32,128]{3,2,1,0:T(8,128)(2,1)} %slice.30.refs_0_), channel_id=1, source_target_pairs={{0,2},{1,3},{2,0},{3,1},{4,6},{5,7},{6,4},{7,5},{8,10},{9,11},{10,... | collective-permute-start | bytes 786440 | tf_op jit(solution)/shard_map/ppermute | solution.py:257
  68.0 13.6 %collective-permute-start.1 = (bf16[16,2,32,128]{3,2,1,0:T(8,128)(2,1)}, bf16[16,2,32,128]{3,2,1,0:T(8,128)(2,1)}, u32[]{:S(2)}, u32[]{:S(2)}) collective-permute-start(bf16[16,2,32,128]{3,2,1,0:T(8,128)(2,1)} %slice.30.refs_0_), channel_id=1, source_target_pairs={{1,0},{2,1},{3,2},{0,3},{5,4},{6,5},{7,6},{4,7},{9,8},{10,9},{11,1... | collective-permute-start | bytes 786440 | tf_op jit(solution)/shard_map/ppermute | solution.py:256
  69.1 12.7 %collective-permute-start = (bf16[16,2,32,128]{3,2,1,0:T(8,128)(2,1)}, bf16[16,2,32,128]{3,2,1,0:T(8,128)(2,1)}, u32[]{:S(2)}, u32[]{:S(2)}) collective-permute-start(bf16[16,2,32,128]{3,2,1,0:T(8,128)(2,1)} %slice.30.refs_0_), channel_id=1, source_target_pairs={{0,1},{1,2},{2,3},{3,0},{4,5},{5,6},{6,7},{7,4},{8,9},{9,10},{10,1... | collective-permute-start | bytes 786440 | tf_op jit(solution)/shard_map/ppermute | solution.py:255
  78.0 15.9 %collective-permute-start.8 = (f32[16,32,128]{2,1,0:T(8,128)S(1)}, f32[16,32,128]{2,1,0:T(8,128)}, u32[]{:S(2)}, u32[]{:S(2)}) collective-permute-start(f32[16,32,128]{2,1,0:T(8,128)S(1)} %get-tuple-element.18), channel_id=1, source_target_pairs={{0,1},{1,2},{2,3},{3,0},{4,5},{5,6},{6,7},{7,4},{8,9},{9,10},{10,1... | collective-permute-start | bytes 786440 | tf_op jit(solution)/shard_map/ppermute | solution.py:255
  78.6 15.3 %collective-permute-start.9 = (f32[16,32,128]{2,1,0:T(8,128)S(1)}, f32[16,32,128]{2,1,0:T(8,128)}, u32[]{:S(2)}, u32[]{:S(2)}) collective-permute-start(f32[16,32,128]{2,1,0:T(8,128)S(1)} %get-tuple-element.19), channel_id=1, source_target_pairs={{1,0},{2,1},{3,2},{0,3},{5,4},{6,5},{7,6},{4,7},{9,8},{10,9},{11,1... | collective-permute-start | bytes 786440 | tf_op jit(solution)/shard_map/ppermute | solution.py:256
  80.7 13.2 %collective-permute-start.10 = (f32[16,32,128]{2,1,0:T(8,128)S(1)}, f32[16,32,128]{2,1,0:T(8,128)}, u32[]{:S(2)}, u32[]{:S(2)}) collective-permute-start(f32[16,32,128]{2,1,0:T(8,128)S(1)} %get-tuple-element.20), channel_id=1, source_target_pairs={{0,2},{1,3},{2,0},{3,1},{4,6},{5,7},{6,4},{7,5},{8,10},{9,11},{10,... | collective-permute-start | bytes 786440 | tf_op jit(solution)/shard_map/ppermute | solution.py:257
  100.1 38.7 %all-to-all-start.2 = ((bf16[64,32,128]{2,1,0:T(8,128)(2,1)}), bf16[64,32,128]{2,1,0:T(8,128)(2,1)S(1)}, u32[]{:S(2)}, u32[]{:S(2)}) async-start(bf16[64,32,128]{2,1,0:T(8,128)(2,1)} %get-tuple-element.27), calls=%async_computation.2 | async-start | bytes 1048576 | tf_op jit(solution)/shard_map/all_to_all | solution.py:286
  111.6 9.9 %collective-permute-start.11 = (bf16[2,128,128]{2,1,0:T(8,128)(2,1)S(1)}, bf16[2,128,128]{2,1,0:T(8,128)(2,1)S(1)}, u32[]{:S(2)}, u32[]{:S(2)}) collective-permute-start(bf16[2,128,128]{2,1,0:T(8,128)(2,1)S(1)} %bitcast.24), channel_id=1, source_target_pairs={{0,4},{4,8},{8,12},{12,16},{16,20},{20,24},{24,28},{28,32},{32,36}... | collective-permute-start | bytes 196616 | tf_op jit(solution)/shard_map/ppermute | solution.py:282
  115.2 10.1 %collective-permute-start.12 = (bf16[2,128,128]{2,1,0:T(8,128)(2,1)S(1)}, bf16[2,128,128]{2,1,0:T(8,128)(2,1)S(1)}, u32[]{:S(2)}, u32[]{:S(2)}) collective-permute-start(bf16[2,128,128]{2,1,0:T(8,128)(2,1)S(1)} %bitcast.22), channel_id=1, source_target_pairs={{4,0},{8,4},{12,8},{16,12},{20,16},{24,20},{28,24},{32,28},{36,32}... | collective-permute-start | bytes 196616 | tf_op jit(solution)/shard_map/ppermute | solution.py:283
  125.3 8.9 %collective-permute-start.15 = (bf16[4,128,128]{2,1,0:T(8,128)(2,1)S(1)}, bf16[4,128,128]{2,1,0:T(8,128)(2,1)S(1)}, u32[]{:S(2)}, u32[]{:S(2)}) collective-permute-start(bf16[4,128,128]{2,1,0:T(8,128)(2,1)S(1)} %constant_dynamic-update-slice_fusion.2.refs_0_.rest_0_), channel_id=1, source_target_pairs={{0,2},{1,3},{2,0},{3,1},{4,6},{5,7},{6,4},{7,5},{8,10},{9,11},{10,... | collective-permute-start | bytes 393224 | tf_op jit(solution)/shard_map/ppermute | solution.py:257
  126.2 11.9 %collective-permute-start.14 = (bf16[4,128,128]{2,1,0:T(8,128)(2,1)S(1)}, bf16[4,128,128]{2,1,0:T(8,128)(2,1)S(1)}, u32[]{:S(2)}, u32[]{:S(2)}) collective-permute-start(bf16[4,128,128]{2,1,0:T(8,128)(2,1)S(1)} %constant_dynamic-update-slice_fusion.2.refs_0_.rest_0_), channel_id=1, source_target_pairs={{1,0},{2,1},{3,2},{0,3},{5,4},{6,5},{7,6},{4,7},{9,8},{10,9},{11,1... | collective-permute-start | bytes 393224 | tf_op jit(solution)/shard_map/ppermute | solution.py:256
  128.6 10.2 %collective-permute-start.13 = (bf16[4,128,128]{2,1,0:T(8,128)(2,1)S(1)}, bf16[4,128,128]{2,1,0:T(8,128)(2,1)}, u32[]{:S(2)}, u32[]{:S(2)}) collective-permute-start(bf16[4,128,128]{2,1,0:T(8,128)(2,1)S(1)} %constant_dynamic-update-slice_fusion.2.refs_0_.rest_0_), channel_id=1, source_target_pairs={{0,1},{1,2},{2,3},{3,0},{4,5},{5,6},{6,7},{7,4},{8,9},{9,10},{10,1... | collective-permute-start | bytes 393224 | tf_op jit(solution)/shard_map/ppermute | solution.py:255
  141.1 39.5 %all-to-all-start.3 = ((bf16[64,32,256]{2,1,0:T(8,128)(2,1)}), bf16[64,32,256]{2,1,0:T(8,128)(2,1)}, u32[]{:S(2)}, u32[]{:S(2)}) async-start(bf16[64,32,256]{2,1,0:T(8,128)(2,1)} %bitcast.20), calls=%async_computation.3 | async-start | bytes 2097152 | tf_op jit(solution)/shard_map/all_to_all | solution.py:291
  160.6 20.0 %collective-permute-start.16 = (f32[16,32,128]{2,1,0:T(8,128)S(1)}, f32[16,32,128]{2,1,0:T(8,128)S(1)}, u32[]{:S(2)}, u32[]{:S(2)}) collective-permute-start(f32[16,32,128]{2,1,0:T(8,128)S(1)} %get-tuple-element.24), channel_id=1, source_target_pairs={{0,1},{1,2},{2,3},{3,0},{4,5},{5,6},{6,7},{7,4},{8,9},{9,10},{10,1... | collective-permute-start | bytes 786440 | tf_op jit(solution)/shard_map/ppermute | solution.py:255
  160.6 20.0 %collective-permute-start.17 = (f32[16,32,128]{2,1,0:T(8,128)S(1)}, f32[16,32,128]{2,1,0:T(8,128)S(1)}, u32[]{:S(2)}, u32[]{:S(2)}) collective-permute-start(f32[16,32,128]{2,1,0:T(8,128)S(1)} %get-tuple-element.25), channel_id=1, source_target_pairs={{1,0},{2,1},{3,2},{0,3},{5,4},{6,5},{7,6},{4,7},{9,8},{10,9},{11,1... | collective-permute-start | bytes 786440 | tf_op jit(solution)/shard_map/ppermute | solution.py:256
  163.3 17.3 %collective-permute-start.18 = (f32[16,32,128]{2,1,0:T(8,128)S(1)}, f32[16,32,128]{2,1,0:T(8,128)S(1)}, u32[]{:S(2)}, u32[]{:S(2)}) collective-permute-start(f32[16,32,128]{2,1,0:T(8,128)S(1)} %get-tuple-element.26), channel_id=1, source_target_pairs={{0,2},{1,3},{2,0},{3,1},{4,6},{5,7},{6,4},{7,5},{8,10},{9,11},{10,... | collective-permute-start | bytes 786440 | tf_op jit(solution)/shard_map/ppermute | solution.py:257
  (18 other events, 115.1 us)
Sparse Core Ops, SparseCore 0:
  9.2 41.7 all-gather.2
  100.2 39.3 all-gather.4

commit v6 on v5

--- a/solution.py
+++ b/solution.py
@@ -97,16 +97,16 @@
     )(held, *in_hbm(after), *operands)
 
 
-def near_product(near_index, counts, places, tiles, own, edges):
+def near_product(near_index, counts, tiles, own, edges):
     blocks, slots, rows, size = tiles.shape
-    cols = own.shape[3]
-    number = len(edges)
+    cols = own[0].shape[2]
+    number = len(own)
     group = 4
     near = [t for t in range(slots) if t not in FAR]
 
-    def kernel(index_ref, count_ref, place_ref, tiles_ref, own_ref, *refs):
-        edge_refs, out_refs = refs[:number], refs[number : 2 * number]
-        panels, sems = refs[2 * number :]
+    def kernel(index_ref, count_ref, tiles_ref, *refs):
+        own_refs, edge_refs, out_refs = [refs[k * number : (k + 1) * number] for k in range(3)]
+        panels, sems = refs[3 * number :]
         step = pl.program_id(0)
 
         @pl.when(step == 0)
@@ -115,7 +115,7 @@
             for n in range(number):
                 moves = (
                     (edge_refs[n].at[:EDGE], panels.at[n, :EDGE]),
-                    (own_ref.at[place_ref[n]], panels.at[n, EDGE : EDGE + blocks]),
+                    (own_refs[n], panels.at[n, EDGE : EDGE + blocks]),
                     (edge_refs[n].at[EDGE:], panels.at[n, EDGE + blocks :]),
                 )
                 for m, (source, target) in enumerate(moves):
@@ -147,13 +147,13 @@
         kernel,
         out_shape=[out_shape] * number,
         grid_spec=pltpu.PrefetchScalarGridSpec(
-            num_scalar_prefetch=3,
+            num_scalar_prefetch=2,
             grid=(blocks // group,),
             in_specs=[pl.BlockSpec((group, slots, rows, size), lambda i, *_: (i, 0, 0, 0))]
-            + [HBM] * (1 + number),
+            + [HBM] * (2 * number),
             out_specs=[pl.BlockSpec((group, rows, cols), lambda i, *_: (i, 0, 0))] * number,
             scratch_shapes=[
-                pltpu.VMEM((number, blocks + 2 * EDGE, size, cols), own.dtype),
+                pltpu.VMEM((number, blocks + 2 * EDGE, size, cols), own[0].dtype),
                 pltpu.SemaphoreType.DMA((number, 3)),
             ],
         ),
@@ -164,7 +164,7 @@
             transcendentals=0,
         ),
         name="near_product",
-    )(near_index, counts, places, tiles, *in_hbm([own, *edges]))
+    )(near_index, counts, tiles, *in_hbm([*own, *edges]))
 
 
 def add_far(offsets, counts, far_tiles, arrived, partials, queries, owners, split):
@@ -266,8 +266,7 @@
     first_block = lax.axis_index("db") * blocks
     far_tiles = from_all([affinity_tiles[:, FAR[0] : FAR[-1] + 1]] * 4)
     place = lax.axis_index("pb")
-    places = jnp.stack([(place + shift) % lax.axis_size("pb") for shift in (0, -1, 1, 2)])
-    offsets = places * rows
+    offsets = jnp.stack([(place + shift) % lax.axis_size("pb") * rows for shift in (0, -1, 1, 2)])
     near_index = jnp.clip(block_ids - first_block + EDGE, 0, blocks + 2 * EDGE - 1)
     far = block_ids[:, FAR[0] : FAR[-1] + 1].reshape(1, -1)
     slots = far.shape[1]
@@ -281,17 +280,22 @@
         own = ranking.reshape(blocks, size, cols)
         low = lax.ppermute(own[blocks - EDGE :], "db", up)
         high = lax.ppermute(own[:EDGE], "db", down)
-        whole = lax.all_gather(own, "pb", axis=0)
+        pieces, low, high = lax.optimization_barrier((pieces, low, high))
+        held = lax.all_to_all(pieces, "db", split_axis=0, concat_axis=0, tiled=True)
         edges = from_all([jnp.concatenate([low, high], axis=0)] * 4)
-        held = lax.all_to_all(pieces, "db", split_axis=0, concat_axis=0, tiled=True)
+        panels = from_all([own] * 4)
+        after = edges + panels[1:3]
         if wanted is None:
-            chosen, wanted = select_pieces(held, slots, edges)
+            chosen, wanted = select_pieces(held, slots, after)
         else:
-            (chosen,) = select_pieces(held, slots, edges, wanted)
+            (chosen,) = select_pieces(held, slots, after, wanted)
         arrived = lax.all_to_all(
             chosen.reshape(owners, slots, -1), "db", split_axis=0, concat_axis=0, tiled=True
         ).reshape(chosen.shape)
-        partials = from_all(near_product(near_index, valid_counts, places, affinity_tiles, whole, edges))
+        products = list(near_product(near_index, valid_counts, affinity_tiles, panels[:3], edges[:3]))
+        products[0], opposite = lax.optimization_barrier((products[0], panels[3]))
+        products += near_product(near_index, valid_counts, affinity_tiles, [opposite], edges[3:])
+        partials = from_all(products)
         done = add_far(offsets, valid_counts, far_tiles, arrived, partials, queries, owners, step < ITERS - 1)
         ranking = done[0]
         pieces = done[-1]

time: 195 us -> 203 us (1.041)
  between operations: 13.7 us -> 0.5 us
  waiting for transfers between devices: 63.6 us -> 73 us
  starting transfers between devices: 75.3 us -> 81.8 us
  local copies, waits for them, and re-layouts: 8.51 us -> 11.9 us
  Pallas kernels: 32.6 us -> 35.3 us
    ppermute x5 -> x7, waiting for transfers between devices: 0.26 us -> 38.1 us  [from_all(): lax.ppermute(mine[2], 'pb', up)]
    all_to_all x2, waiting for transfers between devices: 28.1 us -> 0.01 us  [on_device(): lax.all_to_all(chosen.reshape(owners, slots, -1), 'db', split_axis=0, con...]
    ppermute x5 -> x7, waiting for transfers between devices: 9.31 us -> 31.2 us  [from_all(): lax.ppermute(mine[3], 'pb', across)]
    ppermute x2, waiting for transfers between devices: 12.8 us -> 0.01 us  [on_device(): low = lax.ppermute(own[blocks - EDGE:], 'db', up)]
    ppermute x5 -> x7, starting transfers between devices: 1.53 us -> 7.91 us  [from_all(): lax.ppermute(mine[2], 'pb', up)]
    ppermute x5 -> x7, waiting for transfers between devices: 5.17 us -> 0.02 us  [from_all(): lax.ppermute(mine[1], 'pb', down)]
    pallas_call x2 -> x4, Pallas kernels: 15.5 us -> 19.4 us  [near_product(): pl.pallas_call(kernel, out_shape=[out_shape] * number, grid_spec=pltpu.Pr...]
    ppermute x2, waiting for transfers between devices: 7.19 us -> 3.65 us  [on_device(): high = lax.ppermute(own[:EDGE], 'db', down)]
  transfers between devices with their start and end apart: 25 -> 29, of which waited for: 11 -> 13; matrix products, arithmetic and copies ran while one was open for 2% -> 1% of each run, Pallas kernels for 11% -> 11%
where the time goes in v6:
time: 203 us
  starting transfers between devices  81.8 us (40%)
  waiting for transfers between devices  73 us (36%)
  Pallas kernels  35.3 us (17%)
  local copies, waits for them, and re-layouts  11.9 us (6%)
    ppermute x7, waiting for transfers between devices, from_all(): lax.ppermute(mine[2], 'pb', up)  38.1 us
    ppermute x7, waiting for transfers between devices, from_all(): lax.ppermute(mine[3], 'pb', across)  31.2 us
    all_to_all x2, starting transfers between devices, on_device(): held = lax.all_to_all(pieces, 'db', split_axis=0, concat_axis=0, tiled=True)  23.1 us
    all_to_all x2, starting transfers between devices, on_device(): lax.all_to_all(chosen.reshape(owners, slots, -1), 'db', split_axis=0, con...  22.6 us
    pallas_call x4, Pallas kernels, near_product(): pl.pallas_call(kernel, out_shape=[out_shape] * number, grid_spec=pltpu.Pr...  19.4 us
    pallas_call x2, Pallas kernels, add_far(): pl.pallas_call(kernel, out_shape=out_shape, grid_spec=pltpu.PrefetchScala...  10.6 us
    ppermute x7, starting transfers between devices, from_all(): lax.ppermute(mine[1], 'pb', down)  10.2 us
    unnamed x48, local copies, waits for them, and re-layouts  8.83 us
  transfers between devices with their start and end apart: 29, of which 13 were waited for; matrix products, arithmetic and copies ran while one was open for 1% of the time, Pallas kernels for 11%

profile of v6, /device:TPU:1, one launch (start us, length us, event | category | flops | bytes accessed | tf_op | source)
XLA Modules:
  0.0 202.6 jit_solution(11834625967951797356)
XLA Ops:
  0.9 4.9 %collective-permute-start.5 = (bf16[2,128,128]{2,1,0:T(8,128)(2,1)S(1)}, bf16[2,128,128]{2,1,0:T(8,128)(2,1)S(1)}, u32[]{:S(2)}, u32[]{:S(2)}) collective-permute-start(bf16[2,128,128]{2,1,0:T(8,128)(2,1)S(1)} %bitcast.27), channel_id=1, source_target_pairs={{0,4},{4,8},{8,12},{12,16},{16,20},{20,24},{24,28},{28,32},{32,36}... | collective-permute-start | bytes 196616 | tf_op jit(solution)/shard_map/ppermute | solution.py:281
  11.8 12.9 %all-to-all-start = ((bf16[64,40,128]{2,1,0:T(8,128)(2,1)}), bf16[64,40,128]{2,1,0:T(8,128)(2,1)S(1)}, u32[]{:S(2)}, u32[]{:S(2)}) async-start(bf16[64,40,128]{2,1,0:T(8,128)(2,1)} %split_blocks.1), calls=%async_computation | async-start | bytes 1310720 | tf_op jit(solution)/shard_map/all_to_all | solution.py:284
  30.8 11.4 %collective-permute-done.7.refs_4_.rest_1_ = bf16[4,128,128]{2,1,0:T(8,128)(2,1)S(1)} collective-permute-done((bf16[4,128,128]{2,1,0:T(8,128)(2,1)S(1)}, bf16[4,128,128]{2,1,0:T(8,128)(2,1)S(1)}, u32[]{:S(2)}, u32[]{:S(2)}) %collective-permute-start.7) | collective-permute-done | bytes 131104 | tf_op jit(solution)/shard_map/ppermute | solution.py:255
  42.2 3.9 %collective-permute-done.12.refs_1_.rest_3_ = bf16[4,128,128]{2,1,0:T(8,128)(2,1)S(1)} collective-permute-done((bf16[4,128,128]{2,1,0:T(8,128)(2,1)S(1)}, bf16[4,128,128]{2,1,0:T(8,128)(2,1)S(1)}, u32[]{:S(2)}, u32[]{:S(2)}) %collective-permute-start.12) | collective-permute-done | bytes 131104 | tf_op jit(solution)/shard_map/ppermute | solution.py:257
  50.1 11.4 %all-to-all-start.1 = ((bf16[64,32,256]{2,1,0:T(8,128)(2,1)}), bf16[64,32,256]{2,1,0:T(8,128)(2,1)S(1)}, u32[]{:S(2)}, u32[]{:S(2)}) async-start(bf16[64,32,256]{2,1,0:T(8,128)(2,1)} %bitcast.20), calls=%async_computation.1 | async-start | bytes 2097152 | tf_op jit(solution)/shard_map/all_to_all | solution.py:292
  66.7 6.6 %near_product.4 = (f32[16,32,128]{2,1,0:T(8,128)S(1)}, f32[16,32,128]{2,1,0:T(8,128)}, f32[16,32,128]{2,1,0:T(8,128)}) custom-call(s32[16,16]{1,0:T(8,128)S(1)} %add_clamp_fusion.index_ref, s32[16]{0:T(128)S(1)} %copy-done.7, bf16[16,16,32,128]{3,2,1,0:T(8,128)(2,1)S(1)} %copy-done, bf16[16,128,128]{2,1,0:T(8,128)(2,1)} %bitcast.4.refs_0_, ...), custom_call_target="tpu_custom_call" | custom-call | flops 704643072 | bytes 6291456 | tf_op jit(solution)/shard_map/near_product/pallas_call | solution.py:146
  73.3 3.1 %collective-permute-done.9.refs_0_ = bf16[16,128,128]{2,1,0:T(8,128)(2,1)} collective-permute-done((bf16[16,128,128]{2,1,0:T(8,128)(2,1)}, bf16[16,128,128]{2,1,0:T(8,128)(2,1)}, u32[]{:S(2)}, u32[]{:S(2)}) %collective-permute-start.9) | collective-permute-done | bytes 524320 | tf_op jit(solution)/shard_map/ppermute | solution.py:257
  76.4 3.5 %near_product.5 = f32[16,32,128]{2,1,0:T(8,128)S(1)} custom-call(s32[16,16]{1,0:T(8,128)S(1)} %add_clamp_fusion.index_ref, s32[16]{0:T(128)S(1)} %copy-done.7, bf16[16,16,32,128]{3,2,1,0:T(8,128)(2,1)S(1)} %copy-done, bf16[16,128,128]{2,1,0:T(8,128)(2,1)} %collective-permute-done.9.refs_0_, bf16[4,128,128]{2,1,0:T(8,128)(2,1)} %copy-done.17), custom_call_target="tpu_custom_call" | custom-call | flops 234881024 | bytes 6291456 | tf_op jit(solution)/shard_map/near_product/pallas_call | solution.py:146
  83.7 4.1 %collective-permute-done.2.refs_3_ = bf16[16,2,32,128]{3,2,1,0:T(8,128)(2,1)} collective-permute-done((bf16[16,2,32,128]{3,2,1,0:T(8,128)(2,1)}, bf16[16,2,32,128]{3,2,1,0:T(8,128)(2,1)}, u32[]{:S(2)}, u32[]{:S(2)}) %collective-permute-start.2) | collective-permute-done | bytes 262176 | tf_op jit(solution)/shard_map/ppermute | solution.py:257
  87.7 5.6 %collective-permute-done.13.refs_7_ = f32[16,32,128]{2,1,0:T(8,128)} collective-permute-done((f32[16,32,128]{2,1,0:T(8,128)S(1)}, f32[16,32,128]{2,1,0:T(8,128)}, u32[]{:S(2)}, u32[]{:S(2)}) %collective-permute-start.13) | collective-permute-done | bytes 262176 | tf_op jit(solution)/shard_map/ppermute | solution.py:257
  93.3 6.4 %collective-permute-done.10.refs_5_ = f32[16,32,128]{2,1,0:T(8,128)} collective-permute-done((f32[16,32,128]{2,1,0:T(8,128)}, f32[16,32,128]{2,1,0:T(8,128)}, u32[]{:S(2)}, u32[]{:S(2)}) %collective-permute-start.10) | collective-permute-done | bytes 262176 | tf_op jit(solution)/shard_map/ppermute | solution.py:255
  99.7 5.2 %add_far.2 = (bf16[2048,128]{1,0:T(8,128)(2,1)S(1)}, bf16[64,32,128]{2,1,0:T(8,128)(2,1)S(1)}) custom-call(s32[4]{0:T(128)S(1)} %pad_add_fusion.offset_ref, s32[16]{0:T(128)S(1)} %copy-done.7, bf16[16,2,32,128]{3,2,1,0:T(8,128)(2,1)} %slice.30.refs_0_, bf16[16,2,32,128]{3,2,1,0:T(8,128)(2,1)} %collective-permute-done.refs_1_, ...), custom_call_target="tpu_custom_call" | custom-call | flops 134217728 | bytes 4194304 | tf_op jit(solution)/shard_map/add_far/pallas_call | solution.py:230
  106.6 3.7 %collective-permute-start.16 = (bf16[2,128,128]{2,1,0:T(8,128)(2,1)S(1)}, bf16[2,128,128]{2,1,0:T(8,128)(2,1)S(1)}, u32[]{:S(2)}, u32[]{:S(2)}) collective-permute-start(bf16[2,128,128]{2,1,0:T(8,128)(2,1)S(1)} %bitcast.29), channel_id=1, source_target_pairs={{0,4},{4,8},{8,12},{12,16},{16,20},{20,24},{24,28},{28,32},{32,36}... | collective-permute-start | bytes 196616 | tf_op jit(solution)/shard_map/ppermute | solution.py:281
  112.2 3.6 %collective-permute-done.17 = bf16[2,128,128]{2,1,0:T(8,128)(2,1)S(1)} collective-permute-done((bf16[2,128,128]{2,1,0:T(8,128)(2,1)S(1)}, bf16[2,128,128]{2,1,0:T(8,128)(2,1)S(1)}, u32[]{:S(2)}, u32[]{:S(2)}) %collective-permute-start.17) | collective-permute-done | bytes 65568 | tf_op jit(solution)/shard_map/ppermute | solution.py:282
  115.8 10.2 %all-to-all-start.2 = ((bf16[64,32,128]{2,1,0:T(8,128)(2,1)}), bf16[64,32,128]{2,1,0:T(8,128)(2,1)S(1)}, u32[]{:S(2)}, u32[]{:S(2)}) async-start(bf16[64,32,128]{2,1,0:T(8,128)(2,1)} %copy-done.4), calls=%async_computation.2 | async-start | bytes 1048576 | tf_op jit(solution)/shard_map/all_to_all | solution.py:284
  131.6 11.8 %collective-permute-done.18.refs_4_.rest_1_ = bf16[4,128,128]{2,1,0:T(8,128)(2,1)S(1)} collective-permute-done((bf16[4,128,128]{2,1,0:T(8,128)(2,1)S(1)}, bf16[4,128,128]{2,1,0:T(8,128)(2,1)S(1)}, u32[]{:S(2)}, u32[]{:S(2)}) %collective-permute-start.18) | collective-permute-done | bytes 131104 | tf_op jit(solution)/shard_map/ppermute | solution.py:255
  143.4 3.0 %collective-permute-done.23.refs_1_.rest_3_ = bf16[4,128,128]{2,1,0:T(8,128)(2,1)S(1)} collective-permute-done((bf16[4,128,128]{2,1,0:T(8,128)(2,1)S(1)}, bf16[4,128,128]{2,1,0:T(8,128)(2,1)S(1)}, u32[]{:S(2)}, u32[]{:S(2)}) %collective-permute-start.23) | collective-permute-done | bytes 131104 | tf_op jit(solution)/shard_map/ppermute | solution.py:257
  150.2 11.3 %all-to-all-start.3 = ((bf16[64,32,256]{2,1,0:T(8,128)(2,1)}), bf16[64,32,256]{2,1,0:T(8,128)(2,1)S(1)}, u32[]{:S(2)}, u32[]{:S(2)}) async-start(bf16[64,32,256]{2,1,0:T(8,128)(2,1)} %bitcast.21), calls=%async_computation.3 | async-start | bytes 2097152 | tf_op jit(solution)/shard_map/all_to_all | solution.py:292
  162.7 5.8 %near_product.6 = (f32[16,32,128]{2,1,0:T(8,128)S(1)}, f32[16,32,128]{2,1,0:T(8,128)S(1)}, f32[16,32,128]{2,1,0:T(8,128)S(1)}) custom-call(s32[16,16]{1,0:T(8,128)S(1)} %add_clamp_fusion.index_ref, s32[16]{0:T(128)S(1)} %copy-done.7, bf16[16,16,32,128]{3,2,1,0:T(8,128)(2,1)S(1)} %copy-done, bf16[16,128,128]{2,1,0:T(8,128)(2,1)} %bitcast.25, ...), custom_call_target="tpu_custom_call" | custom-call | flops 704643072 | bytes 6291456 | tf_op jit(solution)/shard_map/near_product/pallas_call | solution.py:146
  169.3 7.2 %collective-permute-done.20.refs_0_ = bf16[16,128,128]{2,1,0:T(8,128)(2,1)S(1)} collective-permute-done((bf16[16,128,128]{2,1,0:T(8,128)(2,1)}, bf16[16,128,128]{2,1,0:T(8,128)(2,1)S(1)}, u32[]{:S(2)}, u32[]{:S(2)}) %collective-permute-start.20) | collective-permute-done | bytes 524320 | tf_op jit(solution)/shard_map/ppermute | solution.py:257
  177.3 3.5 %near_product.7 = f32[16,32,128]{2,1,0:T(8,128)S(1)} custom-call(s32[16,16]{1,0:T(8,128)S(1)} %add_clamp_fusion.index_ref, s32[16]{0:T(128)S(1)} %copy-done.7, bf16[16,16,32,128]{3,2,1,0:T(8,128)(2,1)S(1)} %copy-done, bf16[16,128,128]{2,1,0:T(8,128)(2,1)} %copy-done.10, bf16[4,128,128]{2,1,0:T(8,128)(2,1)} %copy-done.20), custom_call_target="tpu_custom_call" | custom-call | flops 234881024 | bytes 6291456 | tf_op jit(solution)/shard_map/near_product/pallas_call | solution.py:146
  184.5 4.4 %collective-permute-done.24.refs_7_ = f32[16,32,128]{2,1,0:T(8,128)S(1)} collective-permute-done((f32[16,32,128]{2,1,0:T(8,128)S(1)}, f32[16,32,128]{2,1,0:T(8,128)S(1)}, u32[]{:S(2)}, u32[]{:S(2)}) %collective-permute-start.24) | collective-permute-done | bytes 262176 | tf_op jit(solution)/shard_map/ppermute | solution.py:257
  188.9 7.3 %collective-permute-done.21.refs_5_ = f32[16,32,128]{2,1,0:T(8,128)S(1)} collective-permute-done((f32[16,32,128]{2,1,0:T(8,128)S(1)}, f32[16,32,128]{2,1,0:T(8,128)S(1)}, u32[]{:S(2)}, u32[]{:S(2)}) %collective-permute-start.21) | collective-permute-done | bytes 262176 | tf_op jit(solution)/shard_map/ppermute | solution.py:255
  197.0 5.4 %add_far.3 = bf16[2048,128]{1,0:T(8,128)(2,1)} custom-call(s32[4]{0:T(128)S(1)} %pad_add_fusion.offset_ref, s32[16]{0:T(128)S(1)} %copy-done.7, bf16[16,2,32,128]{3,2,1,0:T(8,128)(2,1)} %slice.30.refs_0_, bf16[16,2,32,128]{3,2,1,0:T(8,128)(2,1)} %collective-permute-done.refs_1_, bf16[16,2,32,128]{3,2,1,0:T(8,128)(2,1)} %collective-permute-done.1.refs_2_, ...), custom_call_target="tpu_custom_call" | custom-call | flops 134217728 | bytes 4194304 | tf_op jit(solution)/shard_map/add_far/pallas_call | solution.py:230
  (103 shorter events, 46.0 us)
Async XLA Ops:
  11.8 35.0 %all-to-all-start = ((bf16[64,40,128]{2,1,0:T(8,128)(2,1)}), bf16[64,40,128]{2,1,0:T(8,128)(2,1)S(1)}, u32[]{:S(2)}, u32[]{:S(2)}) async-start(bf16[64,40,128]{2,1,0:T(8,128)(2,1)} %split_blocks.1), calls=%async_computation | async-start | bytes 1310720 | tf_op jit(solution)/shard_map/all_to_all | solution.py:284
  24.7 21.4 %collective-permute-start.3 = (bf16[16,128,128]{2,1,0:T(8,128)(2,1)}, bf16[16,128,128]{2,1,0:T(8,128)(2,1)S(1)}, u32[]{:S(2)}, u32[]{:S(2)}) collective-permute-start(bf16[16,128,128]{2,1,0:T(8,128)(2,1)} %bitcast.4.refs_0_), channel_id=1, source_target_pairs={{0,1},{1,2},{2,3},{3,0},{4,5},{5,6},{6,7},{7,4},{8,9},{9,10},{10,1... | collective-permute-start | bytes 1572872 | tf_op jit(solution)/shard_map/ppermute | solution.py:255
  26.1 20.7 %collective-permute-start.4 = (bf16[16,128,128]{2,1,0:T(8,128)(2,1)}, bf16[16,128,128]{2,1,0:T(8,128)(2,1)}, u32[]{:S(2)}, u32[]{:S(2)}) collective-permute-start(bf16[16,128,128]{2,1,0:T(8,128)(2,1)} %bitcast.4.refs_0_), channel_id=1, source_target_pairs={{1,0},{2,1},{3,2},{0,3},{5,4},{6,5},{7,6},{4,7},{9,8},{10,9},{11,1... | collective-permute-start | bytes 1572872 | tf_op jit(solution)/shard_map/ppermute | solution.py:256
  27.7 14.5 %collective-permute-start.7 = (bf16[4,128,128]{2,1,0:T(8,128)(2,1)S(1)}, bf16[4,128,128]{2,1,0:T(8,128)(2,1)S(1)}, u32[]{:S(2)}, u32[]{:S(2)}) collective-permute-start(bf16[4,128,128]{2,1,0:T(8,128)(2,1)S(1)} %constant_dynamic-update-slice_fusion.refs_3_.rest_0_), channel_id=1, source_target_pairs={{0,1},{1,2},{2,3},{3,0},{4,5},{5,6},{6,7},{7,4},{8,9},{9,10},{10,1... | collective-permute-start | bytes 393224 | tf_op jit(solution)/shard_map/ppermute | solution.py:255
  27.7 14.5 %collective-permute-start.8 = (bf16[4,128,128]{2,1,0:T(8,128)(2,1)S(1)}, bf16[4,128,128]{2,1,0:T(8,128)(2,1)S(1)}, u32[]{:S(2)}, u32[]{:S(2)}) collective-permute-start(bf16[4,128,128]{2,1,0:T(8,128)(2,1)S(1)} %constant_dynamic-update-slice_fusion.refs_3_.rest_0_), channel_id=1, source_target_pairs={{1,0},{2,1},{3,2},{0,3},{5,4},{6,5},{7,6},{4,7},{9,8},{10,9},{11,1... | collective-permute-start | bytes 393224 | tf_op jit(solution)/shard_map/ppermute | solution.py:256
  30.4 15.7 %collective-permute-start.12 = (bf16[4,128,128]{2,1,0:T(8,128)(2,1)S(1)}, bf16[4,128,128]{2,1,0:T(8,128)(2,1)S(1)}, u32[]{:S(2)}, u32[]{:S(2)}) collective-permute-start(bf16[4,128,128]{2,1,0:T(8,128)(2,1)S(1)} %constant_dynamic-update-slice_fusion.refs_3_.rest_0_), channel_id=1, source_target_pairs={{0,2},{1,3},{2,0},{3,1},{4,6},{5,7},{6,4},{7,5},{8,10},{9,11},{10,... | collective-permute-start | bytes 393224 | tf_op jit(solution)/shard_map/ppermute | solution.py:257
  50.1 49.7 %all-to-all-start.1 = ((bf16[64,32,256]{2,1,0:T(8,128)(2,1)}), bf16[64,32,256]{2,1,0:T(8,128)(2,1)S(1)}, u32[]{:S(2)}, u32[]{:S(2)}) async-start(bf16[64,32,256]{2,1,0:T(8,128)(2,1)} %bitcast.20), calls=%async_computation.1 | async-start | bytes 2097152 | tf_op jit(solution)/shard_map/all_to_all | solution.py:292
  61.5 15.0 %collective-permute-start.9 = (bf16[16,128,128]{2,1,0:T(8,128)(2,1)}, bf16[16,128,128]{2,1,0:T(8,128)(2,1)}, u32[]{:S(2)}, u32[]{:S(2)}) collective-permute-start(bf16[16,128,128]{2,1,0:T(8,128)(2,1)} %bitcast.4.refs_0_), channel_id=1, source_target_pairs={{0,2},{1,3},{2,0},{3,1},{4,6},{5,7},{6,4},{7,5},{8,10},{9,11},{10,... | collective-permute-start | bytes 1572872 | tf_op jit(solution)/shard_map/ppermute | solution.py:257
  62.9 20.7 %collective-permute-start = (bf16[16,2,32,128]{3,2,1,0:T(8,128)(2,1)}, bf16[16,2,32,128]{3,2,1,0:T(8,128)(2,1)}, u32[]{:S(2)}, u32[]{:S(2)}) collective-permute-start(bf16[16,2,32,128]{3,2,1,0:T(8,128)(2,1)} %slice.30.refs_0_), channel_id=1, source_target_pairs={{0,1},{1,2},{2,3},{3,0},{4,5},{5,6},{6,7},{7,4},{8,9},{9,10},{10,1... | collective-permute-start | bytes 786440 | tf_op jit(solution)/shard_map/ppermute | solution.py:255
  64.5 19.1 %collective-permute-start.1 = (bf16[16,2,32,128]{3,2,1,0:T(8,128)(2,1)}, bf16[16,2,32,128]{3,2,1,0:T(8,128)(2,1)}, u32[]{:S(2)}, u32[]{:S(2)}) collective-permute-start(bf16[16,2,32,128]{3,2,1,0:T(8,128)(2,1)} %slice.30.refs_0_), channel_id=1, source_target_pairs={{1,0},{2,1},{3,2},{0,3},{5,4},{6,5},{7,6},{4,7},{9,8},{10,9},{11,1... | collective-permute-start | bytes 786440 | tf_op jit(solution)/shard_map/ppermute | solution.py:256
  65.6 22.2 %collective-permute-start.2 = (bf16[16,2,32,128]{3,2,1,0:T(8,128)(2,1)}, bf16[16,2,32,128]{3,2,1,0:T(8,128)(2,1)}, u32[]{:S(2)}, u32[]{:S(2)}) collective-permute-start(bf16[16,2,32,128]{3,2,1,0:T(8,128)(2,1)} %slice.30.refs_0_), channel_id=1, source_target_pairs={{0,2},{1,3},{2,0},{3,1},{4,6},{5,7},{6,4},{7,5},{8,10},{9,11},{10,... | collective-permute-start | bytes 786440 | tf_op jit(solution)/shard_map/ppermute | solution.py:257
  79.9 13.4 %collective-permute-start.13 = (f32[16,32,128]{2,1,0:T(8,128)S(1)}, f32[16,32,128]{2,1,0:T(8,128)}, u32[]{:S(2)}, u32[]{:S(2)}) collective-permute-start(f32[16,32,128]{2,1,0:T(8,128)S(1)} %near_product.5), channel_id=1, source_target_pairs={{0,2},{1,3},{2,0},{3,1},{4,6},{5,7},{6,4},{7,5},{8,10},{9,11},{10,... | collective-permute-start | bytes 786440 | tf_op jit(solution)/shard_map/ppermute | solution.py:257
  80.8 18.9 %collective-permute-start.10 = (f32[16,32,128]{2,1,0:T(8,128)}, f32[16,32,128]{2,1,0:T(8,128)}, u32[]{:S(2)}, u32[]{:S(2)}) collective-permute-start(f32[16,32,128]{2,1,0:T(8,128)} %get-tuple-element.29), channel_id=1, source_target_pairs={{0,1},{1,2},{2,3},{3,0},{4,5},{5,6},{6,7},{7,4},{8,9},{9,10},{10,1... | collective-permute-start | bytes 786440 | tf_op jit(solution)/shard_map/ppermute | solution.py:255
  83.6 16.1 %collective-permute-start.11 = (f32[16,32,128]{2,1,0:T(8,128)}, f32[16,32,128]{2,1,0:T(8,128)}, u32[]{:S(2)}, u32[]{:S(2)}) collective-permute-start(f32[16,32,128]{2,1,0:T(8,128)} %get-tuple-element.30), channel_id=1, source_target_pairs={{1,0},{2,1},{3,2},{0,3},{5,4},{6,5},{7,6},{4,7},{9,8},{10,9},{11,1... | collective-permute-start | bytes 786440 | tf_op jit(solution)/shard_map/ppermute | solution.py:256
  115.8 31.2 %all-to-all-start.2 = ((bf16[64,32,128]{2,1,0:T(8,128)(2,1)}), bf16[64,32,128]{2,1,0:T(8,128)(2,1)S(1)}, u32[]{:S(2)}, u32[]{:S(2)}) async-start(bf16[64,32,128]{2,1,0:T(8,128)(2,1)} %copy-done.4), calls=%async_computation.2 | async-start | bytes 1048576 | tf_op jit(solution)/shard_map/all_to_all | solution.py:284
  126.0 20.3 %collective-permute-start.14 = (bf16[16,128,128]{2,1,0:T(8,128)(2,1)}, bf16[16,128,128]{2,1,0:T(8,128)(2,1)S(1)}, u32[]{:S(2)}, u32[]{:S(2)}) collective-permute-start(bf16[16,128,128]{2,1,0:T(8,128)(2,1)} %bitcast.22), channel_id=1, source_target_pairs={{0,1},{1,2},{2,3},{3,0},{4,5},{5,6},{6,7},{7,4},{8,9},{9,10},{10,1... | collective-permute-start | bytes 1572872 | tf_op jit(solution)/shard_map/ppermute | solution.py:255
  126.9 20.0 %collective-permute-start.15 = (bf16[16,128,128]{2,1,0:T(8,128)(2,1)}, bf16[16,128,128]{2,1,0:T(8,128)(2,1)}, u32[]{:S(2)}, u32[]{:S(2)}) collective-permute-start(bf16[16,128,128]{2,1,0:T(8,128)(2,1)} %bitcast.23), channel_id=1, source_target_pairs={{1,0},{2,1},{3,2},{0,3},{5,4},{6,5},{7,6},{4,7},{9,8},{10,9},{11,1... | collective-permute-start | bytes 1572872 | tf_op jit(solution)/shard_map/ppermute | solution.py:256
  128.8 14.6 %collective-permute-start.18 = (bf16[4,128,128]{2,1,0:T(8,128)(2,1)S(1)}, bf16[4,128,128]{2,1,0:T(8,128)(2,1)S(1)}, u32[]{:S(2)}, u32[]{:S(2)}) collective-permute-start(bf16[4,128,128]{2,1,0:T(8,128)(2,1)S(1)} %constant_dynamic-update-slice_fusion.2.refs_3_.rest_0_), channel_id=1, source_target_pairs={{0,1},{1,2},{2,3},{3,0},{4,5},{5,6},{6,7},{7,4},{8,9},{9,10},{10,1... | collective-permute-start | bytes 393224 | tf_op jit(solution)/shard_map/ppermute | solution.py:255
  128.9 14.5 %collective-permute-start.19 = (bf16[4,128,128]{2,1,0:T(8,128)(2,1)S(1)}, bf16[4,128,128]{2,1,0:T(8,128)(2,1)S(1)}, u32[]{:S(2)}, u32[]{:S(2)}) collective-permute-start(bf16[4,128,128]{2,1,0:T(8,128)(2,1)S(1)} %constant_dynamic-update-slice_fusion.2.refs_3_.rest_0_), channel_id=1, source_target_pairs={{1,0},{2,1},{3,2},{0,3},{5,4},{6,5},{7,6},{4,7},{9,8},{10,9},{11,1... | collective-permute-start | bytes 393224 | tf_op jit(solution)/shard_map/ppermute | solution.py:256
  131.6 14.8 %collective-permute-start.23 = (bf16[4,128,128]{2,1,0:T(8,128)(2,1)S(1)}, bf16[4,128,128]{2,1,0:T(8,128)(2,1)S(1)}, u32[]{:S(2)}, u32[]{:S(2)}) collective-permute-start(bf16[4,128,128]{2,1,0:T(8,128)(2,1)S(1)} %constant_dynamic-update-slice_fusion.2.refs_3_.rest_0_), channel_id=1, source_target_pairs={{0,2},{1,3},{2,0},{3,1},{4,6},{5,7},{6,4},{7,5},{8,10},{9,11},{10,... | collective-permute-start | bytes 393224 | tf_op jit(solution)/shard_map/ppermute | solution.py:257
  150.2 46.0 %all-to-all-start.3 = ((bf16[64,32,256]{2,1,0:T(8,128)(2,1)}), bf16[64,32,256]{2,1,0:T(8,128)(2,1)S(1)}, u32[]{:S(2)}, u32[]{:S(2)}) async-start(bf16[64,32,256]{2,1,0:T(8,128)(2,1)} %bitcast.21), calls=%async_computation.3 | async-start | bytes 2097152 | tf_op jit(solution)/shard_map/all_to_all | solution.py:292
  161.4 15.1 %collective-permute-start.20 = (bf16[16,128,128]{2,1,0:T(8,128)(2,1)}, bf16[16,128,128]{2,1,0:T(8,128)(2,1)S(1)}, u32[]{:S(2)}, u32[]{:S(2)}) collective-permute-start(bf16[16,128,128]{2,1,0:T(8,128)(2,1)} %bitcast.24), channel_id=1, source_target_pairs={{0,2},{1,3},{2,0},{3,1},{4,6},{5,7},{6,4},{7,5},{8,10},{9,11},{10,... | collective-permute-start | bytes 1572872 | tf_op jit(solution)/shard_map/ppermute | solution.py:257
  181.8 14.4 %collective-permute-start.21 = (f32[16,32,128]{2,1,0:T(8,128)S(1)}, f32[16,32,128]{2,1,0:T(8,128)S(1)}, u32[]{:S(2)}, u32[]{:S(2)}) collective-permute-start(f32[16,32,128]{2,1,0:T(8,128)S(1)} %get-tuple-element.40), channel_id=1, source_target_pairs={{0,1},{1,2},{2,3},{3,0},{4,5},{5,6},{6,7},{7,4},{8,9},{9,10},{10,1... | collective-permute-start | bytes 786440 | tf_op jit(solution)/shard_map/ppermute | solution.py:255
  184.0 12.2 %collective-permute-start.22 = (f32[16,32,128]{2,1,0:T(8,128)S(1)}, f32[16,32,128]{2,1,0:T(8,128)S(1)}, u32[]{:S(2)}, u32[]{:S(2)}) collective-permute-start(f32[16,32,128]{2,1,0:T(8,128)S(1)} %get-tuple-element.41), channel_id=1, source_target_pairs={{1,0},{2,1},{3,2},{0,3},{5,4},{6,5},{7,6},{4,7},{9,8},{10,9},{11,1... | collective-permute-start | bytes 786440 | tf_op jit(solution)/shard_map/ppermute | solution.py:256
  (28 other events, 180.2 us)

commit v7 on v2

--- a/solution.py
+++ b/solution.py
@@ -12,7 +12,12 @@
 LOW = tuple(range(1, 9))
 HIGH = tuple(range(9, 16)) + (0,)
 VMEM = pl.BlockSpec(memory_space=pltpu.VMEM)
-SMEM = pl.BlockSpec(memory_space=pltpu.SMEM)
+HBM = pl.BlockSpec(memory_space=pltpu.HBM)
+LIMIT = 12 << 20
+
+
+def in_hbm(arrays):
+    return [pltpu.with_memory_space_constraint(array, pltpu.HBM) for array in arrays]
 
 
 def rows_to_pieces(wide, pieces_ref, blocks, size, owners):
@@ -42,7 +47,7 @@
     )(queries, digits)
 
 
-def select_pieces(held, slots, wanted=None):
+def select_pieces(held, slots, after, wanted=None):
     devices, height, cols = held.shape
     blocks = height // 16 * 8
     parts = 2
@@ -50,6 +55,7 @@
     group = 8
 
     def kernel(held_ref, *rest):
+        rest = rest[len(after) :]
         if wanted is None:
             out_ref, wanted_out, flat = rest
             digits = held_ref[:, parts * blocks :, :].astype(jnp.float32)[:, 0, :].T
@@ -78,19 +84,19 @@
     out_shape = [jax.ShapeDtypeStruct((devices * slots, parts * cols), held.dtype)]
     if wanted is None:
         out_shape.append(jax.ShapeDtypeStruct((slots, devices), jnp.int32))
-    operands = (held,) if wanted is None else (held, wanted)
+    operands = () if wanted is None else (wanted,)
     return pl.pallas_call(
         kernel,
         out_shape=out_shape,
-        in_specs=[VMEM] * len(operands),
+        in_specs=[VMEM] + [HBM] * len(after) + [VMEM] * len(operands),
         out_specs=[VMEM] * len(out_shape),
         scratch_shapes=[pltpu.VMEM((block_total, parts * cols), held.dtype)],
-        compiler_params=pltpu.CompilerParams(vmem_limit_bytes=32 << 20),
+        compiler_params=pltpu.CompilerParams(vmem_limit_bytes=LIMIT),
         cost_estimate=pl.CostEstimate(
             flops=2 * devices * slots * block_total * parts * cols, bytes_accessed=2 << 20, transcendentals=0
         ),
         name="select_pieces",
-    )(*operands)
+    )(held, *in_hbm(after), *operands)
 
 
 def near_product(near_index, counts, quarters, low, own, high):
@@ -103,14 +109,20 @@
 
     def kernel(index_ref, count_ref, *refs):
         tiles = [refs[2 * n : 2 * n + 2] for n in range(number)]
-        low_ref, own_ref, high_ref, out_ref, panels = refs[2 * number :]
+        low_ref, own_ref, high_ref, out_ref, panels, sems = refs[2 * number :]
         step = pl.program_id(0)
 
         @pl.when(step == 0)
         def _():
-            panels[:EDGE] = low_ref[...]
-            panels[EDGE : EDGE + blocks] = own_ref[...]
-            panels[EDGE + blocks :] = high_ref[...]
+            copies = [
+                pltpu.make_async_copy(low_ref, panels.at[:EDGE], sems.at[0]),
+                pltpu.make_async_copy(own_ref, panels.at[EDGE : EDGE + blocks], sems.at[1]),
+                pltpu.make_async_copy(high_ref, panels.at[EDGE + blocks :], sems.at[2]),
+            ]
+            for copy in copies:
+                copy.start()
+            for copy in copies:
+                copy.wait()
 
         for r in range(group):
             b = step * group + r
@@ -139,18 +151,21 @@
                 for pair in quarters
                 for half in pair
             ]
-            + [VMEM] * 3,
+            + [HBM] * 3,
             out_specs=pl.BlockSpec((group, number * rows, cols), lambda i, *_: (i, 0, 0)),
-            scratch_shapes=[pltpu.VMEM((blocks + 2 * EDGE, size, cols), own.dtype)],
-        ),
-        compiler_params=pltpu.CompilerParams(vmem_limit_bytes=32 << 20),
+            scratch_shapes=[
+                pltpu.VMEM((blocks + 2 * EDGE, size, cols), own.dtype),
+                pltpu.SemaphoreType.DMA((3,)),
+            ],
+        ),
+        compiler_params=pltpu.CompilerParams(vmem_limit_bytes=LIMIT),
         cost_estimate=pl.CostEstimate(
             flops=2 * blocks * len(near) * number * rows * size * cols,
             bytes_accessed=number << 21,
             transcendentals=0,
         ),
         name="near_product",
-    )(near_index, counts, *[half for pair in quarters for half in pair], low, own, high)
+    )(near_index, counts, *[half for pair in quarters for half in pair], *in_hbm([low, own, high]))
 
 
 def add_far(offsets, counts, far_tiles, arrived, partials, queries, owners, split):
@@ -160,24 +175,37 @@
     number = len(far_tiles)
 
     def kernel(offset_ref, count_ref, *refs):
-        tiles = refs[:number]
-        arrived_ref = refs[number]
-        partial_refs = refs[number + 1 : number + 1 + len(partials)]
-        q_ref, out_ref, *rest = refs[number + 1 + len(partials) :]
+        tile_refs, partial_refs = refs[:number], refs[number : number + len(partials)]
+        arrived_ref, q_ref, out_ref = refs[number + len(partials) : number + len(partials) + 3]
+        rest = refs[number + len(partials) + 3 :]
         if split:
-            pieces_ref, upper, lower, wide = rest
+            pieces_ref, upper, lower, tiles, sums, sems, wide = rest
         else:
-            upper, lower = rest
+            upper, lower, tiles, sums, sems = rest
+        copies = [
+            pltpu.make_async_copy(ref.at[:, : len(FAR)], tiles.at[n], sems.at[0, n])
+            for n, ref in enumerate(tile_refs)
+        ]
+        first = 0
+        for n, (ref, part) in enumerate(zip(partial_refs, partials)):
+            copies.append(
+                pltpu.make_async_copy(ref, sums.at[:, first : first + part.shape[1]], sems.at[1, n])
+            )
+            first += part.shape[1]
+        for copy in copies:
+            copy.start()
         upper[...] = arrived_ref[:, :cols].astype(jnp.float32)
         lower[...] = arrived_ref[:, cols:].astype(jnp.float32)
+        for copy in copies:
+            copy.wait()
         for b in range(blocks):
             left, right = [], []
             for s, t in enumerate(FAR):
-                tile = jnp.concatenate([ref[b, s] for ref in tiles], axis=0)
+                tile = tiles[:, b, s].reshape(size, size)
                 left.append(jnp.where(t < count_ref[b], tile, jnp.zeros_like(tile)))
                 for half in (upper, lower):
                     right.append(half[pl.ds(2 * b + s, owners, stride=far), :].astype(queries.dtype))
-            total = jnp.concatenate([ref[b] for ref in partial_refs], axis=0) + jnp.dot(
+            total = sums[b] + jnp.dot(
                 jnp.concatenate(left, axis=1),
                 jnp.concatenate(right, axis=0),
                 preferred_element_type=jnp.float32,
@@ -194,7 +222,13 @@
 
     out_shape = [jax.ShapeDtypeStruct(queries.shape, queries.dtype)]
     out_specs = [pl.BlockSpec(queries.shape, lambda i, *_: (0, 0))]
-    scratch = [pltpu.VMEM((owners * far, cols), jnp.float32)] * 2
+    scratch = [
+        pltpu.VMEM((owners * far, cols), jnp.float32),
+        pltpu.VMEM((owners * far, cols), jnp.float32),
+        pltpu.VMEM((number, blocks, len(FAR), rows, size), far_tiles[0].dtype),
+        pltpu.VMEM((blocks, size, cols), jnp.float32),
+        pltpu.SemaphoreType.DMA((2, number)),
+    ]
     if split:
         shape = (owners, size // owners * blocks, cols)
         out_shape.append(jax.ShapeDtypeStruct(shape, queries.dtype))
@@ -206,17 +240,16 @@
         grid_spec=pltpu.PrefetchScalarGridSpec(
             num_scalar_prefetch=2,
             grid=(1,),
-            in_specs=[pl.BlockSpec((blocks, len(FAR), rows, size), lambda i, *_: (0, 0, 0, 0))] * number
-            + [VMEM] * (2 + len(partials)),
+            in_specs=[HBM] * (number + len(partials)) + [VMEM] * 2,
             out_specs=out_specs,
             scratch_shapes=scratch,
         ),
-        compiler_params=pltpu.CompilerParams(vmem_limit_bytes=32 << 20),
+        compiler_params=pltpu.CompilerParams(vmem_limit_bytes=LIMIT),
         cost_estimate=pl.CostEstimate(
             flops=4 * blocks * size * size * cols, bytes_accessed=4 << 20, transcendentals=0
         ),
         name="add_far",
-    )(offsets, counts, *far_tiles, arrived, *partials, queries)
+    )(offsets, counts, *in_hbm(far_tiles), *in_hbm(partials), arrived, queries)
 
 
 def gather_rows(tiles):
@@ -259,9 +292,9 @@
         low = lax.ppermute(own[blocks - EDGE :], "db", up)
         high = lax.ppermute(own[:EDGE], "db", down)
         if wanted is None:
-            chosen, wanted = select_pieces(held, slots)
+            chosen, wanted = select_pieces(held, slots, [low, high])
         else:
-            (chosen,) = select_pieces(held, slots, wanted)
+            (chosen,) = select_pieces(held, slots, [low, high], wanted)
         arrived = lax.all_to_all(
             chosen.reshape(owners, slots, -1), "db", split_axis=0, concat_axis=0, tiled=True
         ).reshape(chosen.shape)

time: 188 us -> 186 us (0.989)
  blocking collectives: 28.8 us -> 0 us
  waiting for transfers between devices: 64.7 us -> 80.5 us
  starting transfers between devices: 46.4 us -> 56.7 us
  Pallas kernels: 29.2 us -> 35.8 us
  local copies, waits for them, and re-layouts: 15.9 us -> 10.1 us
    all_to_all x1 -> x0, blocking collectives: 28.8 us -> none  [on_device(): held = lax.all_to_all(pieces, 'db', split_axis=0, concat_axis=0, tiled=True)]
    all_to_all x2, waiting for transfers between devices: 0.01 us -> 20.9 us  [on_device(): lax.all_to_all(chosen.reshape(owners, slots, -1), 'db', split_axis=0, con...]
    ppermute x1, waiting for transfers between devices: 0.01 us -> 20.8 us  [gather_rows(): after_low = lax.ppermute(low, 'pb', down)]
    ppermute x2, waiting for transfers between devices: 27.3 us -> 7.17 us  [on_device(): low = lax.ppermute(own[blocks - EDGE:], 'db', up)]
    all_to_all x1 -> x2, starting transfers between devices: 13 us -> 24.7 us  [on_device(): held = lax.all_to_all(pieces, 'db', split_axis=0, concat_axis=0, tiled=True)]
    all_to_all x1 -> x2, waiting for transfers between devices: 14.8 us -> 6.5 us  [on_device(): held = lax.all_to_all(pieces, 'db', split_axis=0, concat_axis=0, tiled=True)]
    unnamed x28 -> x42, local copies, waits for them, and re-layouts: 11.3 us -> 6.48 us
    pallas_call x3, Pallas kernels: 14.3 us -> 17.7 us  [near_product(): pl.pallas_call(kernel, out_shape=jax.ShapeDtypeStruct((blocks, number * r...]
  transfers between devices with their start and end apart: 13 -> 14, of which waited for: 6 -> 11; matrix products, arithmetic and copies ran while one was open for 2% -> 2% of each run, Pallas kernels for 9% -> 11%
where the time goes in v7:
time: 186 us; the launch traced here: 185 us
  waiting for transfers between devices  80.5 us (43%)
  starting transfers between devices  56.7 us (30%)
  Pallas kernels  35.8 us (19%)
  local copies, waits for them, and re-layouts  10.1 us (5%)
    all_to_all x2, starting transfers between devices, on_device(): held = lax.all_to_all(pieces, 'db', split_axis=0, concat_axis=0, tiled=True)  24.7 us
    all_to_all x2, waiting for transfers between devices, on_device(): lax.all_to_all(chosen.reshape(owners, slots, -1), 'db', split_axis=0, con...  20.9 us
    ppermute x1, waiting for transfers between devices, gather_rows(): after_low = lax.ppermute(low, 'pb', down)  20.8 us
    pallas_call x3, Pallas kernels, near_product(): pl.pallas_call(kernel, out_shape=jax.ShapeDtypeStruct((blocks, number * r...  17.7 us
    ppermute x1, waiting for transfers between devices, gather_rows(): far_low = lax.ppermute(before_low, 'pb', up)  15.4 us
    all_to_all x2, starting transfers between devices, on_device(): lax.all_to_all(chosen.reshape(owners, slots, -1), 'db', split_axis=0, con...  13.1 us
    pallas_call x2, Pallas kernels, add_far(): pl.pallas_call(kernel, out_shape=out_shape, grid_spec=pltpu.PrefetchScala...  11.8 us
    ppermute x2, waiting for transfers between devices, on_device(): low = lax.ppermute(own[blocks - EDGE:], 'db', up)  7.17 us
  transfers between devices with their start and end apart: 14, of which 11 were waited for; matrix products, arithmetic and copies ran while one was open for 2% of the time, Pallas kernels for 11%

profile of v7, /device:TPU:1, one launch (start us, length us, event | category | flops | bytes accessed | tf_op | source)
XLA Modules:
  0.0 184.8 jit_solution(4570681708284340298)
XLA Ops:
  1.5 2.6 %split_blocks.1 = bf16[64,40,128]{2,1,0:T(8,128)(2,1)} custom-call(bf16[2048,128]{1,0:T(8,128)(2,1)} %refs_6_.1, f32[1,128]{1,0:T(1,128)} %pad.4.digits_ref), custom_call_target="tpu_custom_call" | custom-call | tf_op jit(solution)/shard_map/split_blocks/pallas_call | solution.py:40
  4.0 13.0 %all-to-all-start = ((bf16[64,40,128]{2,1,0:T(8,128)(2,1)}), bf16[64,40,128]{2,1,0:T(8,128)(2,1)S(1)}, u32[]{:S(2)}, u32[]{:S(2)}) async-start(bf16[64,40,128]{2,1,0:T(8,128)(2,1)} %split_blocks.1), calls=%async_computation | async-start | bytes 1310720 | tf_op jit(solution)/shard_map/all_to_all | solution.py:291
  17.9 3.5 %collective-permute-start.6 = (bf16[2,128,128]{2,1,0:T(8,128)(2,1)S(1)}, bf16[2,128,128]{2,1,0:T(8,128)(2,1)S(1)}, u32[]{:S(2)}, u32[]{:S(2)}) collective-permute-start(bf16[2,128,128]{2,1,0:T(8,128)(2,1)S(1)} %bitcast.23), channel_id=1, source_target_pairs={{0,4},{4,8},{8,12},{12,16},{16,20},{20,24},{24,28},{28,32},{32,36}... | collective-permute-start | bytes 196616 | tf_op jit(solution)/shard_map/ppermute | solution.py:292
  21.5 2.1 %collective-permute-start.7 = (bf16[2,128,128]{2,1,0:T(8,128)(2,1)S(1)}, bf16[2,128,128]{2,1,0:T(8,128)(2,1)S(1)}, u32[]{:S(2)}, u32[]{:S(2)}) collective-permute-start(bf16[2,128,128]{2,1,0:T(8,128)(2,1)S(1)} %bitcast.22), channel_id=1, source_target_pairs={{4,0},{8,4},{12,8},{16,12},{20,16},{24,20},{28,24},{32,28},{36,32}... | collective-permute-start | bytes 196616 | tf_op jit(solution)/shard_map/ppermute | solution.py:293
  30.9 3.4 %collective-permute-done.7.refs_8_.refs_4_.rest_1_ = bf16[2,128,128]{2,1,0:T(8,128)(2,1)S(1)} collective-permute-done((bf16[2,128,128]{2,1,0:T(8,128)(2,1)S(1)}, bf16[2,128,128]{2,1,0:T(8,128)(2,1)S(1)}, u32[]{:S(2)}, u32[]{:S(2)}) %collective-permute-start.7) | collective-permute-done | bytes 65568 | tf_op jit(solution)/shard_map/ppermute | solution.py:293
  34.4 3.3 %all-to-all-done.held_ref = bf16[64,40,128]{2,1,0:T(8,128)(2,1)S(1)} async-done(((bf16[64,40,128]{2,1,0:T(8,128)(2,1)}), bf16[64,40,128]{2,1,0:T(8,128)(2,1)S(1)}, u32[]{:S(2)}, u32[]{:S(2)}) %all-to-all-start) | async-done | bytes 655392 | tf_op jit(solution)/shard_map/all_to_all | solution.py:291
  37.7 2.4 %select_pieces.2 = (bf16[2048,256]{1,0:T(8,128)(2,1)}, s32[32,64]{1,0:T(8,128)S(1)}) custom-call(bf16[64,40,128]{2,1,0:T(8,128)(2,1)S(1)} %all-to-all-done.held_ref, bf16[2,128,128]{2,1,0:T(8,128)(2,1)} %copy-done.16, bf16[2,128,128]{2,1,0:T(8,128)(2,1)} %copy-done.17), custom_call_target="tpu_custom_call" | custom-call | flops 1073741824 | bytes 2097152 | tf_op jit(solution)/shard_map/select_pieces/pallas_call | solution.py:88
  40.1 6.8 %all-to-all-start.1 = ((bf16[64,32,256]{2,1,0:T(8,128)(2,1)}), bf16[64,32,256]{2,1,0:T(8,128)(2,1)}, u32[]{:S(2)}, u32[]{:S(2)}) async-start(bf16[64,32,256]{2,1,0:T(8,128)(2,1)} %bitcast.9), calls=%async_computation.1 | async-start | bytes 2097152 | tf_op jit(solution)/shard_map/all_to_all | solution.py:298
  46.9 2.8 %collective-permute-start.1 = (bf16[16,8,32,128]{3,2,1,0:T(8,128)(2,1)S(1)}, bf16[16,8,32,128]{3,2,1,0:T(8,128)(2,1)S(1)}, u32[]{:S(2)}, u32[]{:S(2)}) collective-permute-start(bf16[16,8,32,128]{3,2,1,0:T(8,128)(2,1)S(1)} %slice.36.refs_0_), channel_id=1, source_target_pairs={{1,0},{2,1},{3,2},{0,3},{5,4},{6,5},{7,6},{4,7},{9,8},{10,9},{11,1... | collective-permute-start | bytes 3145736 | tf_op jit(solution)/shard_map/ppermute | solution.py:264
  50.3 2.6 %collective-permute-done.4.refs_5_ = bf16[16,8,32,128]{3,2,1,0:T(8,128)(2,1)} collective-permute-done((bf16[16,8,32,128]{3,2,1,0:T(8,128)(2,1)}, bf16[16,8,32,128]{3,2,1,0:T(8,128)(2,1)}, u32[]{:S(2)}, u32[]{:S(2)}) %collective-permute-start.4) | collective-permute-done | bytes 1048608 | tf_op jit(solution)/shard_map/ppermute | solution.py:262
  54.5 20.8 %collective-permute-done.1.refs_4_.refs_2_ = bf16[16,8,32,128]{3,2,1,0:T(8,128)(2,1)S(1)} collective-permute-done((bf16[16,8,32,128]{3,2,1,0:T(8,128)(2,1)S(1)}, bf16[16,8,32,128]{3,2,1,0:T(8,128)(2,1)S(1)}, u32[]{:S(2)}, u32[]{:S(2)}) %collective-permute-start.1) | collective-permute-done | bytes 1048608 | tf_op jit(solution)/shard_map/ppermute | solution.py:264
  75.3 5.9 %near_product.3.refs_4_ = f32[16,96,128]{2,1,0:T(8,128)S(1)} custom-call(s32[16,16]{1,0:T(8,128)S(1)} %add_clamp_fusion.index_ref, s32[16]{0:T(128)S(1)} %copy-done.15, bf16[16,8,32,128]{3,2,1,0:T(8,128)(2,1)S(1)} %slice.36.refs_0_, bf16[16,8,32,128]{3,2,1,0:T(8,128)(2,1)} %pad_maximum_fusion.refs_1_, ...), custom_call_target="tpu_custom_call" | custom-call | flops 704643072 | bytes 6291456 | tf_op jit(solution)/shard_map/near_product/pallas_call | solution.py:143
  82.2 15.4 %collective-permute-done.2.refs_0_.refs_3_.refs_6_ = bf16[16,8,32,128]{3,2,1,0:T(8,128)(2,1)} collective-permute-done((bf16[16,8,32,128]{3,2,1,0:T(8,128)(2,1)S(1)}, bf16[16,8,32,128]{3,2,1,0:T(8,128)(2,1)}, u32[]{:S(2)}, u32[]{:S(2)}) %collective-permute-start.2) | collective-permute-done | bytes 1048608 | tf_op jit(solution)/shard_map/ppermute | solution.py:265
  97.6 5.2 %near_product.4.refs_5_ = f32[16,32,128]{2,1,0:T(8,128)S(1)} custom-call(s32[16,16]{1,0:T(8,128)S(1)} %add_clamp_fusion.index_ref, s32[16]{0:T(128)S(1)} %copy-done.15, bf16[16,8,32,128]{3,2,1,0:T(8,128)(2,1)} %collective-permute-done.2.refs_0_.refs_3_.refs_6_, bf16[16,8,32,128]{3,2,1,0:T(8,128)(2,1)} %collective-permute-done.5.refs_1_.refs_7_, ...), custom_call_target="tpu_custom_call" | custom-call | flops 234881024 | bytes 2097152 | tf_op jit(solution)/shard_map/near_product/pallas_call | solution.py:143
  103.5 6.2 %add_far.2 = (bf16[2048,128]{1,0:T(8,128)(2,1)S(1)}, bf16[64,32,128]{2,1,0:T(8,128)(2,1)}) custom-call(s32[4]{0:T(128)S(1)} %pad_add_fusion.offset_ref, s32[16]{0:T(128)S(1)} %copy-done.15, bf16[16,8,32,128]{3,2,1,0:T(8,128)(2,1)} %copy-done, bf16[16,8,32,128]{3,2,1,0:T(8,128)(2,1)} %copy-done.2, bf16[16,8,32,128]{3,2,1,0:T(8,128)(2,1)} %copy-done.4, ...), custom_call_target="tpu_custom_call" | custom-call | flops 134217728 | bytes 4194304 | tf_op jit(solution)/shard_map/add_far/pallas_call | solution.py:237
  109.7 11.7 %all-to-all-start.2 = ((bf16[64,32,128]{2,1,0:T(8,128)(2,1)}), bf16[64,32,128]{2,1,0:T(8,128)(2,1)S(1)}, u32[]{:S(2)}, u32[]{:S(2)}) async-start(bf16[64,32,128]{2,1,0:T(8,128)(2,1)} %get-tuple-element.11), calls=%async_computation.2 | async-start | bytes 1048576 | tf_op jit(solution)/shard_map/all_to_all | solution.py:291
  121.4 3.5 %collective-permute-start.8 = (bf16[2,128,128]{2,1,0:T(8,128)(2,1)S(1)}, bf16[2,128,128]{2,1,0:T(8,128)(2,1)S(1)}, u32[]{:S(2)}, u32[]{:S(2)}) collective-permute-start(bf16[2,128,128]{2,1,0:T(8,128)(2,1)S(1)} %bitcast.25), channel_id=1, source_target_pairs={{0,4},{4,8},{8,12},{12,16},{16,20},{20,24},{24,28},{28,32},{32,36}... | collective-permute-start | bytes 196616 | tf_op jit(solution)/shard_map/ppermute | solution.py:292
  126.9 5.3 %collective-permute-done.8.refs_8_.rest_0_ = bf16[2,128,128]{2,1,0:T(8,128)(2,1)S(1)} collective-permute-done((bf16[2,128,128]{2,1,0:T(8,128)(2,1)S(1)}, bf16[2,128,128]{2,1,0:T(8,128)(2,1)S(1)}, u32[]{:S(2)}, u32[]{:S(2)}) %collective-permute-start.8) | collective-permute-done | bytes 65568 | tf_op jit(solution)/shard_map/ppermute | solution.py:292
  132.2 3.6 %collective-permute-done.9.refs_10_.rest_1_ = bf16[2,128,128]{2,1,0:T(8,128)(2,1)S(1)} collective-permute-done((bf16[2,128,128]{2,1,0:T(8,128)(2,1)S(1)}, bf16[2,128,128]{2,1,0:T(8,128)(2,1)S(1)}, u32[]{:S(2)}, u32[]{:S(2)}) %collective-permute-start.9) | collective-permute-done | bytes 65568 | tf_op jit(solution)/shard_map/ppermute | solution.py:293
  135.8 3.2 %all-to-all-done.2.held_ref = bf16[64,32,128]{2,1,0:T(8,128)(2,1)S(1)} async-done(((bf16[64,32,128]{2,1,0:T(8,128)(2,1)}), bf16[64,32,128]{2,1,0:T(8,128)(2,1)S(1)}, u32[]{:S(2)}, u32[]{:S(2)}) %all-to-all-start.2) | async-done | bytes 524320 | tf_op jit(solution)/shard_map/all_to_all | solution.py:291
  143.2 6.3 %all-to-all-start.3 = ((bf16[64,32,256]{2,1,0:T(8,128)(2,1)}), bf16[64,32,256]{2,1,0:T(8,128)(2,1)}, u32[]{:S(2)}, u32[]{:S(2)}) async-start(bf16[64,32,256]{2,1,0:T(8,128)(2,1)} %bitcast.20), calls=%async_computation.3 | async-start | bytes 2097152 | tf_op jit(solution)/shard_map/all_to_all | solution.py:298
  149.5 6.5 %near_product.5.refs_4_ = f32[16,128,128]{2,1,0:T(8,128)S(1)} custom-call(s32[16,16]{1,0:T(8,128)S(1)} %add_clamp_fusion.index_ref, s32[16]{0:T(128)S(1)} %copy-done.15, bf16[16,8,32,128]{3,2,1,0:T(8,128)(2,1)S(1)} %copy-done.1, bf16[16,8,32,128]{3,2,1,0:T(8,128)(2,1)} %pad_maximum_fusion.refs_1_, bf16[16,8,32,128]{3,2,1,0:T(8,128)(2,1)S(1)} %copy-done.3, ...), custom_call_target="tpu_custom_call" | custom-call | flops 939524096 | bytes 8388608 | tf_op jit(solution)/shard_map/near_product/pallas_call | solution.py:143
  157.1 20.9 %all-to-all-done.3 = bf16[64,32,256]{2,1,0:T(8,128)(2,1)} async-done(((bf16[64,32,256]{2,1,0:T(8,128)(2,1)}), bf16[64,32,256]{2,1,0:T(8,128)(2,1)}, u32[]{:S(2)}, u32[]{:S(2)}) %all-to-all-start.3) | async-done | bytes 1048608 | tf_op jit(solution)/shard_map/all_to_all | solution.py:298
  179.0 5.6 %add_far.3 = bf16[2048,128]{1,0:T(8,128)(2,1)} custom-call(s32[4]{0:T(128)S(1)} %pad_add_fusion.offset_ref, s32[16]{0:T(128)S(1)} %copy-done.15, bf16[16,8,32,128]{3,2,1,0:T(8,128)(2,1)} %copy-done, bf16[16,8,32,128]{3,2,1,0:T(8,128)(2,1)} %copy-done.2, bf16[16,8,32,128]{3,2,1,0:T(8,128)(2,1)} %copy-done.4, ...), custom_call_target="tpu_custom_call" | custom-call | flops 134217728 | bytes 4194304 | tf_op jit(solution)/shard_map/add_far/pallas_call | solution.py:237
  (69 shorter events, 21.7 us)
Async XLA Ops:
  4.0 33.6 %all-to-all-start = ((bf16[64,40,128]{2,1,0:T(8,128)(2,1)}), bf16[64,40,128]{2,1,0:T(8,128)(2,1)S(1)}, u32[]{:S(2)}, u32[]{:S(2)}) async-start(bf16[64,40,128]{2,1,0:T(8,128)(2,1)} %split_blocks.1), calls=%async_computation | async-start | bytes 1310720 | tf_op jit(solution)/shard_map/all_to_all | solution.py:291
  17.9 13.0 %collective-permute-start.6 = (bf16[2,128,128]{2,1,0:T(8,128)(2,1)S(1)}, bf16[2,128,128]{2,1,0:T(8,128)(2,1)S(1)}, u32[]{:S(2)}, u32[]{:S(2)}) collective-permute-start(bf16[2,128,128]{2,1,0:T(8,128)(2,1)S(1)} %bitcast.23), channel_id=1, source_target_pairs={{0,4},{4,8},{8,12},{12,16},{16,20},{20,24},{24,28},{28,32},{32,36}... | collective-permute-start | bytes 196616 | tf_op jit(solution)/shard_map/ppermute | solution.py:292
  21.5 12.9 %collective-permute-start.7 = (bf16[2,128,128]{2,1,0:T(8,128)(2,1)S(1)}, bf16[2,128,128]{2,1,0:T(8,128)(2,1)S(1)}, u32[]{:S(2)}, u32[]{:S(2)}) collective-permute-start(bf16[2,128,128]{2,1,0:T(8,128)(2,1)S(1)} %bitcast.22), channel_id=1, source_target_pairs={{4,0},{8,4},{12,8},{16,12},{20,16},{24,20},{28,24},{32,28},{36,32}... | collective-permute-start | bytes 196616 | tf_op jit(solution)/shard_map/ppermute | solution.py:293
  24.9 50.4 %copy-start = (bf16[16,8,32,128]{3,2,1,0:T(8,128)(2,1)}, bf16[16,8,32,128]{3,2,1,0:T(8,128)(2,1)S(1)}, u32[]{:S(2)}) copy-start(bf16[16,8,32,128]{3,2,1,0:T(8,128)(2,1)S(1)} %slice.36.refs_0_) | copy-start | bytes 3145732
  24.9 24.9 %collective-permute-start = (bf16[16,8,32,128]{3,2,1,0:T(8,128)(2,1)S(1)}, bf16[16,8,32,128]{3,2,1,0:T(8,128)(2,1)S(1)}, u32[]{:S(2)}, u32[]{:S(2)}) collective-permute-start(bf16[16,8,32,128]{3,2,1,0:T(8,128)(2,1)S(1)} %slice.36.refs_0_), channel_id=1, source_target_pairs={{0,1},{1,2},{2,3},{3,0},{4,5},{5,6},{6,7},{7,4},{8,9},{9,10},{10,1... | collective-permute-start | bytes 3145736 | tf_op jit(solution)/shard_map/ppermute | solution.py:261
  27.3 25.5 %collective-permute-start.4 = (bf16[16,8,32,128]{3,2,1,0:T(8,128)(2,1)}, bf16[16,8,32,128]{3,2,1,0:T(8,128)(2,1)}, u32[]{:S(2)}, u32[]{:S(2)}) collective-permute-start(bf16[16,8,32,128]{3,2,1,0:T(8,128)(2,1)} %pad_maximum_fusion.refs_1_), channel_id=1, source_target_pairs={{1,0},{2,1},{3,2},{0,3},{5,4},{6,5},{7,6},{4,7},{9,8},{10,9},{11,1... | collective-permute-start | bytes 3145736 | tf_op jit(solution)/shard_map/ppermute | solution.py:262
  40.1 14.4 %copy-start.20 = (s32[16,16]{1,0:T(8,128)S(1)}, s32[16,16]{1,0:T(8,128)}, u32[]{:S(2)}) copy-start(s32[16,16]{1,0:T(8,128)} %param.5) | copy-start | bytes 3076
  40.1 35.2 %copy-start.15 = (s32[16]{0:T(128)S(1)}, s32[16]{0:T(128)}, u32[]{:S(2)}) copy-start(s32[16]{0:T(128)} %count_ref.9) | copy-start | bytes 196
  40.1 63.4 %all-to-all-start.1 = ((bf16[64,32,256]{2,1,0:T(8,128)(2,1)}), bf16[64,32,256]{2,1,0:T(8,128)(2,1)}, u32[]{:S(2)}, u32[]{:S(2)}) async-start(bf16[64,32,256]{2,1,0:T(8,128)(2,1)} %bitcast.9), calls=%async_computation.1 | async-start | bytes 2097152 | tf_op jit(solution)/shard_map/all_to_all | solution.py:298
  46.9 28.4 %collective-permute-start.1 = (bf16[16,8,32,128]{3,2,1,0:T(8,128)(2,1)S(1)}, bf16[16,8,32,128]{3,2,1,0:T(8,128)(2,1)S(1)}, u32[]{:S(2)}, u32[]{:S(2)}) collective-permute-start(bf16[16,8,32,128]{3,2,1,0:T(8,128)(2,1)S(1)} %slice.36.refs_0_), channel_id=1, source_target_pairs={{1,0},{2,1},{3,2},{0,3},{5,4},{6,5},{7,6},{4,7},{9,8},{10,9},{11,1... | collective-permute-start | bytes 3145736 | tf_op jit(solution)/shard_map/ppermute | solution.py:264
  49.7 25.6 %collective-permute-start.3 = (bf16[16,8,32,128]{3,2,1,0:T(8,128)(2,1)}, bf16[16,8,32,128]{3,2,1,0:T(8,128)(2,1)}, u32[]{:S(2)}, u32[]{:S(2)}) collective-permute-start(bf16[16,8,32,128]{3,2,1,0:T(8,128)(2,1)} %pad_maximum_fusion.refs_1_), channel_id=1, source_target_pairs={{0,1},{1,2},{2,3},{3,0},{4,5},{5,6},{6,7},{7,4},{8,9},{9,10},{10,1... | collective-permute-start | bytes 3145736 | tf_op jit(solution)/shard_map/ppermute | solution.py:263
  49.8 31.5 %copy-start.2 = (bf16[16,8,32,128]{3,2,1,0:T(8,128)(2,1)}, bf16[16,8,32,128]{3,2,1,0:T(8,128)(2,1)S(1)}, u32[]{:S(2)}) copy-start(bf16[16,8,32,128]{3,2,1,0:T(8,128)(2,1)S(1)} %collective-permute-done.refs_2_.refs_1_) | copy-start | bytes 3145732
  49.8 47.8 %collective-permute-start.2 = (bf16[16,8,32,128]{3,2,1,0:T(8,128)(2,1)S(1)}, bf16[16,8,32,128]{3,2,1,0:T(8,128)(2,1)}, u32[]{:S(2)}, u32[]{:S(2)}) collective-permute-start(bf16[16,8,32,128]{3,2,1,0:T(8,128)(2,1)S(1)} %collective-permute-done.refs_2_.refs_1_), channel_id=1, source_target_pairs={{0,1},{1,2},{2,3},{3,0},{4,5},{5,6},{6,7},{7,4},{8,9},{9,10},{10,1... | collective-permute-start | bytes 3145736 | tf_op jit(solution)/shard_map/ppermute | solution.py:265
  52.8 44.7 %collective-permute-start.5 = (bf16[16,8,32,128]{3,2,1,0:T(8,128)(2,1)}, bf16[16,8,32,128]{3,2,1,0:T(8,128)(2,1)}, u32[]{:S(2)}, u32[]{:S(2)}) collective-permute-start(bf16[16,8,32,128]{3,2,1,0:T(8,128)(2,1)} %collective-permute-done.4.refs_5_), channel_id=1, source_target_pairs={{1,0},{2,1},{3,2},{0,3},{5,4},{6,5},{7,6},{4,7},{9,8},{10,9},{11,1... | collective-permute-start | bytes 3145736 | tf_op jit(solution)/shard_map/ppermute | solution.py:266
  82.2 21.3 %copy-start.6 = (bf16[2048,128]{1,0:T(8,128)(2,1)S(1)}, bf16[2048,128]{1,0:T(8,128)(2,1)}, u32[]{:S(2)}) copy-start(bf16[2048,128]{1,0:T(8,128)(2,1)} %refs_6_.1) | copy-start | bytes 1572868
  109.7 29.3 %copy-start.12 = (bf16[2048,128]{1,0:T(8,128)(2,1)}, bf16[2048,128]{1,0:T(8,128)(2,1)S(1)}, u32[]{:S(2)}) copy-start(bf16[2048,128]{1,0:T(8,128)(2,1)S(1)} %get-tuple-element.10) | copy-start | bytes 1572868
  109.7 29.3 %all-to-all-start.2 = ((bf16[64,32,128]{2,1,0:T(8,128)(2,1)}), bf16[64,32,128]{2,1,0:T(8,128)(2,1)S(1)}, u32[]{:S(2)}, u32[]{:S(2)}) async-start(bf16[64,32,128]{2,1,0:T(8,128)(2,1)} %get-tuple-element.11), calls=%async_computation.2 | async-start | bytes 1048576 | tf_op jit(solution)/shard_map/all_to_all | solution.py:291
  121.4 10.7 %collective-permute-start.8 = (bf16[2,128,128]{2,1,0:T(8,128)(2,1)S(1)}, bf16[2,128,128]{2,1,0:T(8,128)(2,1)S(1)}, u32[]{:S(2)}, u32[]{:S(2)}) collective-permute-start(bf16[2,128,128]{2,1,0:T(8,128)(2,1)S(1)} %bitcast.25), channel_id=1, source_target_pairs={{0,4},{4,8},{8,12},{12,16},{16,20},{20,24},{24,28},{28,32},{32,36}... | collective-permute-start | bytes 196616 | tf_op jit(solution)/shard_map/ppermute | solution.py:292
  125.0 10.8 %collective-permute-start.9 = (bf16[2,128,128]{2,1,0:T(8,128)(2,1)S(1)}, bf16[2,128,128]{2,1,0:T(8,128)(2,1)S(1)}, u32[]{:S(2)}, u32[]{:S(2)}) collective-permute-start(bf16[2,128,128]{2,1,0:T(8,128)(2,1)S(1)} %bitcast.24), channel_id=1, source_target_pairs={{4,0},{8,4},{12,8},{16,12},{20,16},{24,20},{28,24},{32,28},{36,32}... | collective-permute-start | bytes 196616 | tf_op jit(solution)/shard_map/ppermute | solution.py:293
  132.2 7.6 %copy-start.18 = (bf16[2,128,128]{2,1,0:T(8,128)(2,1)}, bf16[2,128,128]{2,1,0:T(8,128)(2,1)S(1)}, u32[]{:S(2)}) copy-start(bf16[2,128,128]{2,1,0:T(8,128)(2,1)S(1)} %collective-permute-done.8.refs_8_.rest_0_) | copy-start | bytes 196612
  140.9 8.6 %copy-start.1 = (bf16[16,8,32,128]{3,2,1,0:T(8,128)(2,1)S(1)}, bf16[16,8,32,128]{3,2,1,0:T(8,128)(2,1)}, u32[]{:S(2)}) copy-start(bf16[16,8,32,128]{3,2,1,0:T(8,128)(2,1)} %copy-done) | copy-start | bytes 3145732
  140.9 8.6 %copy-start.3 = (bf16[16,8,32,128]{3,2,1,0:T(8,128)(2,1)S(1)}, bf16[16,8,32,128]{3,2,1,0:T(8,128)(2,1)}, u32[]{:S(2)}) copy-start(bf16[16,8,32,128]{3,2,1,0:T(8,128)(2,1)} %copy-done.2) | copy-start | bytes 3145732
  140.9 8.6 %copy-start.5 = (bf16[16,8,32,128]{3,2,1,0:T(8,128)(2,1)S(1)}, bf16[16,8,32,128]{3,2,1,0:T(8,128)(2,1)}, u32[]{:S(2)}) copy-start(bf16[16,8,32,128]{3,2,1,0:T(8,128)(2,1)} %copy-done.4) | copy-start | bytes 3145732
  143.2 34.8 %all-to-all-start.3 = ((bf16[64,32,256]{2,1,0:T(8,128)(2,1)}), bf16[64,32,256]{2,1,0:T(8,128)(2,1)}, u32[]{:S(2)}, u32[]{:S(2)}) async-start(bf16[64,32,256]{2,1,0:T(8,128)(2,1)} %bitcast.20), calls=%async_computation.3 | async-start | bytes 2097152 | tf_op jit(solution)/shard_map/all_to_all | solution.py:298
  (13 other events, 36.1 us)

commit v8 on v7

--- a/solution.py
+++ b/solution.py
@@ -9,8 +9,6 @@
 ITERS = 2
 BASE = 256
 FAR = (1, 2)
-LOW = tuple(range(1, 9))
-HIGH = tuple(range(9, 16)) + (0,)
 VMEM = pl.BlockSpec(memory_space=pltpu.VMEM)
 HBM = pl.BlockSpec(memory_space=pltpu.HBM)
 LIMIT = 12 << 20
@@ -101,15 +99,17 @@
 
 def near_product(near_index, counts, quarters, low, own, high):
     blocks, _, rows, size = quarters[0][0].shape
+    slots = near_index.shape[1]
     cols = own.shape[2]
     group = 4
     number = len(quarters)
-    near = [(half, place, t) for half, names in enumerate((LOW, HIGH)) for place, t in enumerate(names)]
-    near = [entry for entry in near if entry[2] not in FAR]
+    near = [t for t in range(slots) if t not in FAR]
+    flat = [part for quarter in quarters for part in quarter]
 
     def kernel(index_ref, count_ref, *refs):
-        tiles = [refs[2 * n : 2 * n + 2] for n in range(number)]
-        low_ref, own_ref, high_ref, out_ref, panels, sems = refs[2 * number :]
+        parts = iter(refs)
+        tiles = [[next(parts) for _ in quarter] for quarter in quarters]
+        low_ref, own_ref, high_ref, out_ref, panels, sems = parts
         step = pl.program_id(0)
 
         @pl.when(step == 0)
@@ -129,8 +129,11 @@
             total = jnp.zeros((number * rows, cols), jnp.float32)
             for first in range(0, len(near), 2):
                 left, right = [], []
-                for half, place, t in near[first : first + 2]:
-                    tile = jnp.concatenate([pair[half][r, place] for pair in tiles], axis=0)
+                for t in near[first : first + 2]:
+                    tile = jnp.concatenate(
+                        [quarter[t * len(quarter) // slots][r, t % (slots // len(quarter))] for quarter in tiles],
+                        axis=0,
+                    )
                     left.append(jnp.where(t < count_ref[b], tile, jnp.zeros_like(tile)))
                     right.append(panels[index_ref[b, t]])
                 total += jnp.dot(
@@ -147,9 +150,7 @@
             num_scalar_prefetch=2,
             grid=(blocks // group,),
             in_specs=[
-                pl.BlockSpec((group, half.shape[1], rows, size), lambda i, *_: (i, 0, 0, 0))
-                for pair in quarters
-                for half in pair
+                pl.BlockSpec((group,) + part.shape[1:], lambda i, *_: (i, 0, 0, 0)) for part in flat
             ]
             + [HBM] * 3,
             out_specs=pl.BlockSpec((group, number * rows, cols), lambda i, *_: (i, 0, 0)),
@@ -165,7 +166,7 @@
             transcendentals=0,
         ),
         name="near_product",
-    )(near_index, counts, *[half for pair in quarters for half in pair], *in_hbm([low, own, high]))
+    )(near_index, counts, *flat, *in_hbm([low, own, high]))
 
 
 def add_far(offsets, counts, far_tiles, arrived, partials, queries, owners, split):
@@ -183,7 +184,7 @@
         else:
             upper, lower, tiles, sums, sems = rest
         copies = [
-            pltpu.make_async_copy(ref.at[:, : len(FAR)], tiles.at[n], sems.at[0, n])
+            pltpu.make_async_copy(ref.at[:, FAR[0] : FAR[-1] + 1], tiles.at[n], sems.at[0, n])
             for n, ref in enumerate(tile_refs)
         ]
         first = 0
@@ -249,22 +250,18 @@
             flops=4 * blocks * size * size * cols, bytes_accessed=4 << 20, transcendentals=0
         ),
         name="add_far",
-    )(offsets, counts, *in_hbm(far_tiles), *in_hbm(partials), arrived, queries)
+    )(offsets, counts, *in_hbm(far_tiles), *in_hbm(partials), arrived, *in_hbm([queries]))
 
 
 def gather_rows(tiles):
     count = lax.axis_size("pb")
     up = [(i, (i + 1) % count) for i in range(count)]
     down = [((i + 1) % count, i) for i in range(count)]
-    low = tiles[:, LOW[0] : LOW[-1] + 1]
-    high = jnp.concatenate([tiles[:, HIGH[0] :], tiles[:, :1]], axis=1)
-    before_low = lax.ppermute(low, "pb", up)
-    after_high = lax.ppermute(high, "pb", down)
-    before_high = lax.ppermute(high, "pb", up)
-    after_low = lax.ppermute(low, "pb", down)
-    far_low = lax.ppermute(before_low, "pb", up)
-    far_high = lax.ppermute(after_high, "pb", down)
-    return [(low, high), (before_low, before_high), (after_low, after_high), (far_low, far_high)]
+    half = tiles.shape[1] // 2
+    before = lax.ppermute(tiles, "pb", up)
+    after = lax.ppermute(tiles, "pb", down)
+    across = (lax.ppermute(before[:, :half], "pb", up), lax.ppermute(after[:, half:], "pb", down))
+    return [(tiles,), (before,), (after,), across]
 
 
 def on_device(affinity_tiles, block_ids, valid_counts, queries):

time: 186 us -> 185 us (level)
  local copies, waits for them, and re-layouts: 10.1 us -> 14.5 us
  waiting for transfers between devices: 80.5 us -> 77 us
    ppermute x6 -> x4, waiting for transfers between devices: 38.8 us -> 34.1 us  [the longest x1 17.8 us: gather_rows(): after = lax.ppermute(tiles, 'pb', down)]
    ppermute x2, waiting for transfers between devices: 7.17 us -> 9.51 us  [on_device(): low = lax.ppermute(own[blocks - EDGE:], 'db', up)]
    unnamed x42 -> x38, local copies, waits for them, and re-layouts: 6.48 us -> 8.75 us
    slice x5 -> x2, local copies, waits for them, and re-layouts: 1.34 us -> 3.46 us  [the longest x1 2.32 us: gather_rows(): before[:, :half]]
    ppermute x6 -> x4, starting transfers between devices: 7.94 us -> 6.23 us  [the longest x1 3.41 us: gather_rows(): lax.ppermute(after[:, half:], 'pb', down)]
  transfers between devices with their start and end apart: 14 -> 12, of which waited for: 11 -> 10; matrix products, arithmetic and copies ran while one was open for 2% -> 2% of each run, Pallas kernels for 11% -> 11%
where the time goes in v8:
time: 185 us; the launch traced here: 183 us
  waiting for transfers between devices  77 us (42%)
  starting transfers between devices  56 us (30%)
  Pallas kernels  35.3 us (19%)
  local copies, waits for them, and re-layouts  14.5 us (8%)
    all_to_all x2, starting transfers between devices, on_device(): held = lax.all_to_all(pieces, 'db', split_axis=0, concat_axis=0, tiled=True)  25.4 us
    all_to_all x2, waiting for transfers between devices, on_device(): lax.all_to_all(chosen.reshape(owners, slots, -1), 'db', split_axis=0, con...  19.8 us
    ppermute x1, waiting for transfers between devices, gather_rows(): after = lax.ppermute(tiles, 'pb', down)  17.8 us
    pallas_call x3, Pallas kernels, near_product(): pl.pallas_call(kernel, out_shape=jax.ShapeDtypeStruct((blocks, number * r...  16.8 us
    all_to_all x2, starting transfers between devices, on_device(): lax.all_to_all(chosen.reshape(owners, slots, -1), 'db', split_axis=0, con...  13 us
    pallas_call x2, Pallas kernels, add_far(): pl.pallas_call(kernel, out_shape=out_shape, grid_spec=pltpu.PrefetchScala...  12.1 us
    ppermute x1, waiting for transfers between devices, gather_rows(): lax.ppermute(after[:, half:], 'pb', down)  10.9 us
    ppermute x2, waiting for transfers between devices, on_device(): low = lax.ppermute(own[blocks - EDGE:], 'db', up)  9.51 us
  transfers between devices with their start and end apart: 12, of which 10 were waited for; matrix products, arithmetic and copies ran while one was open for 2% of the time, Pallas kernels for 11%

profile of v8, /device:TPU:1, one launch (start us, length us, event | category | flops | bytes accessed | tf_op | source)
XLA Modules:
  0.0 183.4 jit_solution(12204807621163621492)
XLA Ops:
  1.5 2.6 %split_blocks.1 = bf16[64,40,128]{2,1,0:T(8,128)(2,1)} custom-call(bf16[2048,128]{1,0:T(8,128)(2,1)} %refs_6_.1, f32[1,128]{1,0:T(1,128)} %pad.4.digits_ref), custom_call_target="tpu_custom_call" | custom-call | tf_op jit(solution)/shard_map/split_blocks/pallas_call | solution.py:38
  4.0 13.0 %all-to-all-start = ((bf16[64,40,128]{2,1,0:T(8,128)(2,1)}), bf16[64,40,128]{2,1,0:T(8,128)(2,1)S(1)}, u32[]{:S(2)}, u32[]{:S(2)}) async-start(bf16[64,40,128]{2,1,0:T(8,128)(2,1)} %split_blocks.1), calls=%async_computation | async-start | bytes 1310720 | tf_op jit(solution)/shard_map/all_to_all | solution.py:288
  17.0 2.8 %collective-permute-start.1 = (bf16[16,16,32,128]{3,2,1,0:T(8,128)(2,1)}, bf16[16,16,32,128]{3,2,1,0:T(8,128)(2,1)S(1)}, u32[]{:S(2)}, u32[]{:S(2)}) collective-permute-start(bf16[16,16,32,128]{3,2,1,0:T(8,128)(2,1)} %refs_0_.7), channel_id=1, source_target_pairs={{1,0},{2,1},{3,2},{0,3},{5,4},{6,5},{7,6},{4,7},{9,8},{10,9},{11,1... | collective-permute-start | bytes 6291464 | tf_op jit(solution)/shard_map/ppermute | solution.py:262
  20.7 3.8 %collective-permute-start.4 = (bf16[2,128,128]{2,1,0:T(8,128)(2,1)S(1)}, bf16[2,128,128]{2,1,0:T(8,128)(2,1)S(1)}, u32[]{:S(2)}, u32[]{:S(2)}) collective-permute-start(bf16[2,128,128]{2,1,0:T(8,128)(2,1)S(1)} %bitcast.24), channel_id=1, source_target_pairs={{0,4},{4,8},{8,12},{12,16},{16,20},{20,24},{24,28},{28,32},{32,36}... | collective-permute-start | bytes 196616 | tf_op jit(solution)/shard_map/ppermute | solution.py:289
  26.5 4.4 %collective-permute-done.4.refs_3_.refs_2_.rest_0_ = bf16[2,128,128]{2,1,0:T(8,128)(2,1)S(1)} collective-permute-done((bf16[2,128,128]{2,1,0:T(8,128)(2,1)S(1)}, bf16[2,128,128]{2,1,0:T(8,128)(2,1)S(1)}, u32[]{:S(2)}, u32[]{:S(2)}) %collective-permute-start.4) | collective-permute-done | bytes 65568 | tf_op jit(solution)/shard_map/ppermute | solution.py:289
  30.9 3.4 %collective-permute-done.5.refs_5_.refs_4_.rest_1_ = bf16[2,128,128]{2,1,0:T(8,128)(2,1)S(1)} collective-permute-done((bf16[2,128,128]{2,1,0:T(8,128)(2,1)S(1)}, bf16[2,128,128]{2,1,0:T(8,128)(2,1)S(1)}, u32[]{:S(2)}, u32[]{:S(2)}) %collective-permute-start.5) | collective-permute-done | bytes 65568 | tf_op jit(solution)/shard_map/ppermute | solution.py:290
  34.4 3.3 %all-to-all-done.held_ref = bf16[64,40,128]{2,1,0:T(8,128)(2,1)S(1)} async-done(((bf16[64,40,128]{2,1,0:T(8,128)(2,1)}), bf16[64,40,128]{2,1,0:T(8,128)(2,1)S(1)}, u32[]{:S(2)}, u32[]{:S(2)}) %all-to-all-start) | async-done | bytes 655392 | tf_op jit(solution)/shard_map/all_to_all | solution.py:288
  40.2 6.7 %all-to-all-start.1 = ((bf16[64,32,256]{2,1,0:T(8,128)(2,1)}), bf16[64,32,256]{2,1,0:T(8,128)(2,1)}, u32[]{:S(2)}, u32[]{:S(2)}) async-start(bf16[64,32,256]{2,1,0:T(8,128)(2,1)} %bitcast.9), calls=%async_computation.1 | async-start | bytes 2097152 | tf_op jit(solution)/shard_map/all_to_all | solution.py:295
  46.9 17.8 %collective-permute-done.1.refs_2_ = bf16[16,16,32,128]{3,2,1,0:T(8,128)(2,1)S(1)} collective-permute-done((bf16[16,16,32,128]{3,2,1,0:T(8,128)(2,1)}, bf16[16,16,32,128]{3,2,1,0:T(8,128)(2,1)S(1)}, u32[]{:S(2)}, u32[]{:S(2)}) %collective-permute-start.1) | collective-permute-done | bytes 2097184 | tf_op jit(solution)/shard_map/ppermute | solution.py:262
  65.9 3.4 %collective-permute-start.3 = (bf16[16,8,32,128]{3,2,1,0:T(8,128)(2,1)}, bf16[16,8,32,128]{3,2,1,0:T(8,128)(2,1)}, u32[]{:S(2)}, u32[]{:S(2)}) collective-permute-start(bf16[16,8,32,128]{3,2,1,0:T(8,128)(2,1)} %slice.45), channel_id=1, source_target_pairs={{1,0},{2,1},{3,2},{0,3},{5,4},{6,5},{7,6},{4,7},{9,8},{10,9},{11,1... | collective-permute-start | bytes 3145736 | tf_op jit(solution)/shard_map/ppermute | solution.py:263
  73.3 5.7 %near_product.3.refs_4_ = f32[16,96,128]{2,1,0:T(8,128)S(1)} custom-call(s32[16,16]{1,0:T(8,128)S(1)} %add_clamp_fusion.index_ref, s32[16]{0:T(128)S(1)} %copy-done.13, bf16[16,16,32,128]{3,2,1,0:T(8,128)(2,1)S(1)} %copy-done.2, bf16[16,16,32,128]{3,2,1,0:T(8,128)(2,1)} %collective-permute-done.refs_1_, ...), custom_call_target="tpu_custom_call" | custom-call | flops 704643072 | bytes 6291456 | tf_op jit(solution)/shard_map/near_product/pallas_call | solution.py:146
  79.9 10.9 %collective-permute-done.3.refs_1_.refs_4_ = bf16[16,8,32,128]{3,2,1,0:T(8,128)(2,1)} collective-permute-done((bf16[16,8,32,128]{3,2,1,0:T(8,128)(2,1)}, bf16[16,8,32,128]{3,2,1,0:T(8,128)(2,1)}, u32[]{:S(2)}, u32[]{:S(2)}) %collective-permute-start.3) | collective-permute-done | bytes 1048608 | tf_op jit(solution)/shard_map/ppermute | solution.py:263
  90.8 5.4 %collective-permute-done.2.refs_0_.refs_3_ = bf16[16,8,32,128]{3,2,1,0:T(8,128)(2,1)S(1)} collective-permute-done((bf16[16,8,32,128]{3,2,1,0:T(8,128)(2,1)}, bf16[16,8,32,128]{3,2,1,0:T(8,128)(2,1)S(1)}, u32[]{:S(2)}, u32[]{:S(2)}) %collective-permute-start.2) | collective-permute-done | bytes 1048608 | tf_op jit(solution)/shard_map/ppermute | solution.py:263
  96.2 5.0 %near_product.4.refs_5_ = f32[16,32,128]{2,1,0:T(8,128)S(1)} custom-call(s32[16,16]{1,0:T(8,128)S(1)} %add_clamp_fusion.index_ref, s32[16]{0:T(128)S(1)} %copy-done.13, bf16[16,8,32,128]{3,2,1,0:T(8,128)(2,1)S(1)} %collective-permute-done.2.refs_0_.refs_3_, bf16[16,8,32,128]{3,2,1,0:T(8,128)(2,1)} %collective-permute-done.3.refs_1_.refs_4_, ...), custom_call_target="tpu_custom_call" | custom-call | flops 234881024 | bytes 2097152 | tf_op jit(solution)/shard_map/near_product/pallas_call | solution.py:146
  102.0 6.3 %add_far.2 = (bf16[2048,128]{1,0:T(8,128)(2,1)S(1)}, bf16[64,32,128]{2,1,0:T(8,128)(2,1)}) custom-call(s32[4]{0:T(128)S(1)} %pad_add_fusion.offset_ref, s32[16]{0:T(128)S(1)} %copy-done.13, bf16[16,16,32,128]{3,2,1,0:T(8,128)(2,1)} %refs_0_.7, bf16[16,16,32,128]{3,2,1,0:T(8,128)(2,1)} %collective-permute-done.refs_1_, bf16[16,16,32,128]{3,2,1,0:T(8,128)(2,1)} %copy-done, ...), custom_call_target="tpu_custom_call" | custom-call | flops 134217728 | bytes 4194304 | tf_op jit(solution)/shard_map/add_far/pallas_call | solution.py:238
  108.3 12.5 %all-to-all-start.2 = ((bf16[64,32,128]{2,1,0:T(8,128)(2,1)}), bf16[64,32,128]{2,1,0:T(8,128)(2,1)S(1)}, u32[]{:S(2)}, u32[]{:S(2)}) async-start(bf16[64,32,128]{2,1,0:T(8,128)(2,1)} %get-tuple-element.11), calls=%async_computation.2 | async-start | bytes 1048576 | tf_op jit(solution)/shard_map/all_to_all | solution.py:288
  120.8 3.7 %collective-permute-start.6 = (bf16[2,128,128]{2,1,0:T(8,128)(2,1)S(1)}, bf16[2,128,128]{2,1,0:T(8,128)(2,1)S(1)}, u32[]{:S(2)}, u32[]{:S(2)}) collective-permute-start(bf16[2,128,128]{2,1,0:T(8,128)(2,1)S(1)} %bitcast.25), channel_id=1, source_target_pairs={{0,4},{4,8},{8,12},{12,16},{16,20},{20,24},{24,28},{28,32},{32,36}... | collective-permute-start | bytes 196616 | tf_op jit(solution)/shard_map/ppermute | solution.py:289
  126.5 5.1 %collective-permute-done.6.refs_5_.rest_0_ = bf16[2,128,128]{2,1,0:T(8,128)(2,1)S(1)} collective-permute-done((bf16[2,128,128]{2,1,0:T(8,128)(2,1)S(1)}, bf16[2,128,128]{2,1,0:T(8,128)(2,1)S(1)}, u32[]{:S(2)}, u32[]{:S(2)}) %collective-permute-start.6) | collective-permute-done | bytes 65568 | tf_op jit(solution)/shard_map/ppermute | solution.py:289
  131.5 3.6 %collective-permute-done.7.refs_7_.rest_1_ = bf16[2,128,128]{2,1,0:T(8,128)(2,1)S(1)} collective-permute-done((bf16[2,128,128]{2,1,0:T(8,128)(2,1)S(1)}, bf16[2,128,128]{2,1,0:T(8,128)(2,1)S(1)}, u32[]{:S(2)}, u32[]{:S(2)}) %collective-permute-start.7) | collective-permute-done | bytes 65568 | tf_op jit(solution)/shard_map/ppermute | solution.py:290
  135.2 3.2 %all-to-all-done.2.held_ref = bf16[64,32,128]{2,1,0:T(8,128)(2,1)S(1)} async-done(((bf16[64,32,128]{2,1,0:T(8,128)(2,1)}), bf16[64,32,128]{2,1,0:T(8,128)(2,1)S(1)}, u32[]{:S(2)}, u32[]{:S(2)}) %all-to-all-start.2) | async-done | bytes 524320 | tf_op jit(solution)/shard_map/all_to_all | solution.py:288
  142.6 6.3 %all-to-all-start.3 = ((bf16[64,32,256]{2,1,0:T(8,128)(2,1)}), bf16[64,32,256]{2,1,0:T(8,128)(2,1)}, u32[]{:S(2)}, u32[]{:S(2)}) async-start(bf16[64,32,256]{2,1,0:T(8,128)(2,1)} %bitcast.18), calls=%async_computation.3 | async-start | bytes 2097152 | tf_op jit(solution)/shard_map/all_to_all | solution.py:295
  150.6 6.1 %near_product.5.refs_4_ = f32[16,128,128]{2,1,0:T(8,128)S(1)} custom-call(s32[16,16]{1,0:T(8,128)S(1)} %add_clamp_fusion.index_ref, s32[16]{0:T(128)S(1)} %copy-done.13, bf16[16,16,32,128]{3,2,1,0:T(8,128)(2,1)S(1)} %copy-done.3, bf16[16,16,32,128]{3,2,1,0:T(8,128)(2,1)} %collective-permute-done.refs_1_, bf16[16,16,32,128]{3,2,1,0:T(8,128)(2,1)S(1)} %copy-done.1, ...), custom_call_target="tpu_custom_call" | custom-call | flops 939524096 | bytes 8388608 | tf_op jit(solution)/shard_map/near_product/pallas_call | solution.py:146
  157.7 19.8 %all-to-all-done.3 = bf16[64,32,256]{2,1,0:T(8,128)(2,1)} async-done(((bf16[64,32,256]{2,1,0:T(8,128)(2,1)}), bf16[64,32,256]{2,1,0:T(8,128)(2,1)}, u32[]{:S(2)}, u32[]{:S(2)}) %all-to-all-start.3) | async-done | bytes 1048608 | tf_op jit(solution)/shard_map/all_to_all | solution.py:295
  177.5 5.8 %add_far.3 = bf16[2048,128]{1,0:T(8,128)(2,1)} custom-call(s32[4]{0:T(128)S(1)} %pad_add_fusion.offset_ref, s32[16]{0:T(128)S(1)} %copy-done.13, bf16[16,16,32,128]{3,2,1,0:T(8,128)(2,1)} %refs_0_.7, bf16[16,16,32,128]{3,2,1,0:T(8,128)(2,1)} %collective-permute-done.refs_1_, bf16[16,16,32,128]{3,2,1,0:T(8,128)(2,1)} %copy-done, ...), custom_call_target="tpu_custom_call" | custom-call | flops 134217728 | bytes 4194304 | tf_op jit(solution)/shard_map/add_far/pallas_call | solution.py:238
  (57 shorter events, 22.4 us)
Async XLA Ops:
  4.0 33.6 %all-to-all-start = ((bf16[64,40,128]{2,1,0:T(8,128)(2,1)}), bf16[64,40,128]{2,1,0:T(8,128)(2,1)S(1)}, u32[]{:S(2)}, u32[]{:S(2)}) async-start(bf16[64,40,128]{2,1,0:T(8,128)(2,1)} %split_blocks.1), calls=%async_computation | async-start | bytes 1310720 | tf_op jit(solution)/shard_map/all_to_all | solution.py:288
  17.0 47.7 %collective-permute-start.1 = (bf16[16,16,32,128]{3,2,1,0:T(8,128)(2,1)}, bf16[16,16,32,128]{3,2,1,0:T(8,128)(2,1)S(1)}, u32[]{:S(2)}, u32[]{:S(2)}) collective-permute-start(bf16[16,16,32,128]{3,2,1,0:T(8,128)(2,1)} %refs_0_.7), channel_id=1, source_target_pairs={{1,0},{2,1},{3,2},{0,3},{5,4},{6,5},{7,6},{4,7},{9,8},{10,9},{11,1... | collective-permute-start | bytes 6291464 | tf_op jit(solution)/shard_map/ppermute | solution.py:262
  19.8 49.4 %collective-permute-start = (bf16[16,16,32,128]{3,2,1,0:T(8,128)(2,1)}, bf16[16,16,32,128]{3,2,1,0:T(8,128)(2,1)}, u32[]{:S(2)}, u32[]{:S(2)}) collective-permute-start(bf16[16,16,32,128]{3,2,1,0:T(8,128)(2,1)} %refs_0_.7), channel_id=1, source_target_pairs={{0,1},{1,2},{2,3},{3,0},{4,5},{5,6},{6,7},{7,4},{8,9},{9,10},{10,1... | collective-permute-start | bytes 6291464 | tf_op jit(solution)/shard_map/ppermute | solution.py:261
  20.7 10.2 %collective-permute-start.4 = (bf16[2,128,128]{2,1,0:T(8,128)(2,1)S(1)}, bf16[2,128,128]{2,1,0:T(8,128)(2,1)S(1)}, u32[]{:S(2)}, u32[]{:S(2)}) collective-permute-start(bf16[2,128,128]{2,1,0:T(8,128)(2,1)S(1)} %bitcast.24), channel_id=1, source_target_pairs={{0,4},{4,8},{8,12},{12,16},{16,20},{20,24},{24,28},{28,32},{32,36}... | collective-permute-start | bytes 196616 | tf_op jit(solution)/shard_map/ppermute | solution.py:289
  24.6 9.8 %collective-permute-start.5 = (bf16[2,128,128]{2,1,0:T(8,128)(2,1)S(1)}, bf16[2,128,128]{2,1,0:T(8,128)(2,1)S(1)}, u32[]{:S(2)}, u32[]{:S(2)}) collective-permute-start(bf16[2,128,128]{2,1,0:T(8,128)(2,1)S(1)} %bitcast.22), channel_id=1, source_target_pairs={{4,0},{8,4},{12,8},{16,12},{20,16},{24,20},{28,24},{32,28},{36,32}... | collective-permute-start | bytes 196616 | tf_op jit(solution)/shard_map/ppermute | solution.py:290
  30.9 6.8 %copy-start.14 = (bf16[2,128,128]{2,1,0:T(8,128)(2,1)}, bf16[2,128,128]{2,1,0:T(8,128)(2,1)S(1)}, u32[]{:S(2)}) copy-start(bf16[2,128,128]{2,1,0:T(8,128)(2,1)S(1)} %collective-permute-done.4.refs_3_.refs_2_.rest_0_) | copy-start | bytes 196612
  34.4 3.3 %copy-start.15 = (bf16[2,128,128]{2,1,0:T(8,128)(2,1)}, bf16[2,128,128]{2,1,0:T(8,128)(2,1)S(1)}, u32[]{:S(2)}) copy-start(bf16[2,128,128]{2,1,0:T(8,128)(2,1)S(1)} %collective-permute-done.5.refs_5_.refs_4_.rest_1_) | copy-start | bytes 196612
  40.2 61.7 %all-to-all-start.1 = ((bf16[64,32,256]{2,1,0:T(8,128)(2,1)}), bf16[64,32,256]{2,1,0:T(8,128)(2,1)}, u32[]{:S(2)}, u32[]{:S(2)}) async-start(bf16[64,32,256]{2,1,0:T(8,128)(2,1)} %bitcast.9), calls=%async_computation.1 | async-start | bytes 2097152 | tf_op jit(solution)/shard_map/all_to_all | solution.py:295
  46.9 24.8 %copy-start.18 = (s32[16,16]{1,0:T(8,128)S(1)}, s32[16,16]{1,0:T(8,128)}, u32[]{:S(2)}) copy-start(s32[16,16]{1,0:T(8,128)} %param.5) | copy-start | bytes 3076
  46.9 24.8 %copy-start.13 = (s32[16]{0:T(128)S(1)}, s32[16]{0:T(128)}, u32[]{:S(2)}) copy-start(s32[16]{0:T(128)} %count_ref.9) | copy-start | bytes 196
  64.7 7.0 %copy-start = (bf16[16,16,32,128]{3,2,1,0:T(8,128)(2,1)}, bf16[16,16,32,128]{3,2,1,0:T(8,128)(2,1)S(1)}, u32[]{:S(2)}) copy-start(bf16[16,16,32,128]{3,2,1,0:T(8,128)(2,1)S(1)} %collective-permute-done.1.refs_2_) | copy-start | bytes 6291460
  65.9 25.0 %collective-permute-start.3 = (bf16[16,8,32,128]{3,2,1,0:T(8,128)(2,1)}, bf16[16,8,32,128]{3,2,1,0:T(8,128)(2,1)}, u32[]{:S(2)}, u32[]{:S(2)}) collective-permute-start(bf16[16,8,32,128]{3,2,1,0:T(8,128)(2,1)} %slice.45), channel_id=1, source_target_pairs={{1,0},{2,1},{3,2},{0,3},{5,4},{6,5},{7,6},{4,7},{9,8},{10,9},{11,1... | collective-permute-start | bytes 3145736 | tf_op jit(solution)/shard_map/ppermute | solution.py:263
  71.6 24.6 %collective-permute-start.2 = (bf16[16,8,32,128]{3,2,1,0:T(8,128)(2,1)}, bf16[16,8,32,128]{3,2,1,0:T(8,128)(2,1)S(1)}, u32[]{:S(2)}, u32[]{:S(2)}) collective-permute-start(bf16[16,8,32,128]{3,2,1,0:T(8,128)(2,1)} %slice.44), channel_id=1, source_target_pairs={{0,1},{1,2},{2,3},{3,0},{4,5},{5,6},{6,7},{7,4},{8,9},{9,10},{10,1... | collective-permute-start | bytes 3145736 | tf_op jit(solution)/shard_map/ppermute | solution.py:263
  96.2 5.8 %copy-start.4 = (bf16[16,8,32,128]{3,2,1,0:T(8,128)(2,1)}, bf16[16,8,32,128]{3,2,1,0:T(8,128)(2,1)S(1)}, u32[]{:S(2)}) copy-start(bf16[16,8,32,128]{3,2,1,0:T(8,128)(2,1)S(1)} %collective-permute-done.2.refs_0_.refs_3_) | copy-start | bytes 3145732
  108.3 30.1 %copy-start.10 = (bf16[2048,128]{1,0:T(8,128)(2,1)}, bf16[2048,128]{1,0:T(8,128)(2,1)S(1)}, u32[]{:S(2)}) copy-start(bf16[2048,128]{1,0:T(8,128)(2,1)S(1)} %get-tuple-element.10) | copy-start | bytes 1572868
  108.3 30.1 %all-to-all-start.2 = ((bf16[64,32,128]{2,1,0:T(8,128)(2,1)}), bf16[64,32,128]{2,1,0:T(8,128)(2,1)S(1)}, u32[]{:S(2)}, u32[]{:S(2)}) async-start(bf16[64,32,128]{2,1,0:T(8,128)(2,1)} %get-tuple-element.11), calls=%async_computation.2 | async-start | bytes 1048576 | tf_op jit(solution)/shard_map/all_to_all | solution.py:288
  120.8 10.7 %collective-permute-start.6 = (bf16[2,128,128]{2,1,0:T(8,128)(2,1)S(1)}, bf16[2,128,128]{2,1,0:T(8,128)(2,1)S(1)}, u32[]{:S(2)}, u32[]{:S(2)}) collective-permute-start(bf16[2,128,128]{2,1,0:T(8,128)(2,1)S(1)} %bitcast.25), channel_id=1, source_target_pairs={{0,4},{4,8},{8,12},{12,16},{16,20},{20,24},{24,28},{28,32},{32,36}... | collective-permute-start | bytes 196616 | tf_op jit(solution)/shard_map/ppermute | solution.py:289
  124.5 10.7 %collective-permute-start.7 = (bf16[2,128,128]{2,1,0:T(8,128)(2,1)S(1)}, bf16[2,128,128]{2,1,0:T(8,128)(2,1)S(1)}, u32[]{:S(2)}, u32[]{:S(2)}) collective-permute-start(bf16[2,128,128]{2,1,0:T(8,128)(2,1)S(1)} %bitcast.23), channel_id=1, source_target_pairs={{4,0},{8,4},{12,8},{16,12},{20,16},{24,20},{28,24},{32,28},{36,32}... | collective-permute-start | bytes 196616 | tf_op jit(solution)/shard_map/ppermute | solution.py:290
  131.5 7.6 %copy-start.16 = (bf16[2,128,128]{2,1,0:T(8,128)(2,1)}, bf16[2,128,128]{2,1,0:T(8,128)(2,1)S(1)}, u32[]{:S(2)}) copy-start(bf16[2,128,128]{2,1,0:T(8,128)(2,1)S(1)} %collective-permute-done.6.refs_5_.rest_0_) | copy-start | bytes 196612
  135.2 4.0 %copy-start.17 = (bf16[2,128,128]{2,1,0:T(8,128)(2,1)}, bf16[2,128,128]{2,1,0:T(8,128)(2,1)S(1)}, u32[]{:S(2)}) copy-start(bf16[2,128,128]{2,1,0:T(8,128)(2,1)S(1)} %collective-permute-done.7.refs_7_.rest_1_) | copy-start | bytes 196612
  140.2 8.8 %copy-start.1 = (bf16[16,16,32,128]{3,2,1,0:T(8,128)(2,1)S(1)}, bf16[16,16,32,128]{3,2,1,0:T(8,128)(2,1)}, u32[]{:S(2)}) copy-start(bf16[16,16,32,128]{3,2,1,0:T(8,128)(2,1)} %copy-done) | copy-start | bytes 6291460
  140.2 8.8 %copy-start.5 = (bf16[16,8,32,128]{3,2,1,0:T(8,128)(2,1)S(1)}, bf16[16,8,32,128]{3,2,1,0:T(8,128)(2,1)}, u32[]{:S(2)}) copy-start(bf16[16,8,32,128]{3,2,1,0:T(8,128)(2,1)} %copy-done.4) | copy-start | bytes 3145732
  142.6 34.8 %all-to-all-start.3 = ((bf16[64,32,256]{2,1,0:T(8,128)(2,1)}), bf16[64,32,256]{2,1,0:T(8,128)(2,1)}, u32[]{:S(2)}, u32[]{:S(2)}) async-start(bf16[64,32,256]{2,1,0:T(8,128)(2,1)} %bitcast.18), calls=%async_computation.3 | async-start | bytes 2097152 | tf_op jit(solution)/shard_map/all_to_all | solution.py:295
  149.0 1.6 copy-start.3
  (7 other events, 7.2 us)

commit v9 on v8

--- a/solution.py
+++ b/solution.py
@@ -97,10 +97,11 @@
     )(held, *in_hbm(after), *operands)
 
 
-def near_product(near_index, counts, quarters, low, own, high):
+def near_product(near_index, counts, quarters, reach):
     blocks, _, rows, size = quarters[0][0].shape
     slots = near_index.shape[1]
-    cols = own.shape[2]
+    cols = reach[0].shape[2]
+    dtype = reach[0].dtype
     group = 4
     number = len(quarters)
     near = [t for t in range(slots) if t not in FAR]
@@ -109,16 +110,16 @@
     def kernel(index_ref, count_ref, *refs):
         parts = iter(refs)
         tiles = [[next(parts) for _ in quarter] for quarter in quarters]
-        low_ref, own_ref, high_ref, out_ref, panels, sems = parts
+        *reach_refs, out_ref, panels, sems = parts
         step = pl.program_id(0)
 
         @pl.when(step == 0)
         def _():
-            copies = [
-                pltpu.make_async_copy(low_ref, panels.at[:EDGE], sems.at[0]),
-                pltpu.make_async_copy(own_ref, panels.at[EDGE : EDGE + blocks], sems.at[1]),
-                pltpu.make_async_copy(high_ref, panels.at[EDGE + blocks :], sems.at[2]),
-            ]
+            copies, first = [], 0
+            for n, (ref, array) in enumerate(zip(reach_refs, reach)):
+                target = panels.at[first : first + array.shape[0]]
+                copies.append(pltpu.make_async_copy(ref, target, sems.at[n]))
+                first += array.shape[0]
             for copy in copies:
                 copy.start()
             for copy in copies:
@@ -152,11 +153,11 @@
             in_specs=[
                 pl.BlockSpec((group,) + part.shape[1:], lambda i, *_: (i, 0, 0, 0)) for part in flat
             ]
-            + [HBM] * 3,
+            + [HBM] * len(reach),
             out_specs=pl.BlockSpec((group, number * rows, cols), lambda i, *_: (i, 0, 0)),
             scratch_shapes=[
-                pltpu.VMEM((blocks + 2 * EDGE, size, cols), own.dtype),
-                pltpu.SemaphoreType.DMA((3,)),
+                pltpu.VMEM((blocks + 2 * EDGE, size, cols), dtype),
+                pltpu.SemaphoreType.DMA((len(reach),)),
             ],
         ),
         compiler_params=pltpu.CompilerParams(vmem_limit_bytes=LIMIT),
@@ -166,7 +167,7 @@
             transcendentals=0,
         ),
         name="near_product",
-    )(near_index, counts, *flat, *in_hbm([low, own, high]))
+    )(near_index, counts, *flat, *in_hbm(reach))
 
 
 def add_far(offsets, counts, far_tiles, arrived, partials, queries, owners, split):
@@ -184,8 +185,10 @@
         else:
             upper, lower, tiles, sums, sems = rest
         copies = [
-            pltpu.make_async_copy(ref.at[:, FAR[0] : FAR[-1] + 1], tiles.at[n], sems.at[0, n])
-            for n, ref in enumerate(tile_refs)
+            pltpu.make_async_copy(
+                ref if part.shape[1] == len(FAR) else ref.at[:, FAR[0] : FAR[-1] + 1], tiles.at[n], sems.at[0, n]
+            )
+            for n, (ref, part) in enumerate(zip(tile_refs, far_tiles))
         ]
         first = 0
         for n, (ref, part) in enumerate(zip(partial_refs, partials)):
@@ -253,27 +256,22 @@
     )(offsets, counts, *in_hbm(far_tiles), *in_hbm(partials), arrived, *in_hbm([queries]))
 
 
-def gather_rows(tiles):
-    count = lax.axis_size("pb")
-    up = [(i, (i + 1) % count) for i in range(count)]
-    down = [((i + 1) % count, i) for i in range(count)]
-    half = tiles.shape[1] // 2
-    before = lax.ppermute(tiles, "pb", up)
-    after = lax.ppermute(tiles, "pb", down)
-    across = (lax.ppermute(before[:, :half], "pb", up), lax.ppermute(after[:, half:], "pb", down))
-    return [(tiles,), (before,), (after,), across]
-
-
 def on_device(affinity_tiles, block_ids, valid_counts, queries):
     blocks, slots = block_ids.shape
     rows, size = affinity_tiles.shape[2:]
     cols = queries.shape[1]
     owners = lax.axis_size("db")
     first_block = lax.axis_index("db") * blocks
-    quarters = gather_rows(affinity_tiles)
-    far_tiles = [pair[0] for pair in quarters]
+    count = lax.axis_size("pb")
+    forth = [(i, (i + 1) % count) for i in range(count)]
+    back = [((i + 1) % count, i) for i in range(count)]
+    opposite = [(i, (i + 2) % count) for i in range(count)]
+    before = lax.ppermute(affinity_tiles, "pb", forth)
+    after = lax.ppermute(affinity_tiles, "pb", back)
+    across_far = lax.ppermute(affinity_tiles[:, FAR[0] : FAR[-1] + 1], "pb", opposite)
+    far_tiles = [affinity_tiles, before, after, across_far]
     place = lax.axis_index("pb")
-    offsets = jnp.stack([(place + shift) % lax.axis_size("pb") * rows for shift in (0, -1, 1, 2)])
+    offsets = jnp.stack([(place + shift) % count * rows for shift in (0, -1, 1, 2)])
     near_index = jnp.clip(block_ids - first_block + EDGE, 0, blocks + 2 * EDGE - 1)
     far = block_ids[:, FAR[0] : FAR[-1] + 1].reshape(1, -1)
     slots = far.shape[1]
@@ -288,16 +286,21 @@
         held = lax.all_to_all(pieces, "db", split_axis=0, concat_axis=0, tiled=True)
         low = lax.ppermute(own[blocks - EDGE :], "db", up)
         high = lax.ppermute(own[:EDGE], "db", down)
+        beyond = lax.ppermute(own, "pb", opposite)
         if wanted is None:
             chosen, wanted = select_pieces(held, slots, [low, high])
         else:
-            (chosen,) = select_pieces(held, slots, [low, high], wanted)
+            (chosen,) = select_pieces(held, slots, [low, high, beyond], wanted)
         arrived = lax.all_to_all(
             chosen.reshape(owners, slots, -1), "db", split_axis=0, concat_axis=0, tiled=True
         ).reshape(chosen.shape)
+        reach = [lax.ppermute(low, "pb", opposite), beyond, lax.ppermute(high, "pb", opposite)]
+        product = near_product(near_index, valid_counts, [(affinity_tiles,)], reach)
+        product, sides = lax.optimization_barrier((product, (before, after)))
+        quarters = [(affinity_tiles,), (sides[0],), (sides[1],)]
         partials = [
-            near_product(near_index, valid_counts, part, low, own, high)
-            for part in ([quarters[:3], quarters[3:]] if step == 0 else [quarters])
+            near_product(near_index, valid_counts, quarters, [low, own, high]),
+            lax.ppermute(product, "pb", opposite),
         ]
         done = add_far(offsets, valid_counts, far_tiles, arrived, partials, queries, owners, step < ITERS - 1)
         ranking = done[0]

time: 185 us -> 179 us (0.968)
  waiting for transfers between devices: 77 us -> 58.4 us
  starting transfers between devices: 56 us -> 70.9 us
  local copies, waits for them, and re-layouts: 14.5 us -> 12 us
    ppermute x4 -> x11, starting transfers between devices: 6.23 us -> 17.8 us  [the longest x2 4.59 us: on_device(): lax.ppermute(high, 'pb', opposite)]
    all_to_all x2, waiting for transfers between devices: 19.8 us -> 9.28 us  [on_device(): lax.all_to_all(chosen.reshape(owners, slots, -1), 'db', split_axis=0, con...]
    ppermute x4 -> x11, waiting for transfers between devices: 34.1 us -> 27.6 us  [the longest x2 25.8 us: on_device(): lax.ppermute(low, 'pb', opposite)]
    all_to_all x2, starting transfers between devices: 13 us -> 15.8 us  [on_device(): lax.all_to_all(chosen.reshape(owners, slots, -1), 'db', split_axis=0, con...]
    slice x2 -> x1, local copies, waits for them, and re-layouts: 3.46 us -> 0.72 us  [on_device(): affinity_tiles[:, FAR[0]:FAR[-1] + 1]]
    pallas_call x3 -> x4, Pallas kernels: 16.8 us -> 19.3 us  [near_product(): pl.pallas_call(kernel, out_shape=jax.ShapeDtypeStruct((blocks, number * r...]
    unnamed x38 -> x54, local copies, waits for them, and re-layouts: 8.75 us -> 8.84 us
  transfers between devices with their start and end apart: 12 -> 19, of which waited for: 10 -> 11; matrix products, arithmetic and copies ran while one was open for 2% -> 1% of each run, Pallas kernels for 11% -> 12%
where the time goes in v9:
time: 179 us; the launch traced here: 178 us
  starting transfers between devices  70.9 us (40%)
  waiting for transfers between devices  58.4 us (33%)
  Pallas kernels  36.1 us (20%)
  local copies, waits for them, and re-layouts  12 us (7%)
    ppermute x2, waiting for transfers between devices, on_device(): lax.ppermute(low, 'pb', opposite)  25.8 us
    all_to_all x2, starting transfers between devices, on_device(): held = lax.all_to_all(pieces, 'db', split_axis=0, concat_axis=0, tiled=True)  25.8 us
    pallas_call x4, Pallas kernels, near_product(): pl.pallas_call(kernel, out_shape=jax.ShapeDtypeStruct((blocks, number * r...  19.3 us
    all_to_all x2, starting transfers between devices, on_device(): lax.all_to_all(chosen.reshape(owners, slots, -1), 'db', split_axis=0, con...  15.8 us
    pallas_call x2, Pallas kernels, add_far(): pl.pallas_call(kernel, out_shape=out_shape, grid_spec=pltpu.PrefetchScala...  11.4 us
    all_to_all x2, waiting for transfers between devices, on_device(): lax.all_to_all(chosen.reshape(owners, slots, -1), 'db', split_axis=0, con...  9.28 us
    unnamed x54, local copies, waits for them, and re-layouts  8.84 us
    ppermute x2, waiting for transfers between devices, on_device(): low = lax.ppermute(own[blocks - EDGE:], 'db', up)  8.09 us
  transfers between devices with their start and end apart: 19, of which 11 were waited for; matrix products, arithmetic and copies ran while one was open for 1% of the time, Pallas kernels for 12%

profile of v9, /device:TPU:1, one launch (start us, length us, event | category | flops | bytes accessed | tf_op | source)
XLA Modules:
  0.0 177.9 jit_solution(6404965577404594996)
XLA Ops:
  1.6 2.6 %split_blocks.1 = bf16[64,40,128]{2,1,0:T(8,128)(2,1)} custom-call(bf16[2048,128]{1,0:T(8,128)(2,1)} %refs_7_.3, f32[1,128]{1,0:T(1,128)} %pad.4.digits_ref), custom_call_target="tpu_custom_call" | custom-call | tf_op jit(solution)/shard_map/split_blocks/pallas_call | solution.py:38
  4.2 13.0 %all-to-all-start = ((bf16[64,40,128]{2,1,0:T(8,128)(2,1)}), bf16[64,40,128]{2,1,0:T(8,128)(2,1)S(1)}, u32[]{:S(2)}, u32[]{:S(2)}) async-start(bf16[64,40,128]{2,1,0:T(8,128)(2,1)} %split_blocks.1), calls=%async_computation | async-start | bytes 1310720 | tf_op jit(solution)/shard_map/all_to_all | solution.py:286
  17.2 2.8 %collective-permute-start.1 = (bf16[16,16,32,128]{3,2,1,0:T(8,128)(2,1)S(1)}, bf16[16,16,32,128]{3,2,1,0:T(8,128)(2,1)}, u32[]{:S(2)}, u32[]{:S(2)}) collective-permute-start(bf16[16,16,32,128]{3,2,1,0:T(8,128)(2,1)S(1)} %copy-done), channel_id=1, source_target_pairs={{1,0},{2,1},{3,2},{0,3},{5,4},{6,5},{7,6},{4,7},{9,8},{10,9},{11,1... | collective-permute-start | bytes 6291464 | tf_op jit(solution)/shard_map/ppermute | solution.py:270
  20.9 3.8 %collective-permute-start.3 = (bf16[2,128,128]{2,1,0:T(8,128)(2,1)S(1)}, bf16[2,128,128]{2,1,0:T(8,128)(2,1)S(1)}, u32[]{:S(2)}, u32[]{:S(2)}) collective-permute-start(bf16[2,128,128]{2,1,0:T(8,128)(2,1)S(1)} %bitcast.28), channel_id=1, source_target_pairs={{0,4},{4,8},{8,12},{12,16},{16,20},{20,24},{24,28},{28,32},{32,36}... | collective-permute-start | bytes 196616 | tf_op jit(solution)/shard_map/ppermute | solution.py:287
  26.7 4.4 %collective-permute-done.3.refs_3_.rest_0_ = bf16[2,128,128]{2,1,0:T(8,128)(2,1)S(1)} collective-permute-done((bf16[2,128,128]{2,1,0:T(8,128)(2,1)S(1)}, bf16[2,128,128]{2,1,0:T(8,128)(2,1)S(1)}, u32[]{:S(2)}, u32[]{:S(2)}) %collective-permute-start.3) | collective-permute-done | bytes 65568 | tf_op jit(solution)/shard_map/ppermute | solution.py:287
  31.1 3.4 %collective-permute-done.6.refs_5_.rest_1_ = bf16[2,128,128]{2,1,0:T(8,128)(2,1)S(1)} collective-permute-done((bf16[2,128,128]{2,1,0:T(8,128)(2,1)S(1)}, bf16[2,128,128]{2,1,0:T(8,128)(2,1)S(1)}, u32[]{:S(2)}, u32[]{:S(2)}) %collective-permute-start.6) | collective-permute-done | bytes 65568 | tf_op jit(solution)/shard_map/ppermute | solution.py:288
  34.5 3.3 %all-to-all-done.held_ref = bf16[64,40,128]{2,1,0:T(8,128)(2,1)S(1)} async-done(((bf16[64,40,128]{2,1,0:T(8,128)(2,1)}), bf16[64,40,128]{2,1,0:T(8,128)(2,1)S(1)}, u32[]{:S(2)}, u32[]{:S(2)}) %all-to-all-start) | async-done | bytes 655392 | tf_op jit(solution)/shard_map/all_to_all | solution.py:286
  42.2 6.6 %all-to-all-start.1 = ((bf16[64,32,256]{2,1,0:T(8,128)(2,1)}), bf16[64,32,256]{2,1,0:T(8,128)(2,1)S(1)}, u32[]{:S(2)}, u32[]{:S(2)}) async-start(bf16[64,32,256]{2,1,0:T(8,128)(2,1)} %bitcast.20), calls=%async_computation.1 | async-start | bytes 2097152 | tf_op jit(solution)/shard_map/all_to_all | solution.py:294
  48.9 3.0 %collective-permute-start.5 = (bf16[16,128,128]{2,1,0:T(8,128)(2,1)}, bf16[16,128,128]{2,1,0:T(8,128)(2,1)}, u32[]{:S(2)}, u32[]{:S(2)}) collective-permute-start(bf16[16,128,128]{2,1,0:T(8,128)(2,1)} %bitcast.24), channel_id=1, source_target_pairs={{0,2},{1,3},{2,0},{3,1},{4,6},{5,7},{6,4},{7,5},{8,10},{9,11},{10,... | collective-permute-start | bytes 1572872 | tf_op jit(solution)/shard_map/ppermute | solution.py:289
  52.0 2.9 %collective-permute-start.7 = (bf16[2,128,128]{2,1,0:T(8,128)(2,1)S(1)}, bf16[2,128,128]{2,1,0:T(8,128)(2,1)S(1)}, u32[]{:S(2)}, u32[]{:S(2)}) collective-permute-start(bf16[2,128,128]{2,1,0:T(8,128)(2,1)S(1)} %copy-done.17), channel_id=1, source_target_pairs={{0,2},{1,3},{2,0},{3,1},{4,6},{5,7},{6,4},{7,5},{8,10},{9,11},{10,... | collective-permute-start | bytes 196616 | tf_op jit(solution)/shard_map/ppermute | solution.py:297
  55.6 23.8 %collective-permute-done.4.refs_1_ = bf16[2,128,128]{2,1,0:T(8,128)(2,1)S(1)} collective-permute-done((bf16[2,128,128]{2,1,0:T(8,128)(2,1)S(1)}, bf16[2,128,128]{2,1,0:T(8,128)(2,1)S(1)}, u32[]{:S(2)}, u32[]{:S(2)}) %collective-permute-start.4) | collective-permute-done | bytes 65568 | tf_op jit(solution)/shard_map/ppermute | solution.py:297
  81.7 3.5 %near_product.4 = f32[16,32,128]{2,1,0:T(8,128)S(1)} custom-call(s32[16,16]{1,0:T(8,128)S(1)} %add_clamp_fusion.index_ref, s32[16]{0:T(128)S(1)} %copy-done.11, bf16[16,16,32,128]{3,2,1,0:T(8,128)(2,1)S(1)} %copy-done, bf16[2,128,128]{2,1,0:T(8,128)(2,1)} %copy-done.22, bf16[16,128,128]{2,1,0:T(8,128)(2,1)} %collective-permute-done.5.refs_2_, ...), custom_call_target="tpu_custom_call" | custom-call | flops 234881024 | bytes 2097152 | tf_op jit(solution)/shard_map/near_product/pallas_call | solution.py:147
  86.9 6.1 %near_product.5.refs_4_ = f32[16,96,128]{2,1,0:T(8,128)S(1)} custom-call(s32[16,16]{1,0:T(8,128)S(1)} %add_clamp_fusion.index_ref, s32[16]{0:T(128)S(1)} %copy-done.11, bf16[16,16,32,128]{3,2,1,0:T(8,128)(2,1)S(1)} %copy-done, bf16[16,16,32,128]{3,2,1,0:T(8,128)(2,1)} %collective-permute-done.refs_1_, ...), custom_call_target="tpu_custom_call" | custom-call | flops 704643072 | bytes 6291456 | tf_op jit(solution)/shard_map/near_product/pallas_call | solution.py:147
  94.0 6.0 %add_far.2 = (bf16[2048,128]{1,0:T(8,128)(2,1)S(1)}, bf16[64,32,128]{2,1,0:T(8,128)(2,1)}) custom-call(s32[4]{0:T(128)S(1)} %pad_add_fusion.offset_ref, s32[16]{0:T(128)S(1)} %copy-done.11, bf16[16,16,32,128]{3,2,1,0:T(8,128)(2,1)} %refs_0_.11, bf16[16,16,32,128]{3,2,1,0:T(8,128)(2,1)} %collective-permute-done.refs_1_, ...), custom_call_target="tpu_custom_call" | custom-call | flops 134217728 | bytes 4194304 | tf_op jit(solution)/shard_map/add_far/pallas_call | solution.py:241
  100.0 12.8 %all-to-all-start.2 = ((bf16[64,32,128]{2,1,0:T(8,128)(2,1)}), bf16[64,32,128]{2,1,0:T(8,128)(2,1)S(1)}, u32[]{:S(2)}, u32[]{:S(2)}) async-start(bf16[64,32,128]{2,1,0:T(8,128)(2,1)} %get-tuple-element.23), calls=%async_computation.2 | async-start | bytes 1048576 | tf_op jit(solution)/shard_map/all_to_all | solution.py:286
  114.1 3.8 %collective-permute-start.9 = (bf16[2,128,128]{2,1,0:T(8,128)(2,1)S(1)}, bf16[2,128,128]{2,1,0:T(8,128)(2,1)S(1)}, u32[]{:S(2)}, u32[]{:S(2)}) collective-permute-start(bf16[2,128,128]{2,1,0:T(8,128)(2,1)S(1)} %bitcast.29), channel_id=1, source_target_pairs={{0,4},{4,8},{8,12},{12,16},{16,20},{20,24},{24,28},{28,32},{32,36}... | collective-permute-start | bytes 196616 | tf_op jit(solution)/shard_map/ppermute | solution.py:287
  119.9 3.7 %collective-permute-done.9.refs_3_.rest_0_ = bf16[2,128,128]{2,1,0:T(8,128)(2,1)S(1)} collective-permute-done((bf16[2,128,128]{2,1,0:T(8,128)(2,1)S(1)}, bf16[2,128,128]{2,1,0:T(8,128)(2,1)S(1)}, u32[]{:S(2)}, u32[]{:S(2)}) %collective-permute-start.9) | collective-permute-done | bytes 65568 | tf_op jit(solution)/shard_map/ppermute | solution.py:287
  123.6 3.6 %collective-permute-done.12.refs_5_.rest_1_ = bf16[2,128,128]{2,1,0:T(8,128)(2,1)S(1)} collective-permute-done((bf16[2,128,128]{2,1,0:T(8,128)(2,1)S(1)}, bf16[2,128,128]{2,1,0:T(8,128)(2,1)S(1)}, u32[]{:S(2)}, u32[]{:S(2)}) %collective-permute-start.12) | collective-permute-done | bytes 65568 | tf_op jit(solution)/shard_map/ppermute | solution.py:288
  127.5 3.0 %all-to-all-done.2.held_ref = bf16[64,32,128]{2,1,0:T(8,128)(2,1)S(1)} async-done(((bf16[64,32,128]{2,1,0:T(8,128)(2,1)}), bf16[64,32,128]{2,1,0:T(8,128)(2,1)S(1)}, u32[]{:S(2)}, u32[]{:S(2)}) %all-to-all-start.2) | async-done | bytes 524320 | tf_op jit(solution)/shard_map/all_to_all | solution.py:286
  134.6 9.2 %all-to-all-start.3 = ((bf16[64,32,256]{2,1,0:T(8,128)(2,1)}), bf16[64,32,256]{2,1,0:T(8,128)(2,1)S(1)}, u32[]{:S(2)}, u32[]{:S(2)}) async-start(bf16[64,32,256]{2,1,0:T(8,128)(2,1)} %bitcast.21), calls=%async_computation.3 | async-start | bytes 2097152 | tf_op jit(solution)/shard_map/all_to_all | solution.py:294
  151.1 3.5 %near_product.6 = f32[16,32,128]{2,1,0:T(8,128)S(1)} custom-call(s32[16,16]{1,0:T(8,128)S(1)} %add_clamp_fusion.index_ref, s32[16]{0:T(128)S(1)} %copy-done.11, bf16[16,16,32,128]{3,2,1,0:T(8,128)(2,1)S(1)} %copy-done.1, bf16[2,128,128]{2,1,0:T(8,128)(2,1)} %copy-done.24, bf16[16,128,128]{2,1,0:T(8,128)(2,1)} %copy-done.12, bf16[2,128,128]{2,1,0:T(8,128)(2,1)} %copy-done.25), custom_call_target="tpu_custom_call" | custom-call | flops 234881024 | bytes 2097152 | tf_op jit(solution)/shard_map/near_product/pallas_call | solution.py:147
  156.1 6.1 %near_product.7.refs_4_ = f32[16,96,128]{2,1,0:T(8,128)S(1)} custom-call(s32[16,16]{1,0:T(8,128)S(1)} %add_clamp_fusion.index_ref, s32[16]{0:T(128)S(1)} %copy-done.11, bf16[16,16,32,128]{3,2,1,0:T(8,128)(2,1)S(1)} %copy-done.1, bf16[16,16,32,128]{3,2,1,0:T(8,128)(2,1)} %collective-permute-done.refs_1_, ...), custom_call_target="tpu_custom_call" | custom-call | flops 704643072 | bytes 6291456 | tf_op jit(solution)/shard_map/near_product/pallas_call | solution.py:147
  163.1 9.3 %all-to-all-done.3 = bf16[64,32,256]{2,1,0:T(8,128)(2,1)S(1)} async-done(((bf16[64,32,256]{2,1,0:T(8,128)(2,1)}), bf16[64,32,256]{2,1,0:T(8,128)(2,1)S(1)}, u32[]{:S(2)}, u32[]{:S(2)}) %all-to-all-start.3) | async-done | bytes 1048608 | tf_op jit(solution)/shard_map/all_to_all | solution.py:294
  172.4 5.4 %add_far.3 = bf16[2048,128]{1,0:T(8,128)(2,1)} custom-call(s32[4]{0:T(128)S(1)} %pad_add_fusion.offset_ref, s32[16]{0:T(128)S(1)} %copy-done.11, bf16[16,16,32,128]{3,2,1,0:T(8,128)(2,1)} %refs_0_.11, bf16[16,16,32,128]{3,2,1,0:T(8,128)(2,1)} %collective-permute-done.refs_1_, bf16[16,16,32,128]{3,2,1,0:T(8,128)(2,1)} %collective-permute-done.1.refs_2_, ...), custom_call_target="tpu_custom_call" | custom-call | flops 134217728 | bytes 4194304 | tf_op jit(solution)/shard_map/add_far/pallas_call | solution.py:241
  (87 shorter events, 31.7 us)
Async XLA Ops:
  0.0 17.2 %copy-start = (bf16[16,16,32,128]{3,2,1,0:T(8,128)(2,1)S(1)}, bf16[16,16,32,128]{3,2,1,0:T(8,128)(2,1)}, u32[]{:S(2)}) copy-start(bf16[16,16,32,128]{3,2,1,0:T(8,128)(2,1)} %refs_0_.11) | copy-start | bytes 6291460
  4.2 33.6 %all-to-all-start = ((bf16[64,40,128]{2,1,0:T(8,128)(2,1)}), bf16[64,40,128]{2,1,0:T(8,128)(2,1)S(1)}, u32[]{:S(2)}, u32[]{:S(2)}) async-start(bf16[64,40,128]{2,1,0:T(8,128)(2,1)} %split_blocks.1), calls=%async_computation | async-start | bytes 1310720 | tf_op jit(solution)/shard_map/all_to_all | solution.py:286
  17.2 68.0 %collective-permute-start.1 = (bf16[16,16,32,128]{3,2,1,0:T(8,128)(2,1)S(1)}, bf16[16,16,32,128]{3,2,1,0:T(8,128)(2,1)}, u32[]{:S(2)}, u32[]{:S(2)}) collective-permute-start(bf16[16,16,32,128]{3,2,1,0:T(8,128)(2,1)S(1)} %copy-done), channel_id=1, source_target_pairs={{1,0},{2,1},{3,2},{0,3},{5,4},{6,5},{7,6},{4,7},{9,8},{10,9},{11,1... | collective-permute-start | bytes 6291464 | tf_op jit(solution)/shard_map/ppermute | solution.py:270
  20.0 65.2 %collective-permute-start = (bf16[16,16,32,128]{3,2,1,0:T(8,128)(2,1)S(1)}, bf16[16,16,32,128]{3,2,1,0:T(8,128)(2,1)}, u32[]{:S(2)}, u32[]{:S(2)}) collective-permute-start(bf16[16,16,32,128]{3,2,1,0:T(8,128)(2,1)S(1)} %copy-done), channel_id=1, source_target_pairs={{0,1},{1,2},{2,3},{3,0},{4,5},{5,6},{6,7},{7,4},{8,9},{9,10},{10,1... | collective-permute-start | bytes 6291464 | tf_op jit(solution)/shard_map/ppermute | solution.py:269
  20.9 10.2 %collective-permute-start.3 = (bf16[2,128,128]{2,1,0:T(8,128)(2,1)S(1)}, bf16[2,128,128]{2,1,0:T(8,128)(2,1)S(1)}, u32[]{:S(2)}, u32[]{:S(2)}) collective-permute-start(bf16[2,128,128]{2,1,0:T(8,128)(2,1)S(1)} %bitcast.28), channel_id=1, source_target_pairs={{0,4},{4,8},{8,12},{12,16},{16,20},{20,24},{24,28},{28,32},{32,36}... | collective-permute-start | bytes 196616 | tf_op jit(solution)/shard_map/ppermute | solution.py:287
  24.7 9.8 %collective-permute-start.6 = (bf16[2,128,128]{2,1,0:T(8,128)(2,1)S(1)}, bf16[2,128,128]{2,1,0:T(8,128)(2,1)S(1)}, u32[]{:S(2)}, u32[]{:S(2)}) collective-permute-start(bf16[2,128,128]{2,1,0:T(8,128)(2,1)S(1)} %bitcast.26), channel_id=1, source_target_pairs={{4,0},{8,4},{12,8},{16,12},{20,16},{24,20},{28,24},{32,28},{36,32}... | collective-permute-start | bytes 196616 | tf_op jit(solution)/shard_map/ppermute | solution.py:288
  39.8 15.0 %copy-start.26 = (s32[16,16]{1,0:T(8,128)S(1)}, s32[16,16]{1,0:T(8,128)}, u32[]{:S(2)}) copy-start(s32[16,16]{1,0:T(8,128)} %param.5) | copy-start | bytes 3076
  42.2 39.4 %copy-start.11 = (s32[16]{0:T(128)S(1)}, s32[16]{0:T(128)}, u32[]{:S(2)}) copy-start(s32[16]{0:T(128)} %count_ref.11) | copy-start | bytes 196
  42.2 51.7 %all-to-all-start.1 = ((bf16[64,32,256]{2,1,0:T(8,128)(2,1)}), bf16[64,32,256]{2,1,0:T(8,128)(2,1)S(1)}, u32[]{:S(2)}, u32[]{:S(2)}) async-start(bf16[64,32,256]{2,1,0:T(8,128)(2,1)} %bitcast.20), calls=%async_computation.1 | async-start | bytes 2097152 | tf_op jit(solution)/shard_map/all_to_all | solution.py:294
  48.9 32.2 %collective-permute-start.5 = (bf16[16,128,128]{2,1,0:T(8,128)(2,1)}, bf16[16,128,128]{2,1,0:T(8,128)(2,1)}, u32[]{:S(2)}, u32[]{:S(2)}) collective-permute-start(bf16[16,128,128]{2,1,0:T(8,128)(2,1)} %bitcast.24), channel_id=1, source_target_pairs={{0,2},{1,3},{2,0},{3,1},{4,6},{5,7},{6,4},{7,5},{8,10},{9,11},{10,... | collective-permute-start | bytes 1572872 | tf_op jit(solution)/shard_map/ppermute | solution.py:289
  51.9 27.5 %collective-permute-start.4 = (bf16[2,128,128]{2,1,0:T(8,128)(2,1)S(1)}, bf16[2,128,128]{2,1,0:T(8,128)(2,1)S(1)}, u32[]{:S(2)}, u32[]{:S(2)}) collective-permute-start(bf16[2,128,128]{2,1,0:T(8,128)(2,1)S(1)} %copy-done.15), channel_id=1, source_target_pairs={{0,2},{1,3},{2,0},{3,1},{4,6},{5,7},{6,4},{7,5},{8,10},{9,11},{10,... | collective-permute-start | bytes 196616 | tf_op jit(solution)/shard_map/ppermute | solution.py:297
  52.0 29.0 %collective-permute-start.7 = (bf16[2,128,128]{2,1,0:T(8,128)(2,1)S(1)}, bf16[2,128,128]{2,1,0:T(8,128)(2,1)S(1)}, u32[]{:S(2)}, u32[]{:S(2)}) collective-permute-start(bf16[2,128,128]{2,1,0:T(8,128)(2,1)S(1)} %copy-done.17), channel_id=1, source_target_pairs={{0,2},{1,3},{2,0},{3,1},{4,6},{5,7},{6,4},{7,5},{8,10},{9,11},{10,... | collective-permute-start | bytes 196616 | tf_op jit(solution)/shard_map/ppermute | solution.py:297
  79.4 14.5 %collective-permute-start.2 = (bf16[16,2,32,128]{3,2,1,0:T(8,128)(2,1)}, bf16[16,2,32,128]{3,2,1,0:T(8,128)(2,1)}, u32[]{:S(2)}, u32[]{:S(2)}) collective-permute-start(bf16[16,2,32,128]{3,2,1,0:T(8,128)(2,1)} %slice.30), channel_id=1, source_target_pairs={{0,2},{1,3},{2,0},{3,1},{4,6},{5,7},{6,4},{7,5},{8,10},{9,11},{10,... | collective-permute-start | bytes 786440 | tf_op jit(solution)/shard_map/ppermute | solution.py:271
  85.2 8.8 %collective-permute-start.8 = (f32[16,32,128]{2,1,0:T(8,128)S(1)}, f32[16,32,128]{2,1,0:T(8,128)}, u32[]{:S(2)}, u32[]{:S(2)}) collective-permute-start(f32[16,32,128]{2,1,0:T(8,128)S(1)} %near_product.4), channel_id=1, source_target_pairs={{0,2},{1,3},{2,0},{3,1},{4,6},{5,7},{6,4},{7,5},{8,10},{9,11},{10,... | collective-permute-start | bytes 786440 | tf_op jit(solution)/shard_map/ppermute | solution.py:303
  100.0 30.4 %copy-start.6 = (bf16[2048,128]{1,0:T(8,128)(2,1)}, bf16[2048,128]{1,0:T(8,128)(2,1)S(1)}, u32[]{:S(2)}) copy-start(bf16[2048,128]{1,0:T(8,128)(2,1)S(1)} %get-tuple-element.19) | copy-start | bytes 1572868
  100.0 30.4 %all-to-all-start.2 = ((bf16[64,32,128]{2,1,0:T(8,128)(2,1)}), bf16[64,32,128]{2,1,0:T(8,128)(2,1)S(1)}, u32[]{:S(2)}, u32[]{:S(2)}) async-start(bf16[64,32,128]{2,1,0:T(8,128)(2,1)} %get-tuple-element.23), calls=%async_computation.2 | async-start | bytes 1048576 | tf_op jit(solution)/shard_map/all_to_all | solution.py:286
  112.8 14.6 %collective-permute-start.11 = (bf16[16,128,128]{2,1,0:T(8,128)(2,1)S(1)}, bf16[16,128,128]{2,1,0:T(8,128)(2,1)S(1)}, u32[]{:S(2)}, u32[]{:S(2)}) collective-permute-start(bf16[16,128,128]{2,1,0:T(8,128)(2,1)S(1)} %bitcast.22), channel_id=1, source_target_pairs={{0,2},{1,3},{2,0},{3,1},{4,6},{5,7},{6,4},{7,5},{8,10},{9,11},{10,... | collective-permute-start | bytes 1572872 | tf_op jit(solution)/shard_map/ppermute | solution.py:289
  114.1 9.4 %collective-permute-start.9 = (bf16[2,128,128]{2,1,0:T(8,128)(2,1)S(1)}, bf16[2,128,128]{2,1,0:T(8,128)(2,1)S(1)}, u32[]{:S(2)}, u32[]{:S(2)}) collective-permute-start(bf16[2,128,128]{2,1,0:T(8,128)(2,1)S(1)} %bitcast.29), channel_id=1, source_target_pairs={{0,4},{4,8},{8,12},{12,16},{16,20},{20,24},{24,28},{28,32},{32,36}... | collective-permute-start | bytes 196616 | tf_op jit(solution)/shard_map/ppermute | solution.py:287
  118.0 9.3 %collective-permute-start.12 = (bf16[2,128,128]{2,1,0:T(8,128)(2,1)S(1)}, bf16[2,128,128]{2,1,0:T(8,128)(2,1)S(1)}, u32[]{:S(2)}, u32[]{:S(2)}) collective-permute-start(bf16[2,128,128]{2,1,0:T(8,128)(2,1)S(1)} %bitcast.27), channel_id=1, source_target_pairs={{4,0},{8,4},{12,8},{16,12},{20,16},{24,20},{28,24},{32,28},{36,32}... | collective-permute-start | bytes 196616 | tf_op jit(solution)/shard_map/ppermute | solution.py:288
  132.3 18.8 %copy-start.1 = (bf16[16,16,32,128]{3,2,1,0:T(8,128)(2,1)S(1)}, bf16[16,16,32,128]{3,2,1,0:T(8,128)(2,1)}, u32[]{:S(2)}) copy-start(bf16[16,16,32,128]{3,2,1,0:T(8,128)(2,1)} %refs_0_.11) | copy-start | bytes 6291460
  134.6 37.8 %all-to-all-start.3 = ((bf16[64,32,256]{2,1,0:T(8,128)(2,1)}), bf16[64,32,256]{2,1,0:T(8,128)(2,1)S(1)}, u32[]{:S(2)}, u32[]{:S(2)}) async-start(bf16[64,32,256]{2,1,0:T(8,128)(2,1)} %bitcast.21), calls=%async_computation.3 | async-start | bytes 2097152 | tf_op jit(solution)/shard_map/all_to_all | solution.py:294
  143.8 5.0 %collective-permute-start.10 = (bf16[2,128,128]{2,1,0:T(8,128)(2,1)S(1)}, bf16[2,128,128]{2,1,0:T(8,128)(2,1)S(1)}, u32[]{:S(2)}, u32[]{:S(2)}) collective-permute-start(bf16[2,128,128]{2,1,0:T(8,128)(2,1)S(1)} %copy-done.19), channel_id=1, source_target_pairs={{0,2},{1,3},{2,0},{3,1},{4,6},{5,7},{6,4},{7,5},{8,10},{9,11},{10,... | collective-permute-start | bytes 196616 | tf_op jit(solution)/shard_map/ppermute | solution.py:297
  145.1 5.3 %collective-permute-start.13 = (bf16[2,128,128]{2,1,0:T(8,128)(2,1)S(1)}, bf16[2,128,128]{2,1,0:T(8,128)(2,1)S(1)}, u32[]{:S(2)}, u32[]{:S(2)}) collective-permute-start(bf16[2,128,128]{2,1,0:T(8,128)(2,1)S(1)} %copy-done.21), channel_id=1, source_target_pairs={{0,2},{1,3},{2,0},{3,1},{4,6},{5,7},{6,4},{7,5},{8,10},{9,11},{10,... | collective-permute-start | bytes 196616 | tf_op jit(solution)/shard_map/ppermute | solution.py:297
  154.6 8.5 %collective-permute-start.14 = (f32[16,32,128]{2,1,0:T(8,128)S(1)}, f32[16,32,128]{2,1,0:T(8,128)S(1)}, u32[]{:S(2)}, u32[]{:S(2)}) collective-permute-start(f32[16,32,128]{2,1,0:T(8,128)S(1)} %near_product.6), channel_id=1, source_target_pairs={{0,2},{1,3},{2,0},{3,1},{4,6},{5,7},{6,4},{7,5},{8,10},{9,11},{10,... | collective-permute-start | bytes 786440 | tf_op jit(solution)/shard_map/ppermute | solution.py:303
  (22 other events, 85.2 us)

commit v10 on v9

--- a/solution.py
+++ b/solution.py
@@ -283,10 +283,12 @@
     pieces = split_blocks(queries, digits, blocks, size, owners)
     for step in range(ITERS):
         own = ranking.reshape(blocks, size, cols)
+        beyond = lax.ppermute(own, "pb", opposite)
+        if step == 0:
+            pieces, beyond = lax.optimization_barrier((pieces, beyond))
         held = lax.all_to_all(pieces, "db", split_axis=0, concat_axis=0, tiled=True)
         low = lax.ppermute(own[blocks - EDGE :], "db", up)
         high = lax.ppermute(own[:EDGE], "db", down)
-        beyond = lax.ppermute(own, "pb", opposite)
         if wanted is None:
             chosen, wanted = select_pieces(held, slots, [low, high])
         else:

time: 179 us -> 182 us (1.017)
  waiting for transfers between devices: 58.4 us -> 62.2 us
  local copies, waits for them, and re-layouts: 12 us -> 8.86 us
  starting transfers between devices: 70.9 us -> 73.5 us
    ppermute x2, waiting for transfers between devices: 0.23 us -> 7.08 us  [on_device(): beyond = lax.ppermute(own, 'pb', opposite)]
    ppermute x2, waiting for transfers between devices: 25.8 us -> 22.1 us  [on_device(): lax.ppermute(low, 'pb', opposite)]
    unnamed x54 -> x46, local copies, waits for them, and re-layouts: 8.84 us -> 5.86 us
  transfers between devices with their start and end apart: 19 -> 19, of which waited for: 11 -> 13; matrix products, arithmetic and copies ran while one was open for 1% -> 2% of each run, Pallas kernels for 12% -> 13%
where the time goes in v10:
time: 182 us; the launch traced here: 181 us
  starting transfers between devices  73.5 us (40%)
  waiting for transfers between devices  62.2 us (34%)
  Pallas kernels  36.1 us (20%)
  local copies, waits for them, and re-layouts  8.86 us (5%)
    all_to_all x2, starting transfers between devices, on_device(): held = lax.all_to_all(pieces, 'db', split_axis=0, concat_axis=0, tiled=True)  25.4 us
    ppermute x2, waiting for transfers between devices, on_device(): lax.ppermute(low, 'pb', opposite)  22.1 us
    pallas_call x4, Pallas kernels, near_product(): pl.pallas_call(kernel, out_shape=jax.ShapeDtypeStruct((blocks, number * r...  19.3 us
    all_to_all x2, starting transfers between devices, on_device(): lax.all_to_all(chosen.reshape(owners, slots, -1), 'db', split_axis=0, con...  15.8 us
    pallas_call x2, Pallas kernels, add_far(): pl.pallas_call(kernel, out_shape=out_shape, grid_spec=pltpu.PrefetchScala...  11.4 us
    all_to_all x2, waiting for transfers between devices, on_device(): lax.all_to_all(chosen.reshape(owners, slots, -1), 'db', split_axis=0, con...  9.03 us
    ppermute x2, waiting for transfers between devices, on_device(): low = lax.ppermute(own[blocks - EDGE:], 'db', up)  7.71 us
    ppermute x2, starting transfers between devices, on_device(): low = lax.ppermute(own[blocks - EDGE:], 'db', up)  7.64 us
  transfers between devices with their start and end apart: 19, of which 13 were waited for; matrix products, arithmetic and copies ran while one was open for 2% of the time, Pallas kernels for 13%

profile of v10, /device:TPU:1, one launch (start us, length us, event | category | flops | bytes accessed | tf_op | source)
XLA Modules:
  0.0 181.3 jit_solution(10667240565700842249)
XLA Ops:
  0.0 3.7 %collective-permute-start.5 = (bf16[16,128,128]{2,1,0:T(8,128)(2,1)}, bf16[16,128,128]{2,1,0:T(8,128)(2,1)S(1)}, u32[]{:S(2)}, u32[]{:S(2)}) collective-permute-start(bf16[16,128,128]{2,1,0:T(8,128)(2,1)} %bitcast.24), channel_id=1, source_target_pairs={{0,2},{1,3},{2,0},{3,1},{4,6},{5,7},{6,4},{7,5},{8,10},{9,11},{10,... | collective-permute-start | bytes 1572872 | tf_op jit(solution)/shard_map/ppermute | solution.py:286
  7.8 6.9 %collective-permute-done.5.refs_2_ = bf16[16,128,128]{2,1,0:T(8,128)(2,1)S(1)} collective-permute-done((bf16[16,128,128]{2,1,0:T(8,128)(2,1)}, bf16[16,128,128]{2,1,0:T(8,128)(2,1)S(1)}, u32[]{:S(2)}, u32[]{:S(2)}) %collective-permute-start.5) | collective-permute-done | bytes 524320 | tf_op jit(solution)/shard_map/ppermute | solution.py:286
  15.4 13.7 %all-to-all-start = ((bf16[64,40,128]{2,1,0:T(8,128)(2,1)}), bf16[64,40,128]{2,1,0:T(8,128)(2,1)S(1)}, u32[]{:S(2)}, u32[]{:S(2)}) async-start(bf16[64,40,128]{2,1,0:T(8,128)(2,1)} %split_blocks.1), calls=%async_computation | async-start | bytes 1310720 | tf_op jit(solution)/shard_map/all_to_all | solution.py:289
  32.9 3.8 %collective-permute-start.3 = (bf16[2,128,128]{2,1,0:T(8,128)(2,1)S(1)}, bf16[2,128,128]{2,1,0:T(8,128)(2,1)S(1)}, u32[]{:S(2)}, u32[]{:S(2)}) collective-permute-start(bf16[2,128,128]{2,1,0:T(8,128)(2,1)S(1)} %bitcast.28), channel_id=1, source_target_pairs={{0,4},{4,8},{8,12},{12,16},{16,20},{20,24},{24,28},{28,32},{32,36}... | collective-permute-start | bytes 196616 | tf_op jit(solution)/shard_map/ppermute | solution.py:290
  38.6 4.4 %collective-permute-done.3.refs_3_.rest_0_ = bf16[2,128,128]{2,1,0:T(8,128)(2,1)S(1)} collective-permute-done((bf16[2,128,128]{2,1,0:T(8,128)(2,1)S(1)}, bf16[2,128,128]{2,1,0:T(8,128)(2,1)S(1)}, u32[]{:S(2)}, u32[]{:S(2)}) %collective-permute-start.3) | collective-permute-done | bytes 65568 | tf_op jit(solution)/shard_map/ppermute | solution.py:290
  43.1 3.4 %collective-permute-done.6.refs_5_.rest_1_ = bf16[2,128,128]{2,1,0:T(8,128)(2,1)S(1)} collective-permute-done((bf16[2,128,128]{2,1,0:T(8,128)(2,1)S(1)}, bf16[2,128,128]{2,1,0:T(8,128)(2,1)S(1)}, u32[]{:S(2)}, u32[]{:S(2)}) %collective-permute-start.6) | collective-permute-done | bytes 65568 | tf_op jit(solution)/shard_map/ppermute | solution.py:291
  46.5 3.3 %all-to-all-done.held_ref = bf16[64,40,128]{2,1,0:T(8,128)(2,1)S(1)} async-done(((bf16[64,40,128]{2,1,0:T(8,128)(2,1)}), bf16[64,40,128]{2,1,0:T(8,128)(2,1)S(1)}, u32[]{:S(2)}, u32[]{:S(2)}) %all-to-all-start) | async-done | bytes 655392 | tf_op jit(solution)/shard_map/all_to_all | solution.py:289
  52.3 6.6 %all-to-all-start.1 = ((bf16[64,32,256]{2,1,0:T(8,128)(2,1)}), bf16[64,32,256]{2,1,0:T(8,128)(2,1)S(1)}, u32[]{:S(2)}, u32[]{:S(2)}) async-start(bf16[64,32,256]{2,1,0:T(8,128)(2,1)} %bitcast.20), calls=%async_computation.1 | async-start | bytes 2097152 | tf_op jit(solution)/shard_map/all_to_all | solution.py:296
  59.7 2.9 %collective-permute-start.2 = (bf16[16,2,32,128]{3,2,1,0:T(8,128)(2,1)}, bf16[16,2,32,128]{3,2,1,0:T(8,128)(2,1)}, u32[]{:S(2)}, u32[]{:S(2)}) collective-permute-start(bf16[16,2,32,128]{3,2,1,0:T(8,128)(2,1)} %slice.30), channel_id=1, source_target_pairs={{0,2},{1,3},{2,0},{3,1},{4,6},{5,7},{6,4},{7,5},{8,10},{9,11},{10,... | collective-permute-start | bytes 786440 | tf_op jit(solution)/shard_map/ppermute | solution.py:271
  62.6 2.9 %collective-permute-start.7 = (bf16[2,128,128]{2,1,0:T(8,128)(2,1)S(1)}, bf16[2,128,128]{2,1,0:T(8,128)(2,1)S(1)}, u32[]{:S(2)}, u32[]{:S(2)}) collective-permute-start(bf16[2,128,128]{2,1,0:T(8,128)(2,1)S(1)} %copy-done.13), channel_id=1, source_target_pairs={{0,2},{1,3},{2,0},{3,1},{4,6},{5,7},{6,4},{7,5},{8,10},{9,11},{10,... | collective-permute-start | bytes 196616 | tf_op jit(solution)/shard_map/ppermute | solution.py:299
  65.6 20.2 %collective-permute-done.4.refs_1_ = bf16[2,128,128]{2,1,0:T(8,128)(2,1)S(1)} collective-permute-done((bf16[2,128,128]{2,1,0:T(8,128)(2,1)S(1)}, bf16[2,128,128]{2,1,0:T(8,128)(2,1)S(1)}, u32[]{:S(2)}, u32[]{:S(2)}) %collective-permute-start.4) | collective-permute-done | bytes 65568 | tf_op jit(solution)/shard_map/ppermute | solution.py:299
  87.7 3.5 %near_product.4 = f32[16,32,128]{2,1,0:T(8,128)S(1)} custom-call(s32[16,16]{1,0:T(8,128)S(1)} %add_clamp_fusion.index_ref, s32[16]{0:T(128)S(1)} %copy-done.7, bf16[16,16,32,128]{3,2,1,0:T(8,128)(2,1)S(1)} %copy-done, bf16[2,128,128]{2,1,0:T(8,128)(2,1)} %copy-done.18, bf16[16,128,128]{2,1,0:T(8,128)(2,1)} %copy-done.8, bf16[2,128,128]{2,1,0:T(8,128)(2,1)} %copy-done.20), custom_call_target="tpu_custom_call" | custom-call | flops 234881024 | bytes 2097152 | tf_op jit(solution)/shard_map/near_product/pallas_call | solution.py:147
  93.2 6.1 %near_product.5.refs_4_ = f32[16,96,128]{2,1,0:T(8,128)S(1)} custom-call(s32[16,16]{1,0:T(8,128)S(1)} %add_clamp_fusion.index_ref, s32[16]{0:T(128)S(1)} %copy-done.7, bf16[16,16,32,128]{3,2,1,0:T(8,128)(2,1)S(1)} %copy-done, bf16[16,16,32,128]{3,2,1,0:T(8,128)(2,1)} %collective-permute-done.refs_1_, ...), custom_call_target="tpu_custom_call" | custom-call | flops 704643072 | bytes 6291456 | tf_op jit(solution)/shard_map/near_product/pallas_call | solution.py:147
  100.2 6.0 %add_far.2 = (bf16[2048,128]{1,0:T(8,128)(2,1)S(1)}, bf16[64,32,128]{2,1,0:T(8,128)(2,1)}) custom-call(s32[4]{0:T(128)S(1)} %pad_add_fusion.offset_ref, s32[16]{0:T(128)S(1)} %copy-done.7, bf16[16,16,32,128]{3,2,1,0:T(8,128)(2,1)} %refs_0_.11, bf16[16,16,32,128]{3,2,1,0:T(8,128)(2,1)} %collective-permute-done.refs_1_, ...), custom_call_target="tpu_custom_call" | custom-call | flops 134217728 | bytes 4194304 | tf_op jit(solution)/shard_map/add_far/pallas_call | solution.py:241
  106.3 11.7 %all-to-all-start.2 = ((bf16[64,32,128]{2,1,0:T(8,128)(2,1)}), bf16[64,32,128]{2,1,0:T(8,128)(2,1)S(1)}, u32[]{:S(2)}, u32[]{:S(2)}) async-start(bf16[64,32,128]{2,1,0:T(8,128)(2,1)} %get-tuple-element.27), calls=%async_computation.2 | async-start | bytes 1048576 | tf_op jit(solution)/shard_map/all_to_all | solution.py:289
  119.7 3.8 %collective-permute-start.9 = (bf16[2,128,128]{2,1,0:T(8,128)(2,1)S(1)}, bf16[2,128,128]{2,1,0:T(8,128)(2,1)S(1)}, u32[]{:S(2)}, u32[]{:S(2)}) collective-permute-start(bf16[2,128,128]{2,1,0:T(8,128)(2,1)S(1)} %bitcast.29), channel_id=1, source_target_pairs={{0,4},{4,8},{8,12},{12,16},{16,20},{20,24},{24,28},{28,32},{32,36}... | collective-permute-start | bytes 196616 | tf_op jit(solution)/shard_map/ppermute | solution.py:290
  125.4 3.3 %collective-permute-done.9.refs_3_.rest_0_ = bf16[2,128,128]{2,1,0:T(8,128)(2,1)S(1)} collective-permute-done((bf16[2,128,128]{2,1,0:T(8,128)(2,1)S(1)}, bf16[2,128,128]{2,1,0:T(8,128)(2,1)S(1)}, u32[]{:S(2)}, u32[]{:S(2)}) %collective-permute-start.9) | collective-permute-done | bytes 65568 | tf_op jit(solution)/shard_map/ppermute | solution.py:290
  128.7 3.6 %collective-permute-done.12.refs_5_.rest_1_ = bf16[2,128,128]{2,1,0:T(8,128)(2,1)S(1)} collective-permute-done((bf16[2,128,128]{2,1,0:T(8,128)(2,1)S(1)}, bf16[2,128,128]{2,1,0:T(8,128)(2,1)S(1)}, u32[]{:S(2)}, u32[]{:S(2)}) %collective-permute-start.12) | collective-permute-done | bytes 65568 | tf_op jit(solution)/shard_map/ppermute | solution.py:291
  132.6 3.0 %all-to-all-done.2.held_ref = bf16[64,32,128]{2,1,0:T(8,128)(2,1)S(1)} async-done(((bf16[64,32,128]{2,1,0:T(8,128)(2,1)}), bf16[64,32,128]{2,1,0:T(8,128)(2,1)S(1)}, u32[]{:S(2)}, u32[]{:S(2)}) %all-to-all-start.2) | async-done | bytes 524320 | tf_op jit(solution)/shard_map/all_to_all | solution.py:289
  137.9 9.2 %all-to-all-start.3 = ((bf16[64,32,256]{2,1,0:T(8,128)(2,1)}), bf16[64,32,256]{2,1,0:T(8,128)(2,1)S(1)}, u32[]{:S(2)}, u32[]{:S(2)}) async-start(bf16[64,32,256]{2,1,0:T(8,128)(2,1)} %bitcast.21), calls=%async_computation.3 | async-start | bytes 2097152 | tf_op jit(solution)/shard_map/all_to_all | solution.py:296
  154.4 3.5 %near_product.6 = f32[16,32,128]{2,1,0:T(8,128)S(1)} custom-call(s32[16,16]{1,0:T(8,128)S(1)} %add_clamp_fusion.index_ref, s32[16]{0:T(128)S(1)} %copy-done.7, bf16[16,16,32,128]{3,2,1,0:T(8,128)(2,1)S(1)} %copy-done.1, bf16[2,128,128]{2,1,0:T(8,128)(2,1)} %copy-done.19, bf16[16,128,128]{2,1,0:T(8,128)(2,1)} %copy-done.9, bf16[2,128,128]{2,1,0:T(8,128)(2,1)} %copy-done.21), custom_call_target="tpu_custom_call" | custom-call | flops 234881024 | bytes 2097152 | tf_op jit(solution)/shard_map/near_product/pallas_call | solution.py:147
  159.6 6.1 %near_product.7.refs_4_ = f32[16,96,128]{2,1,0:T(8,128)S(1)} custom-call(s32[16,16]{1,0:T(8,128)S(1)} %add_clamp_fusion.index_ref, s32[16]{0:T(128)S(1)} %copy-done.7, bf16[16,16,32,128]{3,2,1,0:T(8,128)(2,1)S(1)} %copy-done.1, bf16[16,16,32,128]{3,2,1,0:T(8,128)(2,1)} %collective-permute-done.refs_1_, ...), custom_call_target="tpu_custom_call" | custom-call | flops 704643072 | bytes 6291456 | tf_op jit(solution)/shard_map/near_product/pallas_call | solution.py:147
  166.7 9.0 %all-to-all-done.3 = bf16[64,32,256]{2,1,0:T(8,128)(2,1)S(1)} async-done(((bf16[64,32,256]{2,1,0:T(8,128)(2,1)}), bf16[64,32,256]{2,1,0:T(8,128)(2,1)S(1)}, u32[]{:S(2)}, u32[]{:S(2)}) %all-to-all-start.3) | async-done | bytes 1048608 | tf_op jit(solution)/shard_map/all_to_all | solution.py:296
  175.7 5.4 %add_far.3 = bf16[2048,128]{1,0:T(8,128)(2,1)} custom-call(s32[4]{0:T(128)S(1)} %pad_add_fusion.offset_ref, s32[16]{0:T(128)S(1)} %copy-done.7, bf16[16,16,32,128]{3,2,1,0:T(8,128)(2,1)} %refs_0_.11, bf16[16,16,32,128]{3,2,1,0:T(8,128)(2,1)} %collective-permute-done.refs_1_, bf16[16,16,32,128]{3,2,1,0:T(8,128)(2,1)} %collective-permute-done.1.refs_2_, ...), custom_call_target="tpu_custom_call" | custom-call | flops 134217728 | bytes 4194304 | tf_op jit(solution)/shard_map/add_far/pallas_call | solution.py:241
  (79 shorter events, 34.5 us)
Async XLA Ops:
  0.0 29.2 %copy-start = (bf16[16,16,32,128]{3,2,1,0:T(8,128)(2,1)S(1)}, bf16[16,16,32,128]{3,2,1,0:T(8,128)(2,1)}, u32[]{:S(2)}) copy-start(bf16[16,16,32,128]{3,2,1,0:T(8,128)(2,1)} %refs_0_.11) | copy-start | bytes 6291460
  0.0 14.7 %collective-permute-start.5 = (bf16[16,128,128]{2,1,0:T(8,128)(2,1)}, bf16[16,128,128]{2,1,0:T(8,128)(2,1)S(1)}, u32[]{:S(2)}, u32[]{:S(2)}) collective-permute-start(bf16[16,128,128]{2,1,0:T(8,128)(2,1)} %bitcast.24), channel_id=1, source_target_pairs={{0,2},{1,3},{2,0},{3,1},{4,6},{5,7},{6,4},{7,5},{8,10},{9,11},{10,... | collective-permute-start | bytes 1572872 | tf_op jit(solution)/shard_map/ppermute | solution.py:286
  15.4 34.4 %all-to-all-start = ((bf16[64,40,128]{2,1,0:T(8,128)(2,1)}), bf16[64,40,128]{2,1,0:T(8,128)(2,1)S(1)}, u32[]{:S(2)}, u32[]{:S(2)}) async-start(bf16[64,40,128]{2,1,0:T(8,128)(2,1)} %split_blocks.1), calls=%async_computation | async-start | bytes 1310720 | tf_op jit(solution)/shard_map/all_to_all | solution.py:289
  29.2 62.0 %collective-permute-start.1 = (bf16[16,16,32,128]{3,2,1,0:T(8,128)(2,1)S(1)}, bf16[16,16,32,128]{3,2,1,0:T(8,128)(2,1)}, u32[]{:S(2)}, u32[]{:S(2)}) collective-permute-start(bf16[16,16,32,128]{3,2,1,0:T(8,128)(2,1)S(1)} %copy-done), channel_id=1, source_target_pairs={{1,0},{2,1},{3,2},{0,3},{5,4},{6,5},{7,6},{4,7},{9,8},{10,9},{11,1... | collective-permute-start | bytes 6291464 | tf_op jit(solution)/shard_map/ppermute | solution.py:270
  32.0 59.2 %collective-permute-start = (bf16[16,16,32,128]{3,2,1,0:T(8,128)(2,1)S(1)}, bf16[16,16,32,128]{3,2,1,0:T(8,128)(2,1)}, u32[]{:S(2)}, u32[]{:S(2)}) collective-permute-start(bf16[16,16,32,128]{3,2,1,0:T(8,128)(2,1)S(1)} %copy-done), channel_id=1, source_target_pairs={{0,1},{1,2},{2,3},{3,0},{4,5},{5,6},{6,7},{7,4},{8,9},{9,10},{10,1... | collective-permute-start | bytes 6291464 | tf_op jit(solution)/shard_map/ppermute | solution.py:269
  32.9 10.2 %collective-permute-start.3 = (bf16[2,128,128]{2,1,0:T(8,128)(2,1)S(1)}, bf16[2,128,128]{2,1,0:T(8,128)(2,1)S(1)}, u32[]{:S(2)}, u32[]{:S(2)}) collective-permute-start(bf16[2,128,128]{2,1,0:T(8,128)(2,1)S(1)} %bitcast.28), channel_id=1, source_target_pairs={{0,4},{4,8},{8,12},{12,16},{16,20},{20,24},{24,28},{28,32},{32,36}... | collective-permute-start | bytes 196616 | tf_op jit(solution)/shard_map/ppermute | solution.py:290
  36.7 9.8 %collective-permute-start.6 = (bf16[2,128,128]{2,1,0:T(8,128)(2,1)S(1)}, bf16[2,128,128]{2,1,0:T(8,128)(2,1)S(1)}, u32[]{:S(2)}, u32[]{:S(2)}) collective-permute-start(bf16[2,128,128]{2,1,0:T(8,128)(2,1)S(1)} %bitcast.26), channel_id=1, source_target_pairs={{4,0},{8,4},{12,8},{16,12},{20,16},{24,20},{28,24},{32,28},{36,32}... | collective-permute-start | bytes 196616 | tf_op jit(solution)/shard_map/ppermute | solution.py:291
  52.3 13.3 %copy-start.22 = (s32[16,16]{1,0:T(8,128)S(1)}, s32[16,16]{1,0:T(8,128)}, u32[]{:S(2)}) copy-start(s32[16,16]{1,0:T(8,128)} %param.5) | copy-start | bytes 3076
  52.3 35.4 %copy-start.7 = (s32[16]{0:T(128)S(1)}, s32[16]{0:T(128)}, u32[]{:S(2)}) copy-start(s32[16]{0:T(128)} %count_ref.11) | copy-start | bytes 196
  52.3 48.0 %all-to-all-start.1 = ((bf16[64,32,256]{2,1,0:T(8,128)(2,1)}), bf16[64,32,256]{2,1,0:T(8,128)(2,1)S(1)}, u32[]{:S(2)}, u32[]{:S(2)}) async-start(bf16[64,32,256]{2,1,0:T(8,128)(2,1)} %bitcast.20), calls=%async_computation.1 | async-start | bytes 2097152 | tf_op jit(solution)/shard_map/all_to_all | solution.py:296
  59.7 40.6 %collective-permute-start.2 = (bf16[16,2,32,128]{3,2,1,0:T(8,128)(2,1)}, bf16[16,2,32,128]{3,2,1,0:T(8,128)(2,1)}, u32[]{:S(2)}, u32[]{:S(2)}) collective-permute-start(bf16[16,2,32,128]{3,2,1,0:T(8,128)(2,1)} %slice.30), channel_id=1, source_target_pairs={{0,2},{1,3},{2,0},{3,1},{4,6},{5,7},{6,4},{7,5},{8,10},{9,11},{10,... | collective-permute-start | bytes 786440 | tf_op jit(solution)/shard_map/ppermute | solution.py:271
  62.6 23.2 %collective-permute-start.4 = (bf16[2,128,128]{2,1,0:T(8,128)(2,1)S(1)}, bf16[2,128,128]{2,1,0:T(8,128)(2,1)S(1)}, u32[]{:S(2)}, u32[]{:S(2)}) collective-permute-start(bf16[2,128,128]{2,1,0:T(8,128)(2,1)S(1)} %copy-done.11), channel_id=1, source_target_pairs={{0,2},{1,3},{2,0},{3,1},{4,6},{5,7},{6,4},{7,5},{8,10},{9,11},{10,... | collective-permute-start | bytes 196616 | tf_op jit(solution)/shard_map/ppermute | solution.py:299
  62.6 24.4 %collective-permute-start.7 = (bf16[2,128,128]{2,1,0:T(8,128)(2,1)S(1)}, bf16[2,128,128]{2,1,0:T(8,128)(2,1)S(1)}, u32[]{:S(2)}, u32[]{:S(2)}) collective-permute-start(bf16[2,128,128]{2,1,0:T(8,128)(2,1)S(1)} %copy-done.13), channel_id=1, source_target_pairs={{0,2},{1,3},{2,0},{3,1},{4,6},{5,7},{6,4},{7,5},{8,10},{9,11},{10,... | collective-permute-start | bytes 196616 | tf_op jit(solution)/shard_map/ppermute | solution.py:299
  91.2 9.0 %collective-permute-start.8 = (f32[16,32,128]{2,1,0:T(8,128)S(1)}, f32[16,32,128]{2,1,0:T(8,128)}, u32[]{:S(2)}, u32[]{:S(2)}) collective-permute-start(f32[16,32,128]{2,1,0:T(8,128)S(1)} %near_product.4), channel_id=1, source_target_pairs={{0,2},{1,3},{2,0},{3,1},{4,6},{5,7},{6,4},{7,5},{8,10},{9,11},{10,... | collective-permute-start | bytes 786440 | tf_op jit(solution)/shard_map/ppermute | solution.py:305
  106.3 29.3 %copy-start.6 = (bf16[2048,128]{1,0:T(8,128)(2,1)}, bf16[2048,128]{1,0:T(8,128)(2,1)S(1)}, u32[]{:S(2)}) copy-start(bf16[2048,128]{1,0:T(8,128)(2,1)S(1)} %get-tuple-element.23) | copy-start | bytes 1572868
  106.3 29.3 %all-to-all-start.2 = ((bf16[64,32,128]{2,1,0:T(8,128)(2,1)}), bf16[64,32,128]{2,1,0:T(8,128)(2,1)S(1)}, u32[]{:S(2)}, u32[]{:S(2)}) async-start(bf16[64,32,128]{2,1,0:T(8,128)(2,1)} %get-tuple-element.27), calls=%async_computation.2 | async-start | bytes 1048576 | tf_op jit(solution)/shard_map/all_to_all | solution.py:289
  118.0 14.6 %collective-permute-start.11 = (bf16[16,128,128]{2,1,0:T(8,128)(2,1)S(1)}, bf16[16,128,128]{2,1,0:T(8,128)(2,1)S(1)}, u32[]{:S(2)}, u32[]{:S(2)}) collective-permute-start(bf16[16,128,128]{2,1,0:T(8,128)(2,1)S(1)} %bitcast.22), channel_id=1, source_target_pairs={{0,2},{1,3},{2,0},{3,1},{4,6},{5,7},{6,4},{7,5},{8,10},{9,11},{10,... | collective-permute-start | bytes 1572872 | tf_op jit(solution)/shard_map/ppermute | solution.py:286
  119.7 9.0 %collective-permute-start.9 = (bf16[2,128,128]{2,1,0:T(8,128)(2,1)S(1)}, bf16[2,128,128]{2,1,0:T(8,128)(2,1)S(1)}, u32[]{:S(2)}, u32[]{:S(2)}) collective-permute-start(bf16[2,128,128]{2,1,0:T(8,128)(2,1)S(1)} %bitcast.29), channel_id=1, source_target_pairs={{0,4},{4,8},{8,12},{12,16},{16,20},{20,24},{24,28},{28,32},{32,36}... | collective-permute-start | bytes 196616 | tf_op jit(solution)/shard_map/ppermute | solution.py:290
  123.5 8.9 %collective-permute-start.12 = (bf16[2,128,128]{2,1,0:T(8,128)(2,1)S(1)}, bf16[2,128,128]{2,1,0:T(8,128)(2,1)S(1)}, u32[]{:S(2)}, u32[]{:S(2)}) collective-permute-start(bf16[2,128,128]{2,1,0:T(8,128)(2,1)S(1)} %bitcast.27), channel_id=1, source_target_pairs={{4,0},{8,4},{12,8},{16,12},{20,16},{24,20},{28,24},{32,28},{36,32}... | collective-permute-start | bytes 196616 | tf_op jit(solution)/shard_map/ppermute | solution.py:291
  135.6 18.8 %copy-start.1 = (bf16[16,16,32,128]{3,2,1,0:T(8,128)(2,1)S(1)}, bf16[16,16,32,128]{3,2,1,0:T(8,128)(2,1)}, u32[]{:S(2)}) copy-start(bf16[16,16,32,128]{3,2,1,0:T(8,128)(2,1)} %refs_0_.11) | copy-start | bytes 6291460
  137.9 37.8 %all-to-all-start.3 = ((bf16[64,32,256]{2,1,0:T(8,128)(2,1)}), bf16[64,32,256]{2,1,0:T(8,128)(2,1)S(1)}, u32[]{:S(2)}, u32[]{:S(2)}) async-start(bf16[64,32,256]{2,1,0:T(8,128)(2,1)} %bitcast.21), calls=%async_computation.3 | async-start | bytes 2097152 | tf_op jit(solution)/shard_map/all_to_all | solution.py:296
  147.1 5.0 %collective-permute-start.10 = (bf16[2,128,128]{2,1,0:T(8,128)(2,1)S(1)}, bf16[2,128,128]{2,1,0:T(8,128)(2,1)S(1)}, u32[]{:S(2)}, u32[]{:S(2)}) collective-permute-start(bf16[2,128,128]{2,1,0:T(8,128)(2,1)S(1)} %copy-done.15), channel_id=1, source_target_pairs={{0,2},{1,3},{2,0},{3,1},{4,6},{5,7},{6,4},{7,5},{8,10},{9,11},{10,... | collective-permute-start | bytes 196616 | tf_op jit(solution)/shard_map/ppermute | solution.py:299
  148.9 4.9 %collective-permute-start.13 = (bf16[2,128,128]{2,1,0:T(8,128)(2,1)S(1)}, bf16[2,128,128]{2,1,0:T(8,128)(2,1)S(1)}, u32[]{:S(2)}, u32[]{:S(2)}) collective-permute-start(bf16[2,128,128]{2,1,0:T(8,128)(2,1)S(1)} %copy-done.17), channel_id=1, source_target_pairs={{0,2},{1,3},{2,0},{3,1},{4,6},{5,7},{6,4},{7,5},{8,10},{9,11},{10,... | collective-permute-start | bytes 196616 | tf_op jit(solution)/shard_map/ppermute | solution.py:299
  157.9 8.8 %collective-permute-start.14 = (f32[16,32,128]{2,1,0:T(8,128)S(1)}, f32[16,32,128]{2,1,0:T(8,128)}, u32[]{:S(2)}, u32[]{:S(2)}) collective-permute-start(f32[16,32,128]{2,1,0:T(8,128)S(1)} %near_product.6), channel_id=1, source_target_pairs={{0,2},{1,3},{2,0},{3,1},{4,6},{5,7},{6,4},{7,5},{8,10},{9,11},{10,... | collective-permute-start | bytes 786440 | tf_op jit(solution)/shard_map/ppermute | solution.py:305
  (18 other events, 72.7 us)

commit v11 on v9

--- a/solution.py
+++ b/solution.py
@@ -181,9 +181,16 @@
         arrived_ref, q_ref, out_ref = refs[number + len(partials) : number + len(partials) + 3]
         rest = refs[number + len(partials) + 3 :]
         if split:
-            pieces_ref, upper, lower, tiles, sums, sems, wide = rest
+            pieces_ref, upper, lower, landed, q_rows, tiles, sums, sems, wide = rest
         else:
-            upper, lower, tiles, sums, sems = rest
+            upper, lower, landed, q_rows, tiles, sums, sems = rest
+        chunks = [slice(c * owners * far // number, (c + 1) * owners * far // number) for c in range(number)]
+        landings = [
+            pltpu.make_async_copy(arrived_ref.at[rows_of], landed.at[rows_of], sems.at[2, c])
+            for c, rows_of in enumerate(chunks)
+        ]
+        for copy in landings:
+            copy.start()
         copies = [
             pltpu.make_async_copy(
                 ref if part.shape[1] == len(FAR) else ref.at[:, FAR[0] : FAR[-1] + 1], tiles.at[n], sems.at[0, n]
@@ -196,10 +203,13 @@
                 pltpu.make_async_copy(ref, sums.at[:, first : first + part.shape[1]], sems.at[1, n])
             )
             first += part.shape[1]
+        copies.append(pltpu.make_async_copy(q_ref, q_rows, sems.at[3, 0]))
         for copy in copies:
             copy.start()
-        upper[...] = arrived_ref[:, :cols].astype(jnp.float32)
-        lower[...] = arrived_ref[:, cols:].astype(jnp.float32)
+        for copy, rows_of in zip(landings, chunks):
+            copy.wait()
+            upper[rows_of, :] = landed[rows_of, :cols].astype(jnp.float32)
+            lower[rows_of, :] = landed[rows_of, cols:].astype(jnp.float32)
         for copy in copies:
             copy.wait()
         for b in range(blocks):
@@ -216,7 +226,7 @@
             )
             for n in range(number):
                 place = pl.ds(pl.multiple_of(b * size + offset_ref[n], rows), rows)
-                result = 0.99 * total[n * rows : (n + 1) * rows] + q_ref[place, :].astype(jnp.float32)
+                result = 0.99 * total[n * rows : (n + 1) * rows] + q_rows[place, :].astype(jnp.float32)
                 result = result.astype(out_ref.dtype)
                 out_ref[place, :] = result
                 if split:
@@ -229,9 +239,11 @@
     scratch = [
         pltpu.VMEM((owners * far, cols), jnp.float32),
         pltpu.VMEM((owners * far, cols), jnp.float32),
+        pltpu.VMEM(arrived.shape, arrived.dtype),
+        pltpu.VMEM(queries.shape, queries.dtype),
         pltpu.VMEM((number, blocks, len(FAR), rows, size), far_tiles[0].dtype),
         pltpu.VMEM((blocks, size, cols), jnp.float32),
-        pltpu.SemaphoreType.DMA((2, number)),
+        pltpu.SemaphoreType.DMA((4, number)),
     ]
     if split:
         shape = (owners, size // owners * blocks, cols)
@@ -244,7 +256,7 @@
         grid_spec=pltpu.PrefetchScalarGridSpec(
             num_scalar_prefetch=2,
             grid=(1,),
-            in_specs=[HBM] * (number + len(partials)) + [VMEM] * 2,
+            in_specs=[HBM] * (number + len(partials) + 2),
             out_specs=out_specs,
             scratch_shapes=scratch,
         ),

time: 179 us -> 178 us (level)
  no operation moved by 1% of the time
where the time goes in v11:
time: 178 us; the launch traced here: 177 us
  starting transfers between devices  70.9 us (40%)
  waiting for transfers between devices  58.4 us (33%)
  Pallas kernels  34.7 us (19%)
  local copies, waits for them, and re-layouts  12 us (7%)
    ppermute x2, waiting for transfers between devices, on_device(): lax.ppermute(low, 'pb', opposite)  25.8 us
    all_to_all x2, starting transfers between devices, on_device(): held = lax.all_to_all(pieces, 'db', split_axis=0, concat_axis=0, tiled=True)  25.8 us
    pallas_call x4, Pallas kernels, near_product(): pl.pallas_call(kernel, out_shape=jax.ShapeDtypeStruct((blocks, number * r...  19.3 us
    all_to_all x2, starting transfers between devices, on_device(): lax.all_to_all(chosen.reshape(owners, slots, -1), 'db', split_axis=0, con...  15.8 us
    pallas_call x2, Pallas kernels, add_far(): pl.pallas_call(kernel, out_shape=out_shape, grid_spec=pltpu.PrefetchScala...  9.99 us
    all_to_all x2, waiting for transfers between devices, on_device(): lax.all_to_all(chosen.reshape(owners, slots, -1), 'db', split_axis=0, con...  9.28 us
    unnamed x54, local copies, waits for them, and re-layouts  8.84 us
    ppermute x2, waiting for transfers between devices, on_device(): low = lax.ppermute(own[blocks - EDGE:], 'db', up)  8.09 us
  transfers between devices with their start and end apart: 19, of which 11 were waited for; matrix products, arithmetic and copies ran while one was open for 1% of the time, Pallas kernels for 12%

profile of v11, /device:TPU:1, one launch (start us, length us, event | category | flops | bytes accessed | tf_op | source)
XLA Modules:
  0.0 176.5 jit_solution(10502961239896522148)
XLA Ops:
  1.6 2.6 %split_blocks.1 = bf16[64,40,128]{2,1,0:T(8,128)(2,1)} custom-call(bf16[2048,128]{1,0:T(8,128)(2,1)} %refs_7_.3, f32[1,128]{1,0:T(1,128)} %pad.4.digits_ref), custom_call_target="tpu_custom_call" | custom-call | tf_op jit(solution)/shard_map/split_blocks/pallas_call | solution.py:38
  4.2 13.0 %all-to-all-start = ((bf16[64,40,128]{2,1,0:T(8,128)(2,1)}), bf16[64,40,128]{2,1,0:T(8,128)(2,1)S(1)}, u32[]{:S(2)}, u32[]{:S(2)}) async-start(bf16[64,40,128]{2,1,0:T(8,128)(2,1)} %split_blocks.1), calls=%async_computation | async-start | bytes 1310720 | tf_op jit(solution)/shard_map/all_to_all | solution.py:298
  17.2 2.8 %collective-permute-start.1 = (bf16[16,16,32,128]{3,2,1,0:T(8,128)(2,1)S(1)}, bf16[16,16,32,128]{3,2,1,0:T(8,128)(2,1)}, u32[]{:S(2)}, u32[]{:S(2)}) collective-permute-start(bf16[16,16,32,128]{3,2,1,0:T(8,128)(2,1)S(1)} %copy-done), channel_id=1, source_target_pairs={{1,0},{2,1},{3,2},{0,3},{5,4},{6,5},{7,6},{4,7},{9,8},{10,9},{11,1... | collective-permute-start | bytes 6291464 | tf_op jit(solution)/shard_map/ppermute | solution.py:282
  20.9 3.8 %collective-permute-start.3 = (bf16[2,128,128]{2,1,0:T(8,128)(2,1)S(1)}, bf16[2,128,128]{2,1,0:T(8,128)(2,1)S(1)}, u32[]{:S(2)}, u32[]{:S(2)}) collective-permute-start(bf16[2,128,128]{2,1,0:T(8,128)(2,1)S(1)} %bitcast.28), channel_id=1, source_target_pairs={{0,4},{4,8},{8,12},{12,16},{16,20},{20,24},{24,28},{28,32},{32,36}... | collective-permute-start | bytes 196616 | tf_op jit(solution)/shard_map/ppermute | solution.py:299
  26.7 4.4 %collective-permute-done.3.refs_3_.rest_0_ = bf16[2,128,128]{2,1,0:T(8,128)(2,1)S(1)} collective-permute-done((bf16[2,128,128]{2,1,0:T(8,128)(2,1)S(1)}, bf16[2,128,128]{2,1,0:T(8,128)(2,1)S(1)}, u32[]{:S(2)}, u32[]{:S(2)}) %collective-permute-start.3) | collective-permute-done | bytes 65568 | tf_op jit(solution)/shard_map/ppermute | solution.py:299
  31.1 3.4 %collective-permute-done.6.refs_5_.rest_1_ = bf16[2,128,128]{2,1,0:T(8,128)(2,1)S(1)} collective-permute-done((bf16[2,128,128]{2,1,0:T(8,128)(2,1)S(1)}, bf16[2,128,128]{2,1,0:T(8,128)(2,1)S(1)}, u32[]{:S(2)}, u32[]{:S(2)}) %collective-permute-start.6) | collective-permute-done | bytes 65568 | tf_op jit(solution)/shard_map/ppermute | solution.py:300
  34.5 3.3 %all-to-all-done.held_ref = bf16[64,40,128]{2,1,0:T(8,128)(2,1)S(1)} async-done(((bf16[64,40,128]{2,1,0:T(8,128)(2,1)}), bf16[64,40,128]{2,1,0:T(8,128)(2,1)S(1)}, u32[]{:S(2)}, u32[]{:S(2)}) %all-to-all-start) | async-done | bytes 655392 | tf_op jit(solution)/shard_map/all_to_all | solution.py:298
  42.2 6.6 %all-to-all-start.1 = ((bf16[64,32,256]{2,1,0:T(8,128)(2,1)}), bf16[64,32,256]{2,1,0:T(8,128)(2,1)S(1)}, u32[]{:S(2)}, u32[]{:S(2)}) async-start(bf16[64,32,256]{2,1,0:T(8,128)(2,1)} %bitcast.20), calls=%async_computation.1 | async-start | bytes 2097152 | tf_op jit(solution)/shard_map/all_to_all | solution.py:306
  48.9 3.0 %collective-permute-start.5 = (bf16[16,128,128]{2,1,0:T(8,128)(2,1)}, bf16[16,128,128]{2,1,0:T(8,128)(2,1)}, u32[]{:S(2)}, u32[]{:S(2)}) collective-permute-start(bf16[16,128,128]{2,1,0:T(8,128)(2,1)} %bitcast.24), channel_id=1, source_target_pairs={{0,2},{1,3},{2,0},{3,1},{4,6},{5,7},{6,4},{7,5},{8,10},{9,11},{10,... | collective-permute-start | bytes 1572872 | tf_op jit(solution)/shard_map/ppermute | solution.py:301
  52.0 2.9 %collective-permute-start.7 = (bf16[2,128,128]{2,1,0:T(8,128)(2,1)S(1)}, bf16[2,128,128]{2,1,0:T(8,128)(2,1)S(1)}, u32[]{:S(2)}, u32[]{:S(2)}) collective-permute-start(bf16[2,128,128]{2,1,0:T(8,128)(2,1)S(1)} %copy-done.17), channel_id=1, source_target_pairs={{0,2},{1,3},{2,0},{3,1},{4,6},{5,7},{6,4},{7,5},{8,10},{9,11},{10,... | collective-permute-start | bytes 196616 | tf_op jit(solution)/shard_map/ppermute | solution.py:309
  55.6 23.8 %collective-permute-done.4.refs_1_ = bf16[2,128,128]{2,1,0:T(8,128)(2,1)S(1)} collective-permute-done((bf16[2,128,128]{2,1,0:T(8,128)(2,1)S(1)}, bf16[2,128,128]{2,1,0:T(8,128)(2,1)S(1)}, u32[]{:S(2)}, u32[]{:S(2)}) %collective-permute-start.4) | collective-permute-done | bytes 65568 | tf_op jit(solution)/shard_map/ppermute | solution.py:309
  81.7 3.5 %near_product.4 = f32[16,32,128]{2,1,0:T(8,128)S(1)} custom-call(s32[16,16]{1,0:T(8,128)S(1)} %add_clamp_fusion.index_ref, s32[16]{0:T(128)S(1)} %copy-done.11, bf16[16,16,32,128]{3,2,1,0:T(8,128)(2,1)S(1)} %copy-done, bf16[2,128,128]{2,1,0:T(8,128)(2,1)} %copy-done.22, bf16[16,128,128]{2,1,0:T(8,128)(2,1)} %collective-permute-done.5.refs_2_, ...), custom_call_target="tpu_custom_call" | custom-call | flops 234881024 | bytes 2097152 | tf_op jit(solution)/shard_map/near_product/pallas_call | solution.py:147
  86.9 6.1 %near_product.5.refs_4_ = f32[16,96,128]{2,1,0:T(8,128)S(1)} custom-call(s32[16,16]{1,0:T(8,128)S(1)} %add_clamp_fusion.index_ref, s32[16]{0:T(128)S(1)} %copy-done.11, bf16[16,16,32,128]{3,2,1,0:T(8,128)(2,1)S(1)} %copy-done, bf16[16,16,32,128]{3,2,1,0:T(8,128)(2,1)} %collective-permute-done.refs_1_, ...), custom_call_target="tpu_custom_call" | custom-call | flops 704643072 | bytes 6291456 | tf_op jit(solution)/shard_map/near_product/pallas_call | solution.py:147
  94.0 5.3 %add_far.2 = (bf16[2048,128]{1,0:T(8,128)(2,1)S(1)}, bf16[64,32,128]{2,1,0:T(8,128)(2,1)}) custom-call(s32[4]{0:T(128)S(1)} %pad_add_fusion.offset_ref, s32[16]{0:T(128)S(1)} %copy-done.11, bf16[16,16,32,128]{3,2,1,0:T(8,128)(2,1)} %refs_0_.11, bf16[16,16,32,128]{3,2,1,0:T(8,128)(2,1)} %collective-permute-done.refs_1_, ...), custom_call_target="tpu_custom_call" | custom-call | flops 134217728 | bytes 4194304 | tf_op jit(solution)/shard_map/add_far/pallas_call | solution.py:253
  99.3 12.8 %all-to-all-start.2 = ((bf16[64,32,128]{2,1,0:T(8,128)(2,1)}), bf16[64,32,128]{2,1,0:T(8,128)(2,1)S(1)}, u32[]{:S(2)}, u32[]{:S(2)}) async-start(bf16[64,32,128]{2,1,0:T(8,128)(2,1)} %get-tuple-element.23), calls=%async_computation.2 | async-start | bytes 1048576 | tf_op jit(solution)/shard_map/all_to_all | solution.py:298
  113.4 3.8 %collective-permute-start.9 = (bf16[2,128,128]{2,1,0:T(8,128)(2,1)S(1)}, bf16[2,128,128]{2,1,0:T(8,128)(2,1)S(1)}, u32[]{:S(2)}, u32[]{:S(2)}) collective-permute-start(bf16[2,128,128]{2,1,0:T(8,128)(2,1)S(1)} %bitcast.29), channel_id=1, source_target_pairs={{0,4},{4,8},{8,12},{12,16},{16,20},{20,24},{24,28},{28,32},{32,36}... | collective-permute-start | bytes 196616 | tf_op jit(solution)/shard_map/ppermute | solution.py:299
  119.2 3.7 %collective-permute-done.9.refs_3_.rest_0_ = bf16[2,128,128]{2,1,0:T(8,128)(2,1)S(1)} collective-permute-done((bf16[2,128,128]{2,1,0:T(8,128)(2,1)S(1)}, bf16[2,128,128]{2,1,0:T(8,128)(2,1)S(1)}, u32[]{:S(2)}, u32[]{:S(2)}) %collective-permute-start.9) | collective-permute-done | bytes 65568 | tf_op jit(solution)/shard_map/ppermute | solution.py:299
  122.8 3.6 %collective-permute-done.12.refs_5_.rest_1_ = bf16[2,128,128]{2,1,0:T(8,128)(2,1)S(1)} collective-permute-done((bf16[2,128,128]{2,1,0:T(8,128)(2,1)S(1)}, bf16[2,128,128]{2,1,0:T(8,128)(2,1)S(1)}, u32[]{:S(2)}, u32[]{:S(2)}) %collective-permute-start.12) | collective-permute-done | bytes 65568 | tf_op jit(solution)/shard_map/ppermute | solution.py:300
  126.7 3.0 %all-to-all-done.2.held_ref = bf16[64,32,128]{2,1,0:T(8,128)(2,1)S(1)} async-done(((bf16[64,32,128]{2,1,0:T(8,128)(2,1)}), bf16[64,32,128]{2,1,0:T(8,128)(2,1)S(1)}, u32[]{:S(2)}, u32[]{:S(2)}) %all-to-all-start.2) | async-done | bytes 524320 | tf_op jit(solution)/shard_map/all_to_all | solution.py:298
  133.9 9.2 %all-to-all-start.3 = ((bf16[64,32,256]{2,1,0:T(8,128)(2,1)}), bf16[64,32,256]{2,1,0:T(8,128)(2,1)S(1)}, u32[]{:S(2)}, u32[]{:S(2)}) async-start(bf16[64,32,256]{2,1,0:T(8,128)(2,1)} %bitcast.21), calls=%async_computation.3 | async-start | bytes 2097152 | tf_op jit(solution)/shard_map/all_to_all | solution.py:306
  150.4 3.5 %near_product.6 = f32[16,32,128]{2,1,0:T(8,128)S(1)} custom-call(s32[16,16]{1,0:T(8,128)S(1)} %add_clamp_fusion.index_ref, s32[16]{0:T(128)S(1)} %copy-done.11, bf16[16,16,32,128]{3,2,1,0:T(8,128)(2,1)S(1)} %copy-done.1, bf16[2,128,128]{2,1,0:T(8,128)(2,1)} %copy-done.24, bf16[16,128,128]{2,1,0:T(8,128)(2,1)} %copy-done.12, bf16[2,128,128]{2,1,0:T(8,128)(2,1)} %copy-done.25), custom_call_target="tpu_custom_call" | custom-call | flops 234881024 | bytes 2097152 | tf_op jit(solution)/shard_map/near_product/pallas_call | solution.py:147
  155.3 6.1 %near_product.7.refs_4_ = f32[16,96,128]{2,1,0:T(8,128)S(1)} custom-call(s32[16,16]{1,0:T(8,128)S(1)} %add_clamp_fusion.index_ref, s32[16]{0:T(128)S(1)} %copy-done.11, bf16[16,16,32,128]{3,2,1,0:T(8,128)(2,1)S(1)} %copy-done.1, bf16[16,16,32,128]{3,2,1,0:T(8,128)(2,1)} %collective-permute-done.refs_1_, ...), custom_call_target="tpu_custom_call" | custom-call | flops 704643072 | bytes 6291456 | tf_op jit(solution)/shard_map/near_product/pallas_call | solution.py:147
  162.4 9.3 %all-to-all-done.3 = bf16[64,32,256]{2,1,0:T(8,128)(2,1)S(1)} async-done(((bf16[64,32,256]{2,1,0:T(8,128)(2,1)}), bf16[64,32,256]{2,1,0:T(8,128)(2,1)S(1)}, u32[]{:S(2)}, u32[]{:S(2)}) %all-to-all-start.3) | async-done | bytes 1048608 | tf_op jit(solution)/shard_map/all_to_all | solution.py:306
  171.7 4.7 %add_far.3 = bf16[2048,128]{1,0:T(8,128)(2,1)} custom-call(s32[4]{0:T(128)S(1)} %pad_add_fusion.offset_ref, s32[16]{0:T(128)S(1)} %copy-done.11, bf16[16,16,32,128]{3,2,1,0:T(8,128)(2,1)} %refs_0_.11, bf16[16,16,32,128]{3,2,1,0:T(8,128)(2,1)} %collective-permute-done.refs_1_, bf16[16,16,32,128]{3,2,1,0:T(8,128)(2,1)} %collective-permute-done.1.refs_2_, ...), custom_call_target="tpu_custom_call" | custom-call | flops 134217728 | bytes 4194304 | tf_op jit(solution)/shard_map/add_far/pallas_call | solution.py:253
  (87 shorter events, 31.7 us)
Async XLA Ops:
  0.0 17.2 %copy-start = (bf16[16,16,32,128]{3,2,1,0:T(8,128)(2,1)S(1)}, bf16[16,16,32,128]{3,2,1,0:T(8,128)(2,1)}, u32[]{:S(2)}) copy-start(bf16[16,16,32,128]{3,2,1,0:T(8,128)(2,1)} %refs_0_.11) | copy-start | bytes 6291460
  4.2 33.6 %all-to-all-start = ((bf16[64,40,128]{2,1,0:T(8,128)(2,1)}), bf16[64,40,128]{2,1,0:T(8,128)(2,1)S(1)}, u32[]{:S(2)}, u32[]{:S(2)}) async-start(bf16[64,40,128]{2,1,0:T(8,128)(2,1)} %split_blocks.1), calls=%async_computation | async-start | bytes 1310720 | tf_op jit(solution)/shard_map/all_to_all | solution.py:298
  17.2 68.0 %collective-permute-start.1 = (bf16[16,16,32,128]{3,2,1,0:T(8,128)(2,1)S(1)}, bf16[16,16,32,128]{3,2,1,0:T(8,128)(2,1)}, u32[]{:S(2)}, u32[]{:S(2)}) collective-permute-start(bf16[16,16,32,128]{3,2,1,0:T(8,128)(2,1)S(1)} %copy-done), channel_id=1, source_target_pairs={{1,0},{2,1},{3,2},{0,3},{5,4},{6,5},{7,6},{4,7},{9,8},{10,9},{11,1... | collective-permute-start | bytes 6291464 | tf_op jit(solution)/shard_map/ppermute | solution.py:282
  20.0 65.2 %collective-permute-start = (bf16[16,16,32,128]{3,2,1,0:T(8,128)(2,1)S(1)}, bf16[16,16,32,128]{3,2,1,0:T(8,128)(2,1)}, u32[]{:S(2)}, u32[]{:S(2)}) collective-permute-start(bf16[16,16,32,128]{3,2,1,0:T(8,128)(2,1)S(1)} %copy-done), channel_id=1, source_target_pairs={{0,1},{1,2},{2,3},{3,0},{4,5},{5,6},{6,7},{7,4},{8,9},{9,10},{10,1... | collective-permute-start | bytes 6291464 | tf_op jit(solution)/shard_map/ppermute | solution.py:281
  20.9 10.2 %collective-permute-start.3 = (bf16[2,128,128]{2,1,0:T(8,128)(2,1)S(1)}, bf16[2,128,128]{2,1,0:T(8,128)(2,1)S(1)}, u32[]{:S(2)}, u32[]{:S(2)}) collective-permute-start(bf16[2,128,128]{2,1,0:T(8,128)(2,1)S(1)} %bitcast.28), channel_id=1, source_target_pairs={{0,4},{4,8},{8,12},{12,16},{16,20},{20,24},{24,28},{28,32},{32,36}... | collective-permute-start | bytes 196616 | tf_op jit(solution)/shard_map/ppermute | solution.py:299
  24.7 9.8 %collective-permute-start.6 = (bf16[2,128,128]{2,1,0:T(8,128)(2,1)S(1)}, bf16[2,128,128]{2,1,0:T(8,128)(2,1)S(1)}, u32[]{:S(2)}, u32[]{:S(2)}) collective-permute-start(bf16[2,128,128]{2,1,0:T(8,128)(2,1)S(1)} %bitcast.26), channel_id=1, source_target_pairs={{4,0},{8,4},{12,8},{16,12},{20,16},{24,20},{28,24},{32,28},{36,32}... | collective-permute-start | bytes 196616 | tf_op jit(solution)/shard_map/ppermute | solution.py:300
  39.8 15.0 %copy-start.26 = (s32[16,16]{1,0:T(8,128)S(1)}, s32[16,16]{1,0:T(8,128)}, u32[]{:S(2)}) copy-start(s32[16,16]{1,0:T(8,128)} %param.5) | copy-start | bytes 3076
  42.2 39.4 %copy-start.11 = (s32[16]{0:T(128)S(1)}, s32[16]{0:T(128)}, u32[]{:S(2)}) copy-start(s32[16]{0:T(128)} %count_ref.11) | copy-start | bytes 196
  42.2 51.7 %all-to-all-start.1 = ((bf16[64,32,256]{2,1,0:T(8,128)(2,1)}), bf16[64,32,256]{2,1,0:T(8,128)(2,1)S(1)}, u32[]{:S(2)}, u32[]{:S(2)}) async-start(bf16[64,32,256]{2,1,0:T(8,128)(2,1)} %bitcast.20), calls=%async_computation.1 | async-start | bytes 2097152 | tf_op jit(solution)/shard_map/all_to_all | solution.py:306
  48.9 32.2 %collective-permute-start.5 = (bf16[16,128,128]{2,1,0:T(8,128)(2,1)}, bf16[16,128,128]{2,1,0:T(8,128)(2,1)}, u32[]{:S(2)}, u32[]{:S(2)}) collective-permute-start(bf16[16,128,128]{2,1,0:T(8,128)(2,1)} %bitcast.24), channel_id=1, source_target_pairs={{0,2},{1,3},{2,0},{3,1},{4,6},{5,7},{6,4},{7,5},{8,10},{9,11},{10,... | collective-permute-start | bytes 1572872 | tf_op jit(solution)/shard_map/ppermute | solution.py:301
  51.9 27.5 %collective-permute-start.4 = (bf16[2,128,128]{2,1,0:T(8,128)(2,1)S(1)}, bf16[2,128,128]{2,1,0:T(8,128)(2,1)S(1)}, u32[]{:S(2)}, u32[]{:S(2)}) collective-permute-start(bf16[2,128,128]{2,1,0:T(8,128)(2,1)S(1)} %copy-done.15), channel_id=1, source_target_pairs={{0,2},{1,3},{2,0},{3,1},{4,6},{5,7},{6,4},{7,5},{8,10},{9,11},{10,... | collective-permute-start | bytes 196616 | tf_op jit(solution)/shard_map/ppermute | solution.py:309
  52.0 29.0 %collective-permute-start.7 = (bf16[2,128,128]{2,1,0:T(8,128)(2,1)S(1)}, bf16[2,128,128]{2,1,0:T(8,128)(2,1)S(1)}, u32[]{:S(2)}, u32[]{:S(2)}) collective-permute-start(bf16[2,128,128]{2,1,0:T(8,128)(2,1)S(1)} %copy-done.17), channel_id=1, source_target_pairs={{0,2},{1,3},{2,0},{3,1},{4,6},{5,7},{6,4},{7,5},{8,10},{9,11},{10,... | collective-permute-start | bytes 196616 | tf_op jit(solution)/shard_map/ppermute | solution.py:309
  79.4 14.5 %collective-permute-start.2 = (bf16[16,2,32,128]{3,2,1,0:T(8,128)(2,1)}, bf16[16,2,32,128]{3,2,1,0:T(8,128)(2,1)}, u32[]{:S(2)}, u32[]{:S(2)}) collective-permute-start(bf16[16,2,32,128]{3,2,1,0:T(8,128)(2,1)} %slice.30), channel_id=1, source_target_pairs={{0,2},{1,3},{2,0},{3,1},{4,6},{5,7},{6,4},{7,5},{8,10},{9,11},{10,... | collective-permute-start | bytes 786440 | tf_op jit(solution)/shard_map/ppermute | solution.py:283
  85.2 8.8 %collective-permute-start.8 = (f32[16,32,128]{2,1,0:T(8,128)S(1)}, f32[16,32,128]{2,1,0:T(8,128)}, u32[]{:S(2)}, u32[]{:S(2)}) collective-permute-start(f32[16,32,128]{2,1,0:T(8,128)S(1)} %near_product.4), channel_id=1, source_target_pairs={{0,2},{1,3},{2,0},{3,1},{4,6},{5,7},{6,4},{7,5},{8,10},{9,11},{10,... | collective-permute-start | bytes 786440 | tf_op jit(solution)/shard_map/ppermute | solution.py:315
  99.3 30.4 %copy-start.6 = (bf16[2048,128]{1,0:T(8,128)(2,1)}, bf16[2048,128]{1,0:T(8,128)(2,1)S(1)}, u32[]{:S(2)}) copy-start(bf16[2048,128]{1,0:T(8,128)(2,1)S(1)} %get-tuple-element.19) | copy-start | bytes 1572868
  99.3 30.4 %all-to-all-start.2 = ((bf16[64,32,128]{2,1,0:T(8,128)(2,1)}), bf16[64,32,128]{2,1,0:T(8,128)(2,1)S(1)}, u32[]{:S(2)}, u32[]{:S(2)}) async-start(bf16[64,32,128]{2,1,0:T(8,128)(2,1)} %get-tuple-element.23), calls=%async_computation.2 | async-start | bytes 1048576 | tf_op jit(solution)/shard_map/all_to_all | solution.py:298
  112.1 14.6 %collective-permute-start.11 = (bf16[16,128,128]{2,1,0:T(8,128)(2,1)S(1)}, bf16[16,128,128]{2,1,0:T(8,128)(2,1)S(1)}, u32[]{:S(2)}, u32[]{:S(2)}) collective-permute-start(bf16[16,128,128]{2,1,0:T(8,128)(2,1)S(1)} %bitcast.22), channel_id=1, source_target_pairs={{0,2},{1,3},{2,0},{3,1},{4,6},{5,7},{6,4},{7,5},{8,10},{9,11},{10,... | collective-permute-start | bytes 1572872 | tf_op jit(solution)/shard_map/ppermute | solution.py:301
  113.4 9.4 %collective-permute-start.9 = (bf16[2,128,128]{2,1,0:T(8,128)(2,1)S(1)}, bf16[2,128,128]{2,1,0:T(8,128)(2,1)S(1)}, u32[]{:S(2)}, u32[]{:S(2)}) collective-permute-start(bf16[2,128,128]{2,1,0:T(8,128)(2,1)S(1)} %bitcast.29), channel_id=1, source_target_pairs={{0,4},{4,8},{8,12},{12,16},{16,20},{20,24},{24,28},{28,32},{32,36}... | collective-permute-start | bytes 196616 | tf_op jit(solution)/shard_map/ppermute | solution.py:299
  117.2 9.3 %collective-permute-start.12 = (bf16[2,128,128]{2,1,0:T(8,128)(2,1)S(1)}, bf16[2,128,128]{2,1,0:T(8,128)(2,1)S(1)}, u32[]{:S(2)}, u32[]{:S(2)}) collective-permute-start(bf16[2,128,128]{2,1,0:T(8,128)(2,1)S(1)} %bitcast.27), channel_id=1, source_target_pairs={{4,0},{8,4},{12,8},{16,12},{20,16},{24,20},{28,24},{32,28},{36,32}... | collective-permute-start | bytes 196616 | tf_op jit(solution)/shard_map/ppermute | solution.py:300
  131.5 18.8 %copy-start.1 = (bf16[16,16,32,128]{3,2,1,0:T(8,128)(2,1)S(1)}, bf16[16,16,32,128]{3,2,1,0:T(8,128)(2,1)}, u32[]{:S(2)}) copy-start(bf16[16,16,32,128]{3,2,1,0:T(8,128)(2,1)} %refs_0_.11) | copy-start | bytes 6291460
  133.9 37.8 %all-to-all-start.3 = ((bf16[64,32,256]{2,1,0:T(8,128)(2,1)}), bf16[64,32,256]{2,1,0:T(8,128)(2,1)S(1)}, u32[]{:S(2)}, u32[]{:S(2)}) async-start(bf16[64,32,256]{2,1,0:T(8,128)(2,1)} %bitcast.21), calls=%async_computation.3 | async-start | bytes 2097152 | tf_op jit(solution)/shard_map/all_to_all | solution.py:306
  143.1 5.0 %collective-permute-start.10 = (bf16[2,128,128]{2,1,0:T(8,128)(2,1)S(1)}, bf16[2,128,128]{2,1,0:T(8,128)(2,1)S(1)}, u32[]{:S(2)}, u32[]{:S(2)}) collective-permute-start(bf16[2,128,128]{2,1,0:T(8,128)(2,1)S(1)} %copy-done.19), channel_id=1, source_target_pairs={{0,2},{1,3},{2,0},{3,1},{4,6},{5,7},{6,4},{7,5},{8,10},{9,11},{10,... | collective-permute-start | bytes 196616 | tf_op jit(solution)/shard_map/ppermute | solution.py:309
  144.4 5.3 %collective-permute-start.13 = (bf16[2,128,128]{2,1,0:T(8,128)(2,1)S(1)}, bf16[2,128,128]{2,1,0:T(8,128)(2,1)S(1)}, u32[]{:S(2)}, u32[]{:S(2)}) collective-permute-start(bf16[2,128,128]{2,1,0:T(8,128)(2,1)S(1)} %copy-done.21), channel_id=1, source_target_pairs={{0,2},{1,3},{2,0},{3,1},{4,6},{5,7},{6,4},{7,5},{8,10},{9,11},{10,... | collective-permute-start | bytes 196616 | tf_op jit(solution)/shard_map/ppermute | solution.py:309
  153.9 8.5 %collective-permute-start.14 = (f32[16,32,128]{2,1,0:T(8,128)S(1)}, f32[16,32,128]{2,1,0:T(8,128)S(1)}, u32[]{:S(2)}, u32[]{:S(2)}) collective-permute-start(f32[16,32,128]{2,1,0:T(8,128)S(1)} %near_product.6), channel_id=1, source_target_pairs={{0,2},{1,3},{2,0},{3,1},{4,6},{5,7},{6,4},{7,5},{8,10},{9,11},{10,... | collective-permute-start | bytes 786440 | tf_op jit(solution)/shard_map/ppermute | solution.py:315
  (22 other events, 85.2 us)

commit v12 on v11

--- a/solution.py
+++ b/solution.py
@@ -55,18 +55,30 @@
     def kernel(held_ref, *rest):
         rest = rest[len(after) :]
         if wanted is None:
-            out_ref, wanted_out, flat = rest
-            digits = held_ref[:, parts * blocks :, :].astype(jnp.float32)[:, 0, :].T
+            out_ref, wanted_out, flat, tail, sems = rest
+        else:
+            wanted_ref, out_ref, flat, tail, sems = rest
+        copies = [
+            pltpu.make_async_copy(
+                held_ref.at[:, part * blocks : (part + 1) * blocks],
+                flat.at[:, :, part * cols : (part + 1) * cols],
+                sems.at[part],
+            )
+            for part in range(parts)
+        ]
+        for copy in copies:
+            copy.start()
+        if wanted is None:
+            copy = pltpu.make_async_copy(held_ref.at[:, parts * blocks :], tail, sems.at[parts])
+            copy.start()
+            copy.wait()
+            digits = tail[...].astype(jnp.float32)[:, 0, :].T
             ids = (digits[:slots] * BASE + digits[slots : 2 * slots]).astype(jnp.int32)
             wanted_out[...] = ids
         else:
-            wanted_ref, out_ref, flat = rest
             ids = wanted_ref[...]
-        for s in range(devices):
-            for part in range(parts):
-                flat[s * blocks : (s + 1) * blocks, part * cols : (part + 1) * cols] = held_ref[
-                    s, part * blocks : (part + 1) * blocks, :
-                ]
+        for copy in copies:
+            copy.wait()
         column = lax.broadcasted_iota(jnp.int32, (slots, block_total), 1)
         for first in range(0, devices, group):
             hits = [
@@ -76,7 +88,7 @@
                 for d in range(first, first + group)
             ]
             out_ref[first * slots : (first + group) * slots, :] = jnp.dot(
-                jnp.concatenate(hits, axis=0), flat[...], preferred_element_type=jnp.float32
+                jnp.concatenate(hits, axis=0), flat[...].reshape(block_total, -1), preferred_element_type=jnp.float32
             ).astype(out_ref.dtype)
 
     out_shape = [jax.ShapeDtypeStruct((devices * slots, parts * cols), held.dtype)]
@@ -86,15 +98,19 @@
     return pl.pallas_call(
         kernel,
         out_shape=out_shape,
-        in_specs=[VMEM] + [HBM] * len(after) + [VMEM] * len(operands),
+        in_specs=[HBM] * (1 + len(after)) + [VMEM] * len(operands),
         out_specs=[VMEM] * len(out_shape),
-        scratch_shapes=[pltpu.VMEM((block_total, parts * cols), held.dtype)],
+        scratch_shapes=[
+            pltpu.VMEM((devices, blocks, parts * cols), held.dtype),
+            pltpu.VMEM((devices, 8, cols), held.dtype),
+            pltpu.SemaphoreType.DMA((parts + 1,)),
+        ],
         compiler_params=pltpu.CompilerParams(vmem_limit_bytes=LIMIT),
         cost_estimate=pl.CostEstimate(
             flops=2 * devices * slots * block_total * parts * cols, bytes_accessed=2 << 20, transcendentals=0
         ),
         name="select_pieces",
-    )(held, *in_hbm(after), *operands)
+    )(*in_hbm([held, *after]), *operands)
 
 
 def near_product(near_index, counts, quarters, reach):

time: 178 us -> 178 us (level)
  local copies, waits for them, and re-layouts: 12 us -> 8.99 us
  Pallas kernels: 34.7 us -> 36.9 us
    unnamed x54 -> x48, local copies, waits for them, and re-layouts: 8.84 us -> 5.85 us
    pallas_call x2, Pallas kernels: 2.78 us -> 5.02 us  [select_pieces(): pl.pallas_call(kernel, out_shape=out_shape, in_specs=[HBM] * (1 + len(aft...]
where the time goes in v12:
time: 178 us; the launch traced here: 177 us
  starting transfers between devices  71 us (40%)
  waiting for transfers between devices  59.3 us (33%)
  Pallas kernels  36.9 us (21%)
  local copies, waits for them, and re-layouts  8.99 us (5%)
    ppermute x2, waiting for transfers between devices, on_device(): lax.ppermute(low, 'pb', opposite)  26.8 us
    all_to_all x2, starting transfers between devices, on_device(): held = lax.all_to_all(pieces, 'db', split_axis=0, concat_axis=0, tiled=True)  26 us
    pallas_call x4, Pallas kernels, near_product(): pl.pallas_call(kernel, out_shape=jax.ShapeDtypeStruct((blocks, number * r...  19.3 us
    all_to_all x2, starting transfers between devices, on_device(): lax.all_to_all(chosen.reshape(owners, slots, -1), 'db', split_axis=0, con...  15.7 us
    pallas_call x2, Pallas kernels, add_far(): pl.pallas_call(kernel, out_shape=out_shape, grid_spec=pltpu.PrefetchScala...  9.99 us
    all_to_all x2, waiting for transfers between devices, on_device(): lax.all_to_all(chosen.reshape(owners, slots, -1), 'db', split_axis=0, con...  9.3 us
    ppermute x2, waiting for transfers between devices, on_device(): low = lax.ppermute(own[blocks - EDGE:], 'db', up)  7.93 us
    ppermute x2, starting transfers between devices, on_device(): low = lax.ppermute(own[blocks - EDGE:], 'db', up)  7.64 us
  transfers between devices with their start and end apart: 19, of which 11 were waited for; matrix products, arithmetic and copies ran while one was open for 1% of the time, Pallas kernels for 12%

profile of v12, /device:TPU:1, one launch (start us, length us, event | category | flops | bytes accessed | tf_op | source)
XLA Modules:
  0.0 176.8 jit_solution(2414318526135764636)
XLA Ops:
  1.6 2.6 %split_blocks.1 = bf16[64,40,128]{2,1,0:T(8,128)(2,1)} custom-call(bf16[2048,128]{1,0:T(8,128)(2,1)} %refs_7_.3, f32[1,128]{1,0:T(1,128)} %pad.4.digits_ref), custom_call_target="tpu_custom_call" | custom-call | tf_op jit(solution)/shard_map/split_blocks/pallas_call | solution.py:38
  4.2 13.2 %all-to-all-start = ((bf16[64,40,128]{2,1,0:T(8,128)(2,1)}), bf16[64,40,128]{2,1,0:T(8,128)(2,1)}, u32[]{:S(2)}, u32[]{:S(2)}) async-start(bf16[64,40,128]{2,1,0:T(8,128)(2,1)} %split_blocks.1), calls=%async_computation | async-start | bytes 1310720 | tf_op jit(solution)/shard_map/all_to_all | solution.py:314
  17.3 2.8 %collective-permute-start.1 = (bf16[16,16,32,128]{3,2,1,0:T(8,128)(2,1)S(1)}, bf16[16,16,32,128]{3,2,1,0:T(8,128)(2,1)}, u32[]{:S(2)}, u32[]{:S(2)}) collective-permute-start(bf16[16,16,32,128]{3,2,1,0:T(8,128)(2,1)S(1)} %copy-done), channel_id=1, source_target_pairs={{1,0},{2,1},{3,2},{0,3},{5,4},{6,5},{7,6},{4,7},{9,8},{10,9},{11,1... | collective-permute-start | bytes 6291464 | tf_op jit(solution)/shard_map/ppermute | solution.py:298
  21.0 3.8 %collective-permute-start.3 = (bf16[2,128,128]{2,1,0:T(8,128)(2,1)S(1)}, bf16[2,128,128]{2,1,0:T(8,128)(2,1)S(1)}, u32[]{:S(2)}, u32[]{:S(2)}) collective-permute-start(bf16[2,128,128]{2,1,0:T(8,128)(2,1)S(1)} %bitcast.28), channel_id=1, source_target_pairs={{0,4},{4,8},{8,12},{12,16},{16,20},{20,24},{24,28},{28,32},{32,36}... | collective-permute-start | bytes 196616 | tf_op jit(solution)/shard_map/ppermute | solution.py:315
  26.8 4.2 %collective-permute-done.3.refs_3_.rest_0_ = bf16[2,128,128]{2,1,0:T(8,128)(2,1)S(1)} collective-permute-done((bf16[2,128,128]{2,1,0:T(8,128)(2,1)S(1)}, bf16[2,128,128]{2,1,0:T(8,128)(2,1)S(1)}, u32[]{:S(2)}, u32[]{:S(2)}) %collective-permute-start.3) | collective-permute-done | bytes 65568 | tf_op jit(solution)/shard_map/ppermute | solution.py:315
  31.1 3.4 %collective-permute-done.6.refs_5_.rest_1_ = bf16[2,128,128]{2,1,0:T(8,128)(2,1)S(1)} collective-permute-done((bf16[2,128,128]{2,1,0:T(8,128)(2,1)S(1)}, bf16[2,128,128]{2,1,0:T(8,128)(2,1)S(1)}, u32[]{:S(2)}, u32[]{:S(2)}) %collective-permute-start.6) | collective-permute-done | bytes 65568 | tf_op jit(solution)/shard_map/ppermute | solution.py:316
  34.5 3.4 %all-to-all-done.held_ref = bf16[64,40,128]{2,1,0:T(8,128)(2,1)} async-done(((bf16[64,40,128]{2,1,0:T(8,128)(2,1)}), bf16[64,40,128]{2,1,0:T(8,128)(2,1)}, u32[]{:S(2)}, u32[]{:S(2)}) %all-to-all-start) | async-done | bytes 655392 | tf_op jit(solution)/shard_map/all_to_all | solution.py:314
  41.5 6.5 %all-to-all-start.1 = ((bf16[64,32,256]{2,1,0:T(8,128)(2,1)}), bf16[64,32,256]{2,1,0:T(8,128)(2,1)S(1)}, u32[]{:S(2)}, u32[]{:S(2)}) async-start(bf16[64,32,256]{2,1,0:T(8,128)(2,1)} %bitcast.20), calls=%async_computation.1 | async-start | bytes 2097152 | tf_op jit(solution)/shard_map/all_to_all | solution.py:322
  48.0 3.0 %collective-permute-start.5 = (bf16[16,128,128]{2,1,0:T(8,128)(2,1)}, bf16[16,128,128]{2,1,0:T(8,128)(2,1)}, u32[]{:S(2)}, u32[]{:S(2)}) collective-permute-start(bf16[16,128,128]{2,1,0:T(8,128)(2,1)} %bitcast.24), channel_id=1, source_target_pairs={{0,2},{1,3},{2,0},{3,1},{4,6},{5,7},{6,4},{7,5},{8,10},{9,11},{10,... | collective-permute-start | bytes 1572872 | tf_op jit(solution)/shard_map/ppermute | solution.py:317
  51.1 2.9 %collective-permute-start.7 = (bf16[2,128,128]{2,1,0:T(8,128)(2,1)S(1)}, bf16[2,128,128]{2,1,0:T(8,128)(2,1)S(1)}, u32[]{:S(2)}, u32[]{:S(2)}) collective-permute-start(bf16[2,128,128]{2,1,0:T(8,128)(2,1)S(1)} %copy-done.14), channel_id=1, source_target_pairs={{0,2},{1,3},{2,0},{3,1},{4,6},{5,7},{6,4},{7,5},{8,10},{9,11},{10,... | collective-permute-start | bytes 196616 | tf_op jit(solution)/shard_map/ppermute | solution.py:325
  54.7 24.8 %collective-permute-done.4.refs_1_ = bf16[2,128,128]{2,1,0:T(8,128)(2,1)S(1)} collective-permute-done((bf16[2,128,128]{2,1,0:T(8,128)(2,1)S(1)}, bf16[2,128,128]{2,1,0:T(8,128)(2,1)S(1)}, u32[]{:S(2)}, u32[]{:S(2)}) %collective-permute-start.4) | collective-permute-done | bytes 65568 | tf_op jit(solution)/shard_map/ppermute | solution.py:325
  81.7 3.5 %near_product.4 = f32[16,32,128]{2,1,0:T(8,128)S(1)} custom-call(s32[16,16]{1,0:T(8,128)S(1)} %add_clamp_fusion.index_ref, s32[16]{0:T(128)S(1)} %copy-done.7, bf16[16,16,32,128]{3,2,1,0:T(8,128)(2,1)S(1)} %copy-done, bf16[2,128,128]{2,1,0:T(8,128)(2,1)} %copy-done.19, bf16[16,128,128]{2,1,0:T(8,128)(2,1)} %collective-permute-done.5.refs_2_, ...), custom_call_target="tpu_custom_call" | custom-call | flops 234881024 | bytes 2097152 | tf_op jit(solution)/shard_map/near_product/pallas_call | solution.py:163
  87.0 6.1 %near_product.5.refs_4_ = f32[16,96,128]{2,1,0:T(8,128)S(1)} custom-call(s32[16,16]{1,0:T(8,128)S(1)} %add_clamp_fusion.index_ref, s32[16]{0:T(128)S(1)} %copy-done.7, bf16[16,16,32,128]{3,2,1,0:T(8,128)(2,1)S(1)} %copy-done, bf16[16,16,32,128]{3,2,1,0:T(8,128)(2,1)} %collective-permute-done.refs_1_, ...), custom_call_target="tpu_custom_call" | custom-call | flops 704643072 | bytes 6291456 | tf_op jit(solution)/shard_map/near_product/pallas_call | solution.py:163
  94.0 5.3 %add_far.2 = (bf16[2048,128]{1,0:T(8,128)(2,1)S(1)}, bf16[64,32,128]{2,1,0:T(8,128)(2,1)}) custom-call(s32[4]{0:T(128)S(1)} %pad_add_fusion.offset_ref, s32[16]{0:T(128)S(1)} %copy-done.7, bf16[16,16,32,128]{3,2,1,0:T(8,128)(2,1)} %refs_0_.11, bf16[16,16,32,128]{3,2,1,0:T(8,128)(2,1)} %collective-permute-done.refs_1_, ...), custom_call_target="tpu_custom_call" | custom-call | flops 134217728 | bytes 4194304 | tf_op jit(solution)/shard_map/add_far/pallas_call | solution.py:269
  99.3 12.9 %all-to-all-start.2 = ((bf16[64,32,128]{2,1,0:T(8,128)(2,1)}), bf16[64,32,128]{2,1,0:T(8,128)(2,1)S(1)}, u32[]{:S(2)}, u32[]{:S(2)}) async-start(bf16[64,32,128]{2,1,0:T(8,128)(2,1)} %get-tuple-element.23), calls=%async_computation.2 | async-start | bytes 1048576 | tf_op jit(solution)/shard_map/all_to_all | solution.py:314
  113.5 3.8 %collective-permute-start.9 = (bf16[2,128,128]{2,1,0:T(8,128)(2,1)S(1)}, bf16[2,128,128]{2,1,0:T(8,128)(2,1)S(1)}, u32[]{:S(2)}, u32[]{:S(2)}) collective-permute-start(bf16[2,128,128]{2,1,0:T(8,128)(2,1)S(1)} %bitcast.29), channel_id=1, source_target_pairs={{0,4},{4,8},{8,12},{12,16},{16,20},{20,24},{24,28},{28,32},{32,36}... | collective-permute-start | bytes 196616 | tf_op jit(solution)/shard_map/ppermute | solution.py:315
  119.3 3.7 %collective-permute-done.9.refs_3_.rest_0_ = bf16[2,128,128]{2,1,0:T(8,128)(2,1)S(1)} collective-permute-done((bf16[2,128,128]{2,1,0:T(8,128)(2,1)S(1)}, bf16[2,128,128]{2,1,0:T(8,128)(2,1)S(1)}, u32[]{:S(2)}, u32[]{:S(2)}) %collective-permute-start.9) | collective-permute-done | bytes 65568 | tf_op jit(solution)/shard_map/ppermute | solution.py:315
  123.0 3.6 %collective-permute-done.12.refs_5_.rest_1_ = bf16[2,128,128]{2,1,0:T(8,128)(2,1)S(1)} collective-permute-done((bf16[2,128,128]{2,1,0:T(8,128)(2,1)S(1)}, bf16[2,128,128]{2,1,0:T(8,128)(2,1)S(1)}, u32[]{:S(2)}, u32[]{:S(2)}) %collective-permute-start.12) | collective-permute-done | bytes 65568 | tf_op jit(solution)/shard_map/ppermute | solution.py:316
  126.9 3.0 %all-to-all-done.2.held_ref = bf16[64,32,128]{2,1,0:T(8,128)(2,1)S(1)} async-done(((bf16[64,32,128]{2,1,0:T(8,128)(2,1)}), bf16[64,32,128]{2,1,0:T(8,128)(2,1)S(1)}, u32[]{:S(2)}, u32[]{:S(2)}) %all-to-all-start.2) | async-done | bytes 524320 | tf_op jit(solution)/shard_map/all_to_all | solution.py:314
  134.2 9.2 %all-to-all-start.3 = ((bf16[64,32,256]{2,1,0:T(8,128)(2,1)}), bf16[64,32,256]{2,1,0:T(8,128)(2,1)S(1)}, u32[]{:S(2)}, u32[]{:S(2)}) async-start(bf16[64,32,256]{2,1,0:T(8,128)(2,1)} %bitcast.21), calls=%async_computation.3 | async-start | bytes 2097152 | tf_op jit(solution)/shard_map/all_to_all | solution.py:322
  150.7 3.5 %near_product.6 = f32[16,32,128]{2,1,0:T(8,128)S(1)} custom-call(s32[16,16]{1,0:T(8,128)S(1)} %add_clamp_fusion.index_ref, s32[16]{0:T(128)S(1)} %copy-done.7, bf16[16,16,32,128]{3,2,1,0:T(8,128)(2,1)S(1)} %copy-done.1, bf16[2,128,128]{2,1,0:T(8,128)(2,1)} %copy-done.21, bf16[16,128,128]{2,1,0:T(8,128)(2,1)} %copy-done.8, bf16[2,128,128]{2,1,0:T(8,128)(2,1)} %copy-done.22), custom_call_target="tpu_custom_call" | custom-call | flops 234881024 | bytes 2097152 | tf_op jit(solution)/shard_map/near_product/pallas_call | solution.py:163
  155.6 6.1 %near_product.7.refs_4_ = f32[16,96,128]{2,1,0:T(8,128)S(1)} custom-call(s32[16,16]{1,0:T(8,128)S(1)} %add_clamp_fusion.index_ref, s32[16]{0:T(128)S(1)} %copy-done.7, bf16[16,16,32,128]{3,2,1,0:T(8,128)(2,1)S(1)} %copy-done.1, bf16[16,16,32,128]{3,2,1,0:T(8,128)(2,1)} %collective-permute-done.refs_1_, ...), custom_call_target="tpu_custom_call" | custom-call | flops 704643072 | bytes 6291456 | tf_op jit(solution)/shard_map/near_product/pallas_call | solution.py:163
  162.7 9.3 %all-to-all-done.3 = bf16[64,32,256]{2,1,0:T(8,128)(2,1)S(1)} async-done(((bf16[64,32,256]{2,1,0:T(8,128)(2,1)}), bf16[64,32,256]{2,1,0:T(8,128)(2,1)S(1)}, u32[]{:S(2)}, u32[]{:S(2)}) %all-to-all-start.3) | async-done | bytes 1048608 | tf_op jit(solution)/shard_map/all_to_all | solution.py:322
  172.0 4.7 %add_far.3 = bf16[2048,128]{1,0:T(8,128)(2,1)} custom-call(s32[4]{0:T(128)S(1)} %pad_add_fusion.offset_ref, s32[16]{0:T(128)S(1)} %copy-done.7, bf16[16,16,32,128]{3,2,1,0:T(8,128)(2,1)} %refs_0_.11, bf16[16,16,32,128]{3,2,1,0:T(8,128)(2,1)} %collective-permute-done.refs_1_, bf16[16,16,32,128]{3,2,1,0:T(8,128)(2,1)} %collective-permute-done.1.refs_2_, ...), custom_call_target="tpu_custom_call" | custom-call | flops 134217728 | bytes 4194304 | tf_op jit(solution)/shard_map/add_far/pallas_call | solution.py:269
  (81 shorter events, 31.0 us)
Async XLA Ops:
  0.0 17.3 %copy-start = (bf16[16,16,32,128]{3,2,1,0:T(8,128)(2,1)S(1)}, bf16[16,16,32,128]{3,2,1,0:T(8,128)(2,1)}, u32[]{:S(2)}) copy-start(bf16[16,16,32,128]{3,2,1,0:T(8,128)(2,1)} %refs_0_.11) | copy-start | bytes 6291460
  4.2 33.7 %all-to-all-start = ((bf16[64,40,128]{2,1,0:T(8,128)(2,1)}), bf16[64,40,128]{2,1,0:T(8,128)(2,1)}, u32[]{:S(2)}, u32[]{:S(2)}) async-start(bf16[64,40,128]{2,1,0:T(8,128)(2,1)} %split_blocks.1), calls=%async_computation | async-start | bytes 1310720 | tf_op jit(solution)/shard_map/all_to_all | solution.py:314
  17.3 67.9 %collective-permute-start.1 = (bf16[16,16,32,128]{3,2,1,0:T(8,128)(2,1)S(1)}, bf16[16,16,32,128]{3,2,1,0:T(8,128)(2,1)}, u32[]{:S(2)}, u32[]{:S(2)}) collective-permute-start(bf16[16,16,32,128]{3,2,1,0:T(8,128)(2,1)S(1)} %copy-done), channel_id=1, source_target_pairs={{1,0},{2,1},{3,2},{0,3},{5,4},{6,5},{7,6},{4,7},{9,8},{10,9},{11,1... | collective-permute-start | bytes 6291464 | tf_op jit(solution)/shard_map/ppermute | solution.py:298
  20.2 65.1 %collective-permute-start = (bf16[16,16,32,128]{3,2,1,0:T(8,128)(2,1)S(1)}, bf16[16,16,32,128]{3,2,1,0:T(8,128)(2,1)}, u32[]{:S(2)}, u32[]{:S(2)}) collective-permute-start(bf16[16,16,32,128]{3,2,1,0:T(8,128)(2,1)S(1)} %copy-done), channel_id=1, source_target_pairs={{0,1},{1,2},{2,3},{3,0},{4,5},{5,6},{6,7},{7,4},{8,9},{9,10},{10,1... | collective-permute-start | bytes 6291464 | tf_op jit(solution)/shard_map/ppermute | solution.py:297
  21.0 10.0 %collective-permute-start.3 = (bf16[2,128,128]{2,1,0:T(8,128)(2,1)S(1)}, bf16[2,128,128]{2,1,0:T(8,128)(2,1)S(1)}, u32[]{:S(2)}, u32[]{:S(2)}) collective-permute-start(bf16[2,128,128]{2,1,0:T(8,128)(2,1)S(1)} %bitcast.28), channel_id=1, source_target_pairs={{0,4},{4,8},{8,12},{12,16},{16,20},{20,24},{24,28},{28,32},{32,36}... | collective-permute-start | bytes 196616 | tf_op jit(solution)/shard_map/ppermute | solution.py:315
  24.9 29.1 %copy-start.23 = (s32[16,16]{1,0:T(8,128)S(1)}, s32[16,16]{1,0:T(8,128)}, u32[]{:S(2)}) copy-start(s32[16,16]{1,0:T(8,128)} %param.5) | copy-start | bytes 3076
  24.9 9.6 %collective-permute-start.6 = (bf16[2,128,128]{2,1,0:T(8,128)(2,1)S(1)}, bf16[2,128,128]{2,1,0:T(8,128)(2,1)S(1)}, u32[]{:S(2)}, u32[]{:S(2)}) collective-permute-start(bf16[2,128,128]{2,1,0:T(8,128)(2,1)S(1)} %bitcast.26), channel_id=1, source_target_pairs={{4,0},{8,4},{12,8},{16,12},{20,16},{24,20},{28,24},{32,28},{36,32}... | collective-permute-start | bytes 196616 | tf_op jit(solution)/shard_map/ppermute | solution.py:316
  41.5 40.3 %copy-start.7 = (s32[16]{0:T(128)S(1)}, s32[16]{0:T(128)}, u32[]{:S(2)}) copy-start(s32[16]{0:T(128)} %count_ref.11) | copy-start | bytes 196
  41.5 52.6 %all-to-all-start.1 = ((bf16[64,32,256]{2,1,0:T(8,128)(2,1)}), bf16[64,32,256]{2,1,0:T(8,128)(2,1)S(1)}, u32[]{:S(2)}, u32[]{:S(2)}) async-start(bf16[64,32,256]{2,1,0:T(8,128)(2,1)} %bitcast.20), calls=%async_computation.1 | async-start | bytes 2097152 | tf_op jit(solution)/shard_map/all_to_all | solution.py:322
  48.0 33.1 %collective-permute-start.5 = (bf16[16,128,128]{2,1,0:T(8,128)(2,1)}, bf16[16,128,128]{2,1,0:T(8,128)(2,1)}, u32[]{:S(2)}, u32[]{:S(2)}) collective-permute-start(bf16[16,128,128]{2,1,0:T(8,128)(2,1)} %bitcast.24), channel_id=1, source_target_pairs={{0,2},{1,3},{2,0},{3,1},{4,6},{5,7},{6,4},{7,5},{8,10},{9,11},{10,... | collective-permute-start | bytes 1572872 | tf_op jit(solution)/shard_map/ppermute | solution.py:317
  51.0 28.5 %collective-permute-start.4 = (bf16[2,128,128]{2,1,0:T(8,128)(2,1)S(1)}, bf16[2,128,128]{2,1,0:T(8,128)(2,1)S(1)}, u32[]{:S(2)}, u32[]{:S(2)}) collective-permute-start(bf16[2,128,128]{2,1,0:T(8,128)(2,1)S(1)} %copy-done.12), channel_id=1, source_target_pairs={{0,2},{1,3},{2,0},{3,1},{4,6},{5,7},{6,4},{7,5},{8,10},{9,11},{10,... | collective-permute-start | bytes 196616 | tf_op jit(solution)/shard_map/ppermute | solution.py:325
  51.1 30.0 %collective-permute-start.7 = (bf16[2,128,128]{2,1,0:T(8,128)(2,1)S(1)}, bf16[2,128,128]{2,1,0:T(8,128)(2,1)S(1)}, u32[]{:S(2)}, u32[]{:S(2)}) collective-permute-start(bf16[2,128,128]{2,1,0:T(8,128)(2,1)S(1)} %copy-done.14), channel_id=1, source_target_pairs={{0,2},{1,3},{2,0},{3,1},{4,6},{5,7},{6,4},{7,5},{8,10},{9,11},{10,... | collective-permute-start | bytes 196616 | tf_op jit(solution)/shard_map/ppermute | solution.py:325
  79.5 14.5 %collective-permute-start.2 = (bf16[16,2,32,128]{3,2,1,0:T(8,128)(2,1)}, bf16[16,2,32,128]{3,2,1,0:T(8,128)(2,1)}, u32[]{:S(2)}, u32[]{:S(2)}) collective-permute-start(bf16[16,2,32,128]{3,2,1,0:T(8,128)(2,1)} %slice.30), channel_id=1, source_target_pairs={{0,2},{1,3},{2,0},{3,1},{4,6},{5,7},{6,4},{7,5},{8,10},{9,11},{10,... | collective-permute-start | bytes 786440 | tf_op jit(solution)/shard_map/ppermute | solution.py:299
  85.3 8.8 %collective-permute-start.8 = (f32[16,32,128]{2,1,0:T(8,128)S(1)}, f32[16,32,128]{2,1,0:T(8,128)}, u32[]{:S(2)}, u32[]{:S(2)}) collective-permute-start(f32[16,32,128]{2,1,0:T(8,128)S(1)} %near_product.4), channel_id=1, source_target_pairs={{0,2},{1,3},{2,0},{3,1},{4,6},{5,7},{6,4},{7,5},{8,10},{9,11},{10,... | collective-permute-start | bytes 786440 | tf_op jit(solution)/shard_map/ppermute | solution.py:331
  99.3 30.5 %copy-start.6 = (bf16[2048,128]{1,0:T(8,128)(2,1)}, bf16[2048,128]{1,0:T(8,128)(2,1)S(1)}, u32[]{:S(2)}) copy-start(bf16[2048,128]{1,0:T(8,128)(2,1)S(1)} %get-tuple-element.19) | copy-start | bytes 1572868
  99.3 30.5 %all-to-all-start.2 = ((bf16[64,32,128]{2,1,0:T(8,128)(2,1)}), bf16[64,32,128]{2,1,0:T(8,128)(2,1)S(1)}, u32[]{:S(2)}, u32[]{:S(2)}) async-start(bf16[64,32,128]{2,1,0:T(8,128)(2,1)} %get-tuple-element.23), calls=%async_computation.2 | async-start | bytes 1048576 | tf_op jit(solution)/shard_map/all_to_all | solution.py:314
  112.2 14.6 %collective-permute-start.11 = (bf16[16,128,128]{2,1,0:T(8,128)(2,1)S(1)}, bf16[16,128,128]{2,1,0:T(8,128)(2,1)S(1)}, u32[]{:S(2)}, u32[]{:S(2)}) collective-permute-start(bf16[16,128,128]{2,1,0:T(8,128)(2,1)S(1)} %bitcast.22), channel_id=1, source_target_pairs={{0,2},{1,3},{2,0},{3,1},{4,6},{5,7},{6,4},{7,5},{8,10},{9,11},{10,... | collective-permute-start | bytes 1572872 | tf_op jit(solution)/shard_map/ppermute | solution.py:317
  113.5 9.4 %collective-permute-start.9 = (bf16[2,128,128]{2,1,0:T(8,128)(2,1)S(1)}, bf16[2,128,128]{2,1,0:T(8,128)(2,1)S(1)}, u32[]{:S(2)}, u32[]{:S(2)}) collective-permute-start(bf16[2,128,128]{2,1,0:T(8,128)(2,1)S(1)} %bitcast.29), channel_id=1, source_target_pairs={{0,4},{4,8},{8,12},{12,16},{16,20},{20,24},{24,28},{28,32},{32,36}... | collective-permute-start | bytes 196616 | tf_op jit(solution)/shard_map/ppermute | solution.py:315
  117.4 9.3 %collective-permute-start.12 = (bf16[2,128,128]{2,1,0:T(8,128)(2,1)S(1)}, bf16[2,128,128]{2,1,0:T(8,128)(2,1)S(1)}, u32[]{:S(2)}, u32[]{:S(2)}) collective-permute-start(bf16[2,128,128]{2,1,0:T(8,128)(2,1)S(1)} %bitcast.27), channel_id=1, source_target_pairs={{4,0},{8,4},{12,8},{16,12},{20,16},{24,20},{28,24},{32,28},{36,32}... | collective-permute-start | bytes 196616 | tf_op jit(solution)/shard_map/ppermute | solution.py:316
  130.6 20.0 %copy-start.1 = (bf16[16,16,32,128]{3,2,1,0:T(8,128)(2,1)S(1)}, bf16[16,16,32,128]{3,2,1,0:T(8,128)(2,1)}, u32[]{:S(2)}) copy-start(bf16[16,16,32,128]{3,2,1,0:T(8,128)(2,1)} %refs_0_.11) | copy-start | bytes 6291460
  134.2 37.8 %all-to-all-start.3 = ((bf16[64,32,256]{2,1,0:T(8,128)(2,1)}), bf16[64,32,256]{2,1,0:T(8,128)(2,1)S(1)}, u32[]{:S(2)}, u32[]{:S(2)}) async-start(bf16[64,32,256]{2,1,0:T(8,128)(2,1)} %bitcast.21), calls=%async_computation.3 | async-start | bytes 2097152 | tf_op jit(solution)/shard_map/all_to_all | solution.py:322
  143.4 5.0 %collective-permute-start.10 = (bf16[2,128,128]{2,1,0:T(8,128)(2,1)S(1)}, bf16[2,128,128]{2,1,0:T(8,128)(2,1)S(1)}, u32[]{:S(2)}, u32[]{:S(2)}) collective-permute-start(bf16[2,128,128]{2,1,0:T(8,128)(2,1)S(1)} %copy-done.16), channel_id=1, source_target_pairs={{0,2},{1,3},{2,0},{3,1},{4,6},{5,7},{6,4},{7,5},{8,10},{9,11},{10,... | collective-permute-start | bytes 196616 | tf_op jit(solution)/shard_map/ppermute | solution.py:325
  144.7 5.3 %collective-permute-start.13 = (bf16[2,128,128]{2,1,0:T(8,128)(2,1)S(1)}, bf16[2,128,128]{2,1,0:T(8,128)(2,1)S(1)}, u32[]{:S(2)}, u32[]{:S(2)}) collective-permute-start(bf16[2,128,128]{2,1,0:T(8,128)(2,1)S(1)} %copy-done.18), channel_id=1, source_target_pairs={{0,2},{1,3},{2,0},{3,1},{4,6},{5,7},{6,4},{7,5},{8,10},{9,11},{10,... | collective-permute-start | bytes 196616 | tf_op jit(solution)/shard_map/ppermute | solution.py:325
  154.2 8.5 %collective-permute-start.14 = (f32[16,32,128]{2,1,0:T(8,128)S(1)}, f32[16,32,128]{2,1,0:T(8,128)S(1)}, u32[]{:S(2)}, u32[]{:S(2)}) collective-permute-start(f32[16,32,128]{2,1,0:T(8,128)S(1)} %near_product.6), channel_id=1, source_target_pairs={{0,2},{1,3},{2,0},{3,1},{4,6},{5,7},{6,4},{7,5},{8,10},{9,11},{10,... | collective-permute-start | bytes 786440 | tf_op jit(solution)/shard_map/ppermute | solution.py:331
  (19 other events, 82.2 us)

commit v13 on v11

--- a/solution.py
+++ b/solution.py
@@ -309,11 +309,11 @@
         reach = [lax.ppermute(low, "pb", opposite), beyond, lax.ppermute(high, "pb", opposite)]
         product = near_product(near_index, valid_counts, [(affinity_tiles,)], reach)
         product, sides = lax.optimization_barrier((product, (before, after)))
-        quarters = [(affinity_tiles,), (sides[0],), (sides[1],)]
-        partials = [
-            near_product(near_index, valid_counts, quarters, [low, own, high]),
-            lax.ppermute(product, "pb", opposite),
-        ]
+        quarters = [[(affinity_tiles,)], [(sides[0],), (sides[1],)]]
+        if step > 0:
+            quarters = [quarters[0] + quarters[1]]
+        partials = [near_product(near_index, valid_counts, part, [low, own, high]) for part in quarters]
+        partials.append(lax.ppermute(product, "pb", opposite))
         done = add_far(offsets, valid_counts, far_tiles, arrived, partials, queries, owners, step < ITERS - 1)
         ranking = done[0]
         pieces = done[-1]

time: 178 us -> 181 us (1.017)
  Pallas kernels: 34.7 us -> 37.8 us
    pallas_call x4 -> x5, Pallas kernels: 19.3 us -> 22.5 us  [near_product(): pl.pallas_call(kernel, out_shape=jax.ShapeDtypeStruct((blocks, number * r...]
    unnamed x54 -> x56, local copies, waits for them, and re-layouts: 8.84 us -> 9.37 us
  transfers between devices with their start and end apart: 19 -> 19, of which waited for: 11 -> 11; matrix products, arithmetic and copies ran while one was open for 1% -> 1% of each run, Pallas kernels for 12% -> 13%
where the time goes in v13:
time: 181 us; the launch traced here: 180 us
  starting transfers between devices  70.9 us (39%)
  waiting for transfers between devices  58.4 us (32%)
  Pallas kernels  37.8 us (21%)
  local copies, waits for them, and re-layouts  12.5 us (7%)
    ppermute x2, waiting for transfers between devices, on_device(): lax.ppermute(low, 'pb', opposite)  25.8 us
    all_to_all x2, starting transfers between devices, on_device(): held = lax.all_to_all(pieces, 'db', split_axis=0, concat_axis=0, tiled=True)  25.8 us
    pallas_call x5, Pallas kernels, near_product(): pl.pallas_call(kernel, out_shape=jax.ShapeDtypeStruct((blocks, number * r...  22.5 us
    all_to_all x2, starting transfers between devices, on_device(): lax.all_to_all(chosen.reshape(owners, slots, -1), 'db', split_axis=0, con...  15.8 us
    pallas_call x2, Pallas kernels, add_far(): pl.pallas_call(kernel, out_shape=out_shape, grid_spec=pltpu.PrefetchScala...  9.98 us
    unnamed x56, local copies, waits for them, and re-layouts  9.37 us
    all_to_all x2, waiting for transfers between devices, on_device(): lax.all_to_all(chosen.reshape(owners, slots, -1), 'db', split_axis=0, con...  9.29 us
    ppermute x2, waiting for transfers between devices, on_device(): low = lax.ppermute(own[blocks - EDGE:], 'db', up)  8.1 us
  transfers between devices with their start and end apart: 19, of which 11 were waited for; matrix products, arithmetic and copies ran while one was open for 1% of the time, Pallas kernels for 13%

profile of v13, /device:TPU:1, one launch (start us, length us, event | category | flops | bytes accessed | tf_op | source)
XLA Modules:
  0.0 180.3 jit_solution(12303843068695297201)
XLA Ops:
  4.2 13.0 %all-to-all-start = ((bf16[64,40,128]{2,1,0:T(8,128)(2,1)}), bf16[64,40,128]{2,1,0:T(8,128)(2,1)S(1)}, u32[]{:S(2)}, u32[]{:S(2)}) async-start(bf16[64,40,128]{2,1,0:T(8,128)(2,1)} %split_blocks.1), calls=%async_computation | async-start | bytes 1310720 | tf_op jit(solution)/shard_map/all_to_all | solution.py:298
  17.2 2.8 %collective-permute-start.1 = (bf16[16,16,32,128]{3,2,1,0:T(8,128)(2,1)S(1)}, bf16[16,16,32,128]{3,2,1,0:T(8,128)(2,1)}, u32[]{:S(2)}, u32[]{:S(2)}) collective-permute-start(bf16[16,16,32,128]{3,2,1,0:T(8,128)(2,1)S(1)} %copy-done), channel_id=1, source_target_pairs={{1,0},{2,1},{3,2},{0,3},{5,4},{6,5},{7,6},{4,7},{9,8},{10,9},{11,1... | collective-permute-start | bytes 6291464 | tf_op jit(solution)/shard_map/ppermute | solution.py:282
  20.9 3.8 %collective-permute-start.3 = (bf16[2,128,128]{2,1,0:T(8,128)(2,1)S(1)}, bf16[2,128,128]{2,1,0:T(8,128)(2,1)S(1)}, u32[]{:S(2)}, u32[]{:S(2)}) collective-permute-start(bf16[2,128,128]{2,1,0:T(8,128)(2,1)S(1)} %bitcast.29), channel_id=1, source_target_pairs={{0,4},{4,8},{8,12},{12,16},{16,20},{20,24},{24,28},{28,32},{32,36}... | collective-permute-start | bytes 196616 | tf_op jit(solution)/shard_map/ppermute | solution.py:299
  26.7 4.4 %collective-permute-done.3.refs_1_.refs_2_.rest_0_ = bf16[2,128,128]{2,1,0:T(8,128)(2,1)S(1)} collective-permute-done((bf16[2,128,128]{2,1,0:T(8,128)(2,1)S(1)}, bf16[2,128,128]{2,1,0:T(8,128)(2,1)S(1)}, u32[]{:S(2)}, u32[]{:S(2)}) %collective-permute-start.3) | collective-permute-done | bytes 65568 | tf_op jit(solution)/shard_map/ppermute | solution.py:299
  31.1 3.4 %collective-permute-done.4.refs_3_.refs_4_.rest_1_ = bf16[2,128,128]{2,1,0:T(8,128)(2,1)S(1)} collective-permute-done((bf16[2,128,128]{2,1,0:T(8,128)(2,1)S(1)}, bf16[2,128,128]{2,1,0:T(8,128)(2,1)S(1)}, u32[]{:S(2)}, u32[]{:S(2)}) %collective-permute-start.4) | collective-permute-done | bytes 65568 | tf_op jit(solution)/shard_map/ppermute | solution.py:300
  34.5 3.3 %all-to-all-done.held_ref = bf16[64,40,128]{2,1,0:T(8,128)(2,1)S(1)} async-done(((bf16[64,40,128]{2,1,0:T(8,128)(2,1)}), bf16[64,40,128]{2,1,0:T(8,128)(2,1)S(1)}, u32[]{:S(2)}, u32[]{:S(2)}) %all-to-all-start) | async-done | bytes 655392 | tf_op jit(solution)/shard_map/all_to_all | solution.py:298
  42.2 6.6 %all-to-all-start.1 = ((bf16[64,32,256]{2,1,0:T(8,128)(2,1)}), bf16[64,32,256]{2,1,0:T(8,128)(2,1)S(1)}, u32[]{:S(2)}, u32[]{:S(2)}) async-start(bf16[64,32,256]{2,1,0:T(8,128)(2,1)} %bitcast.20), calls=%async_computation.1 | async-start | bytes 2097152 | tf_op jit(solution)/shard_map/all_to_all | solution.py:306
  48.8 3.0 %collective-permute-start.6 = (bf16[16,128,128]{2,1,0:T(8,128)(2,1)}, bf16[16,128,128]{2,1,0:T(8,128)(2,1)}, u32[]{:S(2)}, u32[]{:S(2)}) collective-permute-start(bf16[16,128,128]{2,1,0:T(8,128)(2,1)} %bitcast.24), channel_id=1, source_target_pairs={{0,2},{1,3},{2,0},{3,1},{4,6},{5,7},{6,4},{7,5},{8,10},{9,11},{10,... | collective-permute-start | bytes 1572872 | tf_op jit(solution)/shard_map/ppermute | solution.py:301
  52.0 2.9 %collective-permute-start.7 = (bf16[2,128,128]{2,1,0:T(8,128)(2,1)S(1)}, bf16[2,128,128]{2,1,0:T(8,128)(2,1)S(1)}, u32[]{:S(2)}, u32[]{:S(2)}) collective-permute-start(bf16[2,128,128]{2,1,0:T(8,128)(2,1)S(1)} %copy-done.17), channel_id=1, source_target_pairs={{0,2},{1,3},{2,0},{3,1},{4,6},{5,7},{6,4},{7,5},{8,10},{9,11},{10,... | collective-permute-start | bytes 196616 | tf_op jit(solution)/shard_map/ppermute | solution.py:309
  55.5 23.9 %collective-permute-done.5.refs_1_ = bf16[2,128,128]{2,1,0:T(8,128)(2,1)S(1)} collective-permute-done((bf16[2,128,128]{2,1,0:T(8,128)(2,1)S(1)}, bf16[2,128,128]{2,1,0:T(8,128)(2,1)S(1)}, u32[]{:S(2)}, u32[]{:S(2)}) %collective-permute-start.5) | collective-permute-done | bytes 65568 | tf_op jit(solution)/shard_map/ppermute | solution.py:309
  81.6 3.5 %near_product.6 = f32[16,32,128]{2,1,0:T(8,128)S(1)} custom-call(s32[16,16]{1,0:T(8,128)S(1)} %add_clamp_fusion.index_ref, s32[16]{0:T(128)S(1)} %copy-done.12, bf16[16,16,32,128]{3,2,1,0:T(8,128)(2,1)S(1)} %copy-done, bf16[2,128,128]{2,1,0:T(8,128)(2,1)} %copy-done.23, bf16[16,128,128]{2,1,0:T(8,128)(2,1)} %collective-permute-done.6.refs_2_, ...), custom_call_target="tpu_custom_call" | custom-call | flops 234881024 | bytes 2097152 | tf_op jit(solution)/shard_map/near_product/pallas_call | solution.py:147
  86.9 3.5 %near_product.5.refs_4_ = f32[16,32,128]{2,1,0:T(8,128)S(1)} custom-call(s32[16,16]{1,0:T(8,128)S(1)} %add_clamp_fusion.index_ref, s32[16]{0:T(128)S(1)} %copy-done.12, bf16[16,16,32,128]{3,2,1,0:T(8,128)(2,1)S(1)} %copy-done, bf16[2,128,128]{2,1,0:T(8,128)(2,1)} %copy-done.14, bf16[16,128,128]{2,1,0:T(8,128)(2,1)} %bitcast.25, bf16[2,128,128]{2,1,0:T(8,128)(2,1)} %copy-done.16), custom_call_target="tpu_custom_call" | custom-call | flops 234881024 | bytes 2097152 | tf_op jit(solution)/shard_map/near_product/pallas_call | solution.py:147
  91.1 5.8 %near_product.7.refs_5_ = f32[16,64,128]{2,1,0:T(8,128)S(1)} custom-call(s32[16,16]{1,0:T(8,128)S(1)} %add_clamp_fusion.index_ref, s32[16]{0:T(128)S(1)} %copy-done.12, bf16[16,16,32,128]{3,2,1,0:T(8,128)(2,1)} %collective-permute-done.refs_0_.refs_1_, bf16[16,16,32,128]{3,2,1,0:T(8,128)(2,1)} %collective-permute-done.1.refs_1_.refs_2_, ...), custom_call_target="tpu_custom_call" | custom-call | flops 469762048 | bytes 4194304 | tf_op jit(solution)/shard_map/near_product/pallas_call | solution.py:147
  97.8 5.3 %add_far.2 = (bf16[2048,128]{1,0:T(8,128)(2,1)S(1)}, bf16[64,32,128]{2,1,0:T(8,128)(2,1)}) custom-call(s32[4]{0:T(128)S(1)} %pad_add_fusion.offset_ref, s32[16]{0:T(128)S(1)} %copy-done.12, bf16[16,16,32,128]{3,2,1,0:T(8,128)(2,1)} %refs_0_.11, bf16[16,16,32,128]{3,2,1,0:T(8,128)(2,1)} %collective-permute-done.refs_0_.refs_1_, ...), custom_call_target="tpu_custom_call" | custom-call | flops 134217728 | bytes 4194304 | tf_op jit(solution)/shard_map/add_far/pallas_call | solution.py:253
  103.1 12.8 %all-to-all-start.2 = ((bf16[64,32,128]{2,1,0:T(8,128)(2,1)}), bf16[64,32,128]{2,1,0:T(8,128)(2,1)S(1)}, u32[]{:S(2)}, u32[]{:S(2)}) async-start(bf16[64,32,128]{2,1,0:T(8,128)(2,1)} %get-tuple-element.23), calls=%async_computation.2 | async-start | bytes 1048576 | tf_op jit(solution)/shard_map/all_to_all | solution.py:298
  117.2 3.8 %collective-permute-start.9 = (bf16[2,128,128]{2,1,0:T(8,128)(2,1)S(1)}, bf16[2,128,128]{2,1,0:T(8,128)(2,1)S(1)}, u32[]{:S(2)}, u32[]{:S(2)}) collective-permute-start(bf16[2,128,128]{2,1,0:T(8,128)(2,1)S(1)} %bitcast.30), channel_id=1, source_target_pairs={{0,4},{4,8},{8,12},{12,16},{16,20},{20,24},{24,28},{28,32},{32,36}... | collective-permute-start | bytes 196616 | tf_op jit(solution)/shard_map/ppermute | solution.py:299
  123.0 3.7 %collective-permute-done.9.refs_3_.rest_0_ = bf16[2,128,128]{2,1,0:T(8,128)(2,1)S(1)} collective-permute-done((bf16[2,128,128]{2,1,0:T(8,128)(2,1)S(1)}, bf16[2,128,128]{2,1,0:T(8,128)(2,1)S(1)}, u32[]{:S(2)}, u32[]{:S(2)}) %collective-permute-start.9) | collective-permute-done | bytes 65568 | tf_op jit(solution)/shard_map/ppermute | solution.py:299
  126.6 3.6 %collective-permute-done.12.refs_5_.rest_1_ = bf16[2,128,128]{2,1,0:T(8,128)(2,1)S(1)} collective-permute-done((bf16[2,128,128]{2,1,0:T(8,128)(2,1)S(1)}, bf16[2,128,128]{2,1,0:T(8,128)(2,1)S(1)}, u32[]{:S(2)}, u32[]{:S(2)}) %collective-permute-start.12) | collective-permute-done | bytes 65568 | tf_op jit(solution)/shard_map/ppermute | solution.py:300
  130.5 3.0 %all-to-all-done.2.held_ref = bf16[64,32,128]{2,1,0:T(8,128)(2,1)S(1)} async-done(((bf16[64,32,128]{2,1,0:T(8,128)(2,1)}), bf16[64,32,128]{2,1,0:T(8,128)(2,1)S(1)}, u32[]{:S(2)}, u32[]{:S(2)}) %all-to-all-start.2) | async-done | bytes 524320 | tf_op jit(solution)/shard_map/all_to_all | solution.py:298
  137.6 9.2 %all-to-all-start.3 = ((bf16[64,32,256]{2,1,0:T(8,128)(2,1)}), bf16[64,32,256]{2,1,0:T(8,128)(2,1)S(1)}, u32[]{:S(2)}, u32[]{:S(2)}) async-start(bf16[64,32,256]{2,1,0:T(8,128)(2,1)} %bitcast.21), calls=%async_computation.3 | async-start | bytes 2097152 | tf_op jit(solution)/shard_map/all_to_all | solution.py:306
  154.1 3.5 %near_product.8 = f32[16,32,128]{2,1,0:T(8,128)S(1)} custom-call(s32[16,16]{1,0:T(8,128)S(1)} %add_clamp_fusion.index_ref, s32[16]{0:T(128)S(1)} %copy-done.12, bf16[16,16,32,128]{3,2,1,0:T(8,128)(2,1)S(1)} %copy-done.1, bf16[2,128,128]{2,1,0:T(8,128)(2,1)} %copy-done.25, bf16[16,128,128]{2,1,0:T(8,128)(2,1)} %copy-done.13, bf16[2,128,128]{2,1,0:T(8,128)(2,1)} %copy-done.26), custom_call_target="tpu_custom_call" | custom-call | flops 234881024 | bytes 2097152 | tf_op jit(solution)/shard_map/near_product/pallas_call | solution.py:147
  159.1 6.1 %near_product.9.refs_4_ = f32[16,96,128]{2,1,0:T(8,128)S(1)} custom-call(s32[16,16]{1,0:T(8,128)S(1)} %add_clamp_fusion.index_ref, s32[16]{0:T(128)S(1)} %copy-done.12, bf16[16,16,32,128]{3,2,1,0:T(8,128)(2,1)S(1)} %copy-done.1, bf16[16,16,32,128]{3,2,1,0:T(8,128)(2,1)} %collective-permute-done.refs_0_.refs_1_, ...), custom_call_target="tpu_custom_call" | custom-call | flops 704643072 | bytes 6291456 | tf_op jit(solution)/shard_map/near_product/pallas_call | solution.py:147
  166.2 9.3 %all-to-all-done.3 = bf16[64,32,256]{2,1,0:T(8,128)(2,1)S(1)} async-done(((bf16[64,32,256]{2,1,0:T(8,128)(2,1)}), bf16[64,32,256]{2,1,0:T(8,128)(2,1)S(1)}, u32[]{:S(2)}, u32[]{:S(2)}) %all-to-all-start.3) | async-done | bytes 1048608 | tf_op jit(solution)/shard_map/all_to_all | solution.py:306
  175.5 4.7 %add_far.3 = bf16[2048,128]{1,0:T(8,128)(2,1)} custom-call(s32[4]{0:T(128)S(1)} %pad_add_fusion.offset_ref, s32[16]{0:T(128)S(1)} %copy-done.12, bf16[16,16,32,128]{3,2,1,0:T(8,128)(2,1)} %refs_0_.11, bf16[16,16,32,128]{3,2,1,0:T(8,128)(2,1)} %collective-permute-done.refs_0_.refs_1_, bf16[16,16,32,128]{3,2,1,0:T(8,128)(2,1)} %collective-permute-done.1.refs_1_.refs_2_, ...), custom_call_target="tpu_custom_call" | custom-call | flops 134217728 | bytes 4194304 | tf_op jit(solution)/shard_map/add_far/pallas_call | solution.py:253
  (90 shorter events, 34.8 us)
Async XLA Ops:
  0.0 17.2 %copy-start = (bf16[16,16,32,128]{3,2,1,0:T(8,128)(2,1)S(1)}, bf16[16,16,32,128]{3,2,1,0:T(8,128)(2,1)}, u32[]{:S(2)}) copy-start(bf16[16,16,32,128]{3,2,1,0:T(8,128)(2,1)} %refs_0_.11) | copy-start | bytes 6291460
  4.2 33.6 %all-to-all-start = ((bf16[64,40,128]{2,1,0:T(8,128)(2,1)}), bf16[64,40,128]{2,1,0:T(8,128)(2,1)S(1)}, u32[]{:S(2)}, u32[]{:S(2)}) async-start(bf16[64,40,128]{2,1,0:T(8,128)(2,1)} %split_blocks.1), calls=%async_computation | async-start | bytes 1310720 | tf_op jit(solution)/shard_map/all_to_all | solution.py:298
  17.2 68.0 %collective-permute-start.1 = (bf16[16,16,32,128]{3,2,1,0:T(8,128)(2,1)S(1)}, bf16[16,16,32,128]{3,2,1,0:T(8,128)(2,1)}, u32[]{:S(2)}, u32[]{:S(2)}) collective-permute-start(bf16[16,16,32,128]{3,2,1,0:T(8,128)(2,1)S(1)} %copy-done), channel_id=1, source_target_pairs={{1,0},{2,1},{3,2},{0,3},{5,4},{6,5},{7,6},{4,7},{9,8},{10,9},{11,1... | collective-permute-start | bytes 6291464 | tf_op jit(solution)/shard_map/ppermute | solution.py:282
  20.0 65.2 %collective-permute-start = (bf16[16,16,32,128]{3,2,1,0:T(8,128)(2,1)S(1)}, bf16[16,16,32,128]{3,2,1,0:T(8,128)(2,1)}, u32[]{:S(2)}, u32[]{:S(2)}) collective-permute-start(bf16[16,16,32,128]{3,2,1,0:T(8,128)(2,1)S(1)} %copy-done), channel_id=1, source_target_pairs={{0,1},{1,2},{2,3},{3,0},{4,5},{5,6},{6,7},{7,4},{8,9},{9,10},{10,1... | collective-permute-start | bytes 6291464 | tf_op jit(solution)/shard_map/ppermute | solution.py:281
  20.9 10.2 %collective-permute-start.3 = (bf16[2,128,128]{2,1,0:T(8,128)(2,1)S(1)}, bf16[2,128,128]{2,1,0:T(8,128)(2,1)S(1)}, u32[]{:S(2)}, u32[]{:S(2)}) collective-permute-start(bf16[2,128,128]{2,1,0:T(8,128)(2,1)S(1)} %bitcast.29), channel_id=1, source_target_pairs={{0,4},{4,8},{8,12},{12,16},{16,20},{20,24},{24,28},{28,32},{32,36}... | collective-permute-start | bytes 196616 | tf_op jit(solution)/shard_map/ppermute | solution.py:299
  24.7 9.8 %collective-permute-start.4 = (bf16[2,128,128]{2,1,0:T(8,128)(2,1)S(1)}, bf16[2,128,128]{2,1,0:T(8,128)(2,1)S(1)}, u32[]{:S(2)}, u32[]{:S(2)}) collective-permute-start(bf16[2,128,128]{2,1,0:T(8,128)(2,1)S(1)} %bitcast.27), channel_id=1, source_target_pairs={{4,0},{8,4},{12,8},{16,12},{20,16},{24,20},{28,24},{32,28},{36,32}... | collective-permute-start | bytes 196616 | tf_op jit(solution)/shard_map/ppermute | solution.py:300
  39.8 15.0 %copy-start.27 = (s32[16,16]{1,0:T(8,128)S(1)}, s32[16,16]{1,0:T(8,128)}, u32[]{:S(2)}) copy-start(s32[16,16]{1,0:T(8,128)} %param.5) | copy-start | bytes 3076
  42.2 39.4 %copy-start.12 = (s32[16]{0:T(128)S(1)}, s32[16]{0:T(128)}, u32[]{:S(2)}) copy-start(s32[16]{0:T(128)} %count_ref.13) | copy-start | bytes 196
  42.2 55.5 %all-to-all-start.1 = ((bf16[64,32,256]{2,1,0:T(8,128)(2,1)}), bf16[64,32,256]{2,1,0:T(8,128)(2,1)S(1)}, u32[]{:S(2)}, u32[]{:S(2)}) async-start(bf16[64,32,256]{2,1,0:T(8,128)(2,1)} %bitcast.20), calls=%async_computation.1 | async-start | bytes 2097152 | tf_op jit(solution)/shard_map/all_to_all | solution.py:306
  48.8 32.2 %collective-permute-start.6 = (bf16[16,128,128]{2,1,0:T(8,128)(2,1)}, bf16[16,128,128]{2,1,0:T(8,128)(2,1)}, u32[]{:S(2)}, u32[]{:S(2)}) collective-permute-start(bf16[16,128,128]{2,1,0:T(8,128)(2,1)} %bitcast.24), channel_id=1, source_target_pairs={{0,2},{1,3},{2,0},{3,1},{4,6},{5,7},{6,4},{7,5},{8,10},{9,11},{10,... | collective-permute-start | bytes 1572872 | tf_op jit(solution)/shard_map/ppermute | solution.py:301
  51.8 27.6 %collective-permute-start.5 = (bf16[2,128,128]{2,1,0:T(8,128)(2,1)S(1)}, bf16[2,128,128]{2,1,0:T(8,128)(2,1)S(1)}, u32[]{:S(2)}, u32[]{:S(2)}) collective-permute-start(bf16[2,128,128]{2,1,0:T(8,128)(2,1)S(1)} %copy-done.15), channel_id=1, source_target_pairs={{0,2},{1,3},{2,0},{3,1},{4,6},{5,7},{6,4},{7,5},{8,10},{9,11},{10,... | collective-permute-start | bytes 196616 | tf_op jit(solution)/shard_map/ppermute | solution.py:309
  52.0 29.1 %collective-permute-start.7 = (bf16[2,128,128]{2,1,0:T(8,128)(2,1)S(1)}, bf16[2,128,128]{2,1,0:T(8,128)(2,1)S(1)}, u32[]{:S(2)}, u32[]{:S(2)}) collective-permute-start(bf16[2,128,128]{2,1,0:T(8,128)(2,1)S(1)} %copy-done.17), channel_id=1, source_target_pairs={{0,2},{1,3},{2,0},{3,1},{4,6},{5,7},{6,4},{7,5},{8,10},{9,11},{10,... | collective-permute-start | bytes 196616 | tf_op jit(solution)/shard_map/ppermute | solution.py:309
  79.4 18.3 %collective-permute-start.2 = (bf16[16,2,32,128]{3,2,1,0:T(8,128)(2,1)}, bf16[16,2,32,128]{3,2,1,0:T(8,128)(2,1)}, u32[]{:S(2)}, u32[]{:S(2)}) collective-permute-start(bf16[16,2,32,128]{3,2,1,0:T(8,128)(2,1)} %slice.30), channel_id=1, source_target_pairs={{0,2},{1,3},{2,0},{3,1},{4,6},{5,7},{6,4},{7,5},{8,10},{9,11},{10,... | collective-permute-start | bytes 786440 | tf_op jit(solution)/shard_map/ppermute | solution.py:283
  85.2 12.6 %collective-permute-start.8 = (f32[16,32,128]{2,1,0:T(8,128)S(1)}, f32[16,32,128]{2,1,0:T(8,128)}, u32[]{:S(2)}, u32[]{:S(2)}) collective-permute-start(f32[16,32,128]{2,1,0:T(8,128)S(1)} %near_product.6), channel_id=1, source_target_pairs={{0,2},{1,3},{2,0},{3,1},{4,6},{5,7},{6,4},{7,5},{8,10},{9,11},{10,... | collective-permute-start | bytes 786440 | tf_op jit(solution)/shard_map/ppermute | solution.py:316
  103.1 30.4 %copy-start.7 = (bf16[2048,128]{1,0:T(8,128)(2,1)}, bf16[2048,128]{1,0:T(8,128)(2,1)S(1)}, u32[]{:S(2)}) copy-start(bf16[2048,128]{1,0:T(8,128)(2,1)S(1)} %get-tuple-element.19) | copy-start | bytes 1572868
  103.1 30.4 %all-to-all-start.2 = ((bf16[64,32,128]{2,1,0:T(8,128)(2,1)}), bf16[64,32,128]{2,1,0:T(8,128)(2,1)S(1)}, u32[]{:S(2)}, u32[]{:S(2)}) async-start(bf16[64,32,128]{2,1,0:T(8,128)(2,1)} %get-tuple-element.23), calls=%async_computation.2 | async-start | bytes 1048576 | tf_op jit(solution)/shard_map/all_to_all | solution.py:298
  115.9 14.6 %collective-permute-start.11 = (bf16[16,128,128]{2,1,0:T(8,128)(2,1)S(1)}, bf16[16,128,128]{2,1,0:T(8,128)(2,1)S(1)}, u32[]{:S(2)}, u32[]{:S(2)}) collective-permute-start(bf16[16,128,128]{2,1,0:T(8,128)(2,1)S(1)} %bitcast.22), channel_id=1, source_target_pairs={{0,2},{1,3},{2,0},{3,1},{4,6},{5,7},{6,4},{7,5},{8,10},{9,11},{10,... | collective-permute-start | bytes 1572872 | tf_op jit(solution)/shard_map/ppermute | solution.py:301
  117.2 9.4 %collective-permute-start.9 = (bf16[2,128,128]{2,1,0:T(8,128)(2,1)S(1)}, bf16[2,128,128]{2,1,0:T(8,128)(2,1)S(1)}, u32[]{:S(2)}, u32[]{:S(2)}) collective-permute-start(bf16[2,128,128]{2,1,0:T(8,128)(2,1)S(1)} %bitcast.30), channel_id=1, source_target_pairs={{0,4},{4,8},{8,12},{12,16},{16,20},{20,24},{24,28},{28,32},{32,36}... | collective-permute-start | bytes 196616 | tf_op jit(solution)/shard_map/ppermute | solution.py:299
  121.0 9.3 %collective-permute-start.12 = (bf16[2,128,128]{2,1,0:T(8,128)(2,1)S(1)}, bf16[2,128,128]{2,1,0:T(8,128)(2,1)S(1)}, u32[]{:S(2)}, u32[]{:S(2)}) collective-permute-start(bf16[2,128,128]{2,1,0:T(8,128)(2,1)S(1)} %bitcast.28), channel_id=1, source_target_pairs={{4,0},{8,4},{12,8},{16,12},{20,16},{24,20},{28,24},{32,28},{36,32}... | collective-permute-start | bytes 196616 | tf_op jit(solution)/shard_map/ppermute | solution.py:300
  135.3 18.8 %copy-start.1 = (bf16[16,16,32,128]{3,2,1,0:T(8,128)(2,1)S(1)}, bf16[16,16,32,128]{3,2,1,0:T(8,128)(2,1)}, u32[]{:S(2)}) copy-start(bf16[16,16,32,128]{3,2,1,0:T(8,128)(2,1)} %refs_0_.11) | copy-start | bytes 6291460
  137.6 37.8 %all-to-all-start.3 = ((bf16[64,32,256]{2,1,0:T(8,128)(2,1)}), bf16[64,32,256]{2,1,0:T(8,128)(2,1)S(1)}, u32[]{:S(2)}, u32[]{:S(2)}) async-start(bf16[64,32,256]{2,1,0:T(8,128)(2,1)} %bitcast.21), calls=%async_computation.3 | async-start | bytes 2097152 | tf_op jit(solution)/shard_map/all_to_all | solution.py:306
  146.9 5.0 %collective-permute-start.10 = (bf16[2,128,128]{2,1,0:T(8,128)(2,1)S(1)}, bf16[2,128,128]{2,1,0:T(8,128)(2,1)S(1)}, u32[]{:S(2)}, u32[]{:S(2)}) collective-permute-start(bf16[2,128,128]{2,1,0:T(8,128)(2,1)S(1)} %copy-done.20), channel_id=1, source_target_pairs={{0,2},{1,3},{2,0},{3,1},{4,6},{5,7},{6,4},{7,5},{8,10},{9,11},{10,... | collective-permute-start | bytes 196616 | tf_op jit(solution)/shard_map/ppermute | solution.py:309
  148.2 5.3 %collective-permute-start.13 = (bf16[2,128,128]{2,1,0:T(8,128)(2,1)S(1)}, bf16[2,128,128]{2,1,0:T(8,128)(2,1)S(1)}, u32[]{:S(2)}, u32[]{:S(2)}) collective-permute-start(bf16[2,128,128]{2,1,0:T(8,128)(2,1)S(1)} %copy-done.22), channel_id=1, source_target_pairs={{0,2},{1,3},{2,0},{3,1},{4,6},{5,7},{6,4},{7,5},{8,10},{9,11},{10,... | collective-permute-start | bytes 196616 | tf_op jit(solution)/shard_map/ppermute | solution.py:309
  157.7 8.5 %collective-permute-start.14 = (f32[16,32,128]{2,1,0:T(8,128)S(1)}, f32[16,32,128]{2,1,0:T(8,128)S(1)}, u32[]{:S(2)}, u32[]{:S(2)}) collective-permute-start(f32[16,32,128]{2,1,0:T(8,128)S(1)} %near_product.8), channel_id=1, source_target_pairs={{0,2},{1,3},{2,0},{3,1},{4,6},{5,7},{6,4},{7,5},{8,10},{9,11},{10,... | collective-permute-start | bytes 786440 | tf_op jit(solution)/shard_map/ppermute | solution.py:316
  (23 other events, 85.7 us)
